TPU v7x, 32 devices: a whole 2x2x4 slice. The times are simulated.
32 devices in a mesh: member: 2 (over x), patch: 8 (over z, y), feat: 2 (over core).
Axes of the slice: x: 2, y: 2, z: 4, core: 2. Of those that a mesh axis runs over, the one named last changes fastest.
Arguments:
- node_state: bfloat16 [81920, 512], P(('member', 'patch')), parts along dimension 0, may hold values from -6 to 6
- fine_tile: bfloat16 [320, 4, 128, 128], P('patch'), may hold values from -3 to 3
- coarse_tile: bfloat16 [320, 128, 160], P('patch'), may hold values from -3 to 3
- fine_index: int32 [320, 4], P('patch'), may hold values from 0 to 319, as said below
- coarse_index: int32 [320, 4], P('patch'), may hold values from 0 to 7
- node_degree: int32 [40960], P('patch'), may hold values from 4 to 12
- w_msg: bfloat16 [2, 512, 512], P(None, None, 'feat'), may hold values from -0.25 to 0.25
- w_in: bfloat16 [2, 1024, 512], P(None, None, 'feat'), may hold values from -0.1875 to 0.1875
- w_out: bfloat16 [2, 512, 512], P(None, 'feat'), may hold values from -0.25 to 0.25
Outputs:
- new_state: bfloat16 [81920, 512], P(('member', 'patch')), parts along dimension 0
There are 2 independent parts, one for each index of `member`. A program takes and returns all parts, laid end to end along the dimension named above; an argument that names none is the same for every part. Nothing has to cross between parts.
Inputs may be any that keep to these rules, and one draw needn't show every extreme that they name: `fine_index`: slot 0 of row b is b itself; every entry of row b lies within 20 blocks of the block range of the patch that holds block b, and the rows of a patch's first and last blocks reach the farthest such block on the side of a neighbouring patch.
All inputs are finite; a program needn't handle non-finite values.
Results may differ from a plain program's by a relative error of at most 0.014.
Values may be sent and summed in bfloat16 or wider, within the bound.
No kernel may reach another device: no remote copies, remote signals or barrier semaphores. Data moves between devices by JAX's collectives and lax.ppermute only.
A program may use at most 192 MiB of HBM per device.

v0:
```python
import jax
import jax.numpy as jnp
from jax import lax
from jax.sharding import PartitionSpec as P

CN_DEV = 40
LAYERS = 2
HALO_BLK = 20


def padded_2(block, sides, width):
    for axis, dim in sides:
        count = lax.axis_size(axis)
        forward = [(i, i + 1) for i in range(count - 1)]
        backward = [(target, source) for source, target in forward]
        low = lax.ppermute(
            lax.slice_in_dim(block, block.shape[dim] - width, None, axis=dim), axis, forward
        )
        high = lax.ppermute(lax.slice_in_dim(block, 0, width, axis=dim), axis, backward)
        block = jnp.concatenate([low, block, high], axis=dim)
    return block


def layer_norm(values):
    center = values - jnp.mean(values, axis=-1, keepdims=True)
    spread = jnp.mean(center * center, axis=-1, keepdims=True)
    return center * lax.rsqrt(spread + 1e-05)


def shards(
    node_state, fine_tile, coarse_tile, fine_index, coarse_index, node_degree, w_msg, w_in, w_out
):
    patch_pos = lax.axis_index("patch")
    blocks_here = fine_index.shape[0]
    block_size = fine_tile.shape[2]
    offset = patch_pos * blocks_here - HALO_BLK
    local_links = fine_index - offset
    degree = node_degree.reshape(blocks_here, block_size)
    state = node_state
    msg_weights, in_weights, out_weights = (w_msg, w_in, w_out)
    for layer_pos in range(LAYERS):
        normed = layer_norm(state.astype(jnp.float32)).astype(jnp.bfloat16)
        message = jax.nn.silu(
            jnp.dot(normed, msg_weights[layer_pos], preferred_element_type=jnp.float32)
        ).astype(jnp.bfloat16)
        source = lax.all_gather(message, "feat", axis=1, tiled=True)
        columns = source.shape[1]
        padded = padded_2(source, (("patch", 0),), HALO_BLK * block_size)
        padded_blocks = padded.reshape(blocks_here + 2 * HALO_BLK, block_size, columns)
        coarse_all = lax.all_gather(source[:CN_DEV], "patch", axis=0, tiled=True)
        coarse_blocks = coarse_all.reshape(-1, CN_DEV, columns)
        chosen = padded_blocks[local_links]
        summed = jnp.einsum("bkrs,bksw->brw", fine_tile, chosen, preferred_element_type=jnp.float32)
        coarse_chosen = coarse_blocks[coarse_index].reshape(blocks_here, -1, columns)
        summed = summed + jnp.einsum(
            "brc,bcw->brw", coarse_tile, coarse_chosen, preferred_element_type=jnp.float32
        )
        aggregate = (
            (summed / degree[:, :, None].astype(jnp.float32))
            .astype(jnp.bfloat16)
            .reshape(blocks_here * block_size, columns)
        )
        joined = layer_norm(
            jnp.concatenate([state.astype(jnp.float32), aggregate.astype(jnp.float32)], axis=1)
        ).astype(jnp.bfloat16)
        hidden = jax.nn.silu(
            jnp.dot(joined, in_weights[layer_pos], preferred_element_type=jnp.float32)
        ).astype(jnp.bfloat16)
        partial_sum = jnp.dot(hidden, out_weights[layer_pos], preferred_element_type=jnp.float32)
        update = lax.psum(partial_sum.astype(jnp.bfloat16), "feat").astype(jnp.float32)
        state = (state.astype(jnp.float32) + update).astype(jnp.bfloat16)
    return state


def solution(mesh):
    return jax.shard_map(
        shards,
        mesh=mesh,
        in_specs=(
            P(("member", "patch"), None),
            P("patch", None, None, None),
            P("patch", None, None),
            P("patch", None),
            P("patch", None),
            P("patch"),
            P(None, None, "feat"),
            P(None, None, "feat"),
            P(None, "feat", None),
        ),
        out_specs=P(("member", "patch"), None),
        check_vma=False,
    )
```

profile of v0, /device:TPU:9, one launch (start us, length us, event | category | flops | bytes accessed | tf_op | source)
XLA Modules:
  0.0 623.3 jit_solution(5034362499749522666)
XLA Ops:
  6.5 0.0 copy-start
  6.5 0.0 all-gather.3.cloned.1.call-start
  6.5 3.4 convert_reduce_fusion.1
  10.0 5.0 multiply_reduce_fusion.3
  15.0 0.0 copy-done.7
  15.0 0.0 copy-done.1
  15.0 4.3 multiply_convert_fusion.11
  19.3 0.0 all-gather.3.cloned.1.call-update
  19.3 0.0 all-reduce.3.cloned.1.call-start
  19.3 16.3 %all-gather.3.cloned.1.call-done = bf16[5120,512]{1,0:T(8,128)(2,1)} async-done(((bf16[5120,256]{1,0:T(8,128)(2,1)}), bf16[5120,512]{1,0:T(8,128)(2,1)}) %all-gather.3.cloned.1.call-update) | async-done | bytes 5242896 | tf_op jit(solution)/shard_map/all_gather | solution.py:46
  35.6 5.2 fusion.42
  40.9 3.2 collective-permute-start
  44.1 3.1 collective-permute-start.1
  47.2 7.9 %convert_element_type.98 = f32[5120,512]{1,0:T(8,128)} convert(bf16[5120,512]{1,0:T(8,128)(2,1)} %param.9) | non-fusion elementwise | flops 2621440 | bytes 15728640 | tf_op jit(solution)/shard_map/convert_element_type | solution.py:71
  55.2 0.0 copy-done.4
  55.2 0.1 copy.10
  55.3 0.1 reshape.104
  55.4 0.0 copy-done.5
  55.4 0.1 copy.11
  55.5 0.1 reshape.112
  55.6 0.0 copy-done.3
  55.6 0.0 slice-done.2
  55.6 120.1 %all_gather.13 = bf16[320,512]{1,0:T(8,128)(2,1)S(1)} all-gather(bf16[40,512]{1,0:T(8,128)(2,1)S(1)} %slice-done.2), channel_id=1, replica_groups=mesh['member'=2,'patch'=8,'feat'=2] {'patch'}, dimensions={0}, use_global_device_ids=true | all-gather | bytes 368640 | tf_op jit(solution)/shard_map/all_gather | solution.py:50
  175.7 8.5 %gather_fusion.1 = bf16[160,40,512]{2,1,0:T(8,128)(2,1)} fusion(bf16[8,40,512]{2,1,0:T(8,128)(2,1)S(1)} %bitcast.71, s32[1024]{0:T(1024)S(1)} %pad_clamp_fusion), kind=kCustom, calls=%fused_computation.1 | custom fusion | bytes 13107840 | tf_op jit(solution)/shard_map/gather | solution.py:54
  184.2 0.0 copy-done
  184.2 8.5 %fusion.45 = f32[40,512,128]{1,2,0:T(8,128)} fusion(bf16[40,160,512]{2,1,0:T(8,128)(2,1)} %bitcast.75, bf16[40,128,160]{1,2,0:T(8,128)(2,1)S(1)} %copy-done), kind=kOutput, calls=%fused_computation.80 | convolution fusion | flops 838860800 | bytes 18677760 | tf_op jit(solution)/shard_map/brc,bcw->brw/dot_general | solution.py:55
  192.8 0.0 collective-permute-done
  192.8 0.0 collective-permute-done.1
  192.8 0.0 slice-done
  192.8 0.0 slice-done.1
  192.8 19.4 %pad_maximum_fusion = bf16[10240,512]{1,0:T(8,128)(2,1)} fusion(bf16[2560,512]{1,0:T(8,128)(2,1)} %collective-permute-done.1, bf16[5120,512]{1,0:T(8,128)(2,1)S(1)} %bitcast.77, bf16[2560,512]{1,0:T(8,128)(2,1)} %collective-permute-done), kind=kLoop, calls=%fused_computation.10 | loop fusion | flops 31457280 | bytes 20971520 | tf_op jit(solution)/shard_map/concatenate | solution.py:20
  212.2 13.6 %gather_fusion = bf16[160,128,512]{2,1,0:T(8,128)(2,1)} fusion(bf16[80,128,512]{2,1,0:T(8,128)(2,1)} %bitcast.73, s32[1024]{0:T(1024)S(1)} %pad_clamp_fusion.1), kind=kCustom, calls=%fused_computation | custom fusion | bytes 41943680 | tf_op jit(solution)/shard_map/gather | solution.py:52
  225.8 17.5 %fusion.43 = (f32[40,128]{1,0:T(8,128)S(1)}, f32[40,512,128]{1,2,0:T(8,128)}) fusion(f32[40,128]{1,0:T(8,128)S(1)} %convert_bitcast_fusion, f32[40,512,128]{1,2,0:T(8,128)} %fusion.45, bf16[40,4,128,128]{3,2,1,0:T(8,128)(2,1)} %param.10, bf16[40,4,128,512]{3,2,1,0:T(8,128)(2,1)} %bitcast.81), kind=kOutput, calls=%fused_computation.78 | convolution fusion | flops 2697456640 | bytes 47226880 | tf_op jit(solution)/shard_map/bkrs,bksw->brw/dot_general | solution.py:53
  243.3 0.0 copy-start.6
  243.3 8.7 %multiply_reduce_fusion.1 = f32[5120]{0:T(1024)S(1)} fusion(f32[5120,512]{1,0:T(8,128)} %bitcast.84, f32[5120,512]{1,0:T(8,128)} %convert_element_type.98, f32[5120]{0:T(1024)S(1)} %fusion.33), kind=kLoop, calls=%fused_computation.9 | loop fusion | flops 20966400 | bytes 21012480 | tf_op jit(solution)/shard_map/reduce_sum | solution.py:26
  252.0 0.0 copy-done.6
  252.0 13.4 %convolution_convert_fusion.1 = bf16[5120,512]{1,0:T(8,128)(2,1)} fusion(f32[5120,512]{1,0:T(8,128)} %bitcast.85, f32[5120,512]{1,0:T(8,128)} %convert_element_type.98, f32[5120]{0:T(1024)S(1)} %add_rsqrt_fusion.2, f32[5120]{0:T(1024)S(1)} %fusion.33, bf16[2,1024,256]{2,1,0:T(8,128)(2,1)S(1)} %copy-done.6, bf16[2,256,512]{2,1,0:T(8,128)(2,1)} %param.17), kind=kOutput, calls=%fused_computation.29 | convolution fusion | flops 4056678400 | bytes 27041792 | tf_op jit(solution)/shard_map/dot_general | solution.py:69
  265.5 0.0 all-reduce.3.cloned.1.call-update
  265.5 0.0 all-gather.5.cloned.1.call-start
  265.6 36.4 %all-reduce.3.cloned.1.call-done = bf16[5120,512]{1,0:T(8,128)(2,1)} async-done(((bf16[5120,512]{1,0:T(8,128)(2,1)}), bf16[5120,512]{1,0:T(8,128)(2,1)}) %all-reduce.3.cloned.1.call-update) | async-done | bytes 5242896 | tf_op jit(solution)/shard_map/psum | solution.py:70
  301.9 11.9 %fusion.40 = (f32[5120,512]{1,0:T(8,128)}, bf16[5120,512]{1,0:T(8,128)(2,1)}) fusion(bf16[5120,512]{1,0:T(8,128)(2,1)} %all-reduce.3.cloned.1.call-done, bf16[5120,512]{1,0:T(8,128)(2,1)} %param.9), kind=kLoop, calls=%fused_computation.75 | loop fusion | flops 13107200 | bytes 26214400 | tf_op jit(solution)/shard_map/convert_element_type | solution.py:71
  313.9 3.4 convert_reduce_fusion
  317.3 4.9 multiply_reduce_fusion.2
  322.2 0.0 copy-done.2
  322.2 4.3 multiply_convert_fusion.9
  326.6 0.0 all-gather.5.cloned.1.call-update
  326.6 0.0 all-reduce.5.cloned.1.call-start
  326.6 15.6 %all-gather.5.cloned.1.call-done = bf16[5120,512]{1,0:T(8,128)(2,1)} async-done(((bf16[5120,256]{1,0:T(8,128)(2,1)}), bf16[5120,512]{1,0:T(8,128)(2,1)}) %all-gather.5.cloned.1.call-update) | async-done | bytes 5242896 | tf_op jit(solution)/shard_map/all_gather | solution.py:46
  342.2 5.2 fusion.41
  347.4 3.1 collective-permute-start.2
  350.5 3.1 collective-permute-start.3
  353.6 128.5 %all_gather.15 = bf16[320,512]{1,0:T(8,128)(2,1)S(1)} all-gather(bf16[40,512]{1,0:T(8,128)(2,1)S(1)} %slice-done.5), channel_id=1, replica_groups=mesh['member'=2,'patch'=8,'feat'=2] {'patch'}, dimensions={0}, use_global_device_ids=true | all-gather | bytes 368640 | tf_op jit(solution)/shard_map/all_gather | solution.py:50
  482.1 8.9 %gather_fusion.3 = bf16[160,40,512]{2,1,0:T(8,128)(2,1)} fusion(bf16[8,40,512]{2,1,0:T(8,128)(2,1)S(1)} %bitcast.70, s32[1024]{0:T(1024)S(1)} %pad_clamp_fusion), kind=kCustom, calls=%fused_computation.3 | custom fusion | bytes 13107840 | tf_op jit(solution)/shard_map/gather | solution.py:54
  491.0 8.5 %fusion.46 = f32[40,512,128]{1,2,0:T(8,128)} fusion(bf16[40,160,512]{2,1,0:T(8,128)(2,1)} %bitcast.74, bf16[40,128,160]{1,2,0:T(8,128)(2,1)S(1)} %copy-done), kind=kOutput, calls=%fused_computation.81 | convolution fusion | flops 838860800 | bytes 18677760 | tf_op jit(solution)/shard_map/brc,bcw->brw/dot_general | solution.py:55
  499.6 0.0 collective-permute-done.2
  499.6 0.0 collective-permute-done.3
  499.6 19.4 %pad_maximum_fusion.1 = bf16[10240,512]{1,0:T(8,128)(2,1)} fusion(bf16[2560,512]{1,0:T(8,128)(2,1)} %collective-permute-done.3, bf16[5120,512]{1,0:T(8,128)(2,1)S(1)} %bitcast.79, bf16[2560,512]{1,0:T(8,128)(2,1)} %collective-permute-done.2), kind=kLoop, calls=%fused_computation.11 | loop fusion | flops 31457280 | bytes 20971520 | tf_op jit(solution)/shard_map/concatenate | solution.py:20
  519.0 13.6 %gather_fusion.2 = bf16[160,128,512]{2,1,0:T(8,128)(2,1)} fusion(bf16[80,128,512]{2,1,0:T(8,128)(2,1)} %bitcast.72, s32[1024]{0:T(1024)S(1)} %pad_clamp_fusion.1), kind=kCustom, calls=%fused_computation.2 | custom fusion | bytes 41943680 | tf_op jit(solution)/shard_map/gather | solution.py:52
  532.6 17.5 %fusion.44 = (f32[40,128]{1,0:T(8,128)S(1)}, f32[40,512,128]{1,2,0:T(8,128)}) fusion(f32[40,128]{1,0:T(8,128)S(1)} %convert_bitcast_fusion, f32[40,512,128]{1,2,0:T(8,128)} %fusion.46, bf16[40,4,128,128]{3,2,1,0:T(8,128)(2,1)} %param.10, bf16[40,4,128,512]{3,2,1,0:T(8,128)(2,1)} %bitcast.80), kind=kOutput, calls=%fused_computation.79 | convolution fusion | flops 2697456640 | bytes 47226880 | tf_op jit(solution)/shard_map/bkrs,bksw->brw/dot_general | solution.py:53
  550.1 8.6 %multiply_reduce_fusion = f32[5120]{0:T(1024)S(1)} fusion(f32[5120,512]{1,0:T(8,128)} %bitcast.82, f32[5120,512]{1,0:T(8,128)} %get-tuple-element.5, f32[5120]{0:T(1024)S(1)} %fusion.32), kind=kLoop, calls=%fused_computation.7 | loop fusion | flops 20966400 | bytes 21012480 | tf_op jit(solution)/shard_map/reduce_sum | solution.py:26
  558.7 13.4 %convolution_convert_fusion = bf16[5120,512]{1,0:T(8,128)(2,1)} fusion(f32[5120,512]{1,0:T(8,128)} %bitcast.83, f32[5120,512]{1,0:T(8,128)} %get-tuple-element.5, f32[5120]{0:T(1024)S(1)} %add_rsqrt_fusion, f32[5120]{0:T(1024)S(1)} %fusion.32, bf16[2,1024,256]{2,1,0:T(8,128)(2,1)S(1)} %copy-done.6, bf16[2,256,512]{2,1,0:T(8,128)(2,1)} %param.17), kind=kOutput, calls=%fused_computation.28 | convolution fusion | flops 4056678400 | bytes 27041792 | tf_op jit(solution)/shard_map/dot_general | solution.py:69
  572.2 0.0 all-reduce.5.cloned.1.call-update
  572.2 36.4 %all-reduce.5.cloned.1.call-done = bf16[5120,512]{1,0:T(8,128)(2,1)} async-done(((bf16[5120,512]{1,0:T(8,128)(2,1)}), bf16[5120,512]{1,0:T(8,128)(2,1)}) %all-reduce.5.cloned.1.call-update) | async-done | bytes 5242896 | tf_op jit(solution)/shard_map/psum | solution.py:70
  608.6 7.9 %add_convert_fusion = bf16[5120,512]{1,0:T(8,128)(2,1)} fusion(bf16[5120,512]{1,0:T(8,128)(2,1)} %all-reduce.5.cloned.1.call-done, bf16[5120,512]{1,0:T(8,128)(2,1)} %get-tuple-element.6), kind=kLoop, calls=%fused_computation.18 | loop fusion | flops 10485760 | bytes 15728640 | tf_op jit(solution)/shard_map/convert_element_type | solution.py:71
  (32 shorter events, 0.1 us)
Async XLA Ops:
  6.5 177.7 %copy-start = (bf16[40,128,160]{1,2,0:T(8,128)(2,1)S(1)}, bf16[40,128,160]{1,2,0:T(8,128)(2,1)}, u32[]{:S(2)}) copy-start(bf16[40,128,160]{1,2,0:T(8,128)(2,1)} %param.11) | copy-start | bytes 4915204
  6.5 8.4 %copy-start.7 = (bf16[2,512,256]{2,1,0:T(8,128)(2,1)S(1)}, bf16[2,512,256]{2,1,0:T(8,128)(2,1)}, u32[]{:S(2)}) copy-start(bf16[2,512,256]{2,1,0:T(8,128)(2,1)} %param.15) | copy-start | bytes 1572868
  6.5 29.1 %all-gather.3.cloned.1.call-start = ((), (), s32[]{:S(2)}) async-start(), calls=%async_computation | async-start | bytes 7864320 | tf_op jit(solution)/shard_map/all_gather | solution.py:46
  6.5 8.4 %copy-start.1 = (bf16[5120,512]{1,0:T(8,128)(2,1)S(1)}, bf16[5120,512]{1,0:T(8,128)(2,1)}, u32[]{:S(2)}) copy-start(bf16[5120,512]{1,0:T(8,128)(2,1)} %param.9) | copy-start | bytes 15728644
  19.3 282.6 %all-reduce.3.cloned.1.call-start = ((), (), s32[]{:S(2)}) async-start(), calls=%async_computation.1 | async-start | bytes 10485760 | tf_op jit(solution)/shard_map/psum | solution.py:70
  40.9 14.3 %copy-start.4 = (s32[40,4]{0,1:T(4,128)S(1)}, s32[40,4]{0,1:T(4,128)}, u32[]{:S(2)}) copy-start(s32[40,4]{0,1:T(4,128)} %param.12) | copy-start | bytes 1924
  40.9 14.5 %copy-start.5 = (s32[40,4]{0,1:T(4,128)S(1)}, s32[40,4]{0,1:T(4,128)}, u32[]{:S(2)}) copy-start(s32[40,4]{0,1:T(4,128)} %param.13) | copy-start | bytes 1924
  40.9 14.7 %copy-start.3 = (s32[5120]{0:T(1024)S(1)}, s32[5120]{0:T(1024)}, u32[]{:S(2)}) copy-start(s32[5120]{0:T(1024)} %param.14) | copy-start | bytes 61444
  40.9 14.7 %slice-start.2 = ((bf16[5120,512]{1,0:T(8,128)(2,1)}), bf16[40,512]{1,0:T(8,128)(2,1)S(1)}, s32[]{:S(2)}) async-start(bf16[5120,512]{1,0:T(8,128)(2,1)} %all-gather.3.cloned.1.call-done), calls=%async_computation.6 | async-start | bytes 81920 | tf_op jit(solution)/shard_map/slice | solution.py:50
  40.9 151.9 %collective-permute-start = (bf16[2560,512]{1,0:T(8,128)(2,1)}, bf16[2560,512]{1,0:T(8,128)(2,1)}, u32[]{:S(2)}, u32[]{:S(2)}) collective-permute-start(bf16[2560,512]{1,0:T(8,128)(2,1)} %get-tuple-element.9), channel_id=1, source_target_pairs={{0,2},{2,4},{4,6},{6,8},{8,10},{10,12},{12,14},{1,3},{3,5},{5,7},{... | collective-permute-start | bytes 7864328 | tf_op jit(solution)/shard_map/ppermute | solution.py:16
  44.1 148.6 %collective-permute-start.1 = (bf16[2560,512]{1,0:T(8,128)(2,1)}, bf16[2560,512]{1,0:T(8,128)(2,1)}, u32[]{:S(2)}, u32[]{:S(2)}) collective-permute-start(bf16[2560,512]{1,0:T(8,128)(2,1)} %get-tuple-element.10), channel_id=1, source_target_pairs={{2,0},{4,2},{6,4},{8,6},{10,8},{12,10},{14,12},{3,1},{5,3},{7,5},{... | collective-permute-start | bytes 7864328 | tf_op jit(solution)/shard_map/ppermute | solution.py:19
  184.2 8.5 %slice-start = ((s8[5242880]{0:T(1024)(128)(4,1)}), s8[4194304]{0:T(1024)(128)(4,1)S(1)}, s32[]{:S(2)}) async-start(s8[5242880]{0:T(1024)(128)(4,1)} %bitcast.76), calls=%async_computation.4 | async-start | bytes 8388608
  184.2 8.5 %slice-start.1 = ((s8[5242880]{0:T(1024)(128)(4,1)}), s8[1048576]{0:T(1024)(128)(4,1)S(1)}, s32[]{:S(2)}) async-start(s8[5242880]{0:T(1024)(128)(4,1)} %bitcast.76), calls=%async_computation.5 | async-start | bytes 2097152
  243.3 8.8 %copy-start.6 = (bf16[2,1024,256]{2,1,0:T(8,128)(2,1)S(1)}, bf16[2,1024,256]{2,1,0:T(8,128)(2,1)}, u32[]{:S(2)}) copy-start(bf16[2,1024,256]{2,1,0:T(8,128)(2,1)} %param.16) | copy-start | bytes 3145732
  265.5 76.7 %all-gather.5.cloned.1.call-start = ((), (), s32[]{:S(2)}) async-start(), calls=%async_computation.2 | async-start | bytes 7864320 | tf_op jit(solution)/shard_map/all_gather | solution.py:46
  313.9 8.3 %copy-start.2 = (bf16[5120,512]{1,0:T(8,128)(2,1)S(1)}, bf16[5120,512]{1,0:T(8,128)(2,1)}, u32[]{:S(2)}) copy-start(bf16[5120,512]{1,0:T(8,128)(2,1)} %get-tuple-element.6) | copy-start | bytes 15728644
  313.9 8.3 %copy-start.8 = (bf16[2,512,256]{2,1,0:T(8,128)(2,1)S(1)}, bf16[2,512,256]{2,1,0:T(8,128)(2,1)}, u32[]{:S(2)}) copy-start(bf16[2,512,256]{2,1,0:T(8,128)(2,1)} %param.15) | copy-start | bytes 1572868
  326.6 282.0 %all-reduce.5.cloned.1.call-start = ((), (), s32[]{:S(2)}) async-start(), calls=%async_computation.3 | async-start | bytes 10485760 | tf_op jit(solution)/shard_map/psum | solution.py:70
  342.2 11.4 %slice-start.5 = ((bf16[5120,512]{1,0:T(8,128)(2,1)}), bf16[40,512]{1,0:T(8,128)(2,1)S(1)}, s32[]{:S(2)}) async-start(bf16[5120,512]{1,0:T(8,128)(2,1)} %all-gather.5.cloned.1.call-done), calls=%async_computation.9 | async-start | bytes 81920 | tf_op jit(solution)/shard_map/slice | solution.py:50
  347.4 152.1 %collective-permute-start.2 = (bf16[2560,512]{1,0:T(8,128)(2,1)}, bf16[2560,512]{1,0:T(8,128)(2,1)}, u32[]{:S(2)}, u32[]{:S(2)}) collective-permute-start(bf16[2560,512]{1,0:T(8,128)(2,1)} %get-tuple-element.7), channel_id=1, source_target_pairs={{0,2},{2,4},{4,6},{6,8},{8,10},{10,12},{12,14},{1,3},{3,5},{5,7},{... | collective-permute-start | bytes 7864328 | tf_op jit(solution)/shard_map/ppermute | solution.py:16
  350.5 149.0 %collective-permute-start.3 = (bf16[2560,512]{1,0:T(8,128)(2,1)}, bf16[2560,512]{1,0:T(8,128)(2,1)}, u32[]{:S(2)}, u32[]{:S(2)}) collective-permute-start(bf16[2560,512]{1,0:T(8,128)(2,1)} %get-tuple-element.8), channel_id=1, source_target_pairs={{2,0},{4,2},{6,4},{8,6},{10,8},{12,10},{14,12},{3,1},{5,3},{7,5},{... | collective-permute-start | bytes 7864328 | tf_op jit(solution)/shard_map/ppermute | solution.py:19
  491.0 8.5 %slice-start.3 = ((s8[5242880]{0:T(1024)(128)(4,1)}), s8[4194304]{0:T(1024)(128)(4,1)S(1)}, s32[]{:S(2)}) async-start(s8[5242880]{0:T(1024)(128)(4,1)} %bitcast.78), calls=%async_computation.7 | async-start | bytes 8388608
  491.0 8.5 %slice-start.4 = ((s8[5242880]{0:T(1024)(128)(4,1)}), s8[1048576]{0:T(1024)(128)(4,1)S(1)}, s32[]{:S(2)}) async-start(s8[5242880]{0:T(1024)(128)(4,1)} %bitcast.78), calls=%async_computation.8 | async-start | bytes 2097152
Sparse Core Ops, SparseCore 0:
  19.4 16.1 all-gather.2
  265.6 36.2 all-reduce.2
  326.7 15.4 all-gather.4
  572.3 36.2 all-reduce.4
where the time goes:
time: 628 us; the launch traced here: 623 us
  blocking collectives  249 us (40%)
  waiting for transfers between devices  105 us (17%)
  other arithmetic  101 us (16%)
  matrix products  87.5 us (14%)
  local copies, waits for them, and re-layouts  55.5 us (9%)
  between operations  13.6 us (2%)
  starting transfers between devices  12.6 us (2%)
    all_gather x2, blocking collectives, shards(): coarse_all = lax.all_gather(source[:CN_DEV], 'patch', axis=0, tiled=True)  249 us
    psum x2, waiting for transfers between devices, shards(): lax.psum(partial_sum.astype(jnp.bfloat16), 'feat').astype(jnp.float32)  72.8 us
    concatenate x2, other arithmetic, padded_2(): block = jnp.concatenate([low, block, high], axis=dim)  38.7 us
    dot_general x2, matrix products, shards(): jnp.einsum('bkrs,bksw->brw', fine_tile, chosen, preferred_element_type=jn...  34.9 us
    all_gather x2, waiting for transfers between devices, shards(): source = lax.all_gather(message, 'feat', axis=1, tiled=True)  31.9 us
    convert_element_type x3, other arithmetic, shards(): state = (state.astype(jnp.float32) + update).astype(jnp.bfloat16)  27.8 us
    gather x2, local copies, waits for them, and re-layouts, shards(): chosen = padded_blocks[local_links]  27.3 us
    reduce_sum x4, other arithmetic, layer_norm(): spread = jnp.mean(center * center, axis=-1, keepdims=True)  27.2 us
  transfers between devices with their start and end apart: 8, of which 4 were waited for; matrix products, arithmetic and copies ran while one was open for 7% of the time, Pallas kernels for 0%

commit v1 on v0

v1 whole, which is shorter than its diff:
```python
import functools

import jax
import jax.numpy as jnp
from jax import lax
from jax.experimental import pallas as pl
from jax.experimental.pallas import tpu as pltpu
from jax.sharding import PartitionSpec as P

CN_DEV = 40
LAYERS = 2
HALO_BLK = 20
CHUNKS = 2
ROW_TILE = 256
BLOCK_STEP = 5
VMEM_BYTES = 56 << 20
F32 = jnp.float32
BF16 = jnp.bfloat16


def silu(v):
    return 0.5 * v * (1.0 + jnp.tanh(0.5 * v))


def dot(a, b):
    return jnp.dot(a, b, preferred_element_type=F32)


def normalize(parts):
    width = sum(part.shape[-1] for part in parts)
    mean = sum(jnp.sum(part, axis=-1, keepdims=True) for part in parts) / width
    center = [part - mean for part in parts]
    spread = sum(jnp.sum(part * part, axis=-1, keepdims=True) for part in center) / width
    scale = lax.rsqrt(spread + 1e-05)
    return [(part * scale).astype(BF16) for part in center]


def params():
    return pltpu.CompilerParams(vmem_limit_bytes=VMEM_BYTES)


def message_kernel(state_ref, weight_ref, out_ref):
    (normed,) = normalize([state_ref[...].astype(F32)])
    out_ref[...] = silu(dot(normed, weight_ref[...])).astype(BF16)


def message_call(state, weight, start, rows, tile):
    first = start // tile
    return pl.pallas_call(
        message_kernel,
        grid=(rows // tile,),
        in_specs=[
            pl.BlockSpec((tile, state.shape[1]), lambda i: (first + i, 0)),
            pl.BlockSpec(weight.shape, lambda i: (0, 0)),
        ],
        out_specs=pl.BlockSpec((tile, weight.shape[1]), lambda i: (i, 0)),
        out_shape=jax.ShapeDtypeStruct((rows, weight.shape[1]), BF16),
        compiler_params=params(),
        name="message",
    )(state, weight)


def aggregate_kernel(pieces, chunk, half, scal, *refs):
    piece_refs = refs[:pieces]
    coarse_ref, fine_ref, ctile_ref, degree_ref, send_ref, keep_ref, table, coarse_f32, sems = refs[pieces:]
    slot = pl.program_id(0)
    step = pl.program_id(1)
    copies = [
        pltpu.make_async_copy(ref, table.at[pl.ds(scal[1 + pos], ref.shape[0])], sems.at[pos])
        for pos, ref in enumerate(piece_refs)
    ]

    @pl.when((slot == 0) & (step == 0))
    def _():
        for copy in copies:
            copy.start()
        coarse_f32[...] = coarse_ref[...].astype(F32)
        for copy in copies:
            copy.wait()

    feat = scal[0]
    which = jnp.where(slot == 0, 1 - feat, feat)
    count, block, _ = ctile_ref.shape
    kinds = fine_ref.shape[1]
    first = which * half + chunk * (half // CHUNKS) + step * count
    base = 1 + pieces
    coarse_base = base + 2 * half * kinds
    degree = jnp.transpose(degree_ref[0].astype(F32))
    results = []
    for pos in range(count):
        row = (first + pos) * kinds
        chosen = jnp.concatenate([table[scal[base + row + k]] for k in range(kinds)], axis=0)
        tiles = jnp.concatenate([fine_ref[pos, k] for k in range(kinds)], axis=1)
        stacked = jnp.concatenate(
            [
                coarse_f32[pl.ds(pl.multiple_of(scal[coarse_base + row + k], 8), CN_DEV), :]
                for k in range(kinds)
            ],
            axis=0,
        ).astype(BF16)
        summed = dot(tiles, chosen) + dot(ctile_ref[pos], stacked)
        results.append((summed / degree[:, pos : pos + 1]).astype(BF16))

    @pl.when(slot == 0)
    def _():
        for pos in range(count):
            send_ref[pos * block : (pos + 1) * block, :] = results[pos]

    @pl.when(slot == 1)
    def _():
        for pos in range(count):
            keep_ref[pos * block : (pos + 1) * block, :] = results[pos]


def aggregate_call(scal, pieces, coarse, fine_tile, coarse_tile, degree, chunk):
    blocks, kinds, block, _ = fine_tile.shape
    half = blocks // 2
    steps = half // CHUNKS // BLOCK_STEP
    columns = coarse.shape[1]
    rows = half // CHUNKS * block

    def place(slot, step, scal):
        which = jnp.where(slot == 0, 1 - scal[0], scal[0])
        return which * (half // BLOCK_STEP) + chunk * steps + step

    table_blocks = sum(piece.shape[0] for piece in pieces)
    return pl.pallas_call(
        functools.partial(aggregate_kernel, len(pieces), chunk, half),
        grid_spec=pltpu.PrefetchScalarGridSpec(
            num_scalar_prefetch=1,
            grid=(2, steps),
            in_specs=[pl.BlockSpec(memory_space=pl.ANY) for _ in pieces]
            + [
                pl.BlockSpec(coarse.shape, lambda s, i, scal: (0, 0)),
                pl.BlockSpec((BLOCK_STEP, kinds, block, block), lambda s, i, scal: (place(s, i, scal), 0, 0, 0)),
                pl.BlockSpec((BLOCK_STEP, block, coarse_tile.shape[2]), lambda s, i, scal: (place(s, i, scal), 0, 0)),
                pl.BlockSpec((1, BLOCK_STEP, block), lambda s, i, scal: (place(s, i, scal), 0, 0)),
            ],
            out_specs=[
                pl.BlockSpec((BLOCK_STEP * block, columns), lambda s, i, scal: (jnp.where(s == 0, i, steps - 1), 0)),
                pl.BlockSpec((BLOCK_STEP * block, columns), lambda s, i, scal: (jnp.where(s == 1, i, 0), 0)),
            ],
            scratch_shapes=[
                pltpu.VMEM((table_blocks, block, columns), BF16),
                pltpu.VMEM(coarse.shape, F32),
                pltpu.SemaphoreType.DMA((len(pieces),)),
            ],
        ),
        out_shape=[jax.ShapeDtypeStruct((rows, columns), BF16)] * 2,
        compiler_params=params(),
        name="aggregate",
    )(scal, *pieces, coarse, fine_tile, coarse_tile, degree)


def node_kernel(last, scal, state_ref, keep_ref, recv_ref, in_own, in_other, out_own, out_other, *refs):
    feat = scal[0]
    width = state_ref.shape[1]
    columns = keep_ref.shape[1]
    state = state_ref[...].astype(F32)
    joined = normalize([state, keep_ref[...].astype(F32), recv_ref[...].astype(F32)])
    keep_at = pl.multiple_of(width + feat * columns, columns)
    recv_at = pl.multiple_of(width + (1 - feat) * columns, columns)
    update = None
    for in_ref, out_ref in ((in_own, out_own), (in_other, out_other)):
        hidden = (
            dot(joined[0], in_ref[0, :width, :])
            + dot(joined[1], in_ref[0, pl.ds(keep_at, columns), :])
            + dot(joined[2], in_ref[0, pl.ds(recv_at, columns), :])
        )
        part = dot(silu(hidden).astype(BF16), out_ref[0])
        update = part if update is None else update + part
    new_state = (state + update).astype(BF16)
    if last:
        (state_out,) = refs
        state_out[...] = new_state
        return
    msg_own, msg_other, state_out, own_out, other_out = refs
    state_out[...] = new_state
    (normed,) = normalize([new_state.astype(F32)])
    own_out[...] = silu(dot(normed, msg_own[0])).astype(BF16)
    other_out[...] = silu(dot(normed, msg_other[0])).astype(BF16)


def node_call(scal, state, per_half, chunk, keep, recv, weights_in, weights_out, weights_msg, layer):
    rows, columns = keep.shape
    width = state.shape[1]
    last = weights_msg is None
    steps = rows // ROW_TILE

    def place(i, scal):
        return (scal[0] * per_half + chunk) * steps + i, 0

    def whole(array, at):
        return pl.BlockSpec((1,) + array.shape[1:], lambda i, scal: (at, 0, 0))

    tile = pl.BlockSpec((ROW_TILE, columns), lambda i, scal: (i, 0))
    operands = [state, keep, recv, *weights_in, *weights_out]
    in_specs = [pl.BlockSpec((ROW_TILE, width), place), tile, tile]
    in_specs += [whole(array, layer) for array in (*weights_in, *weights_out)]
    out_specs = [pl.BlockSpec((ROW_TILE, width), lambda i, scal: (i, 0))]
    out_shape = [jax.ShapeDtypeStruct((rows, width), BF16)]
    if not last:
        operands += list(weights_msg)
        in_specs += [whole(array, layer) for array in weights_msg]
        out_specs += [tile, tile]
        out_shape += [jax.ShapeDtypeStruct((rows, columns), BF16)] * 2
    return pl.pallas_call(
        functools.partial(node_kernel, last),
        grid_spec=pltpu.PrefetchScalarGridSpec(
            num_scalar_prefetch=1, grid=(steps,), in_specs=in_specs, out_specs=out_specs
        ),
        out_shape=out_shape,
        compiler_params=params(),
        name="node",
    )(scal, *operands)


def assemble_kernel(pieces, scal, *refs):
    piece_refs = refs[:pieces]
    out_ref, sems = refs[pieces:]
    copies = [
        pltpu.make_async_copy(
            ref, out_ref.at[pl.ds(pl.multiple_of(scal[pos], 8), ref.shape[0])], sems.at[pos]
        )
        for pos, ref in enumerate(piece_refs)
    ]
    for copy in copies:
        copy.start()
    for copy in copies:
        copy.wait()


def assemble_call(offsets, pieces):
    rows = sum(piece.shape[0] for piece in pieces)
    return pl.pallas_call(
        functools.partial(assemble_kernel, len(pieces)),
        grid_spec=pltpu.PrefetchScalarGridSpec(
            num_scalar_prefetch=1,
            in_specs=[pl.BlockSpec(memory_space=pl.ANY) for _ in pieces],
            out_specs=pl.BlockSpec(memory_space=pl.ANY),
            scratch_shapes=[pltpu.SemaphoreType.DMA((len(pieces),))],
        ),
        out_shape=jax.ShapeDtypeStruct((rows, pieces[0].shape[1]), pieces[0].dtype),
        compiler_params=params(),
        name="assemble",
    )(offsets, *pieces)


def swap_feat(array):
    return lax.ppermute(array, "feat", [(0, 1), (1, 0)])


def gather_patches(rows):
    count = lax.axis_size("patch")
    held = rows
    have = 1
    while have < count:
        more = min(have, count - have)
        pairs = [(pos, (pos - have) % count) for pos in range(count)]
        got = lax.ppermute(held[: more * rows.shape[0]], "patch", pairs)
        held = jnp.concatenate([held, got], axis=0)
        have += more
    return held


def shards(
    node_state, fine_tile, coarse_tile, fine_index, coarse_index, node_degree, w_msg, w_in, w_out
):
    patches = lax.axis_size("patch")
    patch_pos = lax.axis_index("patch")
    feat = lax.axis_index("feat")
    blocks, kinds, block, _ = fine_tile.shape
    half = blocks // 2
    half_rows = half * block
    halo_rows = HALO_BLK * block
    assert half == HALO_BLK and half % (CHUNKS * BLOCK_STEP) == 0
    columns = w_msg.shape[2]
    degree = node_degree.reshape(blocks // BLOCK_STEP, BLOCK_STEP, block)

    links = (fine_index - (patch_pos * blocks - HALO_BLK)).reshape(-1)
    coarse_links = ((coarse_index - patch_pos) % patches * CN_DEV).reshape(-1)

    def scalars(*places):
        head = jnp.stack([jnp.asarray(value, jnp.int32) for value in (feat, *places)])
        return jnp.concatenate([head, links, coarse_links])

    forward = [(pos, pos + 1) for pos in range(patches - 1)]
    backward = [(target, source) for source, target in forward]
    coarse_state = gather_patches(node_state[:CN_DEV])

    low = message_call(node_state, w_msg[0], 0, half_rows, 512)
    high_halo = lax.ppermute(low, "patch", backward)
    high = message_call(node_state, w_msg[0], half_rows, half_rows, 512)
    low_halo = lax.ppermute(high, "patch", forward)
    w_in, w_out, w_msg_late, _ = lax.optimization_barrier((w_in, w_out, w_msg[1:], high))
    weights_in = (w_in, swap_feat(w_in))
    weights_out = (w_out, swap_feat(w_out))
    weights_msg = (w_msg_late, swap_feat(w_msg_late))
    coarse = message_call(coarse_state, w_msg[0], 0, coarse_state.shape[0], coarse_state.shape[0])

    own_patch = [(2 * src + side, 2 * dst + side) for side, pairs in ((0, backward), (1, forward)) for src, dst in pairs]
    other_patch = [(2 * src + side, 2 * dst + 1 - side) for side, pairs in ((0, backward), (1, forward)) for src, dst in pairs]

    pieces = [low_halo, low, high, high_halo]
    scal = scalars(0, HALO_BLK, HALO_BLK + half, HALO_BLK + blocks)
    chunk_blocks = half // CHUNKS
    late_places = []
    for chunk in range(CHUNKS):
        at = chunk * chunk_blocks
        own = HALO_BLK + feat * half + at
        other = HALO_BLK + (1 - feat) * half + at
        near = jnp.where(feat == 0, HALO_BLK + blocks, 0) + at
        far = jnp.where(feat == 0, 0, HALO_BLK + blocks) + at
        late_places += [own, other, near, far]
    late_scal = scalars(*late_places)

    states = [node_state] * CHUNKS
    for layer in range(LAYERS):
        last = layer == LAYERS - 1
        shaped = [piece.reshape(-1, block, columns) for piece in pieces]
        sums = [
            aggregate_call(scal, shaped, coarse, fine_tile, coarse_tile, degree, chunk)
            for chunk in range(CHUNKS)
        ]
        received = [swap_feat(send) for send, _ in sums]
        new_states = []
        pieces = []
        for chunk in range(CHUNKS):
            results = node_call(
                scal, states[chunk], CHUNKS if layer == 0 else 0, chunk if layer == 0 else 0,
                sums[chunk][1], received[chunk], weights_in, weights_out,
                None if last else weights_msg, layer,
            )
            new_states.append(results[0])
            if not last:
                own, other = results[1:]
                near = lax.ppermute(own, ("patch", "feat"), own_patch)
                far = lax.ppermute(other, ("patch", "feat"), other_patch)
                sibling = swap_feat(other)
                pieces += [own, sibling, near, far]
                if chunk == 0:
                    mine = jnp.where(feat == 0, own[:CN_DEV], sibling[:CN_DEV])
                    coarse = gather_patches(mine)
        states = new_states
        scal = late_scal

    parts = []
    offsets = []
    chunk_rows = half_rows // CHUNKS
    for chunk in range(CHUNKS):
        parts += [states[chunk], swap_feat(states[chunk])]
        offsets += [feat * half_rows + chunk * chunk_rows, (1 - feat) * half_rows + chunk * chunk_rows]
    return assemble_call(jnp.stack(offsets).astype(jnp.int32), parts)


def solution(mesh):
    return jax.shard_map(
        shards,
        mesh=mesh,
        in_specs=(
            P(("member", "patch"), None),
            P("patch", None, None, None),
            P("patch", None, None),
            P("patch", None),
            P("patch", None),
            P("patch"),
            P(None, None, "feat"),
            P(None, None, "feat"),
            P(None, "feat", None),
        ),
        out_specs=P(("member", "patch"), None),
        check_vma=False,
    )
```

time: 628 us -> 400 us (0.64)
  blocking collectives: 249 us -> 0 us
  Pallas kernels: 0 us -> 245 us
  other arithmetic: 101 us -> 5.23 us
  matrix products: 87.5 us -> 0 us
  local copies, waits for them, and re-layouts: 55.5 us -> 15.9 us
  starting transfers between devices: 12.6 us -> 37.5 us
  between operations: 13.6 us -> 0.26 us
  waiting for transfers between devices: 105 us -> 94.8 us
    all_gather x2 -> x0, blocking collectives: 249 us -> none  [shards(): coarse_all = lax.all_gather(source[:CN_DEV], 'patch', axis=0, tiled=True)]
    pallas_call x0 -> x12, Pallas kernels: none -> 245 us  [the longest x1 161 us: assemble_call(): pl.pallas_call(functools.partial(assemble_kernel, len(pieces)), grid_spec...]
    ppermute x4 -> x23, waiting for transfers between devices: 0.01 us -> 94.8 us  [the longest x6 53.7 us: gather_patches(): got = lax.ppermute(held[:more * rows.shape[0]], 'patch', pairs)]
    dot_general x8 -> x0, matrix products: 87.5 us -> none  [the longest x2 34.9 us: shards(): jnp.einsum('bkrs,bksw->brw', fine_tile, chosen, preferred_element_type=jn...]
    psum x2 -> x0, waiting for transfers between devices: 72.8 us -> none  [shards(): lax.psum(partial_sum.astype(jnp.bfloat16), 'feat').astype(jnp.float32)]
    gather x4 -> x0, local copies, waits for them, and re-layouts: 44.7 us -> none  [the longest x2 27.3 us: shards(): chosen = padded_blocks[local_links]]
    concatenate x2 -> x6, other arithmetic: 38.7 us -> 4.6 us  [gather_patches(): held = jnp.concatenate([held, got], axis=0)]
    reduce_sum x6 -> x0, other arithmetic: 34 us -> none  [the longest x4 27.2 us: layer_norm(): spread = jnp.mean(center * center, axis=-1, keepdims=True)]
  transfers between devices with their start and end apart: 8 -> 23, of which waited for: 4 -> 10; matrix products, arithmetic and copies ran while one was open for 7% -> 3% of each run, Pallas kernels for 0% -> 15%
where the time goes in v1:
time: 400 us; the launch traced here: 399 us
  Pallas kernels  245 us (61%)
  waiting for transfers between devices  94.8 us (24%)
  starting transfers between devices  37.5 us (9%)
  local copies, waits for them, and re-layouts  15.9 us (4%)
  other arithmetic  5.23 us (1%)
    pallas_call x1, Pallas kernels, assemble_call(): pl.pallas_call(functools.partial(assemble_kernel, len(pieces)), grid_spec...  161 us
    ppermute x6, waiting for transfers between devices, gather_patches(): got = lax.ppermute(held[:more * rows.shape[0]], 'patch', pairs)  53.7 us
    pallas_call x4, Pallas kernels, node_call(): pl.pallas_call(functools.partial(node_kernel, last), grid_spec=pltpu.Pref...  36.9 us
    pallas_call x4, Pallas kernels, aggregate_call(): pl.pallas_call(functools.partial(aggregate_kernel, len(pieces), chunk, ha...  34 us
    ppermute x2, waiting for transfers between devices, shards(): far = lax.ppermute(other, ('patch', 'feat'), other_patch)  24.9 us
    pallas_call x3, Pallas kernels, message_call(): pl.pallas_call(message_kernel, grid=(rows // tile,), in_specs=[pl.BlockSp...  13.8 us
    ppermute x2, waiting for transfers between devices, shards(): near = lax.ppermute(own, ('patch', 'feat'), own_patch)  11.6 us
    unnamed x45, local copies, waits for them, and re-layouts  10.9 us
  transfers between devices with their start and end apart: 23, of which 10 were waited for; matrix products, arithmetic and copies ran while one was open for 3% of the time, Pallas kernels for 15%

profile of v1, /device:TPU:9, one launch (start us, length us, event | category | flops | bytes accessed | tf_op | source)
XLA Modules:
  0.0 399.1 jit_solution(4721286612592735751)
XLA Ops:
  0.0 1.9 fusion.2
  1.9 5.8 %message.4 = bf16[2560,256]{1,0:T(8,128)(2,1)} custom-call(bf16[5120,512]{1,0:T(8,128)(2,1)} %state_ref.7, bf16[512,256]{1,0:T(8,128)(2,1)} %get-tuple-element.40.weight_ref), custom_call_target="tpu_custom_call" | custom-call | tf_op jit(solution)/shard_map/message/pallas_call | solution.py:49
  7.7 3.2 collective-permute-start.1
  10.9 5.9 %message.3 = bf16[2560,256]{1,0:T(8,128)(2,1)} custom-call(bf16[5120,512]{1,0:T(8,128)(2,1)} %state_ref.7, bf16[512,256]{1,0:T(8,128)(2,1)} %get-tuple-element.40.weight_ref), custom_call_target="tpu_custom_call" | custom-call | tf_op jit(solution)/shard_map/message/pallas_call | solution.py:49
  16.8 2.2 collective-permute-start
  19.0 0.8 slice.18
  19.8 2.0 collective-permute-start.2
  21.8 1.5 collective-permute-start.6
  23.3 45.2 %collective-permute-done.2 = bf16[40,512]{1,0:T(8,128)(2,1)S(1)} collective-permute-done((bf16[40,512]{1,0:T(8,128)(2,1)S(1)}, bf16[40,512]{1,0:T(8,128)(2,1)S(1)}, u32[]{:S(2)}, u32[]{:S(2)}) %collective-permute-start.2) | collective-permute-done | bytes 40992 | tf_op jit(solution)/shard_map/ppermute | solution.py:260
  68.6 0.6 pad_maximum_fusion.3
  69.3 0.1 reshape.46
  69.4 3.4 collective-permute-done.3
  72.8 1.6 pad_maximum_fusion.1
  74.4 4.1 %collective-permute-start.4 = (bf16[160,512]{1,0:T(8,128)(2,1)}, bf16[160,512]{1,0:T(8,128)(2,1)}, u32[]{:S(2)}, u32[]{:S(2)}) collective-permute-start(bf16[160,512]{1,0:T(8,128)(2,1)} %pad_maximum_fusion.1), channel_id=1, source_target_pairs={{0,8},{2,10},{4,12},{6,14},{8,0},{10,2},{12,4},{14,6},{1,9},{3,11}... | collective-permute-start | bytes 491528 | tf_op jit(solution)/shard_map/ppermute | solution.py:260
  78.5 0.1 copy.14
  78.6 0.1 reshape.45
  78.7 0.6 reshape.51.refs_7_.refs_11_
  79.3 3.9 copy.16.refs_6_.refs_10_
  83.3 0.7 concatenate.29.scal
  84.0 1.7 pad_maximum_fusion.state_ref
  85.7 2.2 message.5.refs_4_
  87.8 1.1 copy-done.4
  88.9 8.6 %aggregate.4 = (bf16[1280,256]{1,0:T(8,128)(2,1)}, bf16[1280,256]{1,0:T(8,128)(2,1)}) custom-call(s32[325]{0:T(512)} %concatenate.29.scal, bf16[20,128,256]{2,1,0:T(8,128)(2,1)} %bitcast.14.refs_0_, bf16[20,128,256]{2,1,0:T(8,128)(2,1)} %bitcast.27, bf16[20,128,256]{2,1,0:T(8,128)(2,1)} %bitcast.29, bf16[20,128,256]{2,1,0:T(8,128)(2,1)} %bitcast.31, ...), custom_call_target="tpu_custom_call" | custom-call | tf_op jit(solution)/shard_map/aggregate/pallas_call | solution.py:127
  97.5 3.0 collective-permute-start.5
  100.6 0.4 collective-permute-start.8
  101.1 2.3 collective-permute-done.8.refs_1_
  103.4 0.7 copy-done.14
  104.1 0.2 copy-done.3
  104.3 0.3 copy-done.1
  104.6 0.2 copy-done.16
  104.8 10.3 %node.4 = (bf16[1280,512]{1,0:T(8,128)(2,1)}, bf16[1280,256]{1,0:T(8,128)(2,1)}, bf16[1280,256]{1,0:T(8,128)(2,1)}) custom-call(s32[325]{0:T(512)} %concatenate.29.scal, bf16[5120,512]{1,0:T(8,128)(2,1)} %state_ref.7, bf16[1280,256]{1,0:T(8,128)(2,1)} %get-tuple-element.22.keep_ref, bf16[1280,256]{1,0:T(8,128)(2,1)} %copy-done.16, ...), custom_call_target="tpu_custom_call" | custom-call | tf_op jit(solution)/shard_map/node/pallas_call | solution.py:207
  115.1 0.4 collective-permute-start.9
  115.5 8.5 %aggregate.5 = (bf16[1280,256]{1,0:T(8,128)(2,1)}, bf16[1280,256]{1,0:T(8,128)(2,1)}) custom-call(s32[325]{0:T(512)} %concatenate.29.scal, bf16[20,128,256]{2,1,0:T(8,128)(2,1)} %bitcast.14.refs_0_, bf16[20,128,256]{2,1,0:T(8,128)(2,1)} %bitcast.28, bf16[20,128,256]{2,1,0:T(8,128)(2,1)} %bitcast.30, bf16[20,128,256]{2,1,0:T(8,128)(2,1)} %bitcast.32, ...), custom_call_target="tpu_custom_call" | custom-call | tf_op jit(solution)/shard_map/aggregate/pallas_call | solution.py:127
  124.0 0.3 collective-permute-start.12
  124.5 2.6 collective-permute-done.16
  127.1 0.4 collective-permute-start.17
  127.5 2.5 collective-permute-done.17
  129.9 2.8 collective-permute-start.18
  132.8 7.1 %collective-permute-start.11 = (bf16[1280,256]{1,0:T(8,128)(2,1)}, bf16[1280,256]{1,0:T(8,128)(2,1)S(1)}, u32[]{:S(2)}, u32[]{:S(2)}) collective-permute-start(bf16[1280,256]{1,0:T(8,128)(2,1)} %get-tuple-element.29), channel_id=1, source_target_pairs={{2,1},{4,3},{6,5},{8,7},{10,9},{12,11},{14,13},{1,2},{3,4},{5,6},{... | collective-permute-start | bytes 1966088 | tf_op jit(solution)/shard_map/ppermute | solution.py:338
  139.9 1.9 collective-permute-start.10
  141.9 0.8 copy-done.15
  142.7 10.3 %node.5 = (bf16[1280,512]{1,0:T(8,128)(2,1)}, bf16[1280,256]{1,0:T(8,128)(2,1)}, bf16[1280,256]{1,0:T(8,128)(2,1)}) custom-call(s32[325]{0:T(512)} %concatenate.29.scal, bf16[5120,512]{1,0:T(8,128)(2,1)} %state_ref.7, bf16[1280,256]{1,0:T(8,128)(2,1)} %get-tuple-element.30.keep_ref, bf16[1280,256]{1,0:T(8,128)(2,1)} %copy-done.15, ...), custom_call_target="tpu_custom_call" | custom-call | tf_op jit(solution)/shard_map/node/pallas_call | solution.py:207
  153.0 1.9 collective-permute-start.14
  155.0 1.9 collective-permute-start.15
  156.9 2.8 collective-permute-start.13
  159.7 0.7 concatenate.28.scal
  160.4 0.7 pad_maximum_fusion.2.refs_8_
  161.1 15.4 %collective-permute-done.11 = bf16[1280,256]{1,0:T(8,128)(2,1)S(1)} collective-permute-done((bf16[1280,256]{1,0:T(8,128)(2,1)}, bf16[1280,256]{1,0:T(8,128)(2,1)S(1)}, u32[]{:S(2)}, u32[]{:S(2)}) %collective-permute-start.11) | collective-permute-done | bytes 655392 | tf_op jit(solution)/shard_map/ppermute | solution.py:338
  176.5 4.5 %collective-permute-done.10 = bf16[1280,256]{1,0:T(8,128)(2,1)S(1)} collective-permute-done((bf16[1280,256]{1,0:T(8,128)(2,1)S(1)}, bf16[1280,256]{1,0:T(8,128)(2,1)S(1)}, u32[]{:S(2)}, u32[]{:S(2)}) %collective-permute-start.10) | collective-permute-done | bytes 655392 | tf_op jit(solution)/shard_map/ppermute | solution.py:337
  180.9 7.1 %collective-permute-done.14 = bf16[1280,256]{1,0:T(8,128)(2,1)S(1)} collective-permute-done((bf16[1280,256]{1,0:T(8,128)(2,1)}, bf16[1280,256]{1,0:T(8,128)(2,1)S(1)}, u32[]{:S(2)}, u32[]{:S(2)}) %collective-permute-start.14) | collective-permute-done | bytes 655392 | tf_op jit(solution)/shard_map/ppermute | solution.py:337
  188.1 9.5 %collective-permute-done.15 = bf16[1280,256]{1,0:T(8,128)(2,1)S(1)} collective-permute-done((bf16[1280,256]{1,0:T(8,128)(2,1)}, bf16[1280,256]{1,0:T(8,128)(2,1)S(1)}, u32[]{:S(2)}, u32[]{:S(2)}) %collective-permute-start.15) | collective-permute-done | bytes 655392 | tf_op jit(solution)/shard_map/ppermute | solution.py:338
  197.6 0.8 copy-done.10
  198.4 8.4 %aggregate.6 = (bf16[1280,256]{1,0:T(8,128)(2,1)}, bf16[1280,256]{1,0:T(8,128)(2,1)}) custom-call(s32[329]{0:T(512)} %concatenate.28.scal, bf16[10,128,256]{2,1,0:T(8,128)(2,1)} %bitcast.33, bf16[10,128,256]{2,1,0:T(8,128)(2,1)} %bitcast.35, bf16[10,128,256]{2,1,0:T(8,128)(2,1)} %bitcast.39, bf16[10,128,256]{2,1,0:T(8,128)(2,1)} %bitcast.37, ...), custom_call_target="tpu_custom_call" | custom-call | tf_op jit(solution)/shard_map/aggregate/pallas_call | solution.py:127
  206.9 8.5 %aggregate.7 = (bf16[1280,256]{1,0:T(8,128)(2,1)}, bf16[1280,256]{1,0:T(8,128)(2,1)}) custom-call(s32[329]{0:T(512)} %concatenate.28.scal, bf16[10,128,256]{2,1,0:T(8,128)(2,1)} %bitcast.34, bf16[10,128,256]{2,1,0:T(8,128)(2,1)} %bitcast.36, bf16[10,128,256]{2,1,0:T(8,128)(2,1)} %bitcast.40, bf16[10,128,256]{2,1,0:T(8,128)(2,1)} %bitcast.38, ...), custom_call_target="tpu_custom_call" | custom-call | tf_op jit(solution)/shard_map/aggregate/pallas_call | solution.py:127
  215.4 0.6 collective-permute-start.21
  215.9 0.8 copy-done.17
  216.8 8.2 %node.6.refs_0_ = bf16[1280,512]{1,0:T(8,128)(2,1)} custom-call(s32[329]{0:T(512)} %concatenate.28.scal, bf16[1280,512]{1,0:T(8,128)(2,1)} %get-tuple-element.27.state_ref, bf16[1280,256]{1,0:T(8,128)(2,1)} %get-tuple-element.34.keep_ref, bf16[1280,256]{1,0:T(8,128)(2,1)} %copy-done.17, bf16[2,1024,256]{2,1,0:T(8,128)(2,1)} %in_own.3, ...), custom_call_target="tpu_custom_call" | custom-call | tf_op jit(solution)/shard_map/node/pallas_call | solution.py:207
  225.0 0.8 copy-done.18
  225.8 8.2 %node.7.refs_2_ = bf16[1280,512]{1,0:T(8,128)(2,1)} custom-call(s32[329]{0:T(512)} %concatenate.28.scal, bf16[1280,512]{1,0:T(8,128)(2,1)} %get-tuple-element.36.state_ref, bf16[1280,256]{1,0:T(8,128)(2,1)} %get-tuple-element.37.keep_ref, bf16[1280,256]{1,0:T(8,128)(2,1)} %copy-done.18, bf16[2,1024,256]{2,1,0:T(8,128)(2,1)} %in_own.3, ...), custom_call_target="tpu_custom_call" | custom-call | tf_op jit(solution)/shard_map/node/pallas_call | solution.py:207
  233.9 0.5 collective-permute-start.22
  234.4 0.6 pad_add_fusion.scal
  235.0 2.3 collective-permute-done.22.refs_3_
  237.3 1.1 copy-done.13
  238.4 160.6 %assemble.1 = bf16[5120,512]{1,0:T(8,128)(2,1)} custom-call(s32[4]{0:T(128)} %pad_add_fusion.scal, bf16[1280,512]{1,0:T(8,128)(2,1)} %node.6.refs_0_, bf16[1280,512]{1,0:T(8,128)(2,1)} %copy-done.12, bf16[1280,512]{1,0:T(8,128)(2,1)} %node.7.refs_2_, bf16[1280,512]{1,0:T(8,128)(2,1)} %copy-done.13), custom_call_target="tpu_custom_call" | custom-call | tf_op jit(solution)/shard_map/assemble/pallas_call | solution.py:235
  (58 shorter events, 0.5 us)
Async XLA Ops:
  7.7 14.1 %copy-start = (bf16[2,1024,256]{2,1,0:T(8,128)(2,1)S(1)}, bf16[2,1024,256]{2,1,0:T(8,128)(2,1)}, u32[]{:S(2)}) copy-start(bf16[2,1024,256]{2,1,0:T(8,128)(2,1)} %in_own.3) | copy-start | bytes 3145732
  7.7 61.5 %copy-start.20 = (s32[40,4]{0,1:T(4,128)S(1)}, s32[40,4]{0,1:T(4,128)}, u32[]{:S(2)}) copy-start(s32[40,4]{0,1:T(4,128)} %param.13) | copy-start | bytes 1924
  7.7 70.8 %copy-start.21 = (s32[40,4]{0,1:T(4,128)S(1)}, s32[40,4]{0,1:T(4,128)}, u32[]{:S(2)}) copy-start(s32[40,4]{0,1:T(4,128)} %param.12) | copy-start | bytes 1924
  7.7 71.0 %copy-start.19 = (s32[5120]{0:T(1024)S(1)}, s32[5120]{0:T(1024)}, u32[]{:S(2)}) copy-start(s32[5120]{0:T(1024)} %param.14) | copy-start | bytes 61444
  7.7 80.1 %collective-permute-start.1 = (bf16[2560,256]{1,0:T(8,128)(2,1)}, bf16[2560,256]{1,0:T(8,128)(2,1)S(1)}, u32[]{:S(2)}, u32[]{:S(2)}) collective-permute-start(bf16[2560,256]{1,0:T(8,128)(2,1)} %message.4), channel_id=1, source_target_pairs={{2,0},{4,2},{6,4},{8,6},{10,8},{12,10},{14,12},{3,1},{5,3},{7,5},{... | collective-permute-start | bytes 3932168 | tf_op jit(solution)/shard_map/ppermute | solution.py:292
  16.8 71.1 %collective-permute-start = (bf16[2560,256]{1,0:T(8,128)(2,1)}, bf16[2560,256]{1,0:T(8,128)(2,1)}, u32[]{:S(2)}, u32[]{:S(2)}) collective-permute-start(bf16[2560,256]{1,0:T(8,128)(2,1)} %message.3), channel_id=1, source_target_pairs={{0,2},{2,4},{4,6},{6,8},{8,10},{10,12},{12,14},{1,3},{3,5},{5,7},{... | collective-permute-start | bytes 3932168 | tf_op jit(solution)/shard_map/ppermute | solution.py:294
  19.8 48.8 %collective-permute-start.2 = (bf16[40,512]{1,0:T(8,128)(2,1)S(1)}, bf16[40,512]{1,0:T(8,128)(2,1)S(1)}, u32[]{:S(2)}, u32[]{:S(2)}) collective-permute-start(bf16[40,512]{1,0:T(8,128)(2,1)S(1)} %slice.18), channel_id=1, source_target_pairs={{0,14},{2,0},{4,2},{6,4},{8,6},{10,8},{12,10},{14,12},{1,15},{3,1}... | collective-permute-start | bytes 122888 | tf_op jit(solution)/shard_map/ppermute | solution.py:260
  21.8 81.6 %collective-permute-start.6 = (bf16[2,1024,256]{2,1,0:T(8,128)(2,1)S(1)}, bf16[2,1024,256]{2,1,0:T(8,128)(2,1)S(1)}, u32[]{:S(2)}, u32[]{:S(2)}) collective-permute-start(bf16[2,1024,256]{2,1,0:T(8,128)(2,1)S(1)} %copy-done), channel_id=1, source_target_pairs={{0,1},{1,0},{2,3},{3,2},{4,5},{5,4},{6,7},{7,6},{8,9},{9,8},{10,11... | collective-permute-start | bytes 3145736 | tf_op jit(solution)/shard_map/ppermute | solution.py:250
  69.2 3.6 collective-permute-start.3
  74.4 9.6 %collective-permute-start.4 = (bf16[160,512]{1,0:T(8,128)(2,1)}, bf16[160,512]{1,0:T(8,128)(2,1)}, u32[]{:S(2)}, u32[]{:S(2)}) collective-permute-start(bf16[160,512]{1,0:T(8,128)(2,1)} %pad_maximum_fusion.1), channel_id=1, source_target_pairs={{0,8},{2,10},{4,12},{6,14},{8,0},{10,2},{12,4},{14,6},{1,9},{3,11}... | collective-permute-start | bytes 491528 | tf_op jit(solution)/shard_map/ppermute | solution.py:260
  87.8 1.1 copy-start.4
  88.9 11.6 %copy-start.2 = (bf16[2,256,512]{2,1,0:T(8,128)(2,1)S(1)}, bf16[2,256,512]{2,1,0:T(8,128)(2,1)}, u32[]{:S(2)}) copy-start(bf16[2,256,512]{2,1,0:T(8,128)(2,1)} %out_own.3) | copy-start | bytes 1572868
  88.9 11.7 %copy-start.11 = (bf16[1,512,256]{2,1,0:T(8,128)(2,1)S(1)}, bf16[1,512,256]{2,1,0:T(8,128)(2,1)}, u32[]{:S(2)}) copy-start(bf16[1,512,256]{2,1,0:T(8,128)(2,1)} %get-tuple-element.26.refs_0_) | copy-start | bytes 786436
  97.5 5.9 %collective-permute-start.5 = (bf16[1280,256]{1,0:T(8,128)(2,1)}, bf16[1280,256]{1,0:T(8,128)(2,1)S(1)}, u32[]{:S(2)}, u32[]{:S(2)}) collective-permute-start(bf16[1280,256]{1,0:T(8,128)(2,1)} %get-tuple-element.23), channel_id=1, source_target_pairs={{0,1},{1,0},{2,3},{3,2},{4,5},{5,4},{6,7},{7,6},{8,9},{9,8},{10,11... | collective-permute-start | bytes 1966088 | tf_op jit(solution)/shard_map/ppermute | solution.py:250
  100.6 2.9 collective-permute-start.7
  100.6 2.8 collective-permute-start.8
  103.4 0.7 copy-start.14
  103.4 0.9 copy-start.3
  103.4 1.2 copy-start.1
  103.4 1.4 copy-start.16
  115.1 9.3 %copy-start.5 = (bf16[1280,256]{1,0:T(8,128)(2,1)S(1)}, bf16[1280,256]{1,0:T(8,128)(2,1)}, u32[]{:S(2)}) copy-start(bf16[1280,256]{1,0:T(8,128)(2,1)} %get-tuple-element.28) | copy-start | bytes 1966084
  115.1 9.3 %collective-permute-start.9 = (bf16[1280,256]{1,0:T(8,128)(2,1)}, bf16[1280,256]{1,0:T(8,128)(2,1)S(1)}, u32[]{:S(2)}, u32[]{:S(2)}) collective-permute-start(bf16[1280,256]{1,0:T(8,128)(2,1)} %get-tuple-element.29), channel_id=1, source_target_pairs={{0,1},{1,0},{2,3},{3,2},{4,5},{5,4},{6,7},{7,6},{8,9},{9,8},{10,11... | collective-permute-start | bytes 1966088 | tf_op jit(solution)/shard_map/ppermute | solution.py:250
  124.0 17.8 %collective-permute-start.12 = (bf16[1280,256]{1,0:T(8,128)(2,1)}, bf16[1280,256]{1,0:T(8,128)(2,1)S(1)}, u32[]{:S(2)}, u32[]{:S(2)}) collective-permute-start(bf16[1280,256]{1,0:T(8,128)(2,1)} %get-tuple-element.31), channel_id=1, source_target_pairs={{0,1},{1,0},{2,3},{3,2},{4,5},{5,4},{6,7},{7,6},{8,9},{9,8},{10,11... | collective-permute-start | bytes 1966088 | tf_op jit(solution)/shard_map/ppermute | solution.py:250
  124.4 28.7 %copy-start.6 = (bf16[1280,256]{1,0:T(8,128)(2,1)}, bf16[1280,256]{1,0:T(8,128)(2,1)S(1)}, u32[]{:S(2)}) copy-start(bf16[1280,256]{1,0:T(8,128)(2,1)S(1)} %collective-permute-done.9) | copy-start | bytes 1966084
  124.4 2.7 collective-permute-start.16
  127.1 2.9 collective-permute-start.17
  129.9 26.9 %collective-permute-start.18 = (bf16[160,256]{1,0:T(8,128)(2,1)S(1)}, bf16[160,256]{1,0:T(8,128)(2,1)S(1)}, u32[]{:S(2)}, u32[]{:S(2)}) collective-permute-start(bf16[160,256]{1,0:T(8,128)(2,1)S(1)} %pad_maximum_fusion.4), channel_id=1, source_target_pairs={{0,8},{2,10},{4,12},{6,14},{8,0},{10,2},{12,4},{14,6},{1,9},{3,11}... | collective-permute-start | bytes 245768 | tf_op jit(solution)/shard_map/ppermute | solution.py:260
  132.8 43.7 %collective-permute-start.11 = (bf16[1280,256]{1,0:T(8,128)(2,1)}, bf16[1280,256]{1,0:T(8,128)(2,1)S(1)}, u32[]{:S(2)}, u32[]{:S(2)}) collective-permute-start(bf16[1280,256]{1,0:T(8,128)(2,1)} %get-tuple-element.29), channel_id=1, source_target_pairs={{2,1},{4,3},{6,5},{8,7},{10,9},{12,11},{14,13},{1,2},{3,4},{5,6},{... | collective-permute-start | bytes 1966088 | tf_op jit(solution)/shard_map/ppermute | solution.py:338
  139.9 41.0 %collective-permute-start.10 = (bf16[1280,256]{1,0:T(8,128)(2,1)S(1)}, bf16[1280,256]{1,0:T(8,128)(2,1)S(1)}, u32[]{:S(2)}, u32[]{:S(2)}) collective-permute-start(bf16[1280,256]{1,0:T(8,128)(2,1)S(1)} %copy-done.5), channel_id=1, source_target_pairs={{2,0},{4,2},{6,4},{8,6},{10,8},{12,10},{14,12},{1,3},{3,5},{5,7},{... | collective-permute-start | bytes 1966088 | tf_op jit(solution)/shard_map/ppermute | solution.py:337
  141.8 0.9 copy-start.15
  153.0 35.0 %collective-permute-start.14 = (bf16[1280,256]{1,0:T(8,128)(2,1)}, bf16[1280,256]{1,0:T(8,128)(2,1)S(1)}, u32[]{:S(2)}, u32[]{:S(2)}) collective-permute-start(bf16[1280,256]{1,0:T(8,128)(2,1)} %get-tuple-element.32), channel_id=1, source_target_pairs={{2,0},{4,2},{6,4},{8,6},{10,8},{12,10},{14,12},{1,3},{3,5},{5,7},{... | collective-permute-start | bytes 1966088 | tf_op jit(solution)/shard_map/ppermute | solution.py:337
  155.0 42.6 %collective-permute-start.15 = (bf16[1280,256]{1,0:T(8,128)(2,1)}, bf16[1280,256]{1,0:T(8,128)(2,1)S(1)}, u32[]{:S(2)}, u32[]{:S(2)}) collective-permute-start(bf16[1280,256]{1,0:T(8,128)(2,1)} %get-tuple-element.33), channel_id=1, source_target_pairs={{2,1},{4,3},{6,5},{8,7},{10,9},{12,11},{14,13},{1,2},{3,4},{5,6},{... | collective-permute-start | bytes 1966088 | tf_op jit(solution)/shard_map/ppermute | solution.py:338
  156.9 40.6 %collective-permute-start.13 = (bf16[1280,256]{1,0:T(8,128)(2,1)}, bf16[1280,256]{1,0:T(8,128)(2,1)}, u32[]{:S(2)}, u32[]{:S(2)}) collective-permute-start(bf16[1280,256]{1,0:T(8,128)(2,1)} %get-tuple-element.33), channel_id=1, source_target_pairs={{0,1},{1,0},{2,3},{3,2},{4,5},{5,4},{6,7},{7,6},{8,9},{9,8},{10,11... | collective-permute-start | bytes 1966088 | tf_op jit(solution)/shard_map/ppermute | solution.py:250
  176.5 21.1 %copy-start.7 = (bf16[1280,256]{1,0:T(8,128)(2,1)}, bf16[1280,256]{1,0:T(8,128)(2,1)S(1)}, u32[]{:S(2)}) copy-start(bf16[1280,256]{1,0:T(8,128)(2,1)S(1)} %collective-permute-done.11) | copy-start | bytes 1966084
  180.9 16.6 %copy-start.8 = (bf16[1280,256]{1,0:T(8,128)(2,1)}, bf16[1280,256]{1,0:T(8,128)(2,1)S(1)}, u32[]{:S(2)}) copy-start(bf16[1280,256]{1,0:T(8,128)(2,1)S(1)} %collective-permute-done.10) | copy-start | bytes 1966084
  188.1 9.5 %copy-start.9 = (bf16[1280,256]{1,0:T(8,128)(2,1)}, bf16[1280,256]{1,0:T(8,128)(2,1)S(1)}, u32[]{:S(2)}) copy-start(bf16[1280,256]{1,0:T(8,128)(2,1)S(1)} %collective-permute-done.14) | copy-start | bytes 1966084
  197.5 0.8 copy-start.10
  206.8 9.1 %collective-permute-start.19 = (bf16[1280,256]{1,0:T(8,128)(2,1)}, bf16[1280,256]{1,0:T(8,128)(2,1)S(1)}, u32[]{:S(2)}, u32[]{:S(2)}) collective-permute-start(bf16[1280,256]{1,0:T(8,128)(2,1)} %get-tuple-element.35), channel_id=1, source_target_pairs={{0,1},{1,0},{2,3},{3,2},{4,5},{5,4},{6,7},{7,6},{8,9},{9,8},{10,11... | collective-permute-start | bytes 1966088 | tf_op jit(solution)/shard_map/ppermute | solution.py:250
  215.4 9.6 %collective-permute-start.21 = (bf16[1280,256]{1,0:T(8,128)(2,1)}, bf16[1280,256]{1,0:T(8,128)(2,1)S(1)}, u32[]{:S(2)}, u32[]{:S(2)}) collective-permute-start(bf16[1280,256]{1,0:T(8,128)(2,1)} %get-tuple-element.38), channel_id=1, source_target_pairs={{0,1},{1,0},{2,3},{3,2},{4,5},{5,4},{6,7},{7,6},{8,9},{9,8},{10,11... | collective-permute-start | bytes 1966088 | tf_op jit(solution)/shard_map/ppermute | solution.py:250
  215.9 0.8 copy-start.17
  224.9 10.1 %collective-permute-start.20 = (bf16[1280,512]{1,0:T(8,128)(2,1)}, bf16[1280,512]{1,0:T(8,128)(2,1)S(1)}, u32[]{:S(2)}, u32[]{:S(2)}) collective-permute-start(bf16[1280,512]{1,0:T(8,128)(2,1)} %node.6.refs_0_), channel_id=1, source_target_pairs={{0,1},{1,0},{2,3},{3,2},{4,5},{5,4},{6,7},{7,6},{8,9},{9,8},{10,11... | collective-permute-start | bytes 3932168 | tf_op jit(solution)/shard_map/ppermute | solution.py:250
  225.0 0.8 copy-start.18
  233.9 3.4 collective-permute-start.22
  235.0 2.3 copy-start.12
  237.3 1.1 copy-start.13

commit v2 on v1

--- a/solution.py
+++ b/solution.py
@@ -11,9 +11,10 @@
 LAYERS = 2
 HALO_BLK = 20
 CHUNKS = 2
-ROW_TILE = 256
-BLOCK_STEP = 5
-VMEM_BYTES = 56 << 20
+ROW_TILE = 640
+BLOCK_STEP = 10
+MESSAGE_TILE = 1280
+VMEM_BYTES = 28 << 20
 F32 = jnp.float32
 BF16 = jnp.bfloat16
 
@@ -152,7 +153,7 @@
     )(scal, *pieces, coarse, fine_tile, coarse_tile, degree)
 
 
-def node_kernel(last, scal, state_ref, keep_ref, recv_ref, in_own, in_other, out_own, out_other, *refs):
+def node_kernel(mode, scal, state_ref, keep_ref, recv_ref, in_own, in_other, out_own, out_other, *refs):
     feat = scal[0]
     width = state_ref.shape[1]
     columns = keep_ref.shape[1]
@@ -170,136 +171,169 @@
         part = dot(silu(hidden).astype(BF16), out_ref[0])
         update = part if update is None else update + part
     new_state = (state + update).astype(BF16)
-    if last:
-        (state_out,) = refs
-        state_out[...] = new_state
+    if mode == "last":
+        refs[-2][...] = new_state
+        refs[-1][...] = new_state
+        return
+    (normed,) = normalize([new_state.astype(F32)])
+    if mode == "coarse":
+        msg_own, own_out = refs
+        own_out[...] = silu(dot(normed, msg_own[0])).astype(BF16)
         return
     msg_own, msg_other, state_out, own_out, other_out = refs
     state_out[...] = new_state
-    (normed,) = normalize([new_state.astype(F32)])
     own_out[...] = silu(dot(normed, msg_own[0])).astype(BF16)
     other_out[...] = silu(dot(normed, msg_other[0])).astype(BF16)
 
 
-def node_call(scal, state, per_half, chunk, keep, recv, weights_in, weights_out, weights_msg, layer):
+def node_call(mode, scal, state, per_half, chunk, keep, recv, weights_in, weights_out, weights_msg, layer, out=None, total=0):
     rows, columns = keep.shape
     width = state.shape[1]
-    last = weights_msg is None
-    steps = rows // ROW_TILE
+    row_tile = min(rows, ROW_TILE)
+    steps = rows // row_tile
 
     def place(i, scal):
-        return (scal[0] * per_half + chunk) * steps + i, 0
+        return ((scal[0] * per_half + chunk) * steps if per_half else 0) + i, 0
+
+    def place_out(i, scal):
+        return (scal[0] * CHUNKS + chunk) * steps + i, 0
 
     def whole(array, at):
         return pl.BlockSpec((1,) + array.shape[1:], lambda i, scal: (at, 0, 0))
 
-    tile = pl.BlockSpec((ROW_TILE, columns), lambda i, scal: (i, 0))
+    tile = pl.BlockSpec((row_tile, columns), lambda i, scal: (i, 0))
+    state_tile = pl.BlockSpec((row_tile, width), lambda i, scal: (i, 0))
+    message_shape = jax.ShapeDtypeStruct((rows, columns), BF16)
+    state_shape = jax.ShapeDtypeStruct((rows, width), BF16)
     operands = [state, keep, recv, *weights_in, *weights_out]
-    in_specs = [pl.BlockSpec((ROW_TILE, width), place), tile, tile]
+    in_specs = [pl.BlockSpec((row_tile, width), place), tile, tile]
     in_specs += [whole(array, layer) for array in (*weights_in, *weights_out)]
-    out_specs = [pl.BlockSpec((ROW_TILE, width), lambda i, scal: (i, 0))]
-    out_shape = [jax.ShapeDtypeStruct((rows, width), BF16)]
-    if not last:
-        operands += list(weights_msg)
-        in_specs += [whole(array, layer) for array in weights_msg]
-        out_specs += [tile, tile]
-        out_shape += [jax.ShapeDtypeStruct((rows, columns), BF16)] * 2
+    aliases = {}
+    if mode == "last":
+        out_specs = [state_tile, pl.BlockSpec((row_tile, width), place_out)]
+        out_shape = [state_shape, jax.ShapeDtypeStruct((total, width), BF16)]
+        if out is not None:
+            operands.append(out)
+            in_specs.append(pl.BlockSpec(memory_space=pl.ANY))
+            aliases = {len(operands): 1}
+    else:
+        own_only = mode == "coarse"
+        kept = weights_msg[:1] if own_only else weights_msg
+        operands += list(kept)
+        in_specs += [whole(array, layer) for array in kept]
+        out_specs = [tile] if own_only else [state_tile, tile, tile]
+        out_shape = [message_shape] if own_only else [state_shape, message_shape, message_shape]
     return pl.pallas_call(
-        functools.partial(node_kernel, last),
+        functools.partial(node_kernel, mode),
         grid_spec=pltpu.PrefetchScalarGridSpec(
             num_scalar_prefetch=1, grid=(steps,), in_specs=in_specs, out_specs=out_specs
         ),
         out_shape=out_shape,
+        input_output_aliases=aliases,
         compiler_params=params(),
-        name="node",
+        name="node_" + mode,
     )(scal, *operands)
 
 
-def assemble_kernel(pieces, scal, *refs):
-    piece_refs = refs[:pieces]
-    out_ref, sems = refs[pieces:]
-    copies = [
-        pltpu.make_async_copy(
-            ref, out_ref.at[pl.ds(pl.multiple_of(scal[pos], 8), ref.shape[0])], sems.at[pos]
-        )
-        for pos, ref in enumerate(piece_refs)
-    ]
-    for copy in copies:
-        copy.start()
-    for copy in copies:
-        copy.wait()
-
-
-def assemble_call(offsets, pieces):
-    rows = sum(piece.shape[0] for piece in pieces)
+def assemble_kernel(scal, *refs):
+    pieces = refs[:CHUNKS]
+    out_ref = refs[-1]
+    for pos, ref in enumerate(pieces):
+
+        @pl.when(pl.program_id(0) == pos)
+        def _():
+            out_ref[...] = ref[...]
+
+
+def assemble_call(scal, pieces, out):
+    rows, width = pieces[0].shape
     return pl.pallas_call(
-        functools.partial(assemble_kernel, len(pieces)),
+        assemble_kernel,
         grid_spec=pltpu.PrefetchScalarGridSpec(
             num_scalar_prefetch=1,
-            in_specs=[pl.BlockSpec(memory_space=pl.ANY) for _ in pieces],
-            out_specs=pl.BlockSpec(memory_space=pl.ANY),
-            scratch_shapes=[pltpu.SemaphoreType.DMA((len(pieces),))],
+            grid=(CHUNKS,),
+            in_specs=[pl.BlockSpec((rows, width), lambda i, scal: (0, 0)) for _ in pieces]
+            + [pl.BlockSpec(memory_space=pl.ANY)],
+            out_specs=pl.BlockSpec((rows, width), lambda i, scal: ((1 - scal[0]) * CHUNKS + i, 0)),
         ),
-        out_shape=jax.ShapeDtypeStruct((rows, pieces[0].shape[1]), pieces[0].dtype),
+        out_shape=jax.ShapeDtypeStruct(out.shape, out.dtype),
+        input_output_aliases={len(pieces) + 1: 0},
         compiler_params=params(),
         name="assemble",
-    )(offsets, *pieces)
+    )(scal, *pieces, out)
 
 
 def swap_feat(array):
     return lax.ppermute(array, "feat", [(0, 1), (1, 0)])
 
 
-def gather_patches(rows):
+def strides(count):
+    assert count & (count - 1) == 0
+    stride = count // 2
+    while stride:
+        yield stride
+        stride //= 2
+
+
+def fetch_patches(held, stride):
     count = lax.axis_size("patch")
-    held = rows
-    have = 1
-    while have < count:
-        more = min(have, count - have)
-        pairs = [(pos, (pos - have) % count) for pos in range(count)]
-        got = lax.ppermute(held[: more * rows.shape[0]], "patch", pairs)
-        held = jnp.concatenate([held, got], axis=0)
-        have += more
-    return held
+    pairs = [(pos, (pos - stride) % count) for pos in range(count)]
+    return jnp.concatenate([held, lax.ppermute(held, "patch", pairs)], axis=0)
+
+
+def held_places(count):
+    offsets = [0]
+    for stride in strides(count):
+        offsets += [offset + stride for offset in offsets]
+    return [offsets.index(pos) for pos in range(count)]
 
 
 def shards(
     node_state, fine_tile, coarse_tile, fine_index, coarse_index, node_degree, w_msg, w_in, w_out
 ):
+    barrier = lax.optimization_barrier
     patches = lax.axis_size("patch")
     patch_pos = lax.axis_index("patch")
     feat = lax.axis_index("feat")
     blocks, kinds, block, _ = fine_tile.shape
     half = blocks // 2
     half_rows = half * block
-    halo_rows = HALO_BLK * block
     assert half == HALO_BLK and half % (CHUNKS * BLOCK_STEP) == 0
     columns = w_msg.shape[2]
     degree = node_degree.reshape(blocks // BLOCK_STEP, BLOCK_STEP, block)
 
+    forward = [(pos, pos + 1) for pos in range(patches - 1)]
+    backward = [(target, source) for source, target in forward]
+    sides = ((0, backward), (1, forward))
+    own_patch = [(2 * src + side, 2 * dst + side) for side, pairs in sides for src, dst in pairs]
+    other_patch = [(2 * src + side, 2 * dst + 1 - side) for side, pairs in sides for src, dst in pairs]
+    first_stride, *more_strides = strides(patches)
+
+    held = fetch_patches(node_state[:CN_DEV], first_stride)
+    low = message_call(node_state, w_msg[0], 0, half_rows, MESSAGE_TILE)
+    low, held = barrier((low, held))
+    high_halo = lax.ppermute(low, "patch", backward)
+    high = message_call(node_state, w_msg[0], half_rows, half_rows, MESSAGE_TILE)
+    low_halo = lax.ppermute(high, "patch", forward)
+    for stride in more_strides:
+        held = fetch_patches(held, stride)
+    coarse_state = held
+
     links = (fine_index - (patch_pos * blocks - HALO_BLK)).reshape(-1)
-    coarse_links = ((coarse_index - patch_pos) % patches * CN_DEV).reshape(-1)
+    away = ((coarse_index - patch_pos) % patches).reshape(-1)
+    coarse_links = sum(
+        jnp.where(away == pos, place * CN_DEV, 0) for pos, place in enumerate(held_places(patches))
+    )
 
     def scalars(*places):
         head = jnp.stack([jnp.asarray(value, jnp.int32) for value in (feat, *places)])
         return jnp.concatenate([head, links, coarse_links])
 
-    forward = [(pos, pos + 1) for pos in range(patches - 1)]
-    backward = [(target, source) for source, target in forward]
-    coarse_state = gather_patches(node_state[:CN_DEV])
-
-    low = message_call(node_state, w_msg[0], 0, half_rows, 512)
-    high_halo = lax.ppermute(low, "patch", backward)
-    high = message_call(node_state, w_msg[0], half_rows, half_rows, 512)
-    low_halo = lax.ppermute(high, "patch", forward)
-    w_in, w_out, w_msg_late, _ = lax.optimization_barrier((w_in, w_out, w_msg[1:], high))
+    w_in, w_out, w_msg_late, _ = barrier((w_in, w_out, w_msg[1:], high))
     weights_in = (w_in, swap_feat(w_in))
     weights_out = (w_out, swap_feat(w_out))
     weights_msg = (w_msg_late, swap_feat(w_msg_late))
     coarse = message_call(coarse_state, w_msg[0], 0, coarse_state.shape[0], coarse_state.shape[0])
-
-    own_patch = [(2 * src + side, 2 * dst + side) for side, pairs in ((0, backward), (1, forward)) for src, dst in pairs]
-    other_patch = [(2 * src + side, 2 * dst + 1 - side) for side, pairs in ((0, backward), (1, forward)) for src, dst in pairs]
 
     pieces = [low_halo, low, high, high_halo]
     scal = scalars(0, HALO_BLK, HALO_BLK + half, HALO_BLK + blocks)
@@ -314,43 +348,51 @@
         late_places += [own, other, near, far]
     late_scal = scalars(*late_places)
 
-    states = [node_state] * CHUNKS
-    for layer in range(LAYERS):
-        last = layer == LAYERS - 1
+    def aggregate(scal, pieces, coarse, chunk):
         shaped = [piece.reshape(-1, block, columns) for piece in pieces]
-        sums = [
-            aggregate_call(scal, shaped, coarse, fine_tile, coarse_tile, degree, chunk)
-            for chunk in range(CHUNKS)
-        ]
-        received = [swap_feat(send) for send, _ in sums]
-        new_states = []
-        pieces = []
-        for chunk in range(CHUNKS):
-            results = node_call(
-                scal, states[chunk], CHUNKS if layer == 0 else 0, chunk if layer == 0 else 0,
-                sums[chunk][1], received[chunk], weights_in, weights_out,
-                None if last else weights_msg, layer,
-            )
-            new_states.append(results[0])
-            if not last:
-                own, other = results[1:]
-                near = lax.ppermute(own, ("patch", "feat"), own_patch)
-                far = lax.ppermute(other, ("patch", "feat"), other_patch)
-                sibling = swap_feat(other)
-                pieces += [own, sibling, near, far]
-                if chunk == 0:
-                    mine = jnp.where(feat == 0, own[:CN_DEV], sibling[:CN_DEV])
-                    coarse = gather_patches(mine)
-        states = new_states
-        scal = late_scal
-
-    parts = []
-    offsets = []
-    chunk_rows = half_rows // CHUNKS
+        return aggregate_call(scal, shaped, coarse, fine_tile, coarse_tile, degree, chunk)
+
+    send, keep = aggregate(scal, pieces, coarse, 0)
+    held = fetch_patches(jnp.where(feat == 0, keep[:CN_DEV], send[:CN_DEV]), first_stride)
+    recv = swap_feat(send)
+    send_1, keep_1 = aggregate(scal, pieces, coarse, 1)
+    recv, keep, held, send_1 = barrier((recv, keep, held, send_1))
+    recv_1 = swap_feat(send_1)
+    inputs = [(keep, recv), (keep_1, recv_1)]
+    states = []
+    pieces = []
     for chunk in range(CHUNKS):
-        parts += [states[chunk], swap_feat(states[chunk])]
-        offsets += [feat * half_rows + chunk * chunk_rows, (1 - feat) * half_rows + chunk * chunk_rows]
-    return assemble_call(jnp.stack(offsets).astype(jnp.int32), parts)
+        new_state, own, other = node_call(
+            "mid", scal, node_state, CHUNKS, chunk, *inputs[chunk], weights_in, weights_out, weights_msg, 0
+        )
+        if chunk == 0:
+            held = fetch_patches(held, more_strides[0])
+            own, other, held = barrier((own, other, held))
+        near = lax.ppermute(own, ("patch", "feat"), own_patch)
+        far = lax.ppermute(other, ("patch", "feat"), other_patch)
+        pieces += [own, swap_feat(other), near, far]
+        states.append(new_state)
+    for stride in more_strides[1:]:
+        held = fetch_patches(held, stride)
+    (coarse,) = node_call(
+        "coarse", scal, coarse_state, 0, 0, held, swap_feat(held), weights_in, weights_out, weights_msg, 0
+    )
+
+    send, keep = aggregate(late_scal, pieces, coarse, 0)
+    recv = swap_feat(send)
+    send_1, keep_1 = aggregate(late_scal, pieces, coarse, 1)
+    recv, keep, send_1 = barrier((recv, keep, send_1))
+    recv_1 = swap_feat(send_1)
+    inputs = [(keep, recv), (keep_1, recv_1)]
+    out = None
+    swapped = []
+    for chunk in range(CHUNKS):
+        new_state, out = node_call(
+            "last", late_scal, states[chunk], 0, chunk, *inputs[chunk], weights_in, weights_out, None, 1,
+            out, node_state.shape[0],
+        )
+        swapped.append(swap_feat(new_state))
+    return assemble_call(late_scal, swapped, out)
 
 
 def solution(mesh):

time: 400 us -> 205 us (0.51)
  Pallas kernels: 245 us -> 59.9 us
  waiting for transfers between devices: 94.8 us -> 84.1 us
  local copies, waits for them, and re-layouts: 15.9 us -> 24.3 us
  other arithmetic: 5.23 us -> 0.95 us
    pallas_call x5 -> x6, Pallas kernels: 198 us -> 33.4 us  [the longest x5 31.2 us: node_call(): pl.pallas_call(functools.partial(node_kernel, mode), grid_spec=pltpu.Pref...]
    pallas_call x4, Pallas kernels: 34 us -> 19.5 us  [aggregate_call(): pl.pallas_call(functools.partial(aggregate_kernel, len(pieces), chunk, ha...]
    unnamed x45 -> x60, local copies, waits for them, and re-layouts: 10.9 us -> 21.9 us
    ppermute x2, waiting for transfers between devices: 24.9 us -> 17 us  [shards(): far = lax.ppermute(other, ('patch', 'feat'), other_patch)]
    ppermute x2, waiting for transfers between devices: 11.6 us -> 4.55 us  [shards(): near = lax.ppermute(own, ('patch', 'feat'), own_patch)]
    pallas_call x3, Pallas kernels: 13.8 us -> 6.99 us  [message_call(): pl.pallas_call(message_kernel, grid=(rows // tile,), in_specs=[pl.BlockSp...]
    ppermute x6, waiting for transfers between devices: 53.7 us -> 59.8 us  [fetch_patches(): return jnp.concatenate([held, lax.ppermute(held, 'patch', pairs)], axis=0)]
    ppermute x2, starting transfers between devices: 9.06 us -> 4.29 us  [shards(): far = lax.ppermute(other, ('patch', 'feat'), other_patch)]
  transfers between devices with their start and end apart: 23 -> 24, of which waited for: 10 -> 7; matrix products, arithmetic and copies ran while one was open for 3% -> 3% of each run, Pallas kernels for 15% -> 26%
where the time goes in v2:
time: 205 us
  waiting for transfers between devices  84.1 us (41%)
  Pallas kernels  59.9 us (29%)
  starting transfers between devices  34.9 us (17%)
  local copies, waits for them, and re-layouts  24.3 us (12%)
    ppermute x6, waiting for transfers between devices, fetch_patches(): return jnp.concatenate([held, lax.ppermute(held, 'patch', pairs)], axis=0)  59.8 us
    pallas_call x5, Pallas kernels, node_call(): pl.pallas_call(functools.partial(node_kernel, mode), grid_spec=pltpu.Pref...  31.2 us
    unnamed x60, local copies, waits for them, and re-layouts  21.9 us
    pallas_call x4, Pallas kernels, aggregate_call(): pl.pallas_call(functools.partial(aggregate_kernel, len(pieces), chunk, ha...  19.5 us
    ppermute x2, waiting for transfers between devices, shards(): far = lax.ppermute(other, ('patch', 'feat'), other_patch)  17 us
    ppermute x12, starting transfers between devices, swap_feat(): return lax.ppermute(array, 'feat', [(0, 1), (1, 0)])  12.9 us
    pallas_call x3, Pallas kernels, message_call(): pl.pallas_call(message_kernel, grid=(rows // tile,), in_specs=[pl.BlockSp...  6.99 us
    ppermute x6, starting transfers between devices, fetch_patches(): return jnp.concatenate([held, lax.ppermute(held, 'patch', pairs)], axis=0)  5.76 us
  transfers between devices with their start and end apart: 24, of which 7 were waited for; matrix products, arithmetic and copies ran while one was open for 3% of the time, Pallas kernels for 26%

profile of v2, /device:TPU:9, one launch (start us, length us, event | category | flops | bytes accessed | tf_op | source)
XLA Modules:
  0.0 204.5 jit_solution(10128816556369027644)
XLA Ops:
  0.0 0.8 slice.18
  0.8 2.3 %collective-permute-start.1 = (bf16[40,512]{1,0:T(8,128)(2,1)S(1)}, bf16[40,512]{1,0:T(8,128)(2,1)S(1)}, u32[]{:S(2)}, u32[]{:S(2)}) collective-permute-start(bf16[40,512]{1,0:T(8,128)(2,1)S(1)} %slice.18), channel_id=1, source_target_pairs={{0,8},{2,10},{4,12},{6,14},{8,0},{10,2},{12,4},{14,6},{1,9},{3,11}... | collective-permute-start | bytes 122888 | tf_op jit(solution)/shard_map/ppermute | solution.py:281
  3.1 1.1 fusion.1
  4.2 2.5 %copy-done = bf16[5120,512]{1,0:T(8,128)(2,1)S(1)} copy-done((bf16[5120,512]{1,0:T(8,128)(2,1)S(1)}, bf16[5120,512]{1,0:T(8,128)(2,1)}, u32[]{:S(2)}) %copy-start) | copy-done | bytes 5242904
  6.6 3.3 %message.3 = bf16[2560,256]{1,0:T(8,128)(2,1)} custom-call(bf16[5120,512]{1,0:T(8,128)(2,1)S(1)} %copy-done, bf16[512,256]{1,0:T(8,128)(2,1)S(1)} %get-tuple-element.72.weight_ref), custom_call_target="tpu_custom_call" | custom-call | tf_op jit(solution)/shard_map/message/pallas_call | solution.py:50
  9.9 3.3 %collective-permute-start = (bf16[2560,256]{1,0:T(8,128)(2,1)}, bf16[2560,256]{1,0:T(8,128)(2,1)}, u32[]{:S(2)}, u32[]{:S(2)}) collective-permute-start(bf16[2560,256]{1,0:T(8,128)(2,1)} %message.3), channel_id=1, source_target_pairs={{0,2},{2,4},{4,6},{6,8},{8,10},{10,12},{12,14},{1,3},{3,5},{5,7},{... | collective-permute-start | bytes 3932168 | tf_op jit(solution)/shard_map/ppermute | solution.py:317
  13.2 3.3 %message.4 = bf16[2560,256]{1,0:T(8,128)(2,1)} custom-call(bf16[5120,512]{1,0:T(8,128)(2,1)S(1)} %copy-done, bf16[512,256]{1,0:T(8,128)(2,1)S(1)} %get-tuple-element.72.weight_ref), custom_call_target="tpu_custom_call" | custom-call | tf_op jit(solution)/shard_map/message/pallas_call | solution.py:50
  16.5 3.0 %collective-permute-start.2 = (bf16[2560,256]{1,0:T(8,128)(2,1)}, bf16[2560,256]{1,0:T(8,128)(2,1)}, u32[]{:S(2)}, u32[]{:S(2)}) collective-permute-start(bf16[2560,256]{1,0:T(8,128)(2,1)} %message.4), channel_id=1, source_target_pairs={{2,0},{4,2},{6,4},{8,6},{10,8},{12,10},{14,12},{3,1},{5,3},{7,5},{... | collective-permute-start | bytes 3932168 | tf_op jit(solution)/shard_map/ppermute | solution.py:315
  19.5 1.6 collective-permute-start.7
  21.2 0.1 copy.17
  21.3 0.1 reshape.109
  21.4 0.1 copy.16
  21.5 0.1 reshape.92
  21.6 3.0 %copy.18.refs_6_.refs_10_ = bf16[40,128,160]{2,1,0:T(8,128)(2,1)S(1)} copy(bf16[40,128,160]{1,2,0:T(8,128)(2,1)} %param.11) | data formatting | bytes 3276800 | tf_op args[2]
  24.7 0.1 concatenate.26.scal
  24.7 24.9 %collective-permute-done.3 = bf16[80,512]{1,0:T(8,128)(2,1)S(1)} collective-permute-done((bf16[80,512]{1,0:T(8,128)(2,1)S(1)}, bf16[80,512]{1,0:T(8,128)(2,1)S(1)}, u32[]{:S(2)}, u32[]{:S(2)}) %collective-permute-start.3) | collective-permute-done | bytes 81952 | tf_op jit(solution)/shard_map/ppermute | solution.py:281
  49.7 25.6 %collective-permute-done.4 = bf16[160,512]{1,0:T(8,128)(2,1)S(1)} collective-permute-done((bf16[160,512]{1,0:T(8,128)(2,1)S(1)}, bf16[160,512]{1,0:T(8,128)(2,1)S(1)}, u32[]{:S(2)}, u32[]{:S(2)}) %collective-permute-start.4) | collective-permute-done | bytes 163872 | tf_op jit(solution)/shard_map/ppermute | solution.py:281
  75.4 0.5 message.5.refs_4_
  75.8 0.3 copy-done.9
  76.1 2.5 %copy-done.1 = bf16[40,4,128,128]{3,2,1,0:T(8,128)(2,1)S(1)} copy-done((bf16[40,4,128,128]{3,2,1,0:T(8,128)(2,1)S(1)}, bf16[40,4,128,128]{3,2,1,0:T(8,128)(2,1)}, u32[]{:S(2)}) %copy-start.1) | copy-done | bytes 5242904
  78.6 5.6 %aggregate.4 = (bf16[1280,256]{1,0:T(8,128)(2,1)}, bf16[1280,256]{1,0:T(8,128)(2,1)S(1)}) custom-call(s32[325]{0:T(512)S(1)} %concatenate.26.scal, bf16[20,128,256]{2,1,0:T(8,128)(2,1)} %bitcast.10.refs_0_, bf16[20,128,256]{2,1,0:T(8,128)(2,1)} %bitcast.11.refs_1_, bf16[20,128,256]{2,1,0:T(8,128)(2,1)} %bitcast.12.refs_2_, ...), custom_call_target="tpu_custom_call" | custom-call | tf_op jit(solution)/shard_map/aggregate/pallas_call | solution.py:128
  84.2 0.8 copy-done.17
  85.0 0.5 collective-permute-start.5
  85.5 0.5 collective-permute-start.9
  86.0 0.9 slice_select_fusion
  86.9 0.1 collective-permute-start.6
  87.0 2.9 %copy-done.2 = bf16[40,4,128,128]{3,2,1,0:T(8,128)(2,1)S(1)} copy-done((bf16[40,4,128,128]{3,2,1,0:T(8,128)(2,1)S(1)}, bf16[40,4,128,128]{3,2,1,0:T(8,128)(2,1)}, u32[]{:S(2)}) %copy-start.2) | copy-done | bytes 5242904
  89.9 0.9 copy-done.12
  90.9 4.7 %aggregate.5 = (bf16[1280,256]{1,0:T(8,128)(2,1)S(1)}, bf16[1280,256]{1,0:T(8,128)(2,1)S(1)}) custom-call(s32[325]{0:T(512)S(1)} %concatenate.26.scal, bf16[20,128,256]{2,1,0:T(8,128)(2,1)} %bitcast.10.refs_0_, bf16[20,128,256]{2,1,0:T(8,128)(2,1)} %bitcast.11.refs_1_, bf16[20,128,256]{2,1,0:T(8,128)(2,1)} %bitcast.12.refs_2_, ...), custom_call_target="tpu_custom_call" | custom-call | tf_op jit(solution)/shard_map/aggregate/pallas_call | solution.py:128
  95.6 0.8 collective-permute-start.10
  96.4 0.6 collective-permute-start.14
  97.1 7.7 %node_mid.2 = (bf16[1280,512]{1,0:T(8,128)(2,1)S(1)}, bf16[1280,256]{1,0:T(8,128)(2,1)S(1)}, bf16[1280,256]{1,0:T(8,128)(2,1)}) custom-call(s32[325]{0:T(512)S(1)} %concatenate.26.scal, bf16[5120,512]{1,0:T(8,128)(2,1)S(1)} %bitcast.24, bf16[1280,256]{1,0:T(8,128)(2,1)S(1)} %copy-done.18, bf16[1280,256]{1,0:T(8,128)(2,1)} %collective-permute-done.5.recv_ref, ...), custom_call_target="tpu_custom_call" | custom-call | tf_op jit(solution)/shard_map/node_mid/pallas_call | solution.py:226
  104.8 1.1 copy-done.15
  105.9 1.9 collective-permute-start.12
  107.8 2.4 %collective-permute-start.18 = (bf16[160,256]{1,0:T(8,128)(2,1)S(1)}, bf16[160,256]{1,0:T(8,128)(2,1)S(1)}, u32[]{:S(2)}, u32[]{:S(2)}) collective-permute-start(bf16[160,256]{1,0:T(8,128)(2,1)S(1)} %pad_maximum_fusion.2), channel_id=1, source_target_pairs={{0,14},{2,0},{4,2},{6,4},{8,6},{10,8},{12,10},{14,12},{1,15},{3,1}... | collective-permute-start | bytes 245768 | tf_op jit(solution)/shard_map/ppermute | solution.py:281
  110.2 9.3 %collective-permute-done.18 = bf16[160,256]{1,0:T(8,128)(2,1)S(1)} collective-permute-done((bf16[160,256]{1,0:T(8,128)(2,1)S(1)}, bf16[160,256]{1,0:T(8,128)(2,1)S(1)}, u32[]{:S(2)}, u32[]{:S(2)}) %collective-permute-start.18) | collective-permute-done | bytes 81952 | tf_op jit(solution)/shard_map/ppermute | solution.py:281
  119.5 7.6 %collective-permute-start.19 = (bf16[320,256]{1,0:T(8,128)(2,1)S(1)}, bf16[320,256]{1,0:T(8,128)(2,1)S(1)}, u32[]{:S(2)}, u32[]{:S(2)}) collective-permute-start(bf16[320,256]{1,0:T(8,128)(2,1)S(1)} %constant_dynamic-update-slice_fusion.3.keep_ref), channel_id=1, source_target_pairs={{0,1},{1,0},{2,3},{3,2},{4,5},{5,4},{6,7},{7,6},{8,9},{9,8},{10,11... | collective-permute-start | bytes 491528 | tf_op jit(solution)/shard_map/ppermute | solution.py:267
  127.1 1.9 collective-permute-start.13
  129.0 0.1 collective-permute-start.11
  129.1 7.8 %node_mid.3 = (bf16[1280,512]{1,0:T(8,128)(2,1)S(1)}, bf16[1280,256]{1,0:T(8,128)(2,1)}, bf16[1280,256]{1,0:T(8,128)(2,1)}) custom-call(s32[325]{0:T(512)S(1)} %concatenate.26.scal, bf16[5120,512]{1,0:T(8,128)(2,1)S(1)} %bitcast.24, bf16[1280,256]{1,0:T(8,128)(2,1)S(1)} %get-tuple-element.54.keep_ref, ...), custom_call_target="tpu_custom_call" | custom-call | tf_op jit(solution)/shard_map/node_mid/pallas_call | solution.py:226
  136.9 1.1 copy-done.13
  138.0 3.7 %collective-permute-start.16 = (bf16[1280,256]{1,0:T(8,128)(2,1)}, bf16[1280,256]{1,0:T(8,128)(2,1)}, u32[]{:S(2)}, u32[]{:S(2)}) collective-permute-start(bf16[1280,256]{1,0:T(8,128)(2,1)} %get-tuple-element.56), channel_id=1, source_target_pairs={{2,0},{4,2},{6,4},{8,6},{10,8},{12,10},{14,12},{1,3},{3,5},{5,7},{... | collective-permute-start | bytes 1966088 | tf_op jit(solution)/shard_map/ppermute | solution.py:371
  141.7 0.7 copy-done.21
  142.4 2.4 %collective-permute-start.17 = (bf16[1280,256]{1,0:T(8,128)(2,1)}, bf16[1280,256]{1,0:T(8,128)(2,1)}, u32[]{:S(2)}, u32[]{:S(2)}) collective-permute-start(bf16[1280,256]{1,0:T(8,128)(2,1)} %get-tuple-element.57), channel_id=1, source_target_pairs={{2,1},{4,3},{6,5},{8,7},{10,9},{12,11},{14,13},{1,2},{3,4},{5,6},{... | collective-permute-start | bytes 1966088 | tf_op jit(solution)/shard_map/ppermute | solution.py:372
  144.8 0.8 copy-done.7
  145.6 0.9 collective-permute-start.15
  146.5 0.1 concatenate.25.scal
  146.6 1.0 copy-done.10
  147.6 0.9 copy-done.20
  148.5 0.9 copy-done.22
  149.4 3.4 %node_coarse.1.refs_8_ = bf16[320,256]{1,0:T(8,128)(2,1)S(1)} custom-call(s32[325]{0:T(512)S(1)} %concatenate.26.scal, bf16[320,512]{1,0:T(8,128)(2,1)S(1)} %copy-done.10, bf16[320,256]{1,0:T(8,128)(2,1)S(1)} %copy-done.20, bf16[320,256]{1,0:T(8,128)(2,1)S(1)} %copy-done.22, bf16[2,1024,256]{2,1,0:T(8,128)(2,1)} %in_own.4, ...), custom_call_target="tpu_custom_call" | custom-call | tf_op jit(solution)/shard_map/node_coarse/pallas_call | solution.py:226
  152.8 7.5 %collective-permute-done.13 = bf16[1280,256]{1,0:T(8,128)(2,1)} collective-permute-done((bf16[1280,256]{1,0:T(8,128)(2,1)}, bf16[1280,256]{1,0:T(8,128)(2,1)}, u32[]{:S(2)}, u32[]{:S(2)}) %collective-permute-start.13) | collective-permute-done | bytes 655392 | tf_op jit(solution)/shard_map/ppermute | solution.py:372
  160.4 4.6 %collective-permute-done.16 = bf16[1280,256]{1,0:T(8,128)(2,1)} collective-permute-done((bf16[1280,256]{1,0:T(8,128)(2,1)}, bf16[1280,256]{1,0:T(8,128)(2,1)}, u32[]{:S(2)}, u32[]{:S(2)}) %collective-permute-start.16) | collective-permute-done | bytes 655392 | tf_op jit(solution)/shard_map/ppermute | solution.py:371
  164.9 9.5 %collective-permute-done.17 = bf16[1280,256]{1,0:T(8,128)(2,1)} collective-permute-done((bf16[1280,256]{1,0:T(8,128)(2,1)}, bf16[1280,256]{1,0:T(8,128)(2,1)}, u32[]{:S(2)}, u32[]{:S(2)}) %collective-permute-start.17) | collective-permute-done | bytes 655392 | tf_op jit(solution)/shard_map/ppermute | solution.py:372
  174.5 2.5 %copy-done.3 = bf16[40,4,128,128]{3,2,1,0:T(8,128)(2,1)S(1)} copy-done((bf16[40,4,128,128]{3,2,1,0:T(8,128)(2,1)S(1)}, bf16[40,4,128,128]{3,2,1,0:T(8,128)(2,1)}, u32[]{:S(2)}) %copy-start.3) | copy-done | bytes 5242904
  176.9 4.6 %aggregate.6 = (bf16[1280,256]{1,0:T(8,128)(2,1)S(1)}, bf16[1280,256]{1,0:T(8,128)(2,1)S(1)}) custom-call(s32[329]{0:T(512)S(1)} %concatenate.25.scal, bf16[10,128,256]{2,1,0:T(8,128)(2,1)S(1)} %bitcast.25, bf16[10,128,256]{2,1,0:T(8,128)(2,1)} %bitcast.15.refs_1_, bf16[10,128,256]{2,1,0:T(8,128)(2,1)S(1)} %bitcast.27, ...), custom_call_target="tpu_custom_call" | custom-call | tf_op jit(solution)/shard_map/aggregate/pallas_call | solution.py:128
  181.5 0.1 collective-permute-start.20
  181.6 4.6 %aggregate.7 = (bf16[1280,256]{1,0:T(8,128)(2,1)S(1)}, bf16[1280,256]{1,0:T(8,128)(2,1)S(1)}) custom-call(s32[329]{0:T(512)S(1)} %concatenate.25.scal, bf16[10,128,256]{2,1,0:T(8,128)(2,1)S(1)} %bitcast.26, bf16[10,128,256]{2,1,0:T(8,128)(2,1)} %bitcast.15.refs_1_, bf16[10,128,256]{2,1,0:T(8,128)(2,1)S(1)} %bitcast.28, ...), custom_call_target="tpu_custom_call" | custom-call | tf_op jit(solution)/shard_map/aggregate/pallas_call | solution.py:128
  186.2 0.6 collective-permute-start.22
  186.8 6.2 %node_last.2 = (bf16[1280,512]{1,0:T(8,128)(2,1)S(1)}, bf16[5120,512]{1,0:T(8,128)(2,1)}) custom-call(s32[329]{0:T(512)S(1)} %concatenate.25.scal, bf16[1280,512]{1,0:T(8,128)(2,1)S(1)} %copy-done.16, bf16[1280,256]{1,0:T(8,128)(2,1)S(1)} %get-tuple-element.62.keep_ref, bf16[1280,256]{1,0:T(8,128)(2,1)S(1)} %collective-permute-done.20.recv_ref, ...), custom_call_target="tpu_custom_call" | custom-call | tf_op jit(solution)/shard_map/node_last/pallas_call | solution.py:226
  193.0 6.2 %node_last.3 = (bf16[1280,512]{1,0:T(8,128)(2,1)S(1)}, bf16[5120,512]{1,0:T(8,128)(2,1)}) custom-call(s32[329]{0:T(512)S(1)} %concatenate.25.scal, bf16[1280,512]{1,0:T(8,128)(2,1)S(1)} %copy-done.14, bf16[1280,256]{1,0:T(8,128)(2,1)S(1)} %get-tuple-element.66.keep_ref, ...), custom_call_target="tpu_custom_call", output_to_operand_aliasing={{1}: (8, {})} | custom-call | tf_op jit(solution)/shard_map/node_last/pallas_call | solution.py:226
  199.2 0.5 collective-permute-start.23
  199.7 2.7 %collective-permute-done.23.refs_1_ = bf16[1280,512]{1,0:T(8,128)(2,1)S(1)} collective-permute-done((bf16[1280,512]{1,0:T(8,128)(2,1)S(1)}, bf16[1280,512]{1,0:T(8,128)(2,1)S(1)}, u32[]{:S(2)}, u32[]{:S(2)}) %collective-permute-start.23) | collective-permute-done | bytes 1310752 | tf_op jit(solution)/shard_map/ppermute | solution.py:267
  202.3 2.2 %assemble.1 = bf16[5120,512]{1,0:T(8,128)(2,1)} custom-call(s32[329]{0:T(512)S(1)} %concatenate.25.scal, bf16[1280,512]{1,0:T(8,128)(2,1)S(1)} %collective-permute-done.21.refs_0_, bf16[1280,512]{1,0:T(8,128)(2,1)S(1)} %collective-permute-done.23.refs_1_, bf16[5120,512]{1,0:T(8,128)(2,1)} %get-tuple-element.70.refs_2_), custom_call_target="tpu_custom_call", output_to_operand_aliasing={{}: (3, {})} | custom-call | tf_op jit(solution)/shard_map/assemble/pallas_call | solution.py:250
  (76 shorter events, 0.4 us)
Async XLA Ops:
  0.8 15.7 %collective-permute-start.1 = (bf16[40,512]{1,0:T(8,128)(2,1)S(1)}, bf16[40,512]{1,0:T(8,128)(2,1)S(1)}, u32[]{:S(2)}, u32[]{:S(2)}) collective-permute-start(bf16[40,512]{1,0:T(8,128)(2,1)S(1)} %slice.18), channel_id=1, source_target_pairs={{0,8},{2,10},{4,12},{6,14},{8,0},{10,2},{12,4},{14,6},{1,9},{3,11}... | collective-permute-start | bytes 122888 | tf_op jit(solution)/shard_map/ppermute | solution.py:281
  4.2 2.5 %copy-start = (bf16[5120,512]{1,0:T(8,128)(2,1)S(1)}, bf16[5120,512]{1,0:T(8,128)(2,1)}, u32[]{:S(2)}) copy-start(bf16[5120,512]{1,0:T(8,128)(2,1)} %state_ref.7) | copy-start | bytes 15728644
  9.9 11.2 %copy-start.24 = (s32[40,4]{0,1:T(4,128)S(1)}, s32[40,4]{0,1:T(4,128)}, u32[]{:S(2)}) copy-start(s32[40,4]{0,1:T(4,128)} %param.13) | copy-start | bytes 1924
  9.9 11.3 %copy-start.25 = (s32[40,4]{0,1:T(4,128)S(1)}, s32[40,4]{0,1:T(4,128)}, u32[]{:S(2)}) copy-start(s32[40,4]{0,1:T(4,128)} %param.12) | copy-start | bytes 1924
  9.9 11.7 %copy-start.23 = (s32[5120]{0:T(1024)S(1)}, s32[5120]{0:T(1024)}, u32[]{:S(2)}) copy-start(s32[5120]{0:T(1024)} %param.14) | copy-start | bytes 61444
  9.9 65.9 %collective-permute-start = (bf16[2560,256]{1,0:T(8,128)(2,1)}, bf16[2560,256]{1,0:T(8,128)(2,1)}, u32[]{:S(2)}, u32[]{:S(2)}) collective-permute-start(bf16[2560,256]{1,0:T(8,128)(2,1)} %message.3), channel_id=1, source_target_pairs={{0,2},{2,4},{4,6},{6,8},{8,10},{10,12},{12,14},{1,3},{3,5},{5,7},{... | collective-permute-start | bytes 3932168 | tf_op jit(solution)/shard_map/ppermute | solution.py:317
  16.5 59.4 %collective-permute-start.2 = (bf16[2560,256]{1,0:T(8,128)(2,1)}, bf16[2560,256]{1,0:T(8,128)(2,1)}, u32[]{:S(2)}, u32[]{:S(2)}) collective-permute-start(bf16[2560,256]{1,0:T(8,128)(2,1)} %message.4), channel_id=1, source_target_pairs={{2,0},{4,2},{6,4},{8,6},{10,8},{12,10},{14,12},{3,1},{5,3},{7,5},{... | collective-permute-start | bytes 3932168 | tf_op jit(solution)/shard_map/ppermute | solution.py:315
  19.5 77.5 %collective-permute-start.7 = (bf16[2,1024,256]{2,1,0:T(8,128)(2,1)}, bf16[2,1024,256]{2,1,0:T(8,128)(2,1)}, u32[]{:S(2)}, u32[]{:S(2)}) collective-permute-start(bf16[2,1024,256]{2,1,0:T(8,128)(2,1)} %in_own.4), channel_id=1, source_target_pairs={{0,1},{1,0},{2,3},{3,2},{4,5},{5,4},{6,7},{7,6},{8,9},{9,8},{10,11... | collective-permute-start | bytes 3145736 | tf_op jit(solution)/shard_map/ppermute | solution.py:267
  21.1 28.5 %collective-permute-start.3 = (bf16[80,512]{1,0:T(8,128)(2,1)S(1)}, bf16[80,512]{1,0:T(8,128)(2,1)S(1)}, u32[]{:S(2)}, u32[]{:S(2)}) collective-permute-start(bf16[80,512]{1,0:T(8,128)(2,1)S(1)} %pad_maximum_fusion.1), channel_id=1, source_target_pairs={{0,12},{2,14},{4,0},{6,2},{8,4},{10,6},{12,8},{14,10},{1,13},{3,15... | collective-permute-start | bytes 245768 | tf_op jit(solution)/shard_map/ppermute | solution.py:281
  49.6 25.7 %collective-permute-start.4 = (bf16[160,512]{1,0:T(8,128)(2,1)S(1)}, bf16[160,512]{1,0:T(8,128)(2,1)S(1)}, u32[]{:S(2)}, u32[]{:S(2)}) collective-permute-start(bf16[160,512]{1,0:T(8,128)(2,1)S(1)} %pad_maximum_fusion), channel_id=1, source_target_pairs={{0,14},{2,0},{4,2},{6,4},{8,6},{10,8},{12,10},{14,12},{1,15},{3,1}... | collective-permute-start | bytes 491528 | tf_op jit(solution)/shard_map/ppermute | solution.py:281
  75.3 0.8 copy-start.9
  75.8 8.3 %copy-start.11 = (bf16[320,256]{1,0:T(8,128)(2,1)}, bf16[320,256]{1,0:T(8,128)(2,1)S(1)}, u32[]{:S(2)}) copy-start(bf16[320,256]{1,0:T(8,128)(2,1)S(1)} %message.5.refs_4_) | copy-start | bytes 491524
  76.1 2.5 %copy-start.1 = (bf16[40,4,128,128]{3,2,1,0:T(8,128)(2,1)S(1)}, bf16[40,4,128,128]{3,2,1,0:T(8,128)(2,1)}, u32[]{:S(2)}) copy-start(bf16[40,4,128,128]{3,2,1,0:T(8,128)(2,1)} %refs_9_.3) | copy-start | bytes 15728644
  78.6 6.9 %copy-start.4 = (bf16[2,256,512]{2,1,0:T(8,128)(2,1)S(1)}, bf16[2,256,512]{2,1,0:T(8,128)(2,1)}, u32[]{:S(2)}) copy-start(bf16[2,256,512]{2,1,0:T(8,128)(2,1)} %out_own.4) | copy-start | bytes 1572868
  84.2 0.8 copy-start.17
  85.0 10.6 %collective-permute-start.5 = (bf16[1280,256]{1,0:T(8,128)(2,1)}, bf16[1280,256]{1,0:T(8,128)(2,1)}, u32[]{:S(2)}, u32[]{:S(2)}) collective-permute-start(bf16[1280,256]{1,0:T(8,128)(2,1)} %get-tuple-element.40), channel_id=1, source_target_pairs={{0,1},{1,0},{2,3},{3,2},{4,5},{5,4},{6,7},{7,6},{8,9},{9,8},{10,11... | collective-permute-start | bytes 1966088 | tf_op jit(solution)/shard_map/ppermute | solution.py:267
  85.5 11.6 %collective-permute-start.8 = (bf16[2,256,512]{2,1,0:T(8,128)(2,1)S(1)}, bf16[2,256,512]{2,1,0:T(8,128)(2,1)}, u32[]{:S(2)}, u32[]{:S(2)}) collective-permute-start(bf16[2,256,512]{2,1,0:T(8,128)(2,1)S(1)} %copy-done.4), channel_id=1, source_target_pairs={{0,1},{1,0},{2,3},{3,2},{4,5},{5,4},{6,7},{7,6},{8,9},{9,8},{10,11... | collective-permute-start | bytes 1572872 | tf_op jit(solution)/shard_map/ppermute | solution.py:267
  85.5 11.5 %collective-permute-start.9 = (bf16[1,512,256]{2,1,0:T(8,128)(2,1)S(1)}, bf16[1,512,256]{2,1,0:T(8,128)(2,1)}, u32[]{:S(2)}, u32[]{:S(2)}) collective-permute-start(bf16[1,512,256]{2,1,0:T(8,128)(2,1)S(1)} %get-tuple-element.47.refs_0_), channel_id=1, source_target_pairs={{0,1},{1,0},{2,3},{3,2},{4,5},{5,4},{6,7},{7,6},{8,9},{9,8},{10,11... | collective-permute-start | bytes 786440 | tf_op jit(solution)/shard_map/ppermute | solution.py:267
  86.0 11.0 %slice-start = ((s8[5242880]{0:T(1024)(128)(4,1)}), s8[4194304]{0:T(1024)(128)(4,1)S(1)}, s32[]{:S(2)}) async-start(s8[5242880]{0:T(1024)(128)(4,1)} %bitcast.23), calls=%async_computation | async-start | bytes 8388608
  86.9 10.2 %slice-start.1 = ((s8[5242880]{0:T(1024)(128)(4,1)}), s8[1048576]{0:T(1024)(128)(4,1)S(1)}, s32[]{:S(2)}) async-start(s8[5242880]{0:T(1024)(128)(4,1)} %bitcast.23), calls=%async_computation.1 | async-start | bytes 2097152
  86.9 8.7 %collective-permute-start.6 = (bf16[40,256]{1,0:T(8,128)(2,1)S(1)}, bf16[40,256]{1,0:T(8,128)(2,1)S(1)}, u32[]{:S(2)}, u32[]{:S(2)}) collective-permute-start(bf16[40,256]{1,0:T(8,128)(2,1)S(1)} %slice_select_fusion), channel_id=1, source_target_pairs={{0,8},{2,10},{4,12},{6,14},{8,0},{10,2},{12,4},{14,6},{1,9},{3,11}... | collective-permute-start | bytes 61448 | tf_op jit(solution)/shard_map/ppermute | solution.py:281
  87.0 2.9 %copy-start.2 = (bf16[40,4,128,128]{3,2,1,0:T(8,128)(2,1)S(1)}, bf16[40,4,128,128]{3,2,1,0:T(8,128)(2,1)}, u32[]{:S(2)}) copy-start(bf16[40,4,128,128]{3,2,1,0:T(8,128)(2,1)} %refs_9_.3) | copy-start | bytes 15728644
  89.9 0.9 copy-start.12
  90.9 6.2 %copy-start.18 = (bf16[1280,256]{1,0:T(8,128)(2,1)S(1)}, bf16[1280,256]{1,0:T(8,128)(2,1)}, u32[]{:S(2)}) copy-start(bf16[1280,256]{1,0:T(8,128)(2,1)} %copy-done.17) | copy-start | bytes 1966084
  95.6 10.2 %collective-permute-start.10 = (bf16[80,256]{1,0:T(8,128)(2,1)S(1)}, bf16[80,256]{1,0:T(8,128)(2,1)S(1)}, u32[]{:S(2)}, u32[]{:S(2)}) collective-permute-start(bf16[80,256]{1,0:T(8,128)(2,1)S(1)} %pad_maximum_fusion.3), channel_id=1, source_target_pairs={{0,12},{2,14},{4,0},{6,2},{8,4},{10,6},{12,8},{14,10},{1,13},{3,15... | collective-permute-start | bytes 122888 | tf_op jit(solution)/shard_map/ppermute | solution.py:281
  96.4 32.7 %collective-permute-start.14 = (bf16[1280,256]{1,0:T(8,128)(2,1)S(1)}, bf16[1280,256]{1,0:T(8,128)(2,1)S(1)}, u32[]{:S(2)}, u32[]{:S(2)}) collective-permute-start(bf16[1280,256]{1,0:T(8,128)(2,1)S(1)} %get-tuple-element.55), channel_id=1, source_target_pairs={{0,1},{1,0},{2,3},{3,2},{4,5},{5,4},{6,7},{7,6},{8,9},{9,8},{10,11... | collective-permute-start | bytes 1966088 | tf_op jit(solution)/shard_map/ppermute | solution.py:267
  104.8 1.1 copy-start.15
  105.8 31.0 %copy-start.5 = (bf16[1280,256]{1,0:T(8,128)(2,1)}, bf16[1280,256]{1,0:T(8,128)(2,1)S(1)}, u32[]{:S(2)}) copy-start(bf16[1280,256]{1,0:T(8,128)(2,1)S(1)} %get-tuple-element.52) | copy-start | bytes 1966084
  105.9 38.9 %collective-permute-start.12 = (bf16[1280,256]{1,0:T(8,128)(2,1)S(1)}, bf16[1280,256]{1,0:T(8,128)(2,1)S(1)}, u32[]{:S(2)}, u32[]{:S(2)}) collective-permute-start(bf16[1280,256]{1,0:T(8,128)(2,1)S(1)} %get-tuple-element.52), channel_id=1, source_target_pairs={{2,0},{4,2},{6,4},{8,6},{10,8},{12,10},{14,12},{1,3},{3,5},{5,7},{... | collective-permute-start | bytes 1966088 | tf_op jit(solution)/shard_map/ppermute | solution.py:371
  107.8 11.7 %collective-permute-start.18 = (bf16[160,256]{1,0:T(8,128)(2,1)S(1)}, bf16[160,256]{1,0:T(8,128)(2,1)S(1)}, u32[]{:S(2)}, u32[]{:S(2)}) collective-permute-start(bf16[160,256]{1,0:T(8,128)(2,1)S(1)} %pad_maximum_fusion.2), channel_id=1, source_target_pairs={{0,14},{2,0},{4,2},{6,4},{8,6},{10,8},{12,10},{14,12},{1,15},{3,1}... | collective-permute-start | bytes 245768 | tf_op jit(solution)/shard_map/ppermute | solution.py:281
  119.5 17.4 %copy-start.19 = (bf16[320,256]{1,0:T(8,128)(2,1)}, bf16[320,256]{1,0:T(8,128)(2,1)S(1)}, u32[]{:S(2)}) copy-start(bf16[320,256]{1,0:T(8,128)(2,1)S(1)} %constant_dynamic-update-slice_fusion.3.keep_ref) | copy-start | bytes 491524
  119.5 22.2 %collective-permute-start.19 = (bf16[320,256]{1,0:T(8,128)(2,1)S(1)}, bf16[320,256]{1,0:T(8,128)(2,1)S(1)}, u32[]{:S(2)}, u32[]{:S(2)}) collective-permute-start(bf16[320,256]{1,0:T(8,128)(2,1)S(1)} %constant_dynamic-update-slice_fusion.3.keep_ref), channel_id=1, source_target_pairs={{0,1},{1,0},{2,3},{3,2},{4,5},{5,4},{6,7},{7,6},{8,9},{9,8},{10,11... | collective-permute-start | bytes 491528 | tf_op jit(solution)/shard_map/ppermute | solution.py:267
  127.1 33.3 %collective-permute-start.13 = (bf16[1280,256]{1,0:T(8,128)(2,1)}, bf16[1280,256]{1,0:T(8,128)(2,1)}, u32[]{:S(2)}, u32[]{:S(2)}) collective-permute-start(bf16[1280,256]{1,0:T(8,128)(2,1)} %get-tuple-element.53), channel_id=1, source_target_pairs={{2,1},{4,3},{6,5},{8,7},{10,9},{12,11},{14,13},{1,2},{3,4},{5,6},{... | collective-permute-start | bytes 1966088 | tf_op jit(solution)/shard_map/ppermute | solution.py:372
  129.0 31.4 %collective-permute-start.11 = (bf16[1280,256]{1,0:T(8,128)(2,1)}, bf16[1280,256]{1,0:T(8,128)(2,1)}, u32[]{:S(2)}, u32[]{:S(2)}) collective-permute-start(bf16[1280,256]{1,0:T(8,128)(2,1)} %get-tuple-element.53), channel_id=1, source_target_pairs={{0,1},{1,0},{2,3},{3,2},{4,5},{5,4},{6,7},{7,6},{8,9},{9,8},{10,11... | collective-permute-start | bytes 1966088 | tf_op jit(solution)/shard_map/ppermute | solution.py:267
  136.9 1.1 copy-start.13
  138.0 27.0 %collective-permute-start.16 = (bf16[1280,256]{1,0:T(8,128)(2,1)}, bf16[1280,256]{1,0:T(8,128)(2,1)}, u32[]{:S(2)}, u32[]{:S(2)}) collective-permute-start(bf16[1280,256]{1,0:T(8,128)(2,1)} %get-tuple-element.56), channel_id=1, source_target_pairs={{2,0},{4,2},{6,4},{8,6},{10,8},{12,10},{14,12},{1,3},{3,5},{5,7},{... | collective-permute-start | bytes 1966088 | tf_op jit(solution)/shard_map/ppermute | solution.py:371
  141.7 0.7 copy-start.21
  142.4 32.1 %collective-permute-start.17 = (bf16[1280,256]{1,0:T(8,128)(2,1)}, bf16[1280,256]{1,0:T(8,128)(2,1)}, u32[]{:S(2)}, u32[]{:S(2)}) collective-permute-start(bf16[1280,256]{1,0:T(8,128)(2,1)} %get-tuple-element.57), channel_id=1, source_target_pairs={{2,1},{4,3},{6,5},{8,7},{10,9},{12,11},{14,13},{1,2},{3,4},{5,6},{... | collective-permute-start | bytes 1966088 | tf_op jit(solution)/shard_map/ppermute | solution.py:372
  144.8 0.8 copy-start.7
  145.6 28.8 %collective-permute-start.15 = (bf16[1280,256]{1,0:T(8,128)(2,1)}, bf16[1280,256]{1,0:T(8,128)(2,1)}, u32[]{:S(2)}, u32[]{:S(2)}) collective-permute-start(bf16[1280,256]{1,0:T(8,128)(2,1)} %get-tuple-element.57), channel_id=1, source_target_pairs={{0,1},{1,0},{2,3},{3,2},{4,5},{5,4},{6,7},{7,6},{8,9},{9,8},{10,11... | collective-permute-start | bytes 1966088 | tf_op jit(solution)/shard_map/ppermute | solution.py:267
  146.6 1.0 copy-start.10
  147.6 0.9 copy-start.20
  148.5 0.9 copy-start.22
  149.4 25.0 %copy-start.6 = (bf16[1280,256]{1,0:T(8,128)(2,1)S(1)}, bf16[1280,256]{1,0:T(8,128)(2,1)}, u32[]{:S(2)}) copy-start(bf16[1280,256]{1,0:T(8,128)(2,1)} %copy-done.5) | copy-start | bytes 1966084
  149.4 25.0 %copy-start.8 = (bf16[1280,256]{1,0:T(8,128)(2,1)S(1)}, bf16[1280,256]{1,0:T(8,128)(2,1)}, u32[]{:S(2)}) copy-start(bf16[1280,256]{1,0:T(8,128)(2,1)} %copy-done.7) | copy-start | bytes 1966084
  174.4 2.5 %copy-start.3 = (bf16[40,4,128,128]{3,2,1,0:T(8,128)(2,1)S(1)}, bf16[40,4,128,128]{3,2,1,0:T(8,128)(2,1)}, u32[]{:S(2)}) copy-start(bf16[40,4,128,128]{3,2,1,0:T(8,128)(2,1)} %refs_9_.3) | copy-start | bytes 15728644
  181.5 5.3 %copy-start.16 = (bf16[1280,512]{1,0:T(8,128)(2,1)S(1)}, bf16[1280,512]{1,0:T(8,128)(2,1)}, u32[]{:S(2)}) copy-start(bf16[1280,512]{1,0:T(8,128)(2,1)} %copy-done.15) | copy-start | bytes 3932164
  181.5 4.7 %collective-permute-start.20 = (bf16[1280,256]{1,0:T(8,128)(2,1)S(1)}, bf16[1280,256]{1,0:T(8,128)(2,1)S(1)}, u32[]{:S(2)}, u32[]{:S(2)}) collective-permute-start(bf16[1280,256]{1,0:T(8,128)(2,1)S(1)} %get-tuple-element.59), channel_id=1, source_target_pairs={{0,1},{1,0},{2,3},{3,2},{4,5},{5,4},{6,7},{7,6},{8,9},{9,8},{10,11... | collective-permute-start | bytes 1966088 | tf_op jit(solution)/shard_map/ppermute | solution.py:267
  186.2 6.8 %collective-permute-start.22 = (bf16[1280,256]{1,0:T(8,128)(2,1)S(1)}, bf16[1280,256]{1,0:T(8,128)(2,1)S(1)}, u32[]{:S(2)}, u32[]{:S(2)}) collective-permute-start(bf16[1280,256]{1,0:T(8,128)(2,1)S(1)} %get-tuple-element.67), channel_id=1, source_target_pairs={{0,1},{1,0},{2,3},{3,2},{4,5},{5,4},{6,7},{7,6},{8,9},{9,8},{10,11... | collective-permute-start | bytes 1966088 | tf_op jit(solution)/shard_map/ppermute | solution.py:267
  186.8 6.2 %copy-start.14 = (bf16[1280,512]{1,0:T(8,128)(2,1)S(1)}, bf16[1280,512]{1,0:T(8,128)(2,1)}, u32[]{:S(2)}) copy-start(bf16[1280,512]{1,0:T(8,128)(2,1)} %copy-done.13) | copy-start | bytes 3932164
  193.0 6.7 %collective-permute-start.21 = (bf16[1280,512]{1,0:T(8,128)(2,1)S(1)}, bf16[1280,512]{1,0:T(8,128)(2,1)S(1)}, u32[]{:S(2)}, u32[]{:S(2)}) collective-permute-start(bf16[1280,512]{1,0:T(8,128)(2,1)S(1)} %get-tuple-element.64), channel_id=1, source_target_pairs={{0,1},{1,0},{2,3},{3,2},{4,5},{5,4},{6,7},{7,6},{8,9},{9,8},{10,11... | collective-permute-start | bytes 3932168 | tf_op jit(solution)/shard_map/ppermute | solution.py:267
  199.2 3.1 %collective-permute-start.23 = (bf16[1280,512]{1,0:T(8,128)(2,1)S(1)}, bf16[1280,512]{1,0:T(8,128)(2,1)S(1)}, u32[]{:S(2)}, u32[]{:S(2)}) collective-permute-start(bf16[1280,512]{1,0:T(8,128)(2,1)S(1)} %get-tuple-element.69), channel_id=1, source_target_pairs={{0,1},{1,0},{2,3},{3,2},{4,5},{5,4},{6,7},{7,6},{8,9},{9,8},{10,11... | collective-permute-start | bytes 3932168 | tf_op jit(solution)/shard_map/ppermute | solution.py:267

commit v3 on v0

v3 whole, which is shorter than its diff:
```python
import functools

import jax
import jax.numpy as jnp
from jax import lax
from jax.experimental import pallas as pl
from jax.experimental.pallas import tpu as pltpu
from jax.sharding import PartitionSpec as P

CN_DEV = 40
LAYERS = 2
HALO_BLK = 20
CHUNKS = 2
MESSAGE_TILE = 1280
F32 = jnp.float32
BF16 = jnp.bfloat16
IN_VMEM = pl.BlockSpec(memory_space=pltpu.VMEM)
IN_HBM = pl.BlockSpec(memory_space=pltpu.HBM)


def silu(v):
    return 0.5 * v * (1.0 + jnp.tanh(0.5 * v))


def dot(a, b):
    return jnp.dot(a, b, preferred_element_type=F32)


def normalize(parts):
    width = sum(part.shape[-1] for part in parts)
    mean = sum(jnp.sum(part, axis=-1, keepdims=True) for part in parts) / width
    center = [part - mean for part in parts]
    spread = sum(jnp.sum(part * part, axis=-1, keepdims=True) for part in center) / width
    scale = lax.rsqrt(spread + 1e-05)
    return [(part * scale).astype(BF16) for part in center]


def params(mib):
    return pltpu.CompilerParams(vmem_limit_bytes=mib << 20)


def shaped(array):
    return jax.ShapeDtypeStruct(array.shape, array.dtype)


def run_copies(pairs, sems):
    copies = [pltpu.make_async_copy(src, dst, sems.at[pos]) for pos, (src, dst) in enumerate(pairs)]
    for copy in copies:
        copy.start()
    return copies


def wait_all(copies):
    for copy in copies:
        copy.wait()


def message_kernel(state_ref, weight_ref, out_ref):
    (normed,) = normalize([state_ref[...].astype(F32)])
    message = silu(dot(normed, weight_ref[0])).astype(BF16)
    out_ref[...] = message.astype(out_ref.dtype)


def message_call(state, weight, start, rows, tile):
    first = start // tile
    return pl.pallas_call(
        message_kernel,
        grid=(rows // tile,),
        in_specs=[
            pl.BlockSpec((tile, state.shape[1]), lambda i: (first + i, 0)),
            pl.BlockSpec((1,) + weight.shape[1:], lambda i: (0, 0, 0)),
        ],
        out_specs=pl.BlockSpec((tile, weight.shape[2]), lambda i: (i, 0)),
        out_shape=jax.ShapeDtypeStruct((rows, weight.shape[2]), BF16),
        compiler_params=params(56),
        name="message",
    )(state, weight)


def coarse_message_call(state, weight):
    return pl.pallas_call(
        message_kernel,
        in_specs=[IN_VMEM, IN_VMEM],
        out_specs=IN_VMEM,
        out_shape=pltpu.VMEM((state.shape[0], weight.shape[2]), F32),
        compiler_params=params(12),
        name="coarse_message",
    )(state, weight)


def stage_kernel(count, feat_ref, *refs):
    fine, coarse, state, low, high = refs[:5]
    weights = refs[5 : 5 + count]
    fine_out, coarse_out, state_out, table = refs[5 + count : 9 + count]
    weights_out = refs[9 + count : 9 + 2 * count]
    coarse_buf, sems = refs[9 + 2 * count :]
    block = fine.shape[-1]
    half_rows = low.shape[0]
    pairs = [(coarse, coarse_buf)]
    pairs += [
        (fine.at[:, kind], fine_out.at[:, :, pl.ds(kind * block, block)]) for kind in range(fine.shape[1])
    ]
    start = pl.multiple_of(feat_ref[0] * half_rows, 16)
    pairs.append((state.at[pl.ds(start, half_rows)], state_out))
    pairs.append((low, table.at[pl.ds(HALO_BLK * block, half_rows)]))
    pairs.append((high, table.at[pl.ds(HALO_BLK * block + half_rows, half_rows)]))
    pairs += list(zip(weights, weights_out))
    copies = run_copies(pairs, sems)
    copies[0].wait()

    def turn(pos, carry):
        coarse_out[pos] = jnp.transpose(coarse_buf[pos])
        return carry

    lax.fori_loop(0, coarse.shape[0], turn, 0)
    wait_all(copies[1:])


def stage_call(feat, fine, coarse, state, low, high, weights):
    blocks, kinds, block, _ = fine.shape
    rows, columns = low.shape
    out_shape = [
        pltpu.VMEM((blocks, block, kinds * block), BF16),
        pltpu.VMEM((blocks, block, coarse.shape[1]), BF16),
        pltpu.VMEM((rows, state.shape[1]), BF16),
        pltpu.VMEM((2 * rows + 2 * HALO_BLK * block, columns), BF16),
    ] + [pltpu.VMEM(weight.shape, BF16) for weight in weights]
    copies = 1 + kinds + 3 + len(weights)
    return pl.pallas_call(
        functools.partial(stage_kernel, len(weights)),
        grid_spec=pltpu.PrefetchScalarGridSpec(
            num_scalar_prefetch=1,
            in_specs=[IN_HBM] * (5 + len(weights)),
            out_specs=[IN_VMEM] * len(out_shape),
            scratch_shapes=[pltpu.VMEM(coarse.shape, BF16), pltpu.SemaphoreType.DMA((copies,))],
        ),
        out_shape=out_shape,
        compiler_params=params(12),
        name="stage",
    )(feat, fine, coarse, state, low, high, *weights)


def local_kernel(places, feat_ref, *refs):
    pieces = refs[: len(places)]
    table, sems = refs[-2:]
    pairs = []
    for place, piece in zip(places, pieces):
        start = pl.multiple_of(place(feat_ref[0]), 16)
        pairs.append((piece, table.at[pl.ds(start, piece.shape[0])]))
    wait_all(run_copies(pairs, sems))


def local_call(feat, places, pieces, table):
    return pl.pallas_call(
        functools.partial(local_kernel, places),
        grid_spec=pltpu.PrefetchScalarGridSpec(
            num_scalar_prefetch=1,
            in_specs=[pl.BlockSpec(memory_space=pl.ANY)] * len(pieces) + [IN_VMEM],
            out_specs=IN_VMEM,
            scratch_shapes=[pltpu.SemaphoreType.DMA((len(pieces),))],
        ),
        out_shape=pltpu.VMEM(table.shape, BF16),
        input_output_aliases={len(pieces) + 1: 0},
        compiler_params=params(4),
        name="local_messages",
    )(feat, *pieces, table)


def aggregate_kernel(places, chunk, feat_ref, links, *refs):
    fine, coarse_tile, coarse, degree = refs[:4]
    pieces = refs[4 : 4 + len(places)]
    if places:
        send, keep, first_rows, table, sems = refs[5 + len(places) :]
        pairs = []
        for place, piece in zip(places, pieces):
            start = pl.multiple_of(place(feat_ref[0]), 16)
            pairs.append((piece, table.at[pl.ds(start, piece.shape[0])]))
        copies = run_copies(pairs, sems)
    else:
        table, send, keep = refs[4:]
        copies = []
    blocks, block, fine_width = fine.shape
    kinds = fine_width // block
    count = send.shape[0] // block
    feat = feat_ref[0]
    wait_all(copies)
    for out_ref, which in ((send, 1 - feat), (keep, feat)):
        scale = 1.0 / jnp.transpose(degree[which * CHUNKS + chunk].astype(F32))
        first = which * (blocks // 2) + chunk * count
        for pos in range(count):
            row = (first + pos) * kinds
            chosen = jnp.concatenate(
                [table[pl.ds(pl.multiple_of(links[row + kind], block), block), :] for kind in range(kinds)], axis=0
            )
            base = blocks * kinds + row
            stacked = jnp.concatenate(
                [
                    coarse[pl.ds(pl.multiple_of(links[base + kind], 8), CN_DEV), :]
                    for kind in range(kinds)
                ],
                axis=0,
            ).astype(BF16)
            summed = dot(fine[first + pos], chosen) + dot(coarse_tile[first + pos], stacked)
            result = (summed * scale[:, pos : pos + 1]).astype(BF16)
            out_ref[pos * block : (pos + 1) * block, :] = result
    if places:

        @pl.when(feat == 0)
        def _():
            first_rows[...] = keep[:CN_DEV, :]

        @pl.when(feat != 0)
        def _():
            first_rows[...] = send[:CN_DEV, :]


def aggregate_call(feat, links, staged, coarse, degree, table, chunk, places=(), pieces=()):
    fine, coarse_tile = staged
    blocks, block, _ = fine.shape
    columns = table.shape[1]
    rows = blocks // (2 * CHUNKS) * block
    out_shape = [pltpu.VMEM((rows, columns), BF16)] * 2
    aliases = {}
    scratch = []
    if pieces:
        out_shape += [pltpu.VMEM((CN_DEV, columns), BF16), pltpu.VMEM(table.shape, BF16)]
        aliases = {6 + len(pieces): 3}
        scratch = [pltpu.SemaphoreType.DMA((len(pieces),))]
    return pl.pallas_call(
        functools.partial(aggregate_kernel, places, chunk),
        grid_spec=pltpu.PrefetchScalarGridSpec(
            num_scalar_prefetch=2,
            in_specs=[IN_VMEM] * 4 + [IN_HBM] * len(pieces) + [IN_VMEM],
            out_specs=[IN_VMEM] * len(out_shape),
            scratch_shapes=scratch,
        ),
        out_shape=out_shape,
        input_output_aliases=aliases,
        compiler_params=params(12),
        name="aggregate",
    )(feat, links, fine, coarse_tile, coarse, degree, *pieces, table)


def node_kernel(mode, layer, start, chunk, feat_ref, *refs):
    state_ref, keep, recv, in_own, in_other, out_own, out_other = refs[:7]
    refs = refs[7:]
    feat = feat_ref[0]
    rows, columns = keep.shape
    width = state_ref.shape[1]
    state = state_ref[start : start + rows, :].astype(F32)
    joined = normalize([state, keep[...].astype(F32), recv[...].astype(F32)])
    keep_at = pl.multiple_of(width + feat * columns, columns)
    recv_at = pl.multiple_of(width + (1 - feat) * columns, columns)
    update = None
    for in_ref, out_ref in ((in_own, out_own), (in_other, out_other)):
        hidden = (
            dot(joined[0], in_ref[layer, :width, :])
            + dot(joined[1], in_ref[layer, pl.ds(keep_at, columns), :])
            + dot(joined[2], in_ref[layer, pl.ds(recv_at, columns), :])
        )
        part = dot(silu(hidden).astype(BF16), out_ref[layer])
        update = part if update is None else update + part
    new_state = (state + update).astype(BF16)
    if mode == "last":
        state_out, out, sem = refs[-3:]
        state_out[...] = new_state
        half_rows = rows * CHUNKS
        at = pl.multiple_of(feat * half_rows + chunk * rows, 16)
        copy = pltpu.make_async_copy(state_out, out.at[pl.ds(at, rows)], sem)
        copy.start()
        copy.wait()
        return
    (normed,) = normalize([new_state.astype(F32)])
    if mode == "coarse":
        msg_own, own_out = refs
        own_out[...] = silu(dot(normed, msg_own[layer + 1])).astype(BF16).astype(F32)
        return
    msg_own, msg_other, state_out, own_out, other_out = refs
    own_out[...] = silu(dot(normed, msg_own[layer + 1])).astype(BF16)
    other_out[...] = silu(dot(normed, msg_other[layer + 1])).astype(BF16)
    state_out[...] = new_state


def node_call(mode, layer, feat, state, start, chunk, keep, recv, weights, out=None, total=0):
    rows, columns = keep.shape
    width = state.shape[1]
    operands = [state, keep, recv, *weights[:4]]
    aliases = {}
    scratch = []
    if mode == "last":
        out_shape = [pltpu.VMEM((rows, width), BF16), jax.ShapeDtypeStruct((total, width), BF16)]
        out_specs = [IN_VMEM, pl.BlockSpec(memory_space=pl.ANY)]
        in_specs = [IN_VMEM] * len(operands)
        scratch = [pltpu.SemaphoreType.DMA(())]
        if out is not None:
            aliases = {len(operands) + 1: 1}
            operands.append(out)
            in_specs.append(pl.BlockSpec(memory_space=pl.ANY))
    else:
        if mode == "coarse":
            operands.append(weights[4])
            out_shape = [pltpu.VMEM((rows, columns), F32)]
        else:
            operands += weights[4:]
            out_shape = [pltpu.VMEM((rows, shape), BF16) for shape in (width, columns, columns)]
        in_specs = [IN_VMEM] * len(operands)
        out_specs = [IN_VMEM] * len(out_shape)
    return pl.pallas_call(
        functools.partial(node_kernel, mode, layer, start, chunk),
        grid_spec=pltpu.PrefetchScalarGridSpec(
            num_scalar_prefetch=1, in_specs=in_specs, out_specs=out_specs, scratch_shapes=scratch
        ),
        out_shape=out_shape,
        input_output_aliases=aliases,
        compiler_params=params(28),
        name="node_" + mode,
    )(feat, *operands)


def assemble_kernel(feat_ref, *refs):
    pieces = refs[:CHUNKS]
    out, sems = refs[-2:]
    pairs = []
    for chunk, piece in enumerate(pieces):
        rows = piece.shape[0]
        at = pl.multiple_of((1 - feat_ref[0]) * rows * CHUNKS + chunk * rows, 16)
        pairs.append((piece, out.at[pl.ds(at, rows)]))
    wait_all(run_copies(pairs, sems))


def assemble_call(feat, pieces, out):
    return pl.pallas_call(
        assemble_kernel,
        grid_spec=pltpu.PrefetchScalarGridSpec(
            num_scalar_prefetch=1,
            in_specs=[IN_VMEM] * len(pieces) + [pl.BlockSpec(memory_space=pl.ANY)],
            out_specs=pl.BlockSpec(memory_space=pl.ANY),
            scratch_shapes=[pltpu.SemaphoreType.DMA((len(pieces),))],
        ),
        out_shape=shaped(out),
        input_output_aliases={len(pieces) + 1: 0},
        compiler_params=params(4),
        name="assemble",
    )(feat, *pieces, out)


def swap_feat(array):
    return lax.ppermute(array, "feat", [(0, 1), (1, 0)])


def fetch(held, stride):
    count = lax.axis_size("patch")
    return lax.ppermute(held, "patch", [(pos, (pos - stride) % count) for pos in range(count)])


def even_offsets(count):
    assert count & (count - 1) == 0
    offsets = [0]
    stride = count // 2
    while stride > 1:
        offsets += [offset + stride for offset in offsets]
        stride //= 2
    return offsets


def shards(
    node_state, fine_tile, coarse_tile, fine_index, coarse_index, node_degree, w_msg, w_in, w_out
):
    barrier = lax.optimization_barrier
    patches = lax.axis_size("patch")
    patch_pos = lax.axis_index("patch")
    feat_pos = lax.axis_index("feat")
    feat = feat_pos.astype(jnp.int32).reshape(1)
    blocks, kinds, block, _ = fine_tile.shape
    half = blocks // 2
    half_rows = half * block
    halo_rows = HALO_BLK * block
    assert half == HALO_BLK and half % CHUNKS == 0
    chunk_rows = half_rows // CHUNKS

    forward = [(pos, pos + 1) for pos in range(patches - 1)]
    backward = [(target, source) for source, target in forward]
    sides = ((0, backward), (1, forward))
    own_patch = [(2 * src + side, 2 * dst + side) for side, pairs in sides for src, dst in pairs]
    other_patch = [(2 * src + side, 2 * dst + 1 - side) for side, pairs in sides for src, dst in pairs]
    evens = even_offsets(patches)

    held = node_state[:CN_DEV]
    strides = [patches >> step for step in range(1, patches.bit_length())]
    held = jnp.concatenate([held, fetch(held, strides[0])], axis=0)
    low = message_call(node_state, w_msg, 0, half_rows, MESSAGE_TILE)
    low, held = barrier((low, held))
    high_halo = lax.ppermute(low, "patch", backward)
    high = message_call(node_state, w_msg, half_rows, half_rows, MESSAGE_TILE)
    low_halo = lax.ppermute(high, "patch", forward)
    for stride in strides[1:]:
        held = jnp.concatenate([held, fetch(held, stride)], axis=0)
    coarse_state = held

    offsets = evens + [offset + 1 for offset in evens]
    links = (fine_index - (patch_pos * blocks - HALO_BLK)).reshape(-1) * block
    away = ((coarse_index - patch_pos) % patches).reshape(-1)
    coarse_links = sum(jnp.where(away == offset, pos * CN_DEV, 0) for pos, offset in enumerate(offsets))
    links = jnp.concatenate([links, coarse_links])
    degree = node_degree.reshape(2 * CHUNKS, half // CHUNKS, block)

    w_in, w_out, w_late, _ = barrier((w_in, w_out, w_msg, high))
    weights = [w_in, swap_feat(w_in), w_out, swap_feat(w_out), w_late, swap_feat(w_late)]
    fine, ctile, state, table, *weights = stage_call(
        feat, fine_tile, jnp.swapaxes(coarse_tile, 1, 2), node_state, low, high, weights
    )
    staged = (fine, ctile)
    coarse = coarse_message_call(coarse_state, w_late)

    places = (lambda feat: 0, lambda feat: halo_rows + 2 * half_rows)
    send, keep, first_rows, table = aggregate_call(
        feat, links, staged, coarse, degree, table, 0, places, (low_halo, high_halo)
    )
    recv = swap_feat(send)
    others = [fetch(first_rows, offset) for offset in evens[1:]]
    send_1, keep_1 = aggregate_call(feat, links, staged, coarse, degree, table, 1)
    recv, keep, send_1, others = barrier((recv, keep, send_1, others))
    held = jnp.concatenate([first_rows, *others], axis=0)
    held = jnp.concatenate([held, fetch(held, 1)], axis=0)
    inputs = [(keep, recv), (keep_1, swap_feat(send_1))]
    states = []
    local = []
    halo = []
    for chunk in range(CHUNKS):
        new_state, own, other = node_call(
            "mid", 0, feat, state, chunk * chunk_rows, chunk, *inputs[chunk], weights
        )
        if chunk == 0:
            own, other, held = barrier((own, other, held))
        halo += [lax.ppermute(own, ("patch", "feat"), own_patch), lax.ppermute(other, ("patch", "feat"), other_patch)]
        local += [own, swap_feat(other)]
        states.append(new_state)
    (coarse,) = node_call("coarse", 0, feat, coarse_state, 0, 0, held, swap_feat(held), weights)

    local_places = []
    halo_places = []
    for chunk in range(CHUNKS):
        at = chunk * chunk_rows
        local_places += [
            lambda feat, at=at: halo_rows + feat * half_rows + at,
            lambda feat, at=at: halo_rows + (1 - feat) * half_rows + at,
        ]
        halo_places += [
            lambda feat, at=at: (1 - feat) * (halo_rows + 2 * half_rows) + at,
            lambda feat, at=at: feat * (halo_rows + 2 * half_rows) + at,
        ]
    table = local_call(feat, local_places, local, table)
    send, keep, _, table = aggregate_call(
        feat, links, staged, coarse, degree, table, 0, halo_places, halo
    )
    recv = swap_feat(send)
    send_1, keep_1 = aggregate_call(feat, links, staged, coarse, degree, table, 1)
    recv, keep, send_1 = barrier((recv, keep, send_1))
    inputs = [(keep, recv), (keep_1, swap_feat(send_1))]
    out = None
    swapped = []
    for chunk in range(CHUNKS):
        new_state, out = node_call(
            "last", 1, feat, states[chunk], 0, chunk, *inputs[chunk], weights, out, node_state.shape[0]
        )
        swapped.append(swap_feat(new_state))
    return assemble_call(feat, swapped, out)


def solution(mesh):
    return jax.shard_map(
        shards,
        mesh=mesh,
        in_specs=(
            P(("member", "patch"), None),
            P("patch", None, None, None),
            P("patch", None, None),
            P("patch", None),
            P("patch", None),
            P("patch"),
            P(None, None, "feat"),
            P(None, None, "feat"),
            P(None, "feat", None),
        ),
        out_specs=P(("member", "patch"), None),
        check_vma=False,
    )
```

time: 628 us -> 195 us (0.31)
  blocking collectives: 249 us -> 0 us
  other arithmetic: 101 us -> 4.24 us
  matrix products: 87.5 us -> 0 us
  Pallas kernels: 0 us -> 47 us
  local copies, waits for them, and re-layouts: 55.5 us -> 16.1 us
  starting transfers between devices: 12.6 us -> 28.5 us
  between operations: 13.6 us -> 0.54 us
  waiting for transfers between devices: 105 us -> 97 us
    all_gather x2 -> x0, blocking collectives: 249 us -> none  [shards(): coarse_all = lax.all_gather(source[:CN_DEV], 'patch', axis=0, tiled=True)]
    ppermute x4 -> x25, waiting for transfers between devices: 0.01 us -> 97 us  [the longest x7 51.9 us: fetch(): lax.ppermute(held, 'patch', [(pos, (pos - stride) % count) for pos in ran...]
    dot_general x8 -> x0, matrix products: 87.5 us -> none  [the longest x2 34.9 us: shards(): jnp.einsum('bkrs,bksw->brw', fine_tile, chosen, preferred_element_type=jn...]
    psum x2 -> x0, waiting for transfers between devices: 72.8 us -> none  [shards(): lax.psum(partial_sum.astype(jnp.bfloat16), 'feat').astype(jnp.float32)]
    pallas_call x0 -> x15, Pallas kernels: none -> 47 us  [the longest x5 19.7 us: node_call(): pl.pallas_call(functools.partial(node_kernel, mode, layer, start, chunk),...]
    gather x4 -> x0, local copies, waits for them, and re-layouts: 44.7 us -> none  [the longest x2 27.3 us: shards(): chosen = padded_blocks[local_links]]
    concatenate x2 -> x4, other arithmetic: 38.7 us -> 1.67 us  [the longest x1 0.9 us: shards(): held = jnp.concatenate([held, fetch(held, stride)], axis=0)]
    reduce_sum x6 -> x0, other arithmetic: 34 us -> none  [the longest x4 27.2 us: layer_norm(): spread = jnp.mean(center * center, axis=-1, keepdims=True)]
  transfers between devices with their start and end apart: 8 -> 25, of which waited for: 4 -> 8; matrix products, arithmetic and copies ran while one was open for 7% -> 7% of each run, Pallas kernels for 0% -> 20%
where the time goes in v3:
time: 195 us; the launch traced here: 193 us
  waiting for transfers between devices  97 us (50%)
  Pallas kernels  47 us (24%)
  starting transfers between devices  28.5 us (15%)
  local copies, waits for them, and re-layouts  16.1 us (8%)
  other arithmetic  4.24 us (2%)
    ppermute x7, waiting for transfers between devices, fetch(): lax.ppermute(held, 'patch', [(pos, (pos - stride) % count) for pos in ran...  51.9 us
    ppermute x2, waiting for transfers between devices, shards(): lax.ppermute(own, ('patch', 'feat'), own_patch)  34.2 us
    pallas_call x5, Pallas kernels, node_call(): pl.pallas_call(functools.partial(node_kernel, mode, layer, start, chunk),...  19.7 us
    pallas_call x4, Pallas kernels, aggregate_call(): pl.pallas_call(functools.partial(aggregate_kernel, places, chunk), grid_s...  10.6 us
    pallas_call x2, Pallas kernels, message_call(): pl.pallas_call(message_kernel, grid=(rows // tile,), in_specs=[pl.BlockSp...  9.37 us
    unnamed x20, local copies, waits for them, and re-layouts  8.1 us
    ppermute x2, waiting for transfers between devices, shards(): lax.ppermute(other, ('patch', 'feat'), other_patch)  7.87 us
    ppermute x12, starting transfers between devices, swap_feat(): return lax.ppermute(array, 'feat', [(0, 1), (1, 0)])  6.62 us
  transfers between devices with their start and end apart: 25, of which 8 were waited for; matrix products, arithmetic and copies ran while one was open for 7% of the time, Pallas kernels for 20%

profile of v3, /device:TPU:9, one launch (start us, length us, event | category | flops | bytes accessed | tf_op | source)
XLA Modules:
  0.0 193.3 jit_solution(11543837487128186522)
XLA Ops:
  0.0 0.8 slice.3
  0.8 2.3 %collective-permute-start = (bf16[40,512]{1,0:T(8,128)(2,1)S(1)}, bf16[40,512]{1,0:T(8,128)(2,1)S(1)}, u32[]{:S(2)}, u32[]{:S(2)}) collective-permute-start(bf16[40,512]{1,0:T(8,128)(2,1)S(1)} %slice.3), channel_id=1, source_target_pairs={{0,8},{2,10},{4,12},{6,14},{8,0},{10,2},{12,4},{14,6},{1,9},{3,11}... | collective-permute-start | bytes 122888 | tf_op jit(solution)/shard_map/ppermute | solution.py:353
  3.1 4.6 %message.3.refs_4_ = bf16[2560,256]{1,0:T(8,128)(2,1)} custom-call(bf16[5120,512]{1,0:T(8,128)(2,1)} %refs_2_.1, bf16[2,512,256]{2,1,0:T(8,128)(2,1)} %weight_ref.4), custom_call_target="tpu_custom_call" | custom-call | tf_op jit(solution)/shard_map/message/pallas_call | solution.py:66
  7.7 3.3 %collective-permute-start.6 = (bf16[2560,256]{1,0:T(8,128)(2,1)}, bf16[2560,256]{1,0:T(8,128)(2,1)}, u32[]{:S(2)}, u32[]{:S(2)}) collective-permute-start(bf16[2560,256]{1,0:T(8,128)(2,1)} %message.3.refs_4_), channel_id=1, source_target_pairs={{0,2},{2,4},{4,6},{6,8},{8,10},{10,12},{12,14},{1,3},{3,5},{5,7},{... | collective-permute-start | bytes 3932168 | tf_op jit(solution)/shard_map/ppermute | solution.py:395
  11.0 4.7 %message.2.refs_3_ = bf16[2560,256]{1,0:T(8,128)(2,1)} custom-call(bf16[5120,512]{1,0:T(8,128)(2,1)} %refs_2_.1, bf16[2,512,256]{2,1,0:T(8,128)(2,1)} %weight_ref.4), custom_call_target="tpu_custom_call" | custom-call | tf_op jit(solution)/shard_map/message/pallas_call | solution.py:66
  15.8 3.2 %collective-permute-start.7 = (bf16[2560,256]{1,0:T(8,128)(2,1)}, bf16[2560,256]{1,0:T(8,128)(2,1)}, u32[]{:S(2)}, u32[]{:S(2)}) collective-permute-start(bf16[2560,256]{1,0:T(8,128)(2,1)} %message.2.refs_3_), channel_id=1, source_target_pairs={{2,0},{4,2},{6,4},{8,6},{10,8},{12,10},{14,12},{3,1},{5,3},{7,5},{... | collective-permute-start | bytes 3932168 | tf_op jit(solution)/shard_map/ppermute | solution.py:393
  19.0 0.1 collective-permute-start.4
  19.0 1.6 collective-permute-start.1
  20.6 0.1 collective-permute-start.2
  20.7 28.3 %collective-permute-done.4 = bf16[80,512]{1,0:T(8,128)(2,1)} collective-permute-done((bf16[80,512]{1,0:T(8,128)(2,1)S(1)}, bf16[80,512]{1,0:T(8,128)(2,1)}, u32[]{:S(2)}, u32[]{:S(2)}) %collective-permute-start.4) | collective-permute-done | bytes 81952 | tf_op jit(solution)/shard_map/ppermute | solution.py:353
  49.0 0.9 pad_maximum_fusion
  49.9 0.1 collective-permute-start.5
  50.0 1.3 add_add_fusion
  51.3 22.0 %collective-permute-done.5 = bf16[160,512]{1,0:T(8,128)(2,1)} collective-permute-done((bf16[160,512]{1,0:T(8,128)(2,1)S(1)}, bf16[160,512]{1,0:T(8,128)(2,1)}, u32[]{:S(2)}, u32[]{:S(2)}) %collective-permute-start.5) | collective-permute-done | bytes 163872 | tf_op jit(solution)/shard_map/ppermute | solution.py:353
  73.3 0.5 collective-permute-start.3
  73.8 1.3 subtract_multiply_fusion
  75.0 1.4 copy.16
  76.4 1.4 reshape.52
  77.8 1.4 copy.15
  79.1 1.4 mul.15
  80.6 0.7 reshape.48.refs_3_
  81.3 0.8 pad_add_fusion.links
  82.1 0.9 constant_dynamic-update-slice_fusion.2
  82.9 0.9 constant_dynamic-update-slice_fusion.1
  83.8 0.9 constant_dynamic-update-slice_fusion.state_ref.refs_0_
  84.8 0.5 coarse_message.1.refs_2_
  85.3 2.5 %copy-done = bf16[5120,512]{1,0:T(8,128)(2,1)S(1)} copy-done((bf16[5120,512]{1,0:T(8,128)(2,1)S(1)}, bf16[5120,512]{1,0:T(8,128)(2,1)}, u32[]{:S(2)}) %copy-start) | copy-done | bytes 5242904
  87.8 2.5 %copy-done.2 = bf16[40,4,128,128]{3,2,1,0:T(8,128)(2,1)S(1)} copy-done((bf16[40,4,128,128]{3,2,1,0:T(8,128)(2,1)S(1)}, bf16[40,4,128,128]{3,2,1,0:T(8,128)(2,1)}, u32[]{:S(2)}) %copy-start.2) | copy-done | bytes 5242904
  90.3 1.3 copy-done.4
  91.6 4.5 %stage.1 = (bf16[40,128,512]{2,1,0:T(8,128)(2,1)S(1)}, bf16[40,128,160]{2,1,0:T(8,128)(2,1)S(1)}, bf16[2560,512]{1,0:T(8,128)(2,1)S(1)}, bf16[10240,256]{1,0:T(8...) custom-call(s32[1]{0:T(128)} %bitcast.feat_ref, ...), custom_call_target="tpu_custom_call" | custom-call | tf_op jit(solution)/shard_map/stage/pallas_call | solution.py:129
  96.1 3.6 %aggregate.4 = (bf16[1280,256]{1,0:T(8,128)(2,1)S(1)}, bf16[1280,256]{1,0:T(8,128)(2,1)S(1)}, bf16[40,256]{1,0:T(8,128)(2,1)S(1)}, bf16[10240,256]{1,0:T(8,128)(2,1)S(1)}) custom-call(s32[1]{0:T(128)} %bitcast.feat_ref, s32[320]{0:T(512)S(1)} %pad_add_fusion.links, ...), custom_call_target="tpu_custom_call", output_to_operand_aliasing={{3}: (8, {})} | custom-call | tf_op jit(solution)/shard_map/aggregate/pallas_call | solution.py:229
  99.7 0.1 collective-permute-start.8
  99.8 0.1 collective-permute-start.11
  99.9 1.4 collective-permute-start.10
  101.3 0.1 collective-permute-start.9
  101.4 1.8 aggregate.5
  103.2 1.6 collective-permute-done.9
  104.9 0.2 collective-permute-start.12
  105.1 2.2 %collective-permute-start.16 = (bf16[1280,256]{1,0:T(8,128)(2,1)S(1)}, bf16[1280,256]{1,0:T(8,128)(2,1)S(1)}, u32[]{:S(2)}, u32[]{:S(2)}) collective-permute-start(bf16[1280,256]{1,0:T(8,128)(2,1)S(1)} %get-tuple-element.85), channel_id=1, source_target_pairs={{0,1},{1,0},{2,3},{3,2},{4,5},{5,4},{6,7},{7,6},{8,9},{9,8},{10,11... | collective-permute-start | bytes 1966088 | tf_op jit(solution)/shard_map/ppermute | solution.py:348
  107.3 4.7 %node_mid.2 = (bf16[1280,512]{1,0:T(8,128)(2,1)S(1)}, bf16[1280,256]{1,0:T(8,128)(2,1)S(1)}, bf16[1280,256]{1,0:T(8,128)(2,1)S(1)}) custom-call(s32[1]{0:T(128)} %bitcast.feat_ref, bf16[2560,512]{1,0:T(8,128)(2,1)S(1)} %get-tuple-element.57.refs_0_, bf16[1280,256]{1,0:T(8,128)(2,1)S(1)} %get-tuple-element.67.refs_1_, ...), custom_call_target="tpu_custom_call" | custom-call | tf_op jit(solution)/shard_map/node_mid/pallas_call | solution.py:308
  112.1 0.1 collective-permute-start.19
  112.1 0.5 collective-permute-start.13
  112.6 3.5 %collective-permute-start.15 = (bf16[1280,256]{1,0:T(8,128)(2,1)S(1)}, bf16[1280,256]{1,0:T(8,128)(2,1)S(1)}, u32[]{:S(2)}, u32[]{:S(2)}) collective-permute-start(bf16[1280,256]{1,0:T(8,128)(2,1)S(1)} %get-tuple-element.83), channel_id=1, source_target_pairs={{2,1},{4,3},{6,5},{8,7},{10,9},{12,11},{14,13},{1,2},{3,4},{5,6},{... | collective-permute-start | bytes 1966088 | tf_op jit(solution)/shard_map/ppermute | solution.py:435
  116.2 2.0 %collective-permute-start.14 = (bf16[1280,256]{1,0:T(8,128)(2,1)S(1)}, bf16[1280,256]{1,0:T(8,128)(2,1)S(1)}, u32[]{:S(2)}, u32[]{:S(2)}) collective-permute-start(bf16[1280,256]{1,0:T(8,128)(2,1)S(1)} %get-tuple-element.82.refs_0_), channel_id=1, source_target_pairs={{2,0},{4,2},{6,4},{8,6},{10,8},{12,10},{14,12},{1,3},{3,5},{5,7},{... | collective-permute-start | bytes 1966088 | tf_op jit(solution)/shard_map/ppermute | solution.py:435
  118.2 4.7 %node_mid.3 = (bf16[1280,512]{1,0:T(8,128)(2,1)S(1)}, bf16[1280,256]{1,0:T(8,128)(2,1)S(1)}, bf16[1280,256]{1,0:T(8,128)(2,1)S(1)}) custom-call(s32[1]{0:T(128)} %bitcast.feat_ref, bf16[2560,512]{1,0:T(8,128)(2,1)S(1)} %get-tuple-element.57.refs_0_, bf16[1280,256]{1,0:T(8,128)(2,1)S(1)} %get-tuple-element.84.refs_1_, ...), custom_call_target="tpu_custom_call" | custom-call | tf_op jit(solution)/shard_map/node_mid/pallas_call | solution.py:308
  122.8 0.5 collective-permute-start.20
  123.4 3.2 %collective-permute-start.17 = (bf16[1280,256]{1,0:T(8,128)(2,1)S(1)}, bf16[1280,256]{1,0:T(8,128)(2,1)S(1)}, u32[]{:S(2)}, u32[]{:S(2)}) collective-permute-start(bf16[1280,256]{1,0:T(8,128)(2,1)S(1)} %get-tuple-element.86.refs_2_), channel_id=1, source_target_pairs={{2,0},{4,2},{6,4},{8,6},{10,8},{12,10},{14,12},{1,3},{3,5},{5,7},{... | collective-permute-start | bytes 1966088 | tf_op jit(solution)/shard_map/ppermute | solution.py:435
  126.6 2.5 %collective-permute-start.18 = (bf16[1280,256]{1,0:T(8,128)(2,1)S(1)}, bf16[1280,256]{1,0:T(8,128)(2,1)S(1)}, u32[]{:S(2)}, u32[]{:S(2)}) collective-permute-start(bf16[1280,256]{1,0:T(8,128)(2,1)S(1)} %get-tuple-element.87), channel_id=1, source_target_pairs={{2,1},{4,3},{6,5},{8,7},{10,9},{12,11},{14,13},{1,2},{3,4},{5,6},{... | collective-permute-start | bytes 1966088 | tf_op jit(solution)/shard_map/ppermute | solution.py:435
  129.1 1.6 node_coarse.1.refs_2_
  130.7 0.9 local_messages.1.refs_8_
  131.6 27.2 %collective-permute-done.14.refs_4_ = bf16[1280,256]{1,0:T(8,128)(2,1)S(1)} collective-permute-done((bf16[1280,256]{1,0:T(8,128)(2,1)S(1)}, bf16[1280,256]{1,0:T(8,128)(2,1)S(1)}, u32[]{:S(2)}, u32[]{:S(2)}) %collective-permute-start.14) | collective-permute-done | bytes 655392 | tf_op jit(solution)/shard_map/ppermute | solution.py:435
  158.8 7.0 %collective-permute-done.17.refs_6_ = bf16[1280,256]{1,0:T(8,128)(2,1)S(1)} collective-permute-done((bf16[1280,256]{1,0:T(8,128)(2,1)S(1)}, bf16[1280,256]{1,0:T(8,128)(2,1)S(1)}, u32[]{:S(2)}, u32[]{:S(2)}) %collective-permute-start.17) | collective-permute-done | bytes 655392 | tf_op jit(solution)/shard_map/ppermute | solution.py:435
  165.8 7.9 %collective-permute-done.18.refs_7_ = bf16[1280,256]{1,0:T(8,128)(2,1)S(1)} collective-permute-done((bf16[1280,256]{1,0:T(8,128)(2,1)S(1)}, bf16[1280,256]{1,0:T(8,128)(2,1)S(1)}, u32[]{:S(2)}, u32[]{:S(2)}) %collective-permute-start.18) | collective-permute-done | bytes 655392 | tf_op jit(solution)/shard_map/ppermute | solution.py:435
  173.7 3.3 %aggregate.6 = (bf16[1280,256]{1,0:T(8,128)(2,1)S(1)}, bf16[1280,256]{1,0:T(8,128)(2,1)S(1)}, bf16[40,256]{1,0:T(8,128)(2,1)}, bf16[10240,256]{1,0:T(8,128)(2,1)S(1)}) custom-call(s32[1]{0:T(128)} %bitcast.feat_ref, s32[320]{0:T(512)S(1)} %pad_add_fusion.links, ...), custom_call_target="tpu_custom_call", output_to_operand_aliasing={{3}: (10, {})} | custom-call | tf_op jit(solution)/shard_map/aggregate/pallas_call | solution.py:229
  177.0 0.1 collective-permute-start.21
  177.1 1.8 aggregate.7
  179.0 0.2 collective-permute-done.21.refs_2_
  179.2 0.3 collective-permute-start.23
  179.5 4.4 %node_last.2 = (bf16[1280,512]{1,0:T(8,128)(2,1)S(1)}, bf16[5120,512]{1,0:T(8,128)(2,1)}) custom-call(s32[1]{0:T(128)} %bitcast.feat_ref, bf16[1280,512]{1,0:T(8,128)(2,1)S(1)} %get-tuple-element.75.refs_0_, bf16[1280,256]{1,0:T(8,128)(2,1)S(1)} %get-tuple-element.92.refs_1_, bf16[1280,256]{1,0:T(8,128)(2,1)S(1)} %collective-permute-done.21.refs_2_, ...), custom_call_target="tpu_custom_call" | custom-call | tf_op jit(solution)/shard_map/node_last/pallas_call | solution.py:308
  183.9 0.2 collective-permute-start.22
  184.1 4.4 %node_last.3 = (bf16[1280,512]{1,0:T(8,128)(2,1)S(1)}, bf16[5120,512]{1,0:T(8,128)(2,1)}) custom-call(s32[1]{0:T(128)} %bitcast.feat_ref, bf16[1280,512]{1,0:T(8,128)(2,1)S(1)} %get-tuple-element.95.refs_0_, bf16[1280,256]{1,0:T(8,128)(2,1)S(1)} %get-tuple-element.96.refs_1_, ...), custom_call_target="tpu_custom_call", output_to_operand_aliasing={{1}: (8, {})} | custom-call | tf_op jit(solution)/shard_map/node_last/pallas_call | solution.py:308
  188.5 0.4 collective-permute-start.24
  188.9 2.7 %collective-permute-done.24.refs_1_ = bf16[1280,512]{1,0:T(8,128)(2,1)S(1)} collective-permute-done((bf16[1280,512]{1,0:T(8,128)(2,1)S(1)}, bf16[1280,512]{1,0:T(8,128)(2,1)S(1)}, u32[]{:S(2)}, u32[]{:S(2)}) %collective-permute-start.24) | collective-permute-done | bytes 1310752 | tf_op jit(solution)/shard_map/ppermute | solution.py:348
  191.6 1.5 assemble.1
  (35 shorter events, 0.1 us)
Async XLA Ops:
  0.8 15.0 %collective-permute-start = (bf16[40,512]{1,0:T(8,128)(2,1)S(1)}, bf16[40,512]{1,0:T(8,128)(2,1)S(1)}, u32[]{:S(2)}, u32[]{:S(2)}) collective-permute-start(bf16[40,512]{1,0:T(8,128)(2,1)S(1)} %slice.3), channel_id=1, source_target_pairs={{0,8},{2,10},{4,12},{6,14},{8,0},{10,2},{12,4},{14,6},{1,9},{3,11}... | collective-permute-start | bytes 122888 | tf_op jit(solution)/shard_map/ppermute | solution.py:353
  7.7 65.5 %copy-start.1 = (bf16[2,512,256]{2,1,0:T(8,128)(2,1)S(1)}, bf16[2,512,256]{2,1,0:T(8,128)(2,1)}, u32[]{:S(2)}) copy-start(bf16[2,512,256]{2,1,0:T(8,128)(2,1)} %weight_ref.4) | copy-start | bytes 1572868
  7.7 88.4 %collective-permute-start.6 = (bf16[2560,256]{1,0:T(8,128)(2,1)}, bf16[2560,256]{1,0:T(8,128)(2,1)}, u32[]{:S(2)}, u32[]{:S(2)}) collective-permute-start(bf16[2560,256]{1,0:T(8,128)(2,1)} %message.3.refs_4_), channel_id=1, source_target_pairs={{0,2},{2,4},{4,6},{6,8},{8,10},{10,12},{12,14},{1,3},{3,5},{5,7},{... | collective-permute-start | bytes 3932168 | tf_op jit(solution)/shard_map/ppermute | solution.py:395
  11.0 74.3 %copy-start.5 = (bf16[40,128,160]{1,2,0:T(8,128)(2,1)S(1)}, bf16[40,128,160]{1,2,0:T(8,128)(2,1)}, u32[]{:S(2)}) copy-start(bf16[40,128,160]{1,2,0:T(8,128)(2,1)} %param.11) | copy-start | bytes 4915204
  15.8 69.5 %copy-start.3 = (bf16[2560,256]{1,0:T(8,128)(2,1)S(1)}, bf16[2560,256]{1,0:T(8,128)(2,1)}, u32[]{:S(2)}) copy-start(bf16[2560,256]{1,0:T(8,128)(2,1)} %message.3.refs_4_) | copy-start | bytes 3932164
  15.8 63.4 %copy-start.6 = (bf16[80,512]{1,0:T(8,128)(2,1)}, bf16[80,512]{1,0:T(8,128)(2,1)S(1)}, u32[]{:S(2)}) copy-start(bf16[80,512]{1,0:T(8,128)(2,1)S(1)} %pad_maximum_fusion.1) | copy-start | bytes 245764
  15.8 80.3 %collective-permute-start.7 = (bf16[2560,256]{1,0:T(8,128)(2,1)}, bf16[2560,256]{1,0:T(8,128)(2,1)}, u32[]{:S(2)}, u32[]{:S(2)}) collective-permute-start(bf16[2560,256]{1,0:T(8,128)(2,1)} %message.2.refs_3_), channel_id=1, source_target_pairs={{2,0},{4,2},{6,4},{8,6},{10,8},{12,10},{14,12},{3,1},{5,3},{7,5},{... | collective-permute-start | bytes 3932168 | tf_op jit(solution)/shard_map/ppermute | solution.py:393
  19.0 30.1 %collective-permute-start.4 = (bf16[80,512]{1,0:T(8,128)(2,1)S(1)}, bf16[80,512]{1,0:T(8,128)(2,1)}, u32[]{:S(2)}, u32[]{:S(2)}) collective-permute-start(bf16[80,512]{1,0:T(8,128)(2,1)S(1)} %pad_maximum_fusion.1), channel_id=1, source_target_pairs={{0,12},{2,14},{4,0},{6,2},{8,4},{10,6},{12,8},{14,10},{1,13},{3,15... | collective-permute-start | bytes 245768 | tf_op jit(solution)/shard_map/ppermute | solution.py:353
  19.0 66.2 %collective-permute-start.1 = (bf16[2,1024,256]{2,1,0:T(8,128)(2,1)}, bf16[2,1024,256]{2,1,0:T(8,128)(2,1)}, u32[]{:S(2)}, u32[]{:S(2)}) collective-permute-start(bf16[2,1024,256]{2,1,0:T(8,128)(2,1)} %refs_5_), channel_id=1, source_target_pairs={{0,1},{1,0},{2,3},{3,2},{4,5},{5,4},{6,7},{7,6},{8,9},{9,8},{10,11... | collective-permute-start | bytes 3145736 | tf_op jit(solution)/shard_map/ppermute | solution.py:348
  20.6 64.6 %collective-permute-start.2 = (bf16[2,256,512]{2,1,0:T(8,128)(2,1)}, bf16[2,256,512]{2,1,0:T(8,128)(2,1)}, u32[]{:S(2)}, u32[]{:S(2)}) collective-permute-start(bf16[2,256,512]{2,1,0:T(8,128)(2,1)} %refs_7_), channel_id=1, source_target_pairs={{0,1},{1,0},{2,3},{3,2},{4,5},{5,4},{6,7},{7,6},{8,9},{9,8},{10,11... | collective-permute-start | bytes 1572872 | tf_op jit(solution)/shard_map/ppermute | solution.py:348
  49.9 23.3 %collective-permute-start.5 = (bf16[160,512]{1,0:T(8,128)(2,1)S(1)}, bf16[160,512]{1,0:T(8,128)(2,1)}, u32[]{:S(2)}, u32[]{:S(2)}) collective-permute-start(bf16[160,512]{1,0:T(8,128)(2,1)S(1)} %pad_maximum_fusion), channel_id=1, source_target_pairs={{0,14},{2,0},{4,2},{6,4},{8,6},{10,8},{12,10},{14,12},{1,15},{3,1}... | collective-permute-start | bytes 491528 | tf_op jit(solution)/shard_map/ppermute | solution.py:353
  73.3 12.0 %collective-permute-start.3 = (bf16[2,512,256]{2,1,0:T(8,128)(2,1)S(1)}, bf16[2,512,256]{2,1,0:T(8,128)(2,1)}, u32[]{:S(2)}, u32[]{:S(2)}) collective-permute-start(bf16[2,512,256]{2,1,0:T(8,128)(2,1)S(1)} %copy-done.1), channel_id=1, source_target_pairs={{0,1},{1,0},{2,3},{3,2},{4,5},{5,4},{6,7},{7,6},{8,9},{9,8},{10,11... | collective-permute-start | bytes 1572872 | tf_op jit(solution)/shard_map/ppermute | solution.py:348
  85.3 2.5 %copy-start = (bf16[5120,512]{1,0:T(8,128)(2,1)S(1)}, bf16[5120,512]{1,0:T(8,128)(2,1)}, u32[]{:S(2)}) copy-start(bf16[5120,512]{1,0:T(8,128)(2,1)} %refs_2_.1) | copy-start | bytes 15728644
  87.8 2.5 %copy-start.2 = (bf16[40,4,128,128]{3,2,1,0:T(8,128)(2,1)S(1)}, bf16[40,4,128,128]{3,2,1,0:T(8,128)(2,1)}, u32[]{:S(2)}) copy-start(bf16[40,4,128,128]{3,2,1,0:T(8,128)(2,1)} %refs_0_.1) | copy-start | bytes 15728644
  90.3 1.3 copy-start.4
  99.7 5.2 %collective-permute-start.8 = (bf16[1280,256]{1,0:T(8,128)(2,1)S(1)}, bf16[1280,256]{1,0:T(8,128)(2,1)S(1)}, u32[]{:S(2)}, u32[]{:S(2)}) collective-permute-start(bf16[1280,256]{1,0:T(8,128)(2,1)S(1)} %get-tuple-element.62), channel_id=1, source_target_pairs={{0,1},{1,0},{2,3},{3,2},{4,5},{5,4},{6,7},{7,6},{8,9},{9,8},{10,11... | collective-permute-start | bytes 1966088 | tf_op jit(solution)/shard_map/ppermute | solution.py:348
  99.8 3.4 %collective-permute-start.11 = (bf16[40,256]{1,0:T(8,128)(2,1)S(1)}, bf16[40,256]{1,0:T(8,128)(2,1)S(1)}, u32[]{:S(2)}, u32[]{:S(2)}) collective-permute-start(bf16[40,256]{1,0:T(8,128)(2,1)S(1)} %get-tuple-element.66), channel_id=1, source_target_pairs={{0,4},{2,6},{4,8},{6,10},{8,12},{10,14},{12,0},{14,2},{1,5},{3,7},... | collective-permute-start | bytes 61448 | tf_op jit(solution)/shard_map/ppermute | solution.py:353
  99.9 3.3 %collective-permute-start.10 = (bf16[40,256]{1,0:T(8,128)(2,1)S(1)}, bf16[40,256]{1,0:T(8,128)(2,1)S(1)}, u32[]{:S(2)}, u32[]{:S(2)}) collective-permute-start(bf16[40,256]{1,0:T(8,128)(2,1)S(1)} %get-tuple-element.66), channel_id=1, source_target_pairs={{0,12},{2,14},{4,0},{6,2},{8,4},{10,6},{12,8},{14,10},{1,13},{3,15... | collective-permute-start | bytes 61448 | tf_op jit(solution)/shard_map/ppermute | solution.py:353
  101.3 3.6 %collective-permute-start.9 = (bf16[40,256]{1,0:T(8,128)(2,1)S(1)}, bf16[40,256]{1,0:T(8,128)(2,1)S(1)}, u32[]{:S(2)}, u32[]{:S(2)}) collective-permute-start(bf16[40,256]{1,0:T(8,128)(2,1)S(1)} %get-tuple-element.66), channel_id=1, source_target_pairs={{0,8},{2,10},{4,12},{6,14},{8,0},{10,2},{12,4},{14,6},{1,9},{3,11}... | collective-permute-start | bytes 61448 | tf_op jit(solution)/shard_map/ppermute | solution.py:353
  104.9 7.1 %collective-permute-start.12 = (bf16[160,256]{1,0:T(8,128)(2,1)S(1)}, bf16[160,256]{1,0:T(8,128)(2,1)S(1)}, u32[]{:S(2)}, u32[]{:S(2)}) collective-permute-start(bf16[160,256]{1,0:T(8,128)(2,1)S(1)} %pad_maximum_fusion.2), channel_id=1, source_target_pairs={{0,14},{2,0},{4,2},{6,4},{8,6},{10,8},{12,10},{14,12},{1,15},{3,1}... | collective-permute-start | bytes 245768 | tf_op jit(solution)/shard_map/ppermute | solution.py:353
  105.1 13.0 %collective-permute-start.16 = (bf16[1280,256]{1,0:T(8,128)(2,1)S(1)}, bf16[1280,256]{1,0:T(8,128)(2,1)S(1)}, u32[]{:S(2)}, u32[]{:S(2)}) collective-permute-start(bf16[1280,256]{1,0:T(8,128)(2,1)S(1)} %get-tuple-element.85), channel_id=1, source_target_pairs={{0,1},{1,0},{2,3},{3,2},{4,5},{5,4},{6,7},{7,6},{8,9},{9,8},{10,11... | collective-permute-start | bytes 1966088 | tf_op jit(solution)/shard_map/ppermute | solution.py:348
  112.1 14.5 %collective-permute-start.19 = (bf16[1280,256]{1,0:T(8,128)(2,1)S(1)}, bf16[1280,256]{1,0:T(8,128)(2,1)S(1)}, u32[]{:S(2)}, u32[]{:S(2)}) collective-permute-start(bf16[1280,256]{1,0:T(8,128)(2,1)S(1)} %get-tuple-element.83), channel_id=1, source_target_pairs={{0,1},{1,0},{2,3},{3,2},{4,5},{5,4},{6,7},{7,6},{8,9},{9,8},{10,11... | collective-permute-start | bytes 1966088 | tf_op jit(solution)/shard_map/ppermute | solution.py:348
  112.1 11.3 %collective-permute-start.13 = (bf16[320,256]{1,0:T(8,128)(2,1)S(1)}, bf16[320,256]{1,0:T(8,128)(2,1)S(1)}, u32[]{:S(2)}, u32[]{:S(2)}) collective-permute-start(bf16[320,256]{1,0:T(8,128)(2,1)S(1)} %constant_dynamic-update-slice_fusion.3.refs_1_), channel_id=1, source_target_pairs={{0,1},{1,0},{2,3},{3,2},{4,5},{5,4},{6,7},{7,6},{8,9},{9,8},{10,11... | collective-permute-start | bytes 491528 | tf_op jit(solution)/shard_map/ppermute | solution.py:348
  112.6 46.2 %collective-permute-start.15 = (bf16[1280,256]{1,0:T(8,128)(2,1)S(1)}, bf16[1280,256]{1,0:T(8,128)(2,1)S(1)}, u32[]{:S(2)}, u32[]{:S(2)}) collective-permute-start(bf16[1280,256]{1,0:T(8,128)(2,1)S(1)} %get-tuple-element.83), channel_id=1, source_target_pairs={{2,1},{4,3},{6,5},{8,7},{10,9},{12,11},{14,13},{1,2},{3,4},{5,6},{... | collective-permute-start | bytes 1966088 | tf_op jit(solution)/shard_map/ppermute | solution.py:435
  116.2 42.6 %collective-permute-start.14 = (bf16[1280,256]{1,0:T(8,128)(2,1)S(1)}, bf16[1280,256]{1,0:T(8,128)(2,1)S(1)}, u32[]{:S(2)}, u32[]{:S(2)}) collective-permute-start(bf16[1280,256]{1,0:T(8,128)(2,1)S(1)} %get-tuple-element.82.refs_0_), channel_id=1, source_target_pairs={{2,0},{4,2},{6,4},{8,6},{10,8},{12,10},{14,12},{1,3},{3,5},{5,7},{... | collective-permute-start | bytes 1966088 | tf_op jit(solution)/shard_map/ppermute | solution.py:435
  122.8 7.9 %collective-permute-start.20 = (bf16[1280,256]{1,0:T(8,128)(2,1)S(1)}, bf16[1280,256]{1,0:T(8,128)(2,1)S(1)}, u32[]{:S(2)}, u32[]{:S(2)}) collective-permute-start(bf16[1280,256]{1,0:T(8,128)(2,1)S(1)} %get-tuple-element.87), channel_id=1, source_target_pairs={{0,1},{1,0},{2,3},{3,2},{4,5},{5,4},{6,7},{7,6},{8,9},{9,8},{10,11... | collective-permute-start | bytes 1966088 | tf_op jit(solution)/shard_map/ppermute | solution.py:348
  123.4 42.4 %collective-permute-start.17 = (bf16[1280,256]{1,0:T(8,128)(2,1)S(1)}, bf16[1280,256]{1,0:T(8,128)(2,1)S(1)}, u32[]{:S(2)}, u32[]{:S(2)}) collective-permute-start(bf16[1280,256]{1,0:T(8,128)(2,1)S(1)} %get-tuple-element.86.refs_2_), channel_id=1, source_target_pairs={{2,0},{4,2},{6,4},{8,6},{10,8},{12,10},{14,12},{1,3},{3,5},{5,7},{... | collective-permute-start | bytes 1966088 | tf_op jit(solution)/shard_map/ppermute | solution.py:435
  126.6 47.1 %collective-permute-start.18 = (bf16[1280,256]{1,0:T(8,128)(2,1)S(1)}, bf16[1280,256]{1,0:T(8,128)(2,1)S(1)}, u32[]{:S(2)}, u32[]{:S(2)}) collective-permute-start(bf16[1280,256]{1,0:T(8,128)(2,1)S(1)} %get-tuple-element.87), channel_id=1, source_target_pairs={{2,1},{4,3},{6,5},{8,7},{10,9},{12,11},{14,13},{1,2},{3,4},{5,6},{... | collective-permute-start | bytes 1966088 | tf_op jit(solution)/shard_map/ppermute | solution.py:435
  177.0 2.2 %collective-permute-start.21 = (bf16[1280,256]{1,0:T(8,128)(2,1)S(1)}, bf16[1280,256]{1,0:T(8,128)(2,1)S(1)}, u32[]{:S(2)}, u32[]{:S(2)}) collective-permute-start(bf16[1280,256]{1,0:T(8,128)(2,1)S(1)} %get-tuple-element.88), channel_id=1, source_target_pairs={{0,1},{1,0},{2,3},{3,2},{4,5},{5,4},{6,7},{7,6},{8,9},{9,8},{10,11... | collective-permute-start | bytes 1966088 | tf_op jit(solution)/shard_map/ppermute | solution.py:348
  179.2 5.0 %collective-permute-start.23 = (bf16[1280,256]{1,0:T(8,128)(2,1)S(1)}, bf16[1280,256]{1,0:T(8,128)(2,1)S(1)}, u32[]{:S(2)}, u32[]{:S(2)}) collective-permute-start(bf16[1280,256]{1,0:T(8,128)(2,1)S(1)} %get-tuple-element.97), channel_id=1, source_target_pairs={{0,1},{1,0},{2,3},{3,2},{4,5},{5,4},{6,7},{7,6},{8,9},{9,8},{10,11... | collective-permute-start | bytes 1966088 | tf_op jit(solution)/shard_map/ppermute | solution.py:348
  183.9 5.0 %collective-permute-start.22 = (bf16[1280,512]{1,0:T(8,128)(2,1)S(1)}, bf16[1280,512]{1,0:T(8,128)(2,1)S(1)}, u32[]{:S(2)}, u32[]{:S(2)}) collective-permute-start(bf16[1280,512]{1,0:T(8,128)(2,1)S(1)} %get-tuple-element.94), channel_id=1, source_target_pairs={{0,1},{1,0},{2,3},{3,2},{4,5},{5,4},{6,7},{7,6},{8,9},{9,8},{10,11... | collective-permute-start | bytes 3932168 | tf_op jit(solution)/shard_map/ppermute | solution.py:348
  188.5 3.1 %collective-permute-start.24 = (bf16[1280,512]{1,0:T(8,128)(2,1)S(1)}, bf16[1280,512]{1,0:T(8,128)(2,1)S(1)}, u32[]{:S(2)}, u32[]{:S(2)}) collective-permute-start(bf16[1280,512]{1,0:T(8,128)(2,1)S(1)} %get-tuple-element.99), channel_id=1, source_target_pairs={{0,1},{1,0},{2,3},{3,2},{4,5},{5,4},{6,7},{7,6},{8,9},{9,8},{10,11... | collective-permute-start | bytes 3932168 | tf_op jit(solution)/shard_map/ppermute | solution.py:348

commit v4 on v3

--- a/solution.py
+++ b/solution.py
@@ -14,6 +14,7 @@
 MESSAGE_TILE = 1280
 F32 = jnp.float32
 BF16 = jnp.bfloat16
+SMALL = pl.CostEstimate(flops=1 << 20, transcendentals=0, bytes_accessed=1 << 10)
 IN_VMEM = pl.BlockSpec(memory_space=pltpu.VMEM)
 IN_HBM = pl.BlockSpec(memory_space=pltpu.HBM)
 
@@ -73,6 +74,7 @@
         out_specs=pl.BlockSpec((tile, weight.shape[2]), lambda i: (i, 0)),
         out_shape=jax.ShapeDtypeStruct((rows, weight.shape[2]), BF16),
         compiler_params=params(56),
+        cost_estimate=SMALL,
         name="message",
     )(state, weight)
 
@@ -84,6 +86,7 @@
         out_specs=IN_VMEM,
         out_shape=pltpu.VMEM((state.shape[0], weight.shape[2]), F32),
         compiler_params=params(12),
+        cost_estimate=SMALL,
         name="coarse_message",
     )(state, weight)
 
@@ -135,9 +138,29 @@
             scratch_shapes=[pltpu.VMEM(coarse.shape, BF16), pltpu.SemaphoreType.DMA((copies,))],
         ),
         out_shape=out_shape,
-        compiler_params=params(12),
+        compiler_params=params(36),
+        cost_estimate=SMALL,
         name="stage",
     )(feat, fine, coarse, state, low, high, *weights)
+
+
+def weights_kernel(*refs):
+    sems = refs[-1]
+    count = len(refs) // 2
+    wait_all(run_copies(list(zip(refs[:count], refs[count:-1])), sems))
+
+
+def weights_call(weights):
+    return pl.pallas_call(
+        weights_kernel,
+        in_specs=[IN_HBM] * len(weights),
+        out_specs=[IN_VMEM] * len(weights),
+        scratch_shapes=[pltpu.SemaphoreType.DMA((len(weights),))],
+        out_shape=[pltpu.VMEM(weight.shape, BF16) for weight in weights],
+        compiler_params=params(4),
+        cost_estimate=SMALL,
+        name="weights",
+    )(*weights)
 
 
 def local_kernel(places, feat_ref, *refs):
@@ -162,6 +185,7 @@
         out_shape=pltpu.VMEM(table.shape, BF16),
         input_output_aliases={len(pieces) + 1: 0},
         compiler_params=params(4),
+        cost_estimate=SMALL,
         name="local_messages",
     )(feat, *pieces, table)
 
@@ -237,6 +261,7 @@
         out_shape=out_shape,
         input_output_aliases=aliases,
         compiler_params=params(12),
+        cost_estimate=SMALL,
         name="aggregate",
     )(feat, links, fine, coarse_tile, coarse, degree, *pieces, table)
 
@@ -313,6 +338,7 @@
         out_shape=out_shape,
         input_output_aliases=aliases,
         compiler_params=params(28),
+        cost_estimate=SMALL,
         name="node_" + mode,
     )(feat, *operands)
 
@@ -340,6 +366,7 @@
         out_shape=shaped(out),
         input_output_aliases={len(pieces) + 1: 0},
         compiler_params=params(4),
+        cost_estimate=SMALL,
         name="assemble",
     )(feat, *pieces, out)
 
@@ -386,42 +413,49 @@
     evens = even_offsets(patches)
 
     held = node_state[:CN_DEV]
-    strides = [patches >> step for step in range(1, patches.bit_length())]
-    held = jnp.concatenate([held, fetch(held, strides[0])], axis=0)
+    held = jnp.concatenate([held, fetch(held, 1)], axis=0)
     low = message_call(node_state, w_msg, 0, half_rows, MESSAGE_TILE)
     low, held = barrier((low, held))
     high_halo = lax.ppermute(low, "patch", backward)
     high = message_call(node_state, w_msg, half_rows, half_rows, MESSAGE_TILE)
     low_halo = lax.ppermute(high, "patch", forward)
-    for stride in strides[1:]:
-        held = jnp.concatenate([held, fetch(held, stride)], axis=0)
-    coarse_state = held
-
-    offsets = evens + [offset + 1 for offset in evens]
+
+    offsets = [even + odd for even in evens for odd in (0, 1)]
+    fine_index, coarse_index, node_degree, w_in, w_out, w_late, _ = barrier(
+        (fine_index, coarse_index, node_degree, w_in, w_out, w_msg, high)
+    )
     links = (fine_index - (patch_pos * blocks - HALO_BLK)).reshape(-1) * block
     away = ((coarse_index - patch_pos) % patches).reshape(-1)
     coarse_links = sum(jnp.where(away == offset, pos * CN_DEV, 0) for pos, offset in enumerate(offsets))
     links = jnp.concatenate([links, coarse_links])
     degree = node_degree.reshape(2 * CHUNKS, half // CHUNKS, block)
-
-    w_in, w_out, w_late, _ = barrier((w_in, w_out, w_msg, high))
-    weights = [w_in, swap_feat(w_in), w_out, swap_feat(w_out), w_late, swap_feat(w_late)]
-    fine, ctile, state, table, *weights = stage_call(
-        feat, fine_tile, jnp.swapaxes(coarse_tile, 1, 2), node_state, low, high, weights
+    fine, ctile, state, table, in_own, out_own, msg_own = stage_call(
+        feat, fine_tile, jnp.swapaxes(coarse_tile, 1, 2), node_state, low, high, (w_in, w_out, w_late)
     )
     staged = (fine, ctile)
-    coarse = coarse_message_call(coarse_state, w_late)
+    others = weights_call([swap_feat(w_in), swap_feat(w_out), swap_feat(w_late)])
+    strides = [patches >> step for step in range(1, patches.bit_length() - 1)]
+    for step, stride in enumerate(strides):
+        got = fetch(held, stride)
+        if step == 0:
+            got, links, degree, table = barrier((got, links, degree, table))
+        if step == len(strides) - 1:
+            got, others = barrier((got, others))
+        held = jnp.concatenate([held, got], axis=0)
+    coarse_state = held
+    weights = [in_own, others[0], out_own, others[1], msg_own, others[2]]
+    coarse = coarse_message_call(coarse_state, msg_own)
 
     places = (lambda feat: 0, lambda feat: halo_rows + 2 * half_rows)
     send, keep, first_rows, table = aggregate_call(
         feat, links, staged, coarse, degree, table, 0, places, (low_halo, high_halo)
     )
     recv = swap_feat(send)
-    others = [fetch(first_rows, offset) for offset in evens[1:]]
+    got = fetch(first_rows, 1)
     send_1, keep_1 = aggregate_call(feat, links, staged, coarse, degree, table, 1)
-    recv, keep, send_1, others = barrier((recv, keep, send_1, others))
-    held = jnp.concatenate([first_rows, *others], axis=0)
-    held = jnp.concatenate([held, fetch(held, 1)], axis=0)
+    recv, keep, send_1, got = barrier((recv, keep, send_1, got))
+    held = jnp.concatenate([first_rows, got], axis=0)
+    got = fetch(held, strides[0])
     inputs = [(keep, recv), (keep_1, swap_feat(send_1))]
     states = []
     local = []
@@ -431,11 +465,14 @@
             "mid", 0, feat, state, chunk * chunk_rows, chunk, *inputs[chunk], weights
         )
         if chunk == 0:
-            own, other, held = barrier((own, other, held))
+            own, other, got = barrier((own, other, got))
+            held = jnp.concatenate([held, got], axis=0)
+        sibling = swap_feat(other)
+        if chunk + 1 < CHUNKS:
+            sibling, state = barrier((sibling, state))
         halo += [lax.ppermute(own, ("patch", "feat"), own_patch), lax.ppermute(other, ("patch", "feat"), other_patch)]
-        local += [own, swap_feat(other)]
+        local += [own, sibling]
         states.append(new_state)
-    (coarse,) = node_call("coarse", 0, feat, coarse_state, 0, 0, held, swap_feat(held), weights)
 
     local_places = []
     halo_places = []
@@ -449,9 +486,14 @@
             lambda feat, at=at: (1 - feat) * (halo_rows + 2 * half_rows) + at,
             lambda feat, at=at: feat * (halo_rows + 2 * half_rows) + at,
         ]
-    table = local_call(feat, local_places, local, table)
+    early = 2 * (CHUNKS - 1)
+    table = local_call(feat, local_places + halo_places[:early], local + halo[:early], table)
+    held, table = barrier((held, table))
+    for stride in strides[1:]:
+        held = jnp.concatenate([held, fetch(held, stride)], axis=0)
+    (coarse,) = node_call("coarse", 0, feat, coarse_state, 0, 0, held, swap_feat(held), weights)
     send, keep, _, table = aggregate_call(
-        feat, links, staged, coarse, degree, table, 0, halo_places, halo
+        feat, links, staged, coarse, degree, table, 0, halo_places[early:], halo[early:]
     )
     recv = swap_feat(send)
     send_1, keep_1 = aggregate_call(feat, links, staged, coarse, degree, table, 1)

time: 195 us -> 164 us (0.84)
  waiting for transfers between devices: 97 us -> 76.9 us
  local copies, waits for them, and re-layouts: 16.1 us -> 1.23 us
  starting transfers between devices: 28.5 us -> 37.2 us
  other arithmetic: 4.24 us -> 0.13 us
    ppermute x7 -> x6, waiting for transfers between devices: 51.9 us -> 33.4 us  [fetch(): lax.ppermute(held, 'patch', [(pos, (pos - stride) % count) for pos in ran...]
    unnamed x20 -> x11, local copies, waits for them, and re-layouts: 8.1 us -> 0.04 us
    ppermute x2, waiting for transfers between devices: 34.2 us -> 29.8 us  [shards(): lax.ppermute(own, ('patch', 'feat'), own_patch)]
    ppermute x7 -> x6, starting transfers between devices: 4.24 us -> 8.52 us  [fetch(): lax.ppermute(held, 'patch', [(pos, (pos - stride) % count) for pos in ran...]
    ppermute x1, waiting for transfers between devices: 0.01 us -> 4.02 us  [shards(): high_halo = lax.ppermute(low, 'patch', backward)]
    ppermute x12, starting transfers between devices: 6.62 us -> 10 us  [swap_feat(): return lax.ppermute(array, 'feat', [(0, 1), (1, 0)])]
    ppermute x2, waiting for transfers between devices: 7.87 us -> 4.9 us  [shards(): lax.ppermute(other, ('patch', 'feat'), other_patch)]
    mul x2, local copies, waits for them, and re-layouts: 2.78 us -> 0.19 us  [shards(): links = (fine_index - (patch_pos * blocks - HALO_BLK)).reshape(-1) * block]
  transfers between devices with their start and end apart: 25 -> 24, of which waited for: 8 -> 10; matrix products, arithmetic and copies ran while one was open for 7% -> 0% of each run, Pallas kernels for 20% -> 25%
where the time goes in v4:
time: 164 us
  waiting for transfers between devices  76.9 us (47%)
  Pallas kernels  47.6 us (29%)
  starting transfers between devices  37.2 us (23%)
    ppermute x6, waiting for transfers between devices, fetch(): lax.ppermute(held, 'patch', [(pos, (pos - stride) % count) for pos in ran...  33.4 us
    ppermute x2, waiting for transfers between devices, shards(): lax.ppermute(own, ('patch', 'feat'), own_patch)  29.8 us
    pallas_call x5, Pallas kernels, node_call(): pl.pallas_call(functools.partial(node_kernel, mode, layer, start, chunk),...  19.7 us
    ppermute x12, starting transfers between devices, swap_feat(): return lax.ppermute(array, 'feat', [(0, 1), (1, 0)])  10 us
    pallas_call x2, Pallas kernels, message_call(): pl.pallas_call(message_kernel, grid=(rows // tile,), in_specs=[pl.BlockSp...  9.25 us
    pallas_call x4, Pallas kernels, aggregate_call(): pl.pallas_call(functools.partial(aggregate_kernel, places, chunk), grid_s...  8.82 us
    ppermute x6, starting transfers between devices, fetch(): lax.ppermute(held, 'patch', [(pos, (pos - stride) % count) for pos in ran...  8.52 us
    ppermute x2, starting transfers between devices, shards(): lax.ppermute(other, ('patch', 'feat'), other_patch)  7.63 us
  transfers between devices with their start and end apart: 24, of which 10 were waited for; matrix products, arithmetic and copies ran while one was open for 0% of the time, Pallas kernels for 25%

profile of v4, /device:TPU:9, one launch (start us, length us, event | category | flops | bytes accessed | tf_op | source)
XLA Modules:
  0.0 163.5 jit_solution(13674902072104237525)
XLA Ops:
  0.0 0.8 slice.3
  0.8 1.1 collective-permute-start
  1.9 4.6 %message.3.refs_4_ = bf16[2560,256]{1,0:T(8,128)(2,1)} custom-call(bf16[5120,512]{1,0:T(8,128)(2,1)} %refs_2_.1, bf16[2,512,256]{2,1,0:T(8,128)(2,1)} %refs_7_), custom_call_target="tpu_custom_call" | custom-call | flops 1048576 | bytes 1024 | tf_op jit(solution)/shard_map/message/pallas_call | solution.py:67
  6.5 0.0 copy-start.1
  6.6 2.4 %collective-permute-start.6 = (bf16[2560,256]{1,0:T(8,128)(2,1)}, bf16[2560,256]{1,0:T(8,128)(2,1)S(1)}, u32[]{:S(2)}, u32[]{:S(2)}) collective-permute-start(bf16[2560,256]{1,0:T(8,128)(2,1)} %message.3.refs_4_), channel_id=1, source_target_pairs={{0,2},{2,4},{4,6},{6,8},{8,10},{10,12},{12,14},{1,3},{3,5},{5,7},{... | collective-permute-start | bytes 3932168 | tf_op jit(solution)/shard_map/ppermute | solution.py:421
  8.9 4.6 %message.2.refs_3_ = bf16[2560,256]{1,0:T(8,128)(2,1)} custom-call(bf16[5120,512]{1,0:T(8,128)(2,1)} %refs_2_.1, bf16[2,512,256]{2,1,0:T(8,128)(2,1)} %refs_7_), custom_call_target="tpu_custom_call" | custom-call | flops 1048576 | bytes 1024 | tf_op jit(solution)/shard_map/message/pallas_call | solution.py:67
  13.6 0.0 collective-permute-done
  13.6 3.9 %collective-permute-start.7 = (bf16[2560,256]{1,0:T(8,128)(2,1)}, bf16[2560,256]{1,0:T(8,128)(2,1)S(1)}, u32[]{:S(2)}, u32[]{:S(2)}) collective-permute-start(bf16[2560,256]{1,0:T(8,128)(2,1)} %message.2.refs_3_), channel_id=1, source_target_pairs={{2,0},{4,2},{6,4},{8,6},{10,8},{12,10},{14,12},{3,1},{5,3},{7,5},{... | collective-permute-start | bytes 3932168 | tf_op jit(solution)/shard_map/ppermute | solution.py:419
  17.5 1.6 collective-permute-start.3
  19.1 2.3 %collective-permute-start.1 = (bf16[80,512]{1,0:T(8,128)(2,1)S(1)}, bf16[80,512]{1,0:T(8,128)(2,1)S(1)}, u32[]{:S(2)}, u32[]{:S(2)}) collective-permute-start(bf16[80,512]{1,0:T(8,128)(2,1)S(1)} %pad_maximum_fusion.1), channel_id=1, source_target_pairs={{0,8},{2,10},{4,12},{6,14},{8,0},{10,2},{12,4},{14,6},{1,9},{3,11}... | collective-permute-start | bytes 245768 | tf_op jit(solution)/shard_map/ppermute | solution.py:380
  21.4 0.3 collective-permute-start.4
  21.8 27.4 %collective-permute-done.1 = bf16[80,512]{1,0:T(8,128)(2,1)S(1)} collective-permute-done((bf16[80,512]{1,0:T(8,128)(2,1)S(1)}, bf16[80,512]{1,0:T(8,128)(2,1)S(1)}, u32[]{:S(2)}, u32[]{:S(2)}) %collective-permute-start.1) | collective-permute-done | bytes 81952 | tf_op jit(solution)/shard_map/ppermute | solution.py:380
  49.1 2.5 %collective-permute-start.5 = (bf16[2,512,256]{2,1,0:T(8,128)(2,1)}, bf16[2,512,256]{2,1,0:T(8,128)(2,1)}, u32[]{:S(2)}, u32[]{:S(2)}) collective-permute-start(bf16[2,512,256]{2,1,0:T(8,128)(2,1)} %refs_7_), channel_id=1, source_target_pairs={{0,1},{1,0},{2,3},{3,2},{4,5},{5,4},{6,7},{7,6},{8,9},{9,8},{10,11... | collective-permute-start | bytes 1572872 | tf_op jit(solution)/shard_map/ppermute | solution.py:375
  51.7 0.1 copy.15
  51.8 0.1 mul.15
  51.9 0.1 copy.16
  52.0 0.1 reshape.52
  52.1 0.1 pad_add_fusion.links
  52.2 5.0 %stage.1 = (bf16[40,128,512]{2,1,0:T(8,128)(2,1)S(1)}, bf16[40,128,160]{2,1,0:T(8,128)(2,1)S(1)}, bf16[2560,512]{1,0:T(8,128)(2,1)S(1)}, bf16[10240,256]{1,0:T(8...) custom-call(s32[1]{0:T(128)} %bitcast.feat_ref, ...), custom_call_target="tpu_custom_call" | custom-call | flops 1048576 | bytes 1024 | tf_op jit(solution)/shard_map/stage/pallas_call | solution.py:132
  57.2 0.0 collective-permute-done.4.refs_1_
  57.2 1.9 %collective-permute-start.2 = (bf16[160,512]{1,0:T(8,128)(2,1)S(1)}, bf16[160,512]{1,0:T(8,128)(2,1)S(1)}, u32[]{:S(2)}, u32[]{:S(2)}) collective-permute-start(bf16[160,512]{1,0:T(8,128)(2,1)S(1)} %pad_maximum_fusion), channel_id=1, source_target_pairs={{0,12},{2,14},{4,0},{6,2},{8,4},{10,6},{12,8},{14,10},{1,13},{3,15... | collective-permute-start | bytes 491528 | tf_op jit(solution)/shard_map/ppermute | solution.py:380
  59.1 0.0 collective-permute-done.5.refs_2_
  59.1 0.0 collective-permute-done.3.refs_0_
  59.1 1.5 weights.1
  60.7 2.4 %collective-permute-done.2 = bf16[160,512]{1,0:T(8,128)(2,1)S(1)} collective-permute-done((bf16[160,512]{1,0:T(8,128)(2,1)S(1)}, bf16[160,512]{1,0:T(8,128)(2,1)S(1)}, u32[]{:S(2)}, u32[]{:S(2)}) %collective-permute-start.2) | collective-permute-done | bytes 163872 | tf_op jit(solution)/shard_map/ppermute | solution.py:380
  63.1 0.5 coarse_message.1.refs_2_
  63.6 0.9 collective-permute-done.6.refs_4_
  64.5 4.0 %collective-permute-done.7.refs_5_ = bf16[2560,256]{1,0:T(8,128)(2,1)S(1)} collective-permute-done((bf16[2560,256]{1,0:T(8,128)(2,1)}, bf16[2560,256]{1,0:T(8,128)(2,1)S(1)}, u32[]{:S(2)}, u32[]{:S(2)}) %collective-permute-start.7) | collective-permute-done | bytes 1310752 | tf_op jit(solution)/shard_map/ppermute | solution.py:419
  68.5 2.0 %aggregate.4 = (bf16[1280,256]{1,0:T(8,128)(2,1)S(1)}, bf16[1280,256]{1,0:T(8,128)(2,1)S(1)}, bf16[40,256]{1,0:T(8,128)(2,1)S(1)}, bf16[10240,256]{1,0:T(8,128)(2,1)S(1)}) custom-call(s32[1]{0:T(128)} %bitcast.feat_ref, s32[320]{0:T(512)S(1)} %pad_add_fusion.links, ...), custom_call_target="tpu_custom_call", output_to_operand_aliasing={{3}: (8, {})} | custom-call | flops 1048576 | bytes 1024 | tf_op jit(solution)/shard_map/aggregate/pallas_call | solution.py:253
  70.5 0.6 collective-permute-start.8
  71.1 1.5 collective-permute-start.9
  72.6 1.8 %aggregate.5 = (bf16[1280,256]{1,0:T(8,128)(2,1)S(1)}, bf16[1280,256]{1,0:T(8,128)(2,1)S(1)}) custom-call(s32[1]{0:T(128)} %bitcast.feat_ref, s32[320]{0:T(512)S(1)} %pad_add_fusion.links, bf16[40,128,512]{2,1,0:T(8,128)(2,1)S(1)} %get-tuple-element.77.refs_0_, bf16[40,128,160]{2,1,0:T(8,128)(2,1)S(1)} %get-tuple-element.78.refs_1_, ...), custom_call_target="tpu_custom_call" | custom-call | flops 1048576 | bytes 1024 | tf_op jit(solution)/shard_map/aggregate/pallas_call | solution.py:253
  74.4 0.0 collective-permute-done.9
  74.5 1.6 collective-permute-start.10
  76.1 4.7 %node_mid.2 = (bf16[1280,512]{1,0:T(8,128)(2,1)S(1)}, bf16[1280,256]{1,0:T(8,128)(2,1)S(1)}, bf16[1280,256]{1,0:T(8,128)(2,1)S(1)}) custom-call(s32[1]{0:T(128)} %bitcast.feat_ref, bf16[2560,512]{1,0:T(8,128)(2,1)S(1)} %get-tuple-element.107.refs_0_, bf16[1280,256]{1,0:T(8,128)(2,1)S(1)} %get-tuple-element.92.refs_1_, ...), custom_call_target="tpu_custom_call" | custom-call | flops 1048576 | bytes 1024 | tf_op jit(solution)/shard_map/node_mid/pallas_call | solution.py:333
  80.8 1.6 collective-permute-start.11
  82.4 0.1 collective-permute-start.12
  82.4 4.3 %collective-permute-start.15 = (bf16[1280,256]{1,0:T(8,128)(2,1)S(1)}, bf16[1280,256]{1,0:T(8,128)(2,1)S(1)}, u32[]{:S(2)}, u32[]{:S(2)}) collective-permute-start(bf16[1280,256]{1,0:T(8,128)(2,1)S(1)} %get-tuple-element.105), channel_id=1, source_target_pairs={{2,1},{4,3},{6,5},{8,7},{10,9},{12,11},{14,13},{1,2},{3,4},{5,6},{... | collective-permute-start | bytes 1966088 | tf_op jit(solution)/shard_map/ppermute | solution.py:473
  86.7 2.1 %collective-permute-start.14 = (bf16[1280,256]{1,0:T(8,128)(2,1)S(1)}, bf16[1280,256]{1,0:T(8,128)(2,1)S(1)}, u32[]{:S(2)}, u32[]{:S(2)}) collective-permute-start(bf16[1280,256]{1,0:T(8,128)(2,1)S(1)} %get-tuple-element.104.refs_0_), channel_id=1, source_target_pairs={{2,0},{4,2},{6,4},{8,6},{10,8},{12,10},{14,12},{1,3},{3,5},{5,7},{... | collective-permute-start | bytes 1966088 | tf_op jit(solution)/shard_map/ppermute | solution.py:473
  88.8 0.0 collective-permute-done.11.refs_1_
  88.9 4.7 %node_mid.3 = (bf16[1280,512]{1,0:T(8,128)(2,1)S(1)}, bf16[1280,256]{1,0:T(8,128)(2,1)S(1)}, bf16[1280,256]{1,0:T(8,128)(2,1)S(1)}) custom-call(s32[1]{0:T(128)} %bitcast.feat_ref, bf16[2560,512]{1,0:T(8,128)(2,1)S(1)} %get-tuple-element.107.refs_0_, bf16[1280,256]{1,0:T(8,128)(2,1)S(1)} %get-tuple-element.108.refs_1_, ...), custom_call_target="tpu_custom_call" | custom-call | flops 1048576 | bytes 1024 | tf_op jit(solution)/shard_map/node_mid/pallas_call | solution.py:333
  93.5 0.1 collective-permute-start.13
  93.6 2.6 %collective-permute-start.18 = (bf16[1280,256]{1,0:T(8,128)(2,1)S(1)}, bf16[1280,256]{1,0:T(8,128)(2,1)S(1)}, u32[]{:S(2)}, u32[]{:S(2)}) collective-permute-start(bf16[1280,256]{1,0:T(8,128)(2,1)S(1)} %get-tuple-element.110.refs_2_), channel_id=1, source_target_pairs={{2,0},{4,2},{6,4},{8,6},{10,8},{12,10},{14,12},{1,3},{3,5},{5,7},{... | collective-permute-start | bytes 1966088 | tf_op jit(solution)/shard_map/ppermute | solution.py:473
  96.2 3.4 %collective-permute-start.19 = (bf16[1280,256]{1,0:T(8,128)(2,1)S(1)}, bf16[1280,256]{1,0:T(8,128)(2,1)S(1)}, u32[]{:S(2)}, u32[]{:S(2)}) collective-permute-start(bf16[1280,256]{1,0:T(8,128)(2,1)S(1)} %get-tuple-element.111), channel_id=1, source_target_pairs={{2,1},{4,3},{6,5},{8,7},{10,9},{12,11},{14,13},{1,2},{3,4},{5,6},{... | collective-permute-start | bytes 1966088 | tf_op jit(solution)/shard_map/ppermute | solution.py:473
  99.6 29.8 %collective-permute-done.14.refs_4_ = bf16[1280,256]{1,0:T(8,128)(2,1)S(1)} collective-permute-done((bf16[1280,256]{1,0:T(8,128)(2,1)S(1)}, bf16[1280,256]{1,0:T(8,128)(2,1)S(1)}, u32[]{:S(2)}, u32[]{:S(2)}) %collective-permute-start.14) | collective-permute-done | bytes 655392 | tf_op jit(solution)/shard_map/ppermute | solution.py:473
  129.3 1.3 local_messages.1.refs_6_
  130.6 0.1 collective-permute-start.16
  130.7 3.6 %collective-permute-done.16 = bf16[160,256]{1,0:T(8,128)(2,1)S(1)} collective-permute-done((bf16[160,256]{1,0:T(8,128)(2,1)S(1)}, bf16[160,256]{1,0:T(8,128)(2,1)S(1)}, u32[]{:S(2)}, u32[]{:S(2)}) %collective-permute-start.16) | collective-permute-done | bytes 81952 | tf_op jit(solution)/shard_map/ppermute | solution.py:380
  134.3 2.3 %collective-permute-start.17 = (bf16[320,256]{1,0:T(8,128)(2,1)S(1)}, bf16[320,256]{1,0:T(8,128)(2,1)S(1)}, u32[]{:S(2)}, u32[]{:S(2)}) collective-permute-start(bf16[320,256]{1,0:T(8,128)(2,1)S(1)} %constant_dynamic-update-slice_fusion.3.refs_1_), channel_id=1, source_target_pairs={{0,1},{1,0},{2,3},{3,2},{4,5},{5,4},{6,7},{7,6},{8,9},{9,8},{10,11... | collective-permute-start | bytes 491528 | tf_op jit(solution)/shard_map/ppermute | solution.py:375
  136.6 1.0 collective-permute-done.17.refs_2_
  137.6 1.6 node_coarse.1.refs_2_
  139.2 4.9 %collective-permute-done.19.refs_5_ = bf16[1280,256]{1,0:T(8,128)(2,1)S(1)} collective-permute-done((bf16[1280,256]{1,0:T(8,128)(2,1)S(1)}, bf16[1280,256]{1,0:T(8,128)(2,1)S(1)}, u32[]{:S(2)}, u32[]{:S(2)}) %collective-permute-start.19) | collective-permute-done | bytes 655392 | tf_op jit(solution)/shard_map/ppermute | solution.py:473
  144.1 3.1 %aggregate.6 = (bf16[1280,256]{1,0:T(8,128)(2,1)S(1)}, bf16[1280,256]{1,0:T(8,128)(2,1)S(1)}, bf16[40,256]{1,0:T(8,128)(2,1)}, bf16[10240,256]{1,0:T(8,128)(2,1)S(1)}) custom-call(s32[1]{0:T(128)} %bitcast.feat_ref, s32[320]{0:T(512)S(1)} %pad_add_fusion.links, bf16[40,128,512]{2,1,0:T(8,128)(2,1)S(1)} %get-tuple-element.77.refs_0_, ...), custom_call_target="tpu_custom_call", output_to_operand_aliasing={{3}: (8, {})} | custom-call | flops 1048576 | bytes 1024 | tf_op jit(solution)/shard_map/aggregate/pallas_call | solution.py:253
  147.2 0.1 collective-permute-start.20
  147.3 1.8 %aggregate.7 = (bf16[1280,256]{1,0:T(8,128)(2,1)S(1)}, bf16[1280,256]{1,0:T(8,128)(2,1)S(1)}) custom-call(s32[1]{0:T(128)} %bitcast.feat_ref, s32[320]{0:T(512)S(1)} %pad_add_fusion.links, bf16[40,128,512]{2,1,0:T(8,128)(2,1)S(1)} %get-tuple-element.77.refs_0_, bf16[40,128,160]{2,1,0:T(8,128)(2,1)S(1)} %get-tuple-element.78.refs_1_, ...), custom_call_target="tpu_custom_call" | custom-call | flops 1048576 | bytes 1024 | tf_op jit(solution)/shard_map/aggregate/pallas_call | solution.py:253
  149.2 0.2 collective-permute-done.20.refs_2_
  149.4 0.3 collective-permute-start.22
  149.7 4.4 %node_last.2 = (bf16[1280,512]{1,0:T(8,128)(2,1)S(1)}, bf16[5120,512]{1,0:T(8,128)(2,1)}) custom-call(s32[1]{0:T(128)} %bitcast.feat_ref, bf16[1280,512]{1,0:T(8,128)(2,1)S(1)} %get-tuple-element.99.refs_0_, bf16[1280,256]{1,0:T(8,128)(2,1)S(1)} %get-tuple-element.118.refs_1_, bf16[1280,256]{1,0:T(8,128)(2,1)S(1)} %collective-permute-done.20.refs_2_, ...), custom_call_target="tpu_custom_call" | custom-call | flops 1048576 | bytes 1024 | tf_op jit(solution)/shard_map/node_last/pallas_call | solution.py:333
  154.1 0.3 collective-permute-start.21
  154.4 0.0 collective-permute-done.22.refs_2_
  154.4 4.4 %node_last.3 = (bf16[1280,512]{1,0:T(8,128)(2,1)S(1)}, bf16[5120,512]{1,0:T(8,128)(2,1)}) custom-call(s32[1]{0:T(128)} %bitcast.feat_ref, bf16[1280,512]{1,0:T(8,128)(2,1)S(1)} %get-tuple-element.121.refs_0_, bf16[1280,256]{1,0:T(8,128)(2,1)S(1)} %get-tuple-element.122.refs_1_, ...), custom_call_target="tpu_custom_call", output_to_operand_aliasing={{1}: (8, {})} | custom-call | flops 1048576 | bytes 1024 | tf_op jit(solution)/shard_map/node_last/pallas_call | solution.py:333
  158.8 0.4 collective-permute-start.23
  159.2 2.7 %collective-permute-done.23.refs_1_ = bf16[1280,512]{1,0:T(8,128)(2,1)S(1)} collective-permute-done((bf16[1280,512]{1,0:T(8,128)(2,1)S(1)}, bf16[1280,512]{1,0:T(8,128)(2,1)S(1)}, u32[]{:S(2)}, u32[]{:S(2)}) %collective-permute-start.23) | collective-permute-done | bytes 1310752 | tf_op jit(solution)/shard_map/ppermute | solution.py:375
  161.9 1.5 assemble.1
  (25 shorter events, 0.1 us)
Async XLA Ops:
  0.8 12.8 %collective-permute-start = (bf16[40,512]{1,0:T(8,128)(2,1)S(1)}, bf16[40,512]{1,0:T(8,128)(2,1)S(1)}, u32[]{:S(2)}, u32[]{:S(2)}) collective-permute-start(bf16[40,512]{1,0:T(8,128)(2,1)S(1)} %slice.3), channel_id=1, source_target_pairs={{0,14},{2,0},{4,2},{6,4},{8,6},{10,8},{12,10},{14,12},{1,15},{3,1}... | collective-permute-start | bytes 122888 | tf_op jit(solution)/shard_map/ppermute | solution.py:380
  6.5 14.9 %copy-start = (bf16[2,256,512]{2,1,0:T(8,128)(2,1)S(1)}, bf16[2,256,512]{2,1,0:T(8,128)(2,1)}, u32[]{:S(2)}) copy-start(bf16[2,256,512]{2,1,0:T(8,128)(2,1)} %refs_6_) | copy-start | bytes 1572868
  6.5 45.1 %copy-start.2 = (s32[40,4]{0,1:T(4,128)S(1)}, s32[40,4]{0,1:T(4,128)}, u32[]{:S(2)}) copy-start(s32[40,4]{0,1:T(4,128)} %param.13) | copy-start | bytes 1924
  6.5 45.1 %copy-start.3 = (s32[40,4]{0,1:T(4,128)S(1)}, s32[40,4]{0,1:T(4,128)}, u32[]{:S(2)}) copy-start(s32[40,4]{0,1:T(4,128)} %param.12) | copy-start | bytes 1924
  6.5 45.5 %copy-start.1 = (s32[5120]{0:T(1024)S(1)}, s32[5120]{0:T(1024)}, u32[]{:S(2)}) copy-start(s32[5120]{0:T(1024)} %param.14) | copy-start | bytes 61444
  6.6 57.9 %collective-permute-start.6 = (bf16[2560,256]{1,0:T(8,128)(2,1)}, bf16[2560,256]{1,0:T(8,128)(2,1)S(1)}, u32[]{:S(2)}, u32[]{:S(2)}) collective-permute-start(bf16[2560,256]{1,0:T(8,128)(2,1)} %message.3.refs_4_), channel_id=1, source_target_pairs={{0,2},{2,4},{4,6},{6,8},{8,10},{10,12},{12,14},{1,3},{3,5},{5,7},{... | collective-permute-start | bytes 3932168 | tf_op jit(solution)/shard_map/ppermute | solution.py:421
  13.6 54.9 %collective-permute-start.7 = (bf16[2560,256]{1,0:T(8,128)(2,1)}, bf16[2560,256]{1,0:T(8,128)(2,1)S(1)}, u32[]{:S(2)}, u32[]{:S(2)}) collective-permute-start(bf16[2560,256]{1,0:T(8,128)(2,1)} %message.2.refs_3_), channel_id=1, source_target_pairs={{2,0},{4,2},{6,4},{8,6},{10,8},{12,10},{14,12},{3,1},{5,3},{7,5},{... | collective-permute-start | bytes 3932168 | tf_op jit(solution)/shard_map/ppermute | solution.py:419
  17.5 41.6 %collective-permute-start.3 = (bf16[2,1024,256]{2,1,0:T(8,128)(2,1)}, bf16[2,1024,256]{2,1,0:T(8,128)(2,1)}, u32[]{:S(2)}, u32[]{:S(2)}) collective-permute-start(bf16[2,1024,256]{2,1,0:T(8,128)(2,1)} %refs_5_), channel_id=1, source_target_pairs={{0,1},{1,0},{2,3},{3,2},{4,5},{5,4},{6,7},{7,6},{8,9},{9,8},{10,11... | collective-permute-start | bytes 3145736 | tf_op jit(solution)/shard_map/ppermute | solution.py:375
  19.1 30.0 %collective-permute-start.1 = (bf16[80,512]{1,0:T(8,128)(2,1)S(1)}, bf16[80,512]{1,0:T(8,128)(2,1)S(1)}, u32[]{:S(2)}, u32[]{:S(2)}) collective-permute-start(bf16[80,512]{1,0:T(8,128)(2,1)S(1)} %pad_maximum_fusion.1), channel_id=1, source_target_pairs={{0,8},{2,10},{4,12},{6,14},{8,0},{10,2},{12,4},{14,6},{1,9},{3,11}... | collective-permute-start | bytes 245768 | tf_op jit(solution)/shard_map/ppermute | solution.py:380
  21.4 35.8 %collective-permute-start.4 = (bf16[2,256,512]{2,1,0:T(8,128)(2,1)S(1)}, bf16[2,256,512]{2,1,0:T(8,128)(2,1)}, u32[]{:S(2)}, u32[]{:S(2)}) collective-permute-start(bf16[2,256,512]{2,1,0:T(8,128)(2,1)S(1)} %copy-done), channel_id=1, source_target_pairs={{0,1},{1,0},{2,3},{3,2},{4,5},{5,4},{6,7},{7,6},{8,9},{9,8},{10,11... | collective-permute-start | bytes 1572872 | tf_op jit(solution)/shard_map/ppermute | solution.py:375
  49.1 10.0 %collective-permute-start.5 = (bf16[2,512,256]{2,1,0:T(8,128)(2,1)}, bf16[2,512,256]{2,1,0:T(8,128)(2,1)}, u32[]{:S(2)}, u32[]{:S(2)}) collective-permute-start(bf16[2,512,256]{2,1,0:T(8,128)(2,1)} %refs_7_), channel_id=1, source_target_pairs={{0,1},{1,0},{2,3},{3,2},{4,5},{5,4},{6,7},{7,6},{8,9},{9,8},{10,11... | collective-permute-start | bytes 1572872 | tf_op jit(solution)/shard_map/ppermute | solution.py:375
  57.2 5.9 %collective-permute-start.2 = (bf16[160,512]{1,0:T(8,128)(2,1)S(1)}, bf16[160,512]{1,0:T(8,128)(2,1)S(1)}, u32[]{:S(2)}, u32[]{:S(2)}) collective-permute-start(bf16[160,512]{1,0:T(8,128)(2,1)S(1)} %pad_maximum_fusion), channel_id=1, source_target_pairs={{0,12},{2,14},{4,0},{6,2},{8,4},{10,6},{12,8},{14,10},{1,13},{3,15... | collective-permute-start | bytes 491528 | tf_op jit(solution)/shard_map/ppermute | solution.py:380
  70.5 3.9 %collective-permute-start.8 = (bf16[1280,256]{1,0:T(8,128)(2,1)S(1)}, bf16[1280,256]{1,0:T(8,128)(2,1)S(1)}, u32[]{:S(2)}, u32[]{:S(2)}) collective-permute-start(bf16[1280,256]{1,0:T(8,128)(2,1)S(1)} %get-tuple-element.87), channel_id=1, source_target_pairs={{0,1},{1,0},{2,3},{3,2},{4,5},{5,4},{6,7},{7,6},{8,9},{9,8},{10,11... | collective-permute-start | bytes 1966088 | tf_op jit(solution)/shard_map/ppermute | solution.py:375
  71.1 3.4 %collective-permute-start.9 = (bf16[40,256]{1,0:T(8,128)(2,1)S(1)}, bf16[40,256]{1,0:T(8,128)(2,1)S(1)}, u32[]{:S(2)}, u32[]{:S(2)}) collective-permute-start(bf16[40,256]{1,0:T(8,128)(2,1)S(1)} %get-tuple-element.91), channel_id=1, source_target_pairs={{0,14},{2,0},{4,2},{6,4},{8,6},{10,8},{12,10},{14,12},{1,15},{3,1}... | collective-permute-start | bytes 61448 | tf_op jit(solution)/shard_map/ppermute | solution.py:380
  74.5 6.3 %collective-permute-start.10 = (bf16[80,256]{1,0:T(8,128)(2,1)S(1)}, bf16[80,256]{1,0:T(8,128)(2,1)S(1)}, u32[]{:S(2)}, u32[]{:S(2)}) collective-permute-start(bf16[80,256]{1,0:T(8,128)(2,1)S(1)} %pad_maximum_fusion.3), channel_id=1, source_target_pairs={{0,8},{2,10},{4,12},{6,14},{8,0},{10,2},{12,4},{14,6},{1,9},{3,11}... | collective-permute-start | bytes 122888 | tf_op jit(solution)/shard_map/ppermute | solution.py:380
  80.8 8.0 %collective-permute-start.11 = (bf16[1280,256]{1,0:T(8,128)(2,1)S(1)}, bf16[1280,256]{1,0:T(8,128)(2,1)S(1)}, u32[]{:S(2)}, u32[]{:S(2)}) collective-permute-start(bf16[1280,256]{1,0:T(8,128)(2,1)S(1)} %get-tuple-element.105), channel_id=1, source_target_pairs={{0,1},{1,0},{2,3},{3,2},{4,5},{5,4},{6,7},{7,6},{8,9},{9,8},{10,11... | collective-permute-start | bytes 1966088 | tf_op jit(solution)/shard_map/ppermute | solution.py:375
  82.4 6.5 %collective-permute-start.12 = (bf16[1280,256]{1,0:T(8,128)(2,1)S(1)}, bf16[1280,256]{1,0:T(8,128)(2,1)S(1)}, u32[]{:S(2)}, u32[]{:S(2)}) collective-permute-start(bf16[1280,256]{1,0:T(8,128)(2,1)S(1)} %get-tuple-element.109), channel_id=1, source_target_pairs={{0,1},{1,0},{2,3},{3,2},{4,5},{5,4},{6,7},{7,6},{8,9},{9,8},{10,11... | collective-permute-start | bytes 1966088 | tf_op jit(solution)/shard_map/ppermute | solution.py:375
  82.4 46.9 %collective-permute-start.15 = (bf16[1280,256]{1,0:T(8,128)(2,1)S(1)}, bf16[1280,256]{1,0:T(8,128)(2,1)S(1)}, u32[]{:S(2)}, u32[]{:S(2)}) collective-permute-start(bf16[1280,256]{1,0:T(8,128)(2,1)S(1)} %get-tuple-element.105), channel_id=1, source_target_pairs={{2,1},{4,3},{6,5},{8,7},{10,9},{12,11},{14,13},{1,2},{3,4},{5,6},{... | collective-permute-start | bytes 1966088 | tf_op jit(solution)/shard_map/ppermute | solution.py:473
  86.7 42.6 %collective-permute-start.14 = (bf16[1280,256]{1,0:T(8,128)(2,1)S(1)}, bf16[1280,256]{1,0:T(8,128)(2,1)S(1)}, u32[]{:S(2)}, u32[]{:S(2)}) collective-permute-start(bf16[1280,256]{1,0:T(8,128)(2,1)S(1)} %get-tuple-element.104.refs_0_), channel_id=1, source_target_pairs={{2,0},{4,2},{6,4},{8,6},{10,8},{12,10},{14,12},{1,3},{3,5},{5,7},{... | collective-permute-start | bytes 1966088 | tf_op jit(solution)/shard_map/ppermute | solution.py:473
  93.5 35.8 %collective-permute-start.13 = (bf16[1280,256]{1,0:T(8,128)(2,1)S(1)}, bf16[1280,256]{1,0:T(8,128)(2,1)S(1)}, u32[]{:S(2)}, u32[]{:S(2)}) collective-permute-start(bf16[1280,256]{1,0:T(8,128)(2,1)S(1)} %get-tuple-element.111), channel_id=1, source_target_pairs={{0,1},{1,0},{2,3},{3,2},{4,5},{5,4},{6,7},{7,6},{8,9},{9,8},{10,11... | collective-permute-start | bytes 1966088 | tf_op jit(solution)/shard_map/ppermute | solution.py:375
  93.6 45.6 %collective-permute-start.18 = (bf16[1280,256]{1,0:T(8,128)(2,1)S(1)}, bf16[1280,256]{1,0:T(8,128)(2,1)S(1)}, u32[]{:S(2)}, u32[]{:S(2)}) collective-permute-start(bf16[1280,256]{1,0:T(8,128)(2,1)S(1)} %get-tuple-element.110.refs_2_), channel_id=1, source_target_pairs={{2,0},{4,2},{6,4},{8,6},{10,8},{12,10},{14,12},{1,3},{3,5},{5,7},{... | collective-permute-start | bytes 1966088 | tf_op jit(solution)/shard_map/ppermute | solution.py:473
  96.2 47.9 %collective-permute-start.19 = (bf16[1280,256]{1,0:T(8,128)(2,1)S(1)}, bf16[1280,256]{1,0:T(8,128)(2,1)S(1)}, u32[]{:S(2)}, u32[]{:S(2)}) collective-permute-start(bf16[1280,256]{1,0:T(8,128)(2,1)S(1)} %get-tuple-element.111), channel_id=1, source_target_pairs={{2,1},{4,3},{6,5},{8,7},{10,9},{12,11},{14,13},{1,2},{3,4},{5,6},{... | collective-permute-start | bytes 1966088 | tf_op jit(solution)/shard_map/ppermute | solution.py:473
  130.6 3.6 %collective-permute-start.16 = (bf16[160,256]{1,0:T(8,128)(2,1)S(1)}, bf16[160,256]{1,0:T(8,128)(2,1)S(1)}, u32[]{:S(2)}, u32[]{:S(2)}) collective-permute-start(bf16[160,256]{1,0:T(8,128)(2,1)S(1)} %pad_maximum_fusion.2), channel_id=1, source_target_pairs={{0,12},{2,14},{4,0},{6,2},{8,4},{10,6},{12,8},{14,10},{1,13},{3,15... | collective-permute-start | bytes 245768 | tf_op jit(solution)/shard_map/ppermute | solution.py:380
  134.3 3.3 %collective-permute-start.17 = (bf16[320,256]{1,0:T(8,128)(2,1)S(1)}, bf16[320,256]{1,0:T(8,128)(2,1)S(1)}, u32[]{:S(2)}, u32[]{:S(2)}) collective-permute-start(bf16[320,256]{1,0:T(8,128)(2,1)S(1)} %constant_dynamic-update-slice_fusion.3.refs_1_), channel_id=1, source_target_pairs={{0,1},{1,0},{2,3},{3,2},{4,5},{5,4},{6,7},{7,6},{8,9},{9,8},{10,11... | collective-permute-start | bytes 491528 | tf_op jit(solution)/shard_map/ppermute | solution.py:375
  147.2 2.2 %collective-permute-start.20 = (bf16[1280,256]{1,0:T(8,128)(2,1)S(1)}, bf16[1280,256]{1,0:T(8,128)(2,1)S(1)}, u32[]{:S(2)}, u32[]{:S(2)}) collective-permute-start(bf16[1280,256]{1,0:T(8,128)(2,1)S(1)} %get-tuple-element.114), channel_id=1, source_target_pairs={{0,1},{1,0},{2,3},{3,2},{4,5},{5,4},{6,7},{7,6},{8,9},{9,8},{10,11... | collective-permute-start | bytes 1966088 | tf_op jit(solution)/shard_map/ppermute | solution.py:375
  149.4 5.0 %collective-permute-start.22 = (bf16[1280,256]{1,0:T(8,128)(2,1)S(1)}, bf16[1280,256]{1,0:T(8,128)(2,1)S(1)}, u32[]{:S(2)}, u32[]{:S(2)}) collective-permute-start(bf16[1280,256]{1,0:T(8,128)(2,1)S(1)} %get-tuple-element.123), channel_id=1, source_target_pairs={{0,1},{1,0},{2,3},{3,2},{4,5},{5,4},{6,7},{7,6},{8,9},{9,8},{10,11... | collective-permute-start | bytes 1966088 | tf_op jit(solution)/shard_map/ppermute | solution.py:375
  154.1 5.0 %collective-permute-start.21 = (bf16[1280,512]{1,0:T(8,128)(2,1)S(1)}, bf16[1280,512]{1,0:T(8,128)(2,1)S(1)}, u32[]{:S(2)}, u32[]{:S(2)}) collective-permute-start(bf16[1280,512]{1,0:T(8,128)(2,1)S(1)} %get-tuple-element.120), channel_id=1, source_target_pairs={{0,1},{1,0},{2,3},{3,2},{4,5},{5,4},{6,7},{7,6},{8,9},{9,8},{10,11... | collective-permute-start | bytes 3932168 | tf_op jit(solution)/shard_map/ppermute | solution.py:375
  158.8 3.1 %collective-permute-start.23 = (bf16[1280,512]{1,0:T(8,128)(2,1)S(1)}, bf16[1280,512]{1,0:T(8,128)(2,1)S(1)}, u32[]{:S(2)}, u32[]{:S(2)}) collective-permute-start(bf16[1280,512]{1,0:T(8,128)(2,1)S(1)} %get-tuple-element.125), channel_id=1, source_target_pairs={{0,1},{1,0},{2,3},{3,2},{4,5},{5,4},{6,7},{7,6},{8,9},{9,8},{10,11... | collective-permute-start | bytes 3932168 | tf_op jit(solution)/shard_map/ppermute | solution.py:375

commit v5 on v4

v5 whole, which is shorter than its diff:
```python
import functools

import jax
import jax.numpy as jnp
from jax import lax
from jax.experimental import pallas as pl
from jax.experimental.pallas import tpu as pltpu
from jax.sharding import PartitionSpec as P

CN_DEV = 40
LAYERS = 2
HALO_BLK = 20
MID_BLOCKS = (10, 10)
LAST_BLOCKS = (10, 10)
LAST_ROWS = ((0, 0, 10), (1, 0, 5), (1, 5, 5))
MESSAGE_ROWS = ((0, 20), (20, 20))
MESSAGE_TILE = 640
NODE_SPLIT = 2
F32 = jnp.float32
BF16 = jnp.bfloat16
SMALL = pl.CostEstimate(flops=1 << 20, transcendentals=0, bytes_accessed=1 << 10)
IN_VMEM = pl.BlockSpec(memory_space=pltpu.VMEM)
IN_HBM = pl.BlockSpec(memory_space=pltpu.HBM)


def silu(v):
    return 0.5 * v * (1.0 + jnp.tanh(0.5 * v))


def dot(a, b):
    return jnp.dot(a, b, preferred_element_type=F32)


def normalize(parts):
    width = sum(part.shape[-1] for part in parts)
    mean = sum(jnp.sum(part, axis=-1, keepdims=True) for part in parts) / width
    center = [part - mean for part in parts]
    spread = sum(jnp.sum(part * part, axis=-1, keepdims=True) for part in center) / width
    scale = lax.rsqrt(spread + 1e-05)
    return [(part * scale).astype(BF16) for part in center]


def params(mib):
    return pltpu.CompilerParams(vmem_limit_bytes=mib << 20)


def shaped(array):
    return jax.ShapeDtypeStruct(array.shape, array.dtype)


def run_copies(pairs, sems):
    copies = [pltpu.make_async_copy(src, dst, sems.at[pos]) for pos, (src, dst) in enumerate(pairs)]
    for copy in copies:
        copy.start()
    return copies


def wait_all(copies):
    for copy in copies:
        copy.wait()


def coarse_message_kernel(state_ref, weight_ref, out_ref):
    (normed,) = normalize([state_ref[...].astype(F32)])
    out_ref[...] = silu(dot(normed, weight_ref[0])).astype(BF16).astype(F32)


def message_kernel(start, tile, state, weight, out_ref, state_buf, weight_buf, sems):
    rows = out_ref.shape[0]
    tiles = [(at, tile) for at in range(0, rows, tile)]
    pairs = [(state.at[pl.ds(start + at, size)], state_buf.at[pl.ds(at, size)]) for at, size in tiles]
    copies = run_copies(pairs[:1] + [(weight.at[0], weight_buf)] + pairs[1:], sems)
    weight_copy = copies.pop(1)
    normed = []
    for pos in range(len(tiles) + 1):
        if pos < len(tiles):
            at, size = tiles[pos]
            copies[pos].wait()
            normed += normalize([state_buf[at : at + size, :].astype(F32)])
        if pos == 0:
            weight_copy.wait()
            continue
        at, size = tiles[pos - 1]
        out_ref[at : at + size, :] = silu(dot(normed[pos - 1], weight_buf[...])).astype(BF16)


def message_call(state, weight, start, rows, tile):
    width, columns = weight.shape[1:]
    return pl.pallas_call(
        functools.partial(message_kernel, start, tile),
        in_specs=[IN_HBM, IN_HBM],
        out_specs=IN_VMEM,
        out_shape=pltpu.VMEM((rows, columns), BF16),
        scratch_shapes=[
            pltpu.VMEM((rows, width), BF16),
            pltpu.VMEM((width, columns), BF16),
            pltpu.SemaphoreType.DMA((1 + rows // tile,)),
        ],
        compiler_params=params(58),
        cost_estimate=SMALL,
        name="message",
    )(state, weight)


def coarse_message_call(state, weight):
    return pl.pallas_call(
        coarse_message_kernel,
        in_specs=[IN_VMEM, IN_VMEM],
        out_specs=IN_VMEM,
        out_shape=pltpu.VMEM((state.shape[0], weight.shape[2]), F32),
        compiler_params=params(12),
        cost_estimate=SMALL,
        name="coarse_message",
    )(state, weight)


def stage_kernel(locals_, count, feat_ref, *refs):
    fine, coarse, state = refs[:3]
    pieces = refs[3 : 3 + locals_]
    refs = refs[3 + locals_ :]
    weights = refs[:count]
    fine_out, coarse_out, state_out, table = refs[count : 4 + count]
    weights_out = refs[4 + count : 4 + 2 * count]
    coarse_buf, sems = refs[4 + 2 * count :]
    block = fine.shape[-1]
    half_rows = state_out.shape[0]
    pairs = [(coarse, coarse_buf)]
    pairs += [
        (fine.at[:, kind], fine_out.at[:, :, pl.ds(kind * block, block)]) for kind in range(fine.shape[1])
    ]
    start = pl.multiple_of(feat_ref[0] * half_rows, 16)
    pairs.append((state.at[pl.ds(start, half_rows)], state_out))
    at = HALO_BLK * block
    for piece in pieces:
        pairs.append((piece, table.at[pl.ds(at, piece.shape[0])]))
        at += piece.shape[0]
    pairs += list(zip(weights, weights_out))
    copies = run_copies(pairs, sems)
    copies[0].wait()

    def turn(pos, carry):
        coarse_out[pos] = jnp.transpose(coarse_buf[pos])
        return carry

    lax.fori_loop(0, coarse.shape[0], turn, 0)
    wait_all(copies[1:])


def stage_call(feat, fine, coarse, state, pieces, weights):
    blocks, kinds, block, _ = fine.shape
    rows, columns = blocks // 2 * block, pieces[0].shape[1]
    out_shape = [
        pltpu.VMEM((blocks, block, kinds * block), BF16),
        pltpu.VMEM((blocks, block, coarse.shape[1]), BF16),
        pltpu.VMEM((rows, state.shape[1]), BF16),
        pltpu.VMEM((2 * rows + 2 * HALO_BLK * block, columns), BF16),
    ] + [pltpu.VMEM(weight.shape, BF16) for weight in weights]
    copies = 2 + kinds + len(pieces) + len(weights)
    return pl.pallas_call(
        functools.partial(stage_kernel, len(pieces), len(weights)),
        grid_spec=pltpu.PrefetchScalarGridSpec(
            num_scalar_prefetch=1,
            in_specs=[IN_HBM] * (3 + len(pieces) + len(weights)),
            out_specs=[IN_VMEM] * len(out_shape),
            scratch_shapes=[pltpu.VMEM(coarse.shape, BF16), pltpu.SemaphoreType.DMA((copies,))],
        ),
        out_shape=out_shape,
        compiler_params=params(36),
        cost_estimate=SMALL,
        name="stage",
    )(feat, fine, coarse, state, *pieces, *weights)


def weights_kernel(*refs):
    sems = refs[-1]
    count = len(refs) // 2
    wait_all(run_copies(list(zip(refs[:count], refs[count:-1])), sems))


def weights_call(weights):
    return pl.pallas_call(
        weights_kernel,
        in_specs=[IN_HBM] * len(weights),
        out_specs=[IN_VMEM] * len(weights),
        scratch_shapes=[pltpu.SemaphoreType.DMA((len(weights),))],
        out_shape=[pltpu.VMEM(weight.shape, BF16) for weight in weights],
        compiler_params=params(4),
        cost_estimate=SMALL,
        name="weights",
    )(*weights)


def local_kernel(places, feat_ref, *refs):
    pieces = refs[: len(places)]
    table, sems = refs[-2:]
    pairs = []
    for place, piece in zip(places, pieces):
        start = pl.multiple_of(place(feat_ref[0]), 16)
        pairs.append((piece, table.at[pl.ds(start, piece.shape[0])]))
    wait_all(run_copies(pairs, sems))


def local_call(feat, places, pieces, table):
    return pl.pallas_call(
        functools.partial(local_kernel, places),
        grid_spec=pltpu.PrefetchScalarGridSpec(
            num_scalar_prefetch=1,
            in_specs=[pl.BlockSpec(memory_space=pl.ANY)] * len(pieces) + [IN_VMEM],
            out_specs=IN_VMEM,
            scratch_shapes=[pltpu.SemaphoreType.DMA((len(pieces),))],
        ),
        out_shape=pltpu.VMEM(table.shape, BF16),
        input_output_aliases={len(pieces) + 1: 0},
        compiler_params=params(4),
        cost_estimate=SMALL,
        name="local_messages",
    )(feat, *pieces, table)


def aggregate_kernel(places, start, feat_ref, links, *refs):
    fine, coarse_tile, coarse, degree = refs[:4]
    pieces = refs[4 : 4 + len(places)]
    if places:
        send, keep, first_rows, table, sems = refs[5 + len(places) :]
        pairs = []
        for place, piece in zip(places, pieces):
            at = pl.multiple_of(place(feat_ref[0]), 16)
            pairs.append((piece, table.at[pl.ds(at, piece.shape[0])]))
        copies = run_copies(pairs, sems)
    else:
        table, send, keep = refs[4:]
        copies = []
    blocks, block, fine_width = fine.shape
    kinds = fine_width // block
    count = send.shape[0] // block
    feat = feat_ref[0]
    wait_all(copies)
    for out_ref, which in ((send, 1 - feat), (keep, feat)):
        scale = 1.0 / jnp.transpose(degree[which].astype(F32))
        first = which * (blocks // 2) + start
        for pos in range(count):
            row = (first + pos) * kinds
            chosen = jnp.concatenate(
                [table[pl.ds(pl.multiple_of(links[row + kind], block), block), :] for kind in range(kinds)], axis=0
            )
            base = blocks * kinds + row
            stacked = jnp.concatenate(
                [
                    coarse[pl.ds(pl.multiple_of(links[base + kind], 8), CN_DEV), :]
                    for kind in range(kinds)
                ],
                axis=0,
            ).astype(BF16)
            summed = dot(fine[first + pos], chosen) + dot(coarse_tile[first + pos], stacked)
            result = (summed * scale[:, start + pos : start + pos + 1]).astype(BF16)
            out_ref[pos * block : (pos + 1) * block, :] = result
    if places:

        @pl.when(feat == 0)
        def _():
            first_rows[...] = keep[:CN_DEV, :]

        @pl.when(feat != 0)
        def _():
            first_rows[...] = send[:CN_DEV, :]


def aggregate_call(feat, links, staged, coarse, degree, table, span, places=(), pieces=()):
    fine, coarse_tile = staged
    blocks, block, _ = fine.shape
    columns = table.shape[1]
    start, count = span
    out_shape = [pltpu.VMEM((count * block, columns), BF16)] * 2
    aliases = {}
    scratch = []
    if pieces:
        out_shape += [pltpu.VMEM((CN_DEV, columns), BF16), pltpu.VMEM(table.shape, BF16)]
        aliases = {6 + len(pieces): 3}
        scratch = [pltpu.SemaphoreType.DMA((len(pieces),))]
    return pl.pallas_call(
        functools.partial(aggregate_kernel, places, start),
        grid_spec=pltpu.PrefetchScalarGridSpec(
            num_scalar_prefetch=2,
            in_specs=[IN_VMEM] * 4 + [IN_HBM] * len(pieces) + [IN_VMEM],
            out_specs=[IN_VMEM] * len(out_shape),
            scratch_shapes=scratch,
        ),
        out_shape=out_shape,
        input_output_aliases=aliases,
        compiler_params=params(12),
        cost_estimate=SMALL,
        name="aggregate",
    )(feat, links, fine, coarse_tile, coarse, degree, *pieces, table)


def node_kernel(mode, layer, start, offset, rows, placed, feat_ref, *refs):
    state_ref, keep, recv, in_own, in_other, out_own, out_other = refs[:7]
    refs = refs[7:]
    feat = feat_ref[0]
    columns = keep.shape[1]
    width = state_ref.shape[1]
    if mode == "last":
        state_out, out, sems = refs[-3:]
        half_rows = out.shape[0] // 2
        pairs = []
        for place, piece in zip(placed, refs):
            at = pl.multiple_of((1 - feat) * half_rows + place, 16)
            pairs.append((piece, out.at[pl.ds(at, piece.shape[0])]))
        copies = run_copies(pairs, sems)
    keep_at = pl.multiple_of(width + feat * columns, columns)
    recv_at = pl.multiple_of(width + (1 - feat) * columns, columns)
    split = NODE_SPLIT if rows % (NODE_SPLIT * 640) == 0 else 1
    size = rows // split
    joined, hidden, state = {}, {}, {}

    def join(at):
        joined[at] = normalize(
            [state_ref[start + at : start + at + size, :].astype(F32)]
            + [ref[offset + at : offset + at + size, :].astype(F32) for ref in (keep, recv)]
        )

    def hide(at):
        parts = joined[at]
        hidden[at] = [
            silu(
                dot(parts[0], in_ref[layer, :width, :])
                + dot(parts[1], in_ref[layer, pl.ds(keep_at, columns), :])
                + dot(parts[2], in_ref[layer, pl.ds(recv_at, columns), :])
            ).astype(BF16)
            for in_ref in (in_own, in_other)
        ]

    def update(at):
        change = dot(hidden[at][0], out_own[layer]) + dot(hidden[at][1], out_other[layer])
        state[at] = (state_ref[start + at : start + at + size, :].astype(F32) + change).astype(BF16)
        if mode == "last":
            state_out[at : at + size, :] = state[at]
        elif mode == "mid":
            refs[2][start + at : start + at + size, :] = state[at]

    def norm(at):
        (joined[at],) = normalize([state[at].astype(F32)])

    def tell(at):
        if mode == "coarse":
            refs[1][...] = silu(dot(joined[at], refs[0][layer + 1])).astype(BF16).astype(F32)
            return
        for weight, message in ((refs[0], refs[3]), (refs[1], refs[4])):
            message[at : at + size, :] = silu(dot(joined[at], weight[layer + 1])).astype(BF16)

    stages = [join, hide, update] + ([] if mode == "last" else [norm, tell])
    for step in range(len(stages) + split - 1):
        for pos in range(split):
            if 0 <= step - pos < len(stages):
                stages[step - pos](pos * size)
    if mode == "last":
        at = pl.multiple_of(feat * half_rows + start, 16)
        copy = pltpu.make_async_copy(state_out, out.at[pl.ds(at, rows)], sems.at[len(placed)])
        copy.start()
        wait_all(copies)
        copy.wait()


def node_call(mode, layer, feat, state, start, offset, rows, keep, recv, weights, out=None, total=0, placed=(), pieces=()):
    columns = keep.shape[1]
    width = state.shape[1]
    operands = [state, keep, recv, *weights[:4]]
    aliases = {}
    scratch = []
    in_specs = [IN_VMEM] * len(operands)
    if mode == "last":
        out_shape = [pltpu.VMEM((rows, width), BF16), jax.ShapeDtypeStruct((total, width), BF16)]
        out_specs = [IN_VMEM, pl.BlockSpec(memory_space=pl.ANY)]
        scratch = [pltpu.SemaphoreType.DMA((1 + len(pieces),))]
        operands += pieces
        in_specs += [IN_VMEM] * len(pieces)
        if out is not None:
            aliases = {len(operands) + 1: 1}
            operands.append(out)
            in_specs.append(pl.BlockSpec(memory_space=pl.ANY))
    else:
        if mode == "coarse":
            operands.append(weights[4])
            out_shape = [pltpu.VMEM((rows, columns), F32)]
        else:
            operands += weights[4:]
            out_shape = [pltpu.VMEM(state.shape, BF16)] + [pltpu.VMEM((rows, columns), BF16)] * 2
            aliases = {1: 0}
        in_specs = [IN_VMEM] * len(operands)
        out_specs = [IN_VMEM] * len(out_shape)
    return pl.pallas_call(
        functools.partial(node_kernel, mode, layer, start, offset, rows, placed),
        grid_spec=pltpu.PrefetchScalarGridSpec(
            num_scalar_prefetch=1, in_specs=in_specs, out_specs=out_specs, scratch_shapes=scratch
        ),
        out_shape=out_shape,
        input_output_aliases=aliases,
        compiler_params=params(28),
        cost_estimate=SMALL,
        name="node_" + mode,
    )(feat, *operands)


def assemble_kernel(placed, feat_ref, *refs):
    pieces = refs[: len(placed)]
    out, sems = refs[-2:]
    half_rows = out.shape[0] // 2
    pairs = []
    for place, piece in zip(placed, pieces):
        at = pl.multiple_of((1 - feat_ref[0]) * half_rows + place, 16)
        pairs.append((piece, out.at[pl.ds(at, piece.shape[0])]))
    wait_all(run_copies(pairs, sems))


def assemble_call(feat, placed, pieces, out):
    return pl.pallas_call(
        functools.partial(assemble_kernel, placed),
        grid_spec=pltpu.PrefetchScalarGridSpec(
            num_scalar_prefetch=1,
            in_specs=[IN_VMEM] * len(pieces) + [pl.BlockSpec(memory_space=pl.ANY)],
            out_specs=pl.BlockSpec(memory_space=pl.ANY),
            scratch_shapes=[pltpu.SemaphoreType.DMA((len(pieces),))],
        ),
        out_shape=shaped(out),
        input_output_aliases={len(pieces) + 1: 0},
        compiler_params=params(4),
        cost_estimate=SMALL,
        name="assemble",
    )(feat, *pieces, out)


def swap_feat(array):
    return lax.ppermute(array, "feat", [(0, 1), (1, 0)])


def fetch(held, stride):
    count = lax.axis_size("patch")
    return lax.ppermute(held, "patch", [(pos, (pos - stride) % count) for pos in range(count)])


def even_offsets(count):
    assert count & (count - 1) == 0
    offsets = [0]
    stride = count // 2
    while stride > 1:
        offsets += [offset + stride for offset in offsets]
        stride //= 2
    return offsets


def shards(
    node_state, fine_tile, coarse_tile, fine_index, coarse_index, node_degree, w_msg, w_in, w_out
):
    barrier = lax.optimization_barrier
    patches = lax.axis_size("patch")
    patch_pos = lax.axis_index("patch")
    feat_pos = lax.axis_index("feat")
    feat = feat_pos.astype(jnp.int32).reshape(1)
    blocks, kinds, block, _ = fine_tile.shape
    half = blocks // 2
    half_rows = half * block
    halo_rows = HALO_BLK * block
    assert half == HALO_BLK == sum(MID_BLOCKS) == sum(LAST_BLOCKS)

    forward = [(pos, pos + 1) for pos in range(patches - 1)]
    backward = [(target, source) for source, target in forward]
    sides = ((0, backward), (1, forward))
    own_patch = [(2 * src + side, 2 * dst + side) for side, pairs in sides for src, dst in pairs]
    other_patch = [(2 * src + side, 2 * dst + 1 - side) for side, pairs in sides for src, dst in pairs]
    evens = even_offsets(patches)

    held = node_state[:CN_DEV]
    held = jnp.concatenate([held, fetch(held, 1)], axis=0)
    sends = []
    halo = []
    for first, count in MESSAGE_ROWS:
        message = message_call(node_state, w_msg, first * block, count * block, MESSAGE_TILE)
        if not sends:
            message, held = barrier((message, held))
        sends.append(message)
        halo.append(lax.ppermute(message, "patch", backward if first < half else forward))
    high = sends[-1]

    offsets = [even + odd for even in evens for odd in (0, 1)]
    fine_index, coarse_index, node_degree, w_in, w_out, w_late, _ = barrier(
        (fine_index, coarse_index, node_degree, w_in, w_out, w_msg, high)
    )
    links = (fine_index - (patch_pos * blocks - HALO_BLK)).reshape(-1) * block
    away = ((coarse_index - patch_pos) % patches).reshape(-1)
    coarse_links = sum(jnp.where(away == offset, pos * CN_DEV, 0) for pos, offset in enumerate(offsets))
    links = jnp.concatenate([links, coarse_links])
    degree = node_degree.reshape(2, half, block)
    fine, ctile, state, table, in_own, out_own, msg_own = stage_call(
        feat, fine_tile, jnp.swapaxes(coarse_tile, 1, 2), node_state, sends, (w_in, w_out, w_late)
    )
    staged = (fine, ctile)
    others = weights_call([swap_feat(w_in), swap_feat(w_out), swap_feat(w_late)])
    strides = [patches >> step for step in range(1, patches.bit_length() - 1)]
    for step, stride in enumerate(strides):
        got = fetch(held, stride)
        if step == 0:
            got, links, degree, table = barrier((got, links, degree, table))
        if step == len(strides) - 1:
            got, others = barrier((got, others))
        held = jnp.concatenate([held, got], axis=0)
    coarse_state = held
    weights = [in_own, others[0], out_own, others[1], msg_own, others[2]]
    coarse = coarse_message_call(coarse_state, msg_own)

    halo_places = [
        lambda feat, at=first * block: halo_rows + 2 * half_rows + at if at < half_rows else at - half_rows
        for first, _ in MESSAGE_ROWS
    ]
    first_span, last_span = (0, MID_BLOCKS[0]), MID_BLOCKS
    send, keep, first_rows, table = aggregate_call(
        feat, links, staged, coarse, degree, table, first_span, halo_places, halo
    )
    recv = swap_feat(send)
    got = fetch(first_rows, 1)
    send_1, keep_1 = aggregate_call(feat, links, staged, coarse, degree, table, last_span)
    recv, keep, send_1, got = barrier((recv, keep, send_1, got))
    held = jnp.concatenate([first_rows, got], axis=0)
    got = fetch(held, strides[0])
    inputs = [(keep, recv), (keep_1, swap_feat(send_1))]
    local = []
    local_places = []
    halo = []
    halo_places = []
    at = 0
    for chunk, count in enumerate(MID_BLOCKS):
        rows = count * block
        state, own, other = node_call("mid", 0, feat, state, at, 0, rows, *inputs[chunk], weights)
        if chunk == 0:
            own, other, got = barrier((own, other, got))
            held = jnp.concatenate([held, got], axis=0)
        sibling = swap_feat(other)
        if chunk == 0:
            sibling, state = barrier((sibling, state))
        halo += [lax.ppermute(own, ("patch", "feat"), own_patch), lax.ppermute(other, ("patch", "feat"), other_patch)]
        local += [own, sibling]
        local_places += [
            lambda feat, at=at: halo_rows + feat * half_rows + at,
            lambda feat, at=at: halo_rows + (1 - feat) * half_rows + at,
        ]
        halo_places += [
            lambda feat, at=at: (1 - feat) * (halo_rows + 2 * half_rows) + at,
            lambda feat, at=at: feat * (halo_rows + 2 * half_rows) + at,
        ]
        at += rows

    early = len(halo) - 2
    table = local_call(feat, local_places + halo_places[:early], local + halo[:early], table)
    held, table = barrier((held, table))
    for stride in strides[1:]:
        held = jnp.concatenate([held, fetch(held, stride)], axis=0)
    (coarse,) = node_call(
        "coarse", 0, feat, coarse_state, 0, 0, held.shape[0], held, swap_feat(held), weights
    )
    send, keep, _, table = aggregate_call(
        feat, links, staged, coarse, degree, table, (0, LAST_BLOCKS[0]), halo_places[early:], halo[early:]
    )
    recv = swap_feat(send)
    send_1, keep_1 = aggregate_call(feat, links, staged, coarse, degree, table, LAST_BLOCKS)
    recv, keep, send_1 = barrier((recv, keep, send_1))
    inputs = [(keep, recv), (keep_1, swap_feat(send_1))]
    out = None
    swapped = []
    placed = []
    for chunk, offset, count in LAST_ROWS:
        at = (chunk * LAST_BLOCKS[0] + offset) * block
        done = 1 if len(swapped) == len(LAST_ROWS) - 1 else 0
        new_state, out = node_call(
            "last", 1, feat, state, at, offset * block, count * block, *inputs[chunk], weights,
            out, node_state.shape[0], placed[:done], swapped[:done],
        )
        swapped.append(swap_feat(new_state))
        placed.append(at)
    return assemble_call(feat, placed[1:], swapped[1:], out)


def solution(mesh):
    return jax.shard_map(
        shards,
        mesh=mesh,
        in_specs=(
            P(("member", "patch"), None),
            P("patch", None, None, None),
            P("patch", None, None),
            P("patch", None),
            P("patch", None),
            P("patch"),
            P(None, None, "feat"),
            P(None, None, "feat"),
            P(None, "feat", None),
        ),
        out_specs=P(("member", "patch"), None),
        check_vma=False,
    )
```

time: 164 us -> 167 us (1.018)
  waiting for transfers between devices: 76.9 us -> 80.9 us
    ppermute x12 -> x13, waiting for transfers between devices: 4 us -> 6.6 us  [swap_feat(): return lax.ppermute(array, 'feat', [(0, 1), (1, 0)])]
    pallas_call x14 -> x15, Pallas kernels: 44.7 us -> 43.1 us  [the longest x6 19.8 us: node_call(): pl.pallas_call(functools.partial(node_kernel, mode, layer, start, offset,...]
    ppermute x12 -> x13, starting transfers between devices: 10 us -> 10.5 us  [swap_feat(): return lax.ppermute(array, 'feat', [(0, 1), (1, 0)])]
  transfers between devices with their start and end apart: 24 -> 25, of which waited for: 10 -> 11; matrix products, arithmetic and copies ran while one was open for 0% -> 0% of each run, Pallas kernels for 25% -> 21%
where the time goes in v5:
time: 167 us; the launch traced here: 166 us
  waiting for transfers between devices  80.9 us (48%)
  Pallas kernels  46 us (28%)
  starting transfers between devices  37.4 us (22%)
    ppermute x6, waiting for transfers between devices, fetch(): lax.ppermute(held, 'patch', [(pos, (pos - stride) % count) for pos in ran...  33.3 us
    ppermute x2, waiting for transfers between devices, shards(): lax.ppermute(own, ('patch', 'feat'), own_patch)  30.2 us
    pallas_call x6, Pallas kernels, node_call(): pl.pallas_call(functools.partial(node_kernel, mode, layer, start, offset,...  19.8 us
    ppermute x13, starting transfers between devices, swap_feat(): return lax.ppermute(array, 'feat', [(0, 1), (1, 0)])  10.5 us
    pallas_call x4, Pallas kernels, aggregate_call(): pl.pallas_call(functools.partial(aggregate_kernel, places, start), grid_s...  10 us
    ppermute x6, starting transfers between devices, fetch(): lax.ppermute(held, 'patch', [(pos, (pos - stride) % count) for pos in ran...  8.75 us
    ppermute x2, starting transfers between devices, shards(): lax.ppermute(other, ('patch', 'feat'), other_patch)  7.18 us
    pallas_call x2, Pallas kernels, message_call(): pl.pallas_call(functools.partial(message_kernel, start, tile), in_specs=[...  6.74 us
  transfers between devices with their start and end apart: 25, of which 11 were waited for; matrix products, arithmetic and copies ran while one was open for 0% of the time, Pallas kernels for 21%

profile of v5, /device:TPU:9, one launch (start us, length us, event | category | flops | bytes accessed | tf_op | source)
XLA Modules:
  0.0 166.3 jit_solution(2835413255692854398)
XLA Ops:
  0.0 0.8 slice.3
  0.8 1.1 collective-permute-start
  1.9 3.4 %message.3.refs_4_ = bf16[2560,256]{1,0:T(8,128)(2,1)S(1)} custom-call(bf16[5120,512]{1,0:T(8,128)(2,1)} %refs_2_.1, bf16[2,512,256]{2,1,0:T(8,128)(2,1)} %refs_7_), custom_call_target="tpu_custom_call" | custom-call | flops 1048576 | bytes 1024 | tf_op jit(solution)/shard_map/message/pallas_call | solution.py:89
  5.3 0.0 copy-start.2
  5.3 0.0 copy-start.4
  5.3 0.0 copy-start.5
  5.3 0.0 copy-start.3
  5.3 2.4 %collective-permute-start.7 = (bf16[2560,256]{1,0:T(8,128)(2,1)S(1)}, bf16[2560,256]{1,0:T(8,128)(2,1)}, u32[]{:S(2)}, u32[]{:S(2)}) collective-permute-start(bf16[2560,256]{1,0:T(8,128)(2,1)S(1)} %message.3.refs_4_), channel_id=1, source_target_pairs={{0,2},{2,4},{4,6},{6,8},{8,10},{10,12},{12,14},{1,3},{3,5},{5,7},{... | collective-permute-start | bytes 3932168 | tf_op jit(solution)/shard_map/ppermute | solution.py:481
  7.7 3.4 %message.2.refs_3_ = bf16[2560,256]{1,0:T(8,128)(2,1)S(1)} custom-call(bf16[5120,512]{1,0:T(8,128)(2,1)} %refs_2_.1, bf16[2,512,256]{2,1,0:T(8,128)(2,1)} %refs_7_), custom_call_target="tpu_custom_call" | custom-call | flops 1048576 | bytes 1024 | tf_op jit(solution)/shard_map/message/pallas_call | solution.py:89
  11.1 0.0 copy-start.1
  11.1 3.9 %collective-permute-start.6 = (bf16[2560,256]{1,0:T(8,128)(2,1)S(1)}, bf16[2560,256]{1,0:T(8,128)(2,1)}, u32[]{:S(2)}, u32[]{:S(2)}) collective-permute-start(bf16[2560,256]{1,0:T(8,128)(2,1)S(1)} %message.2.refs_3_), channel_id=1, source_target_pairs={{2,0},{4,2},{6,4},{8,6},{10,8},{12,10},{14,12},{3,1},{5,3},{7,5},{... | collective-permute-start | bytes 3932168 | tf_op jit(solution)/shard_map/ppermute | solution.py:481
  15.1 1.6 collective-permute-start.3
  16.7 2.3 %collective-permute-start.1 = (bf16[80,512]{1,0:T(8,128)(2,1)S(1)}, bf16[80,512]{1,0:T(8,128)(2,1)S(1)}, u32[]{:S(2)}, u32[]{:S(2)}) collective-permute-start(bf16[80,512]{1,0:T(8,128)(2,1)S(1)} %pad_maximum_fusion.1), channel_id=1, source_target_pairs={{0,8},{2,10},{4,12},{6,14},{8,0},{10,2},{12,4},{14,6},{1,9},{3,11}... | collective-permute-start | bytes 245768 | tf_op jit(solution)/shard_map/ppermute | solution.py:438
  19.0 0.3 collective-permute-start.4
  19.3 27.2 %collective-permute-done.1 = bf16[80,512]{1,0:T(8,128)(2,1)S(1)} collective-permute-done((bf16[80,512]{1,0:T(8,128)(2,1)S(1)}, bf16[80,512]{1,0:T(8,128)(2,1)S(1)}, u32[]{:S(2)}, u32[]{:S(2)}) %collective-permute-start.1) | collective-permute-done | bytes 81952 | tf_op jit(solution)/shard_map/ppermute | solution.py:438
  46.5 2.5 %collective-permute-start.5 = (bf16[2,512,256]{2,1,0:T(8,128)(2,1)}, bf16[2,512,256]{2,1,0:T(8,128)(2,1)}, u32[]{:S(2)}, u32[]{:S(2)}) collective-permute-start(bf16[2,512,256]{2,1,0:T(8,128)(2,1)} %refs_7_), channel_id=1, source_target_pairs={{0,1},{1,0},{2,3},{3,2},{4,5},{5,4},{6,7},{7,6},{8,9},{9,8},{10,11... | collective-permute-start | bytes 1572872 | tf_op jit(solution)/shard_map/ppermute | solution.py:433
  49.0 0.1 copy.18
  49.1 0.1 mul.15
  49.2 0.1 copy.19
  49.3 0.1 reshape.52
  49.5 0.1 pad_add_fusion.links
  49.5 5.0 %stage.1 = (bf16[40,128,512]{2,1,0:T(8,128)(2,1)S(1)}, bf16[40,128,160]{2,1,0:T(8,128)(2,1)S(1)}, bf16[2560,512]{1,0:T(8,128)(2,1)S(1)}, bf16[10240,256]{1,0:T(8...) custom-call(s32[1]{0:T(128)} %bitcast.feat_ref, ...), custom_call_target="tpu_custom_call" | custom-call | flops 1048576 | bytes 1024 | tf_op jit(solution)/shard_map/stage/pallas_call | solution.py:159
  54.6 1.9 %collective-permute-start.2 = (bf16[160,512]{1,0:T(8,128)(2,1)S(1)}, bf16[160,512]{1,0:T(8,128)(2,1)S(1)}, u32[]{:S(2)}, u32[]{:S(2)}) collective-permute-start(bf16[160,512]{1,0:T(8,128)(2,1)S(1)} %pad_maximum_fusion), channel_id=1, source_target_pairs={{0,12},{2,14},{4,0},{6,2},{8,4},{10,6},{12,8},{14,10},{1,13},{3,15... | collective-permute-start | bytes 491528 | tf_op jit(solution)/shard_map/ppermute | solution.py:438
  56.5 1.5 weights.1
  58.0 2.5 %collective-permute-done.2 = bf16[160,512]{1,0:T(8,128)(2,1)S(1)} collective-permute-done((bf16[160,512]{1,0:T(8,128)(2,1)S(1)}, bf16[160,512]{1,0:T(8,128)(2,1)S(1)}, u32[]{:S(2)}, u32[]{:S(2)}) %collective-permute-start.2) | collective-permute-done | bytes 163872 | tf_op jit(solution)/shard_map/ppermute | solution.py:438
  60.6 0.5 coarse_message.1.refs_2_
  61.0 1.9 %collective-permute-done.7.refs_5_ = bf16[2560,256]{1,0:T(8,128)(2,1)} collective-permute-done((bf16[2560,256]{1,0:T(8,128)(2,1)S(1)}, bf16[2560,256]{1,0:T(8,128)(2,1)}, u32[]{:S(2)}, u32[]{:S(2)}) %collective-permute-start.7) | collective-permute-done | bytes 1310752 | tf_op jit(solution)/shard_map/ppermute | solution.py:481
  62.9 4.2 %collective-permute-done.6.refs_4_ = bf16[2560,256]{1,0:T(8,128)(2,1)} collective-permute-done((bf16[2560,256]{1,0:T(8,128)(2,1)S(1)}, bf16[2560,256]{1,0:T(8,128)(2,1)}, u32[]{:S(2)}, u32[]{:S(2)}) %collective-permute-start.6) | collective-permute-done | bytes 1310752 | tf_op jit(solution)/shard_map/ppermute | solution.py:481
  67.2 3.5 %aggregate.4 = (bf16[1280,256]{1,0:T(8,128)(2,1)S(1)}, bf16[1280,256]{1,0:T(8,128)(2,1)S(1)}, bf16[40,256]{1,0:T(8,128)(2,1)S(1)}, bf16[10240,256]{1,0:T(8,128)(2,1)S(1)}) custom-call(s32[1]{0:T(128)} %bitcast.feat_ref, s32[320]{0:T(512)S(1)} %pad_add_fusion.links, ...), custom_call_target="tpu_custom_call", output_to_operand_aliasing={{3}: (8, {})} | custom-call | flops 1048576 | bytes 1024 | tf_op jit(solution)/shard_map/aggregate/pallas_call | solution.py:280
  70.7 0.6 collective-permute-start.8
  71.3 1.5 collective-permute-start.9
  72.8 1.8 %aggregate.5 = (bf16[1280,256]{1,0:T(8,128)(2,1)S(1)}, bf16[1280,256]{1,0:T(8,128)(2,1)S(1)}) custom-call(s32[1]{0:T(128)} %bitcast.feat_ref, s32[320]{0:T(512)S(1)} %pad_add_fusion.links, bf16[40,128,512]{2,1,0:T(8,128)(2,1)S(1)} %get-tuple-element.79.refs_0_, bf16[40,128,160]{2,1,0:T(8,128)(2,1)S(1)} %get-tuple-element.80.refs_1_, ...), custom_call_target="tpu_custom_call" | custom-call | flops 1048576 | bytes 1024 | tf_op jit(solution)/shard_map/aggregate/pallas_call | solution.py:280
  74.7 1.6 collective-permute-start.10
  76.3 4.4 %node_mid.2 = (bf16[2560,512]{1,0:T(8,128)(2,1)S(1)}, bf16[1280,256]{1,0:T(8,128)(2,1)S(1)}, bf16[1280,256]{1,0:T(8,128)(2,1)S(1)}) custom-call(s32[1]{0:T(128)} %bitcast.feat_ref, bf16[2560,512]{1,0:T(8,128)(2,1)S(1)} %get-tuple-element.72.refs_0_, bf16[1280,256]{1,0:T(8,128)(2,1)S(1)} %get-tuple-element.94.refs_1_, ...), custom_call_target="tpu_custom_call", output_to_operand_aliasing={{0}: (1, {})} | custom-call | flops 1048576 | bytes 1024 | tf_op jit(solution)/shard_map/node_mid/pallas_call | solution.py:391
  80.7 1.8 %collective-permute-start.11 = (bf16[1280,256]{1,0:T(8,128)(2,1)S(1)}, bf16[1280,256]{1,0:T(8,128)(2,1)S(1)}, u32[]{:S(2)}, u32[]{:S(2)}) collective-permute-start(bf16[1280,256]{1,0:T(8,128)(2,1)S(1)} %get-tuple-element.104), channel_id=1, source_target_pairs={{0,1},{1,0},{2,3},{3,2},{4,5},{5,4},{6,7},{7,6},{8,9},{9,8},{10,11... | collective-permute-start | bytes 1966088 | tf_op jit(solution)/shard_map/ppermute | solution.py:433
  82.5 0.1 collective-permute-start.12
  82.5 4.1 %collective-permute-start.15 = (bf16[1280,256]{1,0:T(8,128)(2,1)S(1)}, bf16[1280,256]{1,0:T(8,128)(2,1)S(1)}, u32[]{:S(2)}, u32[]{:S(2)}) collective-permute-start(bf16[1280,256]{1,0:T(8,128)(2,1)S(1)} %get-tuple-element.104), channel_id=1, source_target_pairs={{2,1},{4,3},{6,5},{8,7},{10,9},{12,11},{14,13},{1,2},{3,4},{5,6},{... | collective-permute-start | bytes 1966088 | tf_op jit(solution)/shard_map/ppermute | solution.py:539
  86.6 1.9 %collective-permute-start.14 = (bf16[1280,256]{1,0:T(8,128)(2,1)S(1)}, bf16[1280,256]{1,0:T(8,128)(2,1)S(1)}, u32[]{:S(2)}, u32[]{:S(2)}) collective-permute-start(bf16[1280,256]{1,0:T(8,128)(2,1)S(1)} %get-tuple-element.111.refs_0_), channel_id=1, source_target_pairs={{2,0},{4,2},{6,4},{8,6},{10,8},{12,10},{14,12},{1,3},{3,5},{5,7},{... | collective-permute-start | bytes 1966088 | tf_op jit(solution)/shard_map/ppermute | solution.py:539
  88.6 4.4 %node_mid.3 = (bf16[2560,512]{1,0:T(8,128)(2,1)S(1)}, bf16[1280,256]{1,0:T(8,128)(2,1)S(1)}, bf16[1280,256]{1,0:T(8,128)(2,1)S(1)}) custom-call(s32[1]{0:T(128)} %bitcast.feat_ref, bf16[2560,512]{1,0:T(8,128)(2,1)S(1)} %get-tuple-element.106.refs_0_, bf16[1280,256]{1,0:T(8,128)(2,1)S(1)} %get-tuple-element.107.refs_1_, ...), custom_call_target="tpu_custom_call", output_to_operand_aliasing={{0}: (1, {})} | custom-call | flops 1048576 | bytes 1024 | tf_op jit(solution)/shard_map/node_mid/pallas_call | solution.py:391
  93.0 0.1 collective-permute-start.13
  93.1 2.8 %collective-permute-start.18 = (bf16[1280,256]{1,0:T(8,128)(2,1)S(1)}, bf16[1280,256]{1,0:T(8,128)(2,1)S(1)}, u32[]{:S(2)}, u32[]{:S(2)}) collective-permute-start(bf16[1280,256]{1,0:T(8,128)(2,1)S(1)} %get-tuple-element.113.refs_2_), channel_id=1, source_target_pairs={{2,0},{4,2},{6,4},{8,6},{10,8},{12,10},{14,12},{1,3},{3,5},{5,7},{... | collective-permute-start | bytes 1966088 | tf_op jit(solution)/shard_map/ppermute | solution.py:539
  95.9 3.1 %collective-permute-start.19 = (bf16[1280,256]{1,0:T(8,128)(2,1)S(1)}, bf16[1280,256]{1,0:T(8,128)(2,1)S(1)}, u32[]{:S(2)}, u32[]{:S(2)}) collective-permute-start(bf16[1280,256]{1,0:T(8,128)(2,1)S(1)} %get-tuple-element.114), channel_id=1, source_target_pairs={{2,1},{4,3},{6,5},{8,7},{10,9},{12,11},{14,13},{1,2},{3,4},{5,6},{... | collective-permute-start | bytes 1966088 | tf_op jit(solution)/shard_map/ppermute | solution.py:539
  99.0 30.2 %collective-permute-done.14.refs_4_ = bf16[1280,256]{1,0:T(8,128)(2,1)S(1)} collective-permute-done((bf16[1280,256]{1,0:T(8,128)(2,1)S(1)}, bf16[1280,256]{1,0:T(8,128)(2,1)S(1)}, u32[]{:S(2)}, u32[]{:S(2)}) %collective-permute-start.14) | collective-permute-done | bytes 655392 | tf_op jit(solution)/shard_map/ppermute | solution.py:539
  129.2 1.3 local_messages.1.refs_6_
  130.5 0.3 collective-permute-start.16
  130.8 3.6 %collective-permute-done.16 = bf16[160,256]{1,0:T(8,128)(2,1)S(1)} collective-permute-done((bf16[160,256]{1,0:T(8,128)(2,1)S(1)}, bf16[160,256]{1,0:T(8,128)(2,1)S(1)}, u32[]{:S(2)}, u32[]{:S(2)}) %collective-permute-start.16) | collective-permute-done | bytes 81952 | tf_op jit(solution)/shard_map/ppermute | solution.py:438
  134.4 2.3 %collective-permute-start.17 = (bf16[320,256]{1,0:T(8,128)(2,1)S(1)}, bf16[320,256]{1,0:T(8,128)(2,1)S(1)}, u32[]{:S(2)}, u32[]{:S(2)}) collective-permute-start(bf16[320,256]{1,0:T(8,128)(2,1)S(1)} %constant_dynamic-update-slice_fusion.3.refs_1_), channel_id=1, source_target_pairs={{0,1},{1,0},{2,3},{3,2},{4,5},{5,4},{6,7},{7,6},{8,9},{9,8},{10,11... | collective-permute-start | bytes 491528 | tf_op jit(solution)/shard_map/ppermute | solution.py:433
  136.7 1.0 collective-permute-done.17.refs_2_
  137.7 1.6 node_coarse.1.refs_2_
  139.3 4.7 %collective-permute-done.19.refs_5_ = bf16[1280,256]{1,0:T(8,128)(2,1)S(1)} collective-permute-done((bf16[1280,256]{1,0:T(8,128)(2,1)S(1)}, bf16[1280,256]{1,0:T(8,128)(2,1)S(1)}, u32[]{:S(2)}, u32[]{:S(2)}) %collective-permute-start.19) | collective-permute-done | bytes 655392 | tf_op jit(solution)/shard_map/ppermute | solution.py:539
  144.0 2.9 %aggregate.6 = (bf16[1280,256]{1,0:T(8,128)(2,1)S(1)}, bf16[1280,256]{1,0:T(8,128)(2,1)S(1)}, bf16[40,256]{1,0:T(8,128)(2,1)}, bf16[10240,256]{1,0:T(8,128)(2,1)S(1)}) custom-call(s32[1]{0:T(128)} %bitcast.feat_ref, s32[320]{0:T(512)S(1)} %pad_add_fusion.links, bf16[40,128,512]{2,1,0:T(8,128)(2,1)S(1)} %get-tuple-element.79.refs_0_, ...), custom_call_target="tpu_custom_call", output_to_operand_aliasing={{3}: (8, {})} | custom-call | flops 1048576 | bytes 1024 | tf_op jit(solution)/shard_map/aggregate/pallas_call | solution.py:280
  146.9 0.1 collective-permute-start.20
  147.0 1.8 %aggregate.7 = (bf16[1280,256]{1,0:T(8,128)(2,1)S(1)}, bf16[1280,256]{1,0:T(8,128)(2,1)S(1)}) custom-call(s32[1]{0:T(128)} %bitcast.feat_ref, s32[320]{0:T(512)S(1)} %pad_add_fusion.links, bf16[40,128,512]{2,1,0:T(8,128)(2,1)S(1)} %get-tuple-element.79.refs_0_, bf16[40,128,160]{2,1,0:T(8,128)(2,1)S(1)} %get-tuple-element.80.refs_1_, ...), custom_call_target="tpu_custom_call" | custom-call | flops 1048576 | bytes 1024 | tf_op jit(solution)/shard_map/aggregate/pallas_call | solution.py:280
  148.8 0.2 collective-permute-done.20.refs_2_
  149.0 4.2 %node_last.3 = (bf16[1280,512]{1,0:T(8,128)(2,1)S(1)}, bf16[5120,512]{1,0:T(8,128)(2,1)}) custom-call(s32[1]{0:T(128)} %bitcast.feat_ref, bf16[2560,512]{1,0:T(8,128)(2,1)S(1)} %get-tuple-element.109.refs_0_, bf16[1280,256]{1,0:T(8,128)(2,1)S(1)} %get-tuple-element.123.refs_1_, bf16[1280,256]{1,0:T(8,128)(2,1)S(1)} %collective-permute-done.20.refs_2_, ...), custom_call_target="tpu_custom_call" | custom-call | flops 1048576 | bytes 1024 | tf_op jit(solution)/shard_map/node_last/pallas_call | solution.py:391
  153.3 0.3 collective-permute-start.23
  153.6 0.3 collective-permute-start.21
  153.8 3.5 %collective-permute-done.21.refs_2_ = bf16[1280,256]{1,0:T(8,128)(2,1)S(1)} collective-permute-done((bf16[1280,256]{1,0:T(8,128)(2,1)S(1)}, bf16[1280,256]{1,0:T(8,128)(2,1)S(1)}, u32[]{:S(2)}, u32[]{:S(2)}) %collective-permute-start.21) | collective-permute-done | bytes 655392 | tf_op jit(solution)/shard_map/ppermute | solution.py:433
  157.3 2.6 %node_last.4 = (bf16[640,512]{1,0:T(8,128)(2,1)S(1)}, bf16[5120,512]{1,0:T(8,128)(2,1)}) custom-call(s32[1]{0:T(128)} %bitcast.feat_ref, bf16[2560,512]{1,0:T(8,128)(2,1)S(1)} %get-tuple-element.109.refs_0_, bf16[1280,256]{1,0:T(8,128)(2,1)S(1)} %get-tuple-element.118.refs_1_, ...), custom_call_target="tpu_custom_call", output_to_operand_aliasing={{1}: (8, {})} | custom-call | flops 1048576 | bytes 1024 | tf_op jit(solution)/shard_map/node_last/pallas_call | solution.py:391
  159.9 0.3 collective-permute-start.22
  160.2 2.6 %node_last.5 = (bf16[640,512]{1,0:T(8,128)(2,1)S(1)}, bf16[5120,512]{1,0:T(8,128)(2,1)}) custom-call(s32[1]{0:T(128)} %bitcast.feat_ref, bf16[2560,512]{1,0:T(8,128)(2,1)S(1)} %get-tuple-element.109.refs_0_, bf16[1280,256]{1,0:T(8,128)(2,1)S(1)} %get-tuple-element.118.refs_1_, ...), custom_call_target="tpu_custom_call", output_to_operand_aliasing={{1}: (9, {})} | custom-call | flops 1048576 | bytes 1024 | tf_op jit(solution)/shard_map/node_last/pallas_call | solution.py:391
  162.9 0.3 collective-permute-start.24
  163.2 1.8 %collective-permute-done.24.refs_1_ = bf16[640,512]{1,0:T(8,128)(2,1)S(1)} collective-permute-done((bf16[640,512]{1,0:T(8,128)(2,1)S(1)}, bf16[640,512]{1,0:T(8,128)(2,1)S(1)}, u32[]{:S(2)}, u32[]{:S(2)}) %collective-permute-start.24) | collective-permute-done | bytes 655392 | tf_op jit(solution)/shard_map/ppermute | solution.py:433
  165.0 1.1 assemble.1
  (32 shorter events, 0.1 us)
Async XLA Ops:
  0.8 10.3 %collective-permute-start = (bf16[40,512]{1,0:T(8,128)(2,1)S(1)}, bf16[40,512]{1,0:T(8,128)(2,1)S(1)}, u32[]{:S(2)}, u32[]{:S(2)}) collective-permute-start(bf16[40,512]{1,0:T(8,128)(2,1)S(1)} %slice.3), channel_id=1, source_target_pairs={{0,14},{2,0},{4,2},{6,4},{8,6},{10,8},{12,10},{14,12},{1,15},{3,1}... | collective-permute-start | bytes 122888 | tf_op jit(solution)/shard_map/ppermute | solution.py:438
  5.3 44.2 %copy-start = (bf16[2560,256]{1,0:T(8,128)(2,1)}, bf16[2560,256]{1,0:T(8,128)(2,1)S(1)}, u32[]{:S(2)}) copy-start(bf16[2560,256]{1,0:T(8,128)(2,1)S(1)} %message.3.refs_4_) | copy-start | bytes 3932164
  5.3 13.7 %copy-start.2 = (bf16[2,256,512]{2,1,0:T(8,128)(2,1)S(1)}, bf16[2,256,512]{2,1,0:T(8,128)(2,1)}, u32[]{:S(2)}) copy-start(bf16[2,256,512]{2,1,0:T(8,128)(2,1)} %refs_6_) | copy-start | bytes 1572868
  5.3 43.7 %copy-start.4 = (s32[40,4]{0,1:T(4,128)S(1)}, s32[40,4]{0,1:T(4,128)}, u32[]{:S(2)}) copy-start(s32[40,4]{0,1:T(4,128)} %param.13) | copy-start | bytes 1924
  5.3 43.7 %copy-start.5 = (s32[40,4]{0,1:T(4,128)S(1)}, s32[40,4]{0,1:T(4,128)}, u32[]{:S(2)}) copy-start(s32[40,4]{0,1:T(4,128)} %param.12) | copy-start | bytes 1924
  5.3 44.1 %copy-start.3 = (s32[5120]{0:T(1024)S(1)}, s32[5120]{0:T(1024)}, u32[]{:S(2)}) copy-start(s32[5120]{0:T(1024)} %param.14) | copy-start | bytes 61444
  5.3 57.6 %collective-permute-start.7 = (bf16[2560,256]{1,0:T(8,128)(2,1)S(1)}, bf16[2560,256]{1,0:T(8,128)(2,1)}, u32[]{:S(2)}, u32[]{:S(2)}) collective-permute-start(bf16[2560,256]{1,0:T(8,128)(2,1)S(1)} %message.3.refs_4_), channel_id=1, source_target_pairs={{0,2},{2,4},{4,6},{6,8},{8,10},{10,12},{12,14},{1,3},{3,5},{5,7},{... | collective-permute-start | bytes 3932168 | tf_op jit(solution)/shard_map/ppermute | solution.py:481
  11.1 38.4 %copy-start.1 = (bf16[2560,256]{1,0:T(8,128)(2,1)}, bf16[2560,256]{1,0:T(8,128)(2,1)S(1)}, u32[]{:S(2)}) copy-start(bf16[2560,256]{1,0:T(8,128)(2,1)S(1)} %message.2.refs_3_) | copy-start | bytes 3932164
  11.1 56.0 %collective-permute-start.6 = (bf16[2560,256]{1,0:T(8,128)(2,1)S(1)}, bf16[2560,256]{1,0:T(8,128)(2,1)}, u32[]{:S(2)}, u32[]{:S(2)}) collective-permute-start(bf16[2560,256]{1,0:T(8,128)(2,1)S(1)} %message.2.refs_3_), channel_id=1, source_target_pairs={{2,0},{4,2},{6,4},{8,6},{10,8},{12,10},{14,12},{3,1},{5,3},{7,5},{... | collective-permute-start | bytes 3932168 | tf_op jit(solution)/shard_map/ppermute | solution.py:481
  15.1 41.4 %collective-permute-start.3 = (bf16[2,1024,256]{2,1,0:T(8,128)(2,1)}, bf16[2,1024,256]{2,1,0:T(8,128)(2,1)}, u32[]{:S(2)}, u32[]{:S(2)}) collective-permute-start(bf16[2,1024,256]{2,1,0:T(8,128)(2,1)} %refs_5_), channel_id=1, source_target_pairs={{0,1},{1,0},{2,3},{3,2},{4,5},{5,4},{6,7},{7,6},{8,9},{9,8},{10,11... | collective-permute-start | bytes 3145736 | tf_op jit(solution)/shard_map/ppermute | solution.py:433
  16.7 29.8 %collective-permute-start.1 = (bf16[80,512]{1,0:T(8,128)(2,1)S(1)}, bf16[80,512]{1,0:T(8,128)(2,1)S(1)}, u32[]{:S(2)}, u32[]{:S(2)}) collective-permute-start(bf16[80,512]{1,0:T(8,128)(2,1)S(1)} %pad_maximum_fusion.1), channel_id=1, source_target_pairs={{0,8},{2,10},{4,12},{6,14},{8,0},{10,2},{12,4},{14,6},{1,9},{3,11}... | collective-permute-start | bytes 245768 | tf_op jit(solution)/shard_map/ppermute | solution.py:438
  19.0 35.6 %collective-permute-start.4 = (bf16[2,256,512]{2,1,0:T(8,128)(2,1)S(1)}, bf16[2,256,512]{2,1,0:T(8,128)(2,1)}, u32[]{:S(2)}, u32[]{:S(2)}) collective-permute-start(bf16[2,256,512]{2,1,0:T(8,128)(2,1)S(1)} %copy-done.2), channel_id=1, source_target_pairs={{0,1},{1,0},{2,3},{3,2},{4,5},{5,4},{6,7},{7,6},{8,9},{9,8},{10,11... | collective-permute-start | bytes 1572872 | tf_op jit(solution)/shard_map/ppermute | solution.py:433
  46.5 10.0 %collective-permute-start.5 = (bf16[2,512,256]{2,1,0:T(8,128)(2,1)}, bf16[2,512,256]{2,1,0:T(8,128)(2,1)}, u32[]{:S(2)}, u32[]{:S(2)}) collective-permute-start(bf16[2,512,256]{2,1,0:T(8,128)(2,1)} %refs_7_), channel_id=1, source_target_pairs={{0,1},{1,0},{2,3},{3,2},{4,5},{5,4},{6,7},{7,6},{8,9},{9,8},{10,11... | collective-permute-start | bytes 1572872 | tf_op jit(solution)/shard_map/ppermute | solution.py:433
  54.6 6.0 %collective-permute-start.2 = (bf16[160,512]{1,0:T(8,128)(2,1)S(1)}, bf16[160,512]{1,0:T(8,128)(2,1)S(1)}, u32[]{:S(2)}, u32[]{:S(2)}) collective-permute-start(bf16[160,512]{1,0:T(8,128)(2,1)S(1)} %pad_maximum_fusion), channel_id=1, source_target_pairs={{0,12},{2,14},{4,0},{6,2},{8,4},{10,6},{12,8},{14,10},{1,13},{3,15... | collective-permute-start | bytes 491528 | tf_op jit(solution)/shard_map/ppermute | solution.py:438
  70.7 3.9 %collective-permute-start.8 = (bf16[1280,256]{1,0:T(8,128)(2,1)S(1)}, bf16[1280,256]{1,0:T(8,128)(2,1)S(1)}, u32[]{:S(2)}, u32[]{:S(2)}) collective-permute-start(bf16[1280,256]{1,0:T(8,128)(2,1)S(1)} %get-tuple-element.89), channel_id=1, source_target_pairs={{0,1},{1,0},{2,3},{3,2},{4,5},{5,4},{6,7},{7,6},{8,9},{9,8},{10,11... | collective-permute-start | bytes 1966088 | tf_op jit(solution)/shard_map/ppermute | solution.py:433
  71.3 3.4 %collective-permute-start.9 = (bf16[40,256]{1,0:T(8,128)(2,1)S(1)}, bf16[40,256]{1,0:T(8,128)(2,1)S(1)}, u32[]{:S(2)}, u32[]{:S(2)}) collective-permute-start(bf16[40,256]{1,0:T(8,128)(2,1)S(1)} %get-tuple-element.93), channel_id=1, source_target_pairs={{0,14},{2,0},{4,2},{6,4},{8,6},{10,8},{12,10},{14,12},{1,15},{3,1}... | collective-permute-start | bytes 61448 | tf_op jit(solution)/shard_map/ppermute | solution.py:438
  74.7 6.0 %collective-permute-start.10 = (bf16[80,256]{1,0:T(8,128)(2,1)S(1)}, bf16[80,256]{1,0:T(8,128)(2,1)S(1)}, u32[]{:S(2)}, u32[]{:S(2)}) collective-permute-start(bf16[80,256]{1,0:T(8,128)(2,1)S(1)} %pad_maximum_fusion.3), channel_id=1, source_target_pairs={{0,8},{2,10},{4,12},{6,14},{8,0},{10,2},{12,4},{14,6},{1,9},{3,11}... | collective-permute-start | bytes 122888 | tf_op jit(solution)/shard_map/ppermute | solution.py:438
  80.7 7.8 %collective-permute-start.11 = (bf16[1280,256]{1,0:T(8,128)(2,1)S(1)}, bf16[1280,256]{1,0:T(8,128)(2,1)S(1)}, u32[]{:S(2)}, u32[]{:S(2)}) collective-permute-start(bf16[1280,256]{1,0:T(8,128)(2,1)S(1)} %get-tuple-element.104), channel_id=1, source_target_pairs={{0,1},{1,0},{2,3},{3,2},{4,5},{5,4},{6,7},{7,6},{8,9},{9,8},{10,11... | collective-permute-start | bytes 1966088 | tf_op jit(solution)/shard_map/ppermute | solution.py:433
  82.5 6.1 %collective-permute-start.12 = (bf16[1280,256]{1,0:T(8,128)(2,1)S(1)}, bf16[1280,256]{1,0:T(8,128)(2,1)S(1)}, u32[]{:S(2)}, u32[]{:S(2)}) collective-permute-start(bf16[1280,256]{1,0:T(8,128)(2,1)S(1)} %get-tuple-element.108), channel_id=1, source_target_pairs={{0,1},{1,0},{2,3},{3,2},{4,5},{5,4},{6,7},{7,6},{8,9},{9,8},{10,11... | collective-permute-start | bytes 1966088 | tf_op jit(solution)/shard_map/ppermute | solution.py:433
  82.5 46.7 %collective-permute-start.15 = (bf16[1280,256]{1,0:T(8,128)(2,1)S(1)}, bf16[1280,256]{1,0:T(8,128)(2,1)S(1)}, u32[]{:S(2)}, u32[]{:S(2)}) collective-permute-start(bf16[1280,256]{1,0:T(8,128)(2,1)S(1)} %get-tuple-element.104), channel_id=1, source_target_pairs={{2,1},{4,3},{6,5},{8,7},{10,9},{12,11},{14,13},{1,2},{3,4},{5,6},{... | collective-permute-start | bytes 1966088 | tf_op jit(solution)/shard_map/ppermute | solution.py:539
  86.6 42.6 %collective-permute-start.14 = (bf16[1280,256]{1,0:T(8,128)(2,1)S(1)}, bf16[1280,256]{1,0:T(8,128)(2,1)S(1)}, u32[]{:S(2)}, u32[]{:S(2)}) collective-permute-start(bf16[1280,256]{1,0:T(8,128)(2,1)S(1)} %get-tuple-element.111.refs_0_), channel_id=1, source_target_pairs={{2,0},{4,2},{6,4},{8,6},{10,8},{12,10},{14,12},{1,3},{3,5},{5,7},{... | collective-permute-start | bytes 1966088 | tf_op jit(solution)/shard_map/ppermute | solution.py:539
  93.0 36.3 %collective-permute-start.13 = (bf16[1280,256]{1,0:T(8,128)(2,1)S(1)}, bf16[1280,256]{1,0:T(8,128)(2,1)S(1)}, u32[]{:S(2)}, u32[]{:S(2)}) collective-permute-start(bf16[1280,256]{1,0:T(8,128)(2,1)S(1)} %get-tuple-element.114), channel_id=1, source_target_pairs={{0,1},{1,0},{2,3},{3,2},{4,5},{5,4},{6,7},{7,6},{8,9},{9,8},{10,11... | collective-permute-start | bytes 1966088 | tf_op jit(solution)/shard_map/ppermute | solution.py:433
  93.1 46.3 %collective-permute-start.18 = (bf16[1280,256]{1,0:T(8,128)(2,1)S(1)}, bf16[1280,256]{1,0:T(8,128)(2,1)S(1)}, u32[]{:S(2)}, u32[]{:S(2)}) collective-permute-start(bf16[1280,256]{1,0:T(8,128)(2,1)S(1)} %get-tuple-element.113.refs_2_), channel_id=1, source_target_pairs={{2,0},{4,2},{6,4},{8,6},{10,8},{12,10},{14,12},{1,3},{3,5},{5,7},{... | collective-permute-start | bytes 1966088 | tf_op jit(solution)/shard_map/ppermute | solution.py:539
  95.9 48.1 %collective-permute-start.19 = (bf16[1280,256]{1,0:T(8,128)(2,1)S(1)}, bf16[1280,256]{1,0:T(8,128)(2,1)S(1)}, u32[]{:S(2)}, u32[]{:S(2)}) collective-permute-start(bf16[1280,256]{1,0:T(8,128)(2,1)S(1)} %get-tuple-element.114), channel_id=1, source_target_pairs={{2,1},{4,3},{6,5},{8,7},{10,9},{12,11},{14,13},{1,2},{3,4},{5,6},{... | collective-permute-start | bytes 1966088 | tf_op jit(solution)/shard_map/ppermute | solution.py:539
  130.5 3.9 %collective-permute-start.16 = (bf16[160,256]{1,0:T(8,128)(2,1)S(1)}, bf16[160,256]{1,0:T(8,128)(2,1)S(1)}, u32[]{:S(2)}, u32[]{:S(2)}) collective-permute-start(bf16[160,256]{1,0:T(8,128)(2,1)S(1)} %pad_maximum_fusion.2), channel_id=1, source_target_pairs={{0,12},{2,14},{4,0},{6,2},{8,4},{10,6},{12,8},{14,10},{1,13},{3,15... | collective-permute-start | bytes 245768 | tf_op jit(solution)/shard_map/ppermute | solution.py:438
  134.4 3.3 %collective-permute-start.17 = (bf16[320,256]{1,0:T(8,128)(2,1)S(1)}, bf16[320,256]{1,0:T(8,128)(2,1)S(1)}, u32[]{:S(2)}, u32[]{:S(2)}) collective-permute-start(bf16[320,256]{1,0:T(8,128)(2,1)S(1)} %constant_dynamic-update-slice_fusion.3.refs_1_), channel_id=1, source_target_pairs={{0,1},{1,0},{2,3},{3,2},{4,5},{5,4},{6,7},{7,6},{8,9},{9,8},{10,11... | collective-permute-start | bytes 491528 | tf_op jit(solution)/shard_map/ppermute | solution.py:433
  146.9 2.2 %collective-permute-start.20 = (bf16[1280,256]{1,0:T(8,128)(2,1)S(1)}, bf16[1280,256]{1,0:T(8,128)(2,1)S(1)}, u32[]{:S(2)}, u32[]{:S(2)}) collective-permute-start(bf16[1280,256]{1,0:T(8,128)(2,1)S(1)} %get-tuple-element.119), channel_id=1, source_target_pairs={{0,1},{1,0},{2,3},{3,2},{4,5},{5,4},{6,7},{7,6},{8,9},{9,8},{10,11... | collective-permute-start | bytes 1966088 | tf_op jit(solution)/shard_map/ppermute | solution.py:433
  153.3 7.0 %collective-permute-start.23 = (bf16[1280,512]{1,0:T(8,128)(2,1)S(1)}, bf16[1280,512]{1,0:T(8,128)(2,1)S(1)}, u32[]{:S(2)}, u32[]{:S(2)}) collective-permute-start(bf16[1280,512]{1,0:T(8,128)(2,1)S(1)} %get-tuple-element.127), channel_id=1, source_target_pairs={{0,1},{1,0},{2,3},{3,2},{4,5},{5,4},{6,7},{7,6},{8,9},{9,8},{10,11... | collective-permute-start | bytes 3932168 | tf_op jit(solution)/shard_map/ppermute | solution.py:433
  153.6 3.7 %collective-permute-start.21 = (bf16[1280,256]{1,0:T(8,128)(2,1)S(1)}, bf16[1280,256]{1,0:T(8,128)(2,1)S(1)}, u32[]{:S(2)}, u32[]{:S(2)}) collective-permute-start(bf16[1280,256]{1,0:T(8,128)(2,1)S(1)} %get-tuple-element.122), channel_id=1, source_target_pairs={{0,1},{1,0},{2,3},{3,2},{4,5},{5,4},{6,7},{7,6},{8,9},{9,8},{10,11... | collective-permute-start | bytes 1966088 | tf_op jit(solution)/shard_map/ppermute | solution.py:433
  159.9 3.3 %collective-permute-start.22 = (bf16[640,512]{1,0:T(8,128)(2,1)S(1)}, bf16[640,512]{1,0:T(8,128)(2,1)S(1)}, u32[]{:S(2)}, u32[]{:S(2)}) collective-permute-start(bf16[640,512]{1,0:T(8,128)(2,1)S(1)} %get-tuple-element.126), channel_id=1, source_target_pairs={{0,1},{1,0},{2,3},{3,2},{4,5},{5,4},{6,7},{7,6},{8,9},{9,8},{10,11... | collective-permute-start | bytes 1966088 | tf_op jit(solution)/shard_map/ppermute | solution.py:433
  162.9 2.2 %collective-permute-start.24 = (bf16[640,512]{1,0:T(8,128)(2,1)S(1)}, bf16[640,512]{1,0:T(8,128)(2,1)S(1)}, u32[]{:S(2)}, u32[]{:S(2)}) collective-permute-start(bf16[640,512]{1,0:T(8,128)(2,1)S(1)} %get-tuple-element.129), channel_id=1, source_target_pairs={{0,1},{1,0},{2,3},{3,2},{4,5},{5,4},{6,7},{7,6},{8,9},{9,8},{10,11... | collective-permute-start | bytes 1966088 | tf_op jit(solution)/shard_map/ppermute | solution.py:433

commit v6 on v5

--- a/solution.py
+++ b/solution.py
@@ -18,6 +18,7 @@
 NODE_SPLIT = 2
 F32 = jnp.float32
 BF16 = jnp.bfloat16
+LONG = pl.CostEstimate(flops=1 << 33, transcendentals=0, bytes_accessed=1 << 10)
 SMALL = pl.CostEstimate(flops=1 << 20, transcendentals=0, bytes_accessed=1 << 10)
 IN_VMEM = pl.BlockSpec(memory_space=pltpu.VMEM)
 IN_HBM = pl.BlockSpec(memory_space=pltpu.HBM)
@@ -65,7 +66,7 @@
     out_ref[...] = silu(dot(normed, weight_ref[0])).astype(BF16).astype(F32)
 
 
-def message_kernel(start, tile, state, weight, out_ref, state_buf, weight_buf, sems):
+def message_kernel(start, tile, state, weight, out, state_buf, weight_buf, out_ref, sems):
     rows = out_ref.shape[0]
     tiles = [(at, tile) for at in range(0, rows, tile)]
     pairs = [(state.at[pl.ds(start + at, size)], state_buf.at[pl.ds(at, size)]) for at, size in tiles]
@@ -82,6 +83,11 @@
             continue
         at, size = tiles[pos - 1]
         out_ref[at : at + size, :] = silu(dot(normed[pos - 1], weight_buf[...])).astype(BF16)
+        span = pl.ds(at, size)
+        copy = pltpu.make_async_copy(out_ref.at[span], out.at[span], sems.at[len(tiles) + pos])
+        copy.start()
+        copies.append(copy)
+    wait_all(copies[len(tiles) :])
 
 
 def message_call(state, weight, start, rows, tile):
@@ -89,14 +95,15 @@
     return pl.pallas_call(
         functools.partial(message_kernel, start, tile),
         in_specs=[IN_HBM, IN_HBM],
-        out_specs=IN_VMEM,
-        out_shape=pltpu.VMEM((rows, columns), BF16),
+        out_specs=IN_HBM,
+        out_shape=jax.ShapeDtypeStruct((rows, columns), BF16),
         scratch_shapes=[
             pltpu.VMEM((rows, width), BF16),
             pltpu.VMEM((width, columns), BF16),
-            pltpu.SemaphoreType.DMA((1 + rows // tile,)),
+            pltpu.VMEM((rows, columns), BF16),
+            pltpu.SemaphoreType.DMA((1 + 2 * (rows // tile),)),
         ],
-        compiler_params=params(58),
+        compiler_params=params(56),
         cost_estimate=SMALL,
         name="message",
     )(state, weight)
@@ -396,7 +403,7 @@
         out_shape=out_shape,
         input_output_aliases=aliases,
         compiler_params=params(28),
-        cost_estimate=SMALL,
+        cost_estimate=LONG if mode == "last" else SMALL,
         name="node_" + mode,
     )(feat, *operands)
 

time: 167 us -> 163 us (0.976)
  waiting for transfers between devices: 80.9 us -> 76.8 us
    ppermute x13, waiting for transfers between devices: 6.6 us -> 3.18 us  [swap_feat(): return lax.ppermute(array, 'feat', [(0, 1), (1, 0)])]
  transfers between devices with their start and end apart: 25 -> 25, of which waited for: 11 -> 10; matrix products, arithmetic and copies ran while one was open for 0% -> 0% of each run, Pallas kernels for 21% -> 25%
where the time goes in v6:
time: 163 us; the launch traced here: 162 us
  waiting for transfers between devices  76.8 us (47%)
  Pallas kernels  46 us (28%)
  starting transfers between devices  37.6 us (23%)
    ppermute x6, waiting for transfers between devices, fetch(): lax.ppermute(held, 'patch', [(pos, (pos - stride) % count) for pos in ran...  33.3 us
    ppermute x2, waiting for transfers between devices, shards(): lax.ppermute(own, ('patch', 'feat'), own_patch)  30.2 us
    pallas_call x6, Pallas kernels, node_call(): pl.pallas_call(functools.partial(node_kernel, mode, layer, start, offset,...  19.9 us
    ppermute x13, starting transfers between devices, swap_feat(): return lax.ppermute(array, 'feat', [(0, 1), (1, 0)])  10.5 us
    ppermute x6, starting transfers between devices, fetch(): lax.ppermute(held, 'patch', [(pos, (pos - stride) % count) for pos in ran...  8.74 us
    pallas_call x4, Pallas kernels, aggregate_call(): pl.pallas_call(functools.partial(aggregate_kernel, places, start), grid_s...  8.54 us
    pallas_call x2, Pallas kernels, message_call(): pl.pallas_call(functools.partial(message_kernel, start, tile), in_specs=[...  8.25 us
    ppermute x2, starting transfers between devices, shards(): lax.ppermute(other, ('patch', 'feat'), other_patch)  7.63 us
  transfers between devices with their start and end apart: 25, of which 10 were waited for; matrix products, arithmetic and copies ran while one was open for 0% of the time, Pallas kernels for 25%

profile of v6, /device:TPU:9, one launch (start us, length us, event | category | flops | bytes accessed | tf_op | source)
XLA Modules:
  0.0 162.4 jit_solution(17605139439448631369)
XLA Ops:
  0.0 0.8 slice.3
  0.8 1.1 collective-permute-start
  1.9 4.1 %message.3.refs_4_ = bf16[2560,256]{1,0:T(8,128)(2,1)} custom-call(bf16[5120,512]{1,0:T(8,128)(2,1)} %refs_2_.1, bf16[2,512,256]{2,1,0:T(8,128)(2,1)} %refs_7_), custom_call_target="tpu_custom_call" | custom-call | flops 1048576 | bytes 1024 | tf_op jit(solution)/shard_map/message/pallas_call | solution.py:95
  6.0 0.0 copy-start
  6.0 0.0 copy-start.2
  6.1 0.0 copy-start.3
  6.1 0.0 copy-start.1
  6.1 2.4 %collective-permute-start.7 = (bf16[2560,256]{1,0:T(8,128)(2,1)}, bf16[2560,256]{1,0:T(8,128)(2,1)S(1)}, u32[]{:S(2)}, u32[]{:S(2)}) collective-permute-start(bf16[2560,256]{1,0:T(8,128)(2,1)} %message.3.refs_4_), channel_id=1, source_target_pairs={{0,2},{2,4},{4,6},{6,8},{8,10},{10,12},{12,14},{1,3},{3,5},{5,7},{... | collective-permute-start | bytes 3932168 | tf_op jit(solution)/shard_map/ppermute | solution.py:488
  8.5 4.1 %message.2.refs_3_ = bf16[2560,256]{1,0:T(8,128)(2,1)} custom-call(bf16[5120,512]{1,0:T(8,128)(2,1)} %refs_2_.1, bf16[2,512,256]{2,1,0:T(8,128)(2,1)} %refs_7_), custom_call_target="tpu_custom_call" | custom-call | flops 1048576 | bytes 1024 | tf_op jit(solution)/shard_map/message/pallas_call | solution.py:95
  12.6 0.0 collective-permute-done
  12.6 3.9 %collective-permute-start.6 = (bf16[2560,256]{1,0:T(8,128)(2,1)}, bf16[2560,256]{1,0:T(8,128)(2,1)S(1)}, u32[]{:S(2)}, u32[]{:S(2)}) collective-permute-start(bf16[2560,256]{1,0:T(8,128)(2,1)} %message.2.refs_3_), channel_id=1, source_target_pairs={{2,0},{4,2},{6,4},{8,6},{10,8},{12,10},{14,12},{3,1},{5,3},{7,5},{... | collective-permute-start | bytes 3932168 | tf_op jit(solution)/shard_map/ppermute | solution.py:488
  16.6 1.6 collective-permute-start.3
  18.2 2.3 %collective-permute-start.1 = (bf16[80,512]{1,0:T(8,128)(2,1)S(1)}, bf16[80,512]{1,0:T(8,128)(2,1)S(1)}, u32[]{:S(2)}, u32[]{:S(2)}) collective-permute-start(bf16[80,512]{1,0:T(8,128)(2,1)S(1)} %pad_maximum_fusion.1), channel_id=1, source_target_pairs={{0,8},{2,10},{4,12},{6,14},{8,0},{10,2},{12,4},{14,6},{1,9},{3,11}... | collective-permute-start | bytes 245768 | tf_op jit(solution)/shard_map/ppermute | solution.py:445
  20.5 0.3 collective-permute-start.4
  20.8 27.4 %collective-permute-done.1 = bf16[80,512]{1,0:T(8,128)(2,1)S(1)} collective-permute-done((bf16[80,512]{1,0:T(8,128)(2,1)S(1)}, bf16[80,512]{1,0:T(8,128)(2,1)S(1)}, u32[]{:S(2)}, u32[]{:S(2)}) %collective-permute-start.1) | collective-permute-done | bytes 81952 | tf_op jit(solution)/shard_map/ppermute | solution.py:445
  48.2 2.5 %collective-permute-start.5 = (bf16[2,512,256]{2,1,0:T(8,128)(2,1)}, bf16[2,512,256]{2,1,0:T(8,128)(2,1)}, u32[]{:S(2)}, u32[]{:S(2)}) collective-permute-start(bf16[2,512,256]{2,1,0:T(8,128)(2,1)} %refs_7_), channel_id=1, source_target_pairs={{0,1},{1,0},{2,3},{3,2},{4,5},{5,4},{6,7},{7,6},{8,9},{9,8},{10,11... | collective-permute-start | bytes 1572872 | tf_op jit(solution)/shard_map/ppermute | solution.py:440
  50.7 0.1 copy.18
  50.8 0.1 mul.15
  50.9 0.1 copy.19
  51.0 0.1 reshape.52
  51.1 0.1 pad_add_fusion.links
  51.2 5.0 %stage.1 = (bf16[40,128,512]{2,1,0:T(8,128)(2,1)S(1)}, bf16[40,128,160]{2,1,0:T(8,128)(2,1)S(1)}, bf16[2560,512]{1,0:T(8,128)(2,1)S(1)}, bf16[10240,256]{1,0:T(8...) custom-call(s32[1]{0:T(128)} %bitcast.feat_ref, ...), custom_call_target="tpu_custom_call" | custom-call | flops 1048576 | bytes 1024 | tf_op jit(solution)/shard_map/stage/pallas_call | solution.py:166
  56.2 0.0 collective-permute-done.4.refs_1_
  56.3 1.9 %collective-permute-start.2 = (bf16[160,512]{1,0:T(8,128)(2,1)S(1)}, bf16[160,512]{1,0:T(8,128)(2,1)S(1)}, u32[]{:S(2)}, u32[]{:S(2)}) collective-permute-start(bf16[160,512]{1,0:T(8,128)(2,1)S(1)} %pad_maximum_fusion), channel_id=1, source_target_pairs={{0,12},{2,14},{4,0},{6,2},{8,4},{10,6},{12,8},{14,10},{1,13},{3,15... | collective-permute-start | bytes 491528 | tf_op jit(solution)/shard_map/ppermute | solution.py:445
  58.2 1.5 weights.1
  59.7 2.4 %collective-permute-done.2 = bf16[160,512]{1,0:T(8,128)(2,1)S(1)} collective-permute-done((bf16[160,512]{1,0:T(8,128)(2,1)S(1)}, bf16[160,512]{1,0:T(8,128)(2,1)S(1)}, u32[]{:S(2)}, u32[]{:S(2)}) %collective-permute-start.2) | collective-permute-done | bytes 163872 | tf_op jit(solution)/shard_map/ppermute | solution.py:445
  62.2 0.5 coarse_message.1.refs_2_
  62.6 1.3 collective-permute-done.7.refs_5_
  64.0 4.0 %collective-permute-done.6.refs_4_ = bf16[2560,256]{1,0:T(8,128)(2,1)S(1)} collective-permute-done((bf16[2560,256]{1,0:T(8,128)(2,1)}, bf16[2560,256]{1,0:T(8,128)(2,1)S(1)}, u32[]{:S(2)}, u32[]{:S(2)}) %collective-permute-start.6) | collective-permute-done | bytes 1310752 | tf_op jit(solution)/shard_map/ppermute | solution.py:488
  68.0 2.0 %aggregate.4 = (bf16[1280,256]{1,0:T(8,128)(2,1)S(1)}, bf16[1280,256]{1,0:T(8,128)(2,1)S(1)}, bf16[40,256]{1,0:T(8,128)(2,1)S(1)}, bf16[10240,256]{1,0:T(8,128)(2,1)S(1)}) custom-call(s32[1]{0:T(128)} %bitcast.feat_ref, s32[320]{0:T(512)S(1)} %pad_add_fusion.links, ...), custom_call_target="tpu_custom_call", output_to_operand_aliasing={{3}: (8, {})} | custom-call | flops 1048576 | bytes 1024 | tf_op jit(solution)/shard_map/aggregate/pallas_call | solution.py:287
  70.0 0.6 collective-permute-start.8
  70.6 1.5 collective-permute-start.9
  72.1 1.8 %aggregate.5 = (bf16[1280,256]{1,0:T(8,128)(2,1)S(1)}, bf16[1280,256]{1,0:T(8,128)(2,1)S(1)}) custom-call(s32[1]{0:T(128)} %bitcast.feat_ref, s32[320]{0:T(512)S(1)} %pad_add_fusion.links, bf16[40,128,512]{2,1,0:T(8,128)(2,1)S(1)} %get-tuple-element.79.refs_0_, bf16[40,128,160]{2,1,0:T(8,128)(2,1)S(1)} %get-tuple-element.80.refs_1_, ...), custom_call_target="tpu_custom_call" | custom-call | flops 1048576 | bytes 1024 | tf_op jit(solution)/shard_map/aggregate/pallas_call | solution.py:287
  74.0 1.6 collective-permute-start.10
  75.6 4.4 %node_mid.2 = (bf16[2560,512]{1,0:T(8,128)(2,1)S(1)}, bf16[1280,256]{1,0:T(8,128)(2,1)S(1)}, bf16[1280,256]{1,0:T(8,128)(2,1)S(1)}) custom-call(s32[1]{0:T(128)} %bitcast.feat_ref, bf16[2560,512]{1,0:T(8,128)(2,1)S(1)} %get-tuple-element.72.refs_0_, bf16[1280,256]{1,0:T(8,128)(2,1)S(1)} %get-tuple-element.94.refs_1_, ...), custom_call_target="tpu_custom_call", output_to_operand_aliasing={{0}: (1, {})} | custom-call | flops 1048576 | bytes 1024 | tf_op jit(solution)/shard_map/node_mid/pallas_call | solution.py:398
  80.0 1.7 %collective-permute-start.11 = (bf16[1280,256]{1,0:T(8,128)(2,1)S(1)}, bf16[1280,256]{1,0:T(8,128)(2,1)S(1)}, u32[]{:S(2)}, u32[]{:S(2)}) collective-permute-start(bf16[1280,256]{1,0:T(8,128)(2,1)S(1)} %get-tuple-element.104), channel_id=1, source_target_pairs={{0,1},{1,0},{2,3},{3,2},{4,5},{5,4},{6,7},{7,6},{8,9},{9,8},{10,11... | collective-permute-start | bytes 1966088 | tf_op jit(solution)/shard_map/ppermute | solution.py:440
  81.8 0.1 collective-permute-start.12
  81.8 4.3 %collective-permute-start.15 = (bf16[1280,256]{1,0:T(8,128)(2,1)S(1)}, bf16[1280,256]{1,0:T(8,128)(2,1)S(1)}, u32[]{:S(2)}, u32[]{:S(2)}) collective-permute-start(bf16[1280,256]{1,0:T(8,128)(2,1)S(1)} %get-tuple-element.104), channel_id=1, source_target_pairs={{2,1},{4,3},{6,5},{8,7},{10,9},{12,11},{14,13},{1,2},{3,4},{5,6},{... | collective-permute-start | bytes 1966088 | tf_op jit(solution)/shard_map/ppermute | solution.py:546
  86.1 1.9 %collective-permute-start.14 = (bf16[1280,256]{1,0:T(8,128)(2,1)S(1)}, bf16[1280,256]{1,0:T(8,128)(2,1)S(1)}, u32[]{:S(2)}, u32[]{:S(2)}) collective-permute-start(bf16[1280,256]{1,0:T(8,128)(2,1)S(1)} %get-tuple-element.111.refs_0_), channel_id=1, source_target_pairs={{2,0},{4,2},{6,4},{8,6},{10,8},{12,10},{14,12},{1,3},{3,5},{5,7},{... | collective-permute-start | bytes 1966088 | tf_op jit(solution)/shard_map/ppermute | solution.py:546
  88.1 4.4 %node_mid.3 = (bf16[2560,512]{1,0:T(8,128)(2,1)S(1)}, bf16[1280,256]{1,0:T(8,128)(2,1)S(1)}, bf16[1280,256]{1,0:T(8,128)(2,1)S(1)}) custom-call(s32[1]{0:T(128)} %bitcast.feat_ref, bf16[2560,512]{1,0:T(8,128)(2,1)S(1)} %get-tuple-element.106.refs_0_, bf16[1280,256]{1,0:T(8,128)(2,1)S(1)} %get-tuple-element.107.refs_1_, ...), custom_call_target="tpu_custom_call", output_to_operand_aliasing={{0}: (1, {})} | custom-call | flops 1048576 | bytes 1024 | tf_op jit(solution)/shard_map/node_mid/pallas_call | solution.py:398
  92.5 0.1 collective-permute-start.13
  92.6 2.6 %collective-permute-start.18 = (bf16[1280,256]{1,0:T(8,128)(2,1)S(1)}, bf16[1280,256]{1,0:T(8,128)(2,1)S(1)}, u32[]{:S(2)}, u32[]{:S(2)}) collective-permute-start(bf16[1280,256]{1,0:T(8,128)(2,1)S(1)} %get-tuple-element.113.refs_2_), channel_id=1, source_target_pairs={{2,0},{4,2},{6,4},{8,6},{10,8},{12,10},{14,12},{1,3},{3,5},{5,7},{... | collective-permute-start | bytes 1966088 | tf_op jit(solution)/shard_map/ppermute | solution.py:546
  95.2 3.3 %collective-permute-start.19 = (bf16[1280,256]{1,0:T(8,128)(2,1)S(1)}, bf16[1280,256]{1,0:T(8,128)(2,1)S(1)}, u32[]{:S(2)}, u32[]{:S(2)}) collective-permute-start(bf16[1280,256]{1,0:T(8,128)(2,1)S(1)} %get-tuple-element.114), channel_id=1, source_target_pairs={{2,1},{4,3},{6,5},{8,7},{10,9},{12,11},{14,13},{1,2},{3,4},{5,6},{... | collective-permute-start | bytes 1966088 | tf_op jit(solution)/shard_map/ppermute | solution.py:546
  98.5 30.2 %collective-permute-done.14.refs_4_ = bf16[1280,256]{1,0:T(8,128)(2,1)S(1)} collective-permute-done((bf16[1280,256]{1,0:T(8,128)(2,1)S(1)}, bf16[1280,256]{1,0:T(8,128)(2,1)S(1)}, u32[]{:S(2)}, u32[]{:S(2)}) %collective-permute-start.14) | collective-permute-done | bytes 655392 | tf_op jit(solution)/shard_map/ppermute | solution.py:546
  128.8 1.3 local_messages.1.refs_6_
  130.1 0.3 collective-permute-start.16
  130.4 3.6 %collective-permute-done.16 = bf16[160,256]{1,0:T(8,128)(2,1)S(1)} collective-permute-done((bf16[160,256]{1,0:T(8,128)(2,1)S(1)}, bf16[160,256]{1,0:T(8,128)(2,1)S(1)}, u32[]{:S(2)}, u32[]{:S(2)}) %collective-permute-start.16) | collective-permute-done | bytes 81952 | tf_op jit(solution)/shard_map/ppermute | solution.py:445
  133.9 2.3 %collective-permute-start.17 = (bf16[320,256]{1,0:T(8,128)(2,1)S(1)}, bf16[320,256]{1,0:T(8,128)(2,1)S(1)}, u32[]{:S(2)}, u32[]{:S(2)}) collective-permute-start(bf16[320,256]{1,0:T(8,128)(2,1)S(1)} %constant_dynamic-update-slice_fusion.3.refs_1_), channel_id=1, source_target_pairs={{0,1},{1,0},{2,3},{3,2},{4,5},{5,4},{6,7},{7,6},{8,9},{9,8},{10,11... | collective-permute-start | bytes 491528 | tf_op jit(solution)/shard_map/ppermute | solution.py:440
  136.2 1.0 collective-permute-done.17.refs_2_
  137.2 1.6 node_coarse.1.refs_2_
  138.8 4.7 %collective-permute-done.19.refs_5_ = bf16[1280,256]{1,0:T(8,128)(2,1)S(1)} collective-permute-done((bf16[1280,256]{1,0:T(8,128)(2,1)S(1)}, bf16[1280,256]{1,0:T(8,128)(2,1)S(1)}, u32[]{:S(2)}, u32[]{:S(2)}) %collective-permute-start.19) | collective-permute-done | bytes 655392 | tf_op jit(solution)/shard_map/ppermute | solution.py:546
  143.5 2.9 %aggregate.6 = (bf16[1280,256]{1,0:T(8,128)(2,1)S(1)}, bf16[1280,256]{1,0:T(8,128)(2,1)S(1)}, bf16[40,256]{1,0:T(8,128)(2,1)}, bf16[10240,256]{1,0:T(8,128)(2,1)S(1)}) custom-call(s32[1]{0:T(128)} %bitcast.feat_ref, s32[320]{0:T(512)S(1)} %pad_add_fusion.links, bf16[40,128,512]{2,1,0:T(8,128)(2,1)S(1)} %get-tuple-element.79.refs_0_, ...), custom_call_target="tpu_custom_call", output_to_operand_aliasing={{3}: (8, {})} | custom-call | flops 1048576 | bytes 1024 | tf_op jit(solution)/shard_map/aggregate/pallas_call | solution.py:287
  146.4 0.1 collective-permute-start.20
  146.5 1.8 %aggregate.7 = (bf16[1280,256]{1,0:T(8,128)(2,1)S(1)}, bf16[1280,256]{1,0:T(8,128)(2,1)S(1)}) custom-call(s32[1]{0:T(128)} %bitcast.feat_ref, s32[320]{0:T(512)S(1)} %pad_add_fusion.links, bf16[40,128,512]{2,1,0:T(8,128)(2,1)S(1)} %get-tuple-element.79.refs_0_, bf16[40,128,160]{2,1,0:T(8,128)(2,1)S(1)} %get-tuple-element.80.refs_1_, ...), custom_call_target="tpu_custom_call" | custom-call | flops 1048576 | bytes 1024 | tf_op jit(solution)/shard_map/aggregate/pallas_call | solution.py:287
  148.3 0.2 collective-permute-done.20.refs_2_
  148.5 0.3 collective-permute-start.21
  148.9 4.2 %node_last.3 = (bf16[1280,512]{1,0:T(8,128)(2,1)S(1)}, bf16[5120,512]{1,0:T(8,128)(2,1)}) custom-call(s32[1]{0:T(128)} %bitcast.feat_ref, bf16[2560,512]{1,0:T(8,128)(2,1)S(1)} %get-tuple-element.109.refs_0_, bf16[1280,256]{1,0:T(8,128)(2,1)S(1)} %get-tuple-element.123.refs_1_, bf16[1280,256]{1,0:T(8,128)(2,1)S(1)} %collective-permute-done.20.refs_2_, ...), custom_call_target="tpu_custom_call" | custom-call | flops 8589934592 | bytes 1024 | tf_op jit(solution)/shard_map/node_last/pallas_call | solution.py:398
  153.1 0.3 collective-permute-start.23
  153.4 2.6 %node_last.4 = (bf16[640,512]{1,0:T(8,128)(2,1)S(1)}, bf16[5120,512]{1,0:T(8,128)(2,1)}) custom-call(s32[1]{0:T(128)} %bitcast.feat_ref, bf16[2560,512]{1,0:T(8,128)(2,1)S(1)} %get-tuple-element.109.refs_0_, bf16[1280,256]{1,0:T(8,128)(2,1)S(1)} %get-tuple-element.118.refs_1_, ...), custom_call_target="tpu_custom_call", output_to_operand_aliasing={{1}: (8, {})} | custom-call | flops 8589934592 | bytes 1024 | tf_op jit(solution)/shard_map/node_last/pallas_call | solution.py:398
  156.0 0.4 collective-permute-start.22
  156.3 2.6 %node_last.5 = (bf16[640,512]{1,0:T(8,128)(2,1)S(1)}, bf16[5120,512]{1,0:T(8,128)(2,1)}) custom-call(s32[1]{0:T(128)} %bitcast.feat_ref, bf16[2560,512]{1,0:T(8,128)(2,1)S(1)} %get-tuple-element.109.refs_0_, bf16[1280,256]{1,0:T(8,128)(2,1)S(1)} %get-tuple-element.118.refs_1_, ...), custom_call_target="tpu_custom_call", output_to_operand_aliasing={{1}: (9, {})} | custom-call | flops 8589934592 | bytes 1024 | tf_op jit(solution)/shard_map/node_last/pallas_call | solution.py:398
  159.0 0.3 collective-permute-start.24
  159.2 1.9 %collective-permute-done.24.refs_1_ = bf16[640,512]{1,0:T(8,128)(2,1)S(1)} collective-permute-done((bf16[640,512]{1,0:T(8,128)(2,1)S(1)}, bf16[640,512]{1,0:T(8,128)(2,1)S(1)}, u32[]{:S(2)}, u32[]{:S(2)}) %collective-permute-start.24) | collective-permute-done | bytes 655392 | tf_op jit(solution)/shard_map/ppermute | solution.py:440
  161.1 1.1 assemble.1
  (28 shorter events, 0.1 us)
Async XLA Ops:
  0.8 11.8 %collective-permute-start = (bf16[40,512]{1,0:T(8,128)(2,1)S(1)}, bf16[40,512]{1,0:T(8,128)(2,1)S(1)}, u32[]{:S(2)}, u32[]{:S(2)}) collective-permute-start(bf16[40,512]{1,0:T(8,128)(2,1)S(1)} %slice.3), channel_id=1, source_target_pairs={{0,14},{2,0},{4,2},{6,4},{8,6},{10,8},{12,10},{14,12},{1,15},{3,1}... | collective-permute-start | bytes 122888 | tf_op jit(solution)/shard_map/ppermute | solution.py:445
  6.0 14.5 %copy-start = (bf16[2,256,512]{2,1,0:T(8,128)(2,1)S(1)}, bf16[2,256,512]{2,1,0:T(8,128)(2,1)}, u32[]{:S(2)}) copy-start(bf16[2,256,512]{2,1,0:T(8,128)(2,1)} %refs_6_) | copy-start | bytes 1572868
  6.0 44.7 %copy-start.2 = (s32[40,4]{0,1:T(4,128)S(1)}, s32[40,4]{0,1:T(4,128)}, u32[]{:S(2)}) copy-start(s32[40,4]{0,1:T(4,128)} %param.13) | copy-start | bytes 1924
  6.1 44.7 %copy-start.3 = (s32[40,4]{0,1:T(4,128)S(1)}, s32[40,4]{0,1:T(4,128)}, u32[]{:S(2)}) copy-start(s32[40,4]{0,1:T(4,128)} %param.12) | copy-start | bytes 1924
  6.1 45.1 %copy-start.1 = (s32[5120]{0:T(1024)S(1)}, s32[5120]{0:T(1024)}, u32[]{:S(2)}) copy-start(s32[5120]{0:T(1024)} %param.14) | copy-start | bytes 61444
  6.1 57.9 %collective-permute-start.7 = (bf16[2560,256]{1,0:T(8,128)(2,1)}, bf16[2560,256]{1,0:T(8,128)(2,1)S(1)}, u32[]{:S(2)}, u32[]{:S(2)}) collective-permute-start(bf16[2560,256]{1,0:T(8,128)(2,1)} %message.3.refs_4_), channel_id=1, source_target_pairs={{0,2},{2,4},{4,6},{6,8},{8,10},{10,12},{12,14},{1,3},{3,5},{5,7},{... | collective-permute-start | bytes 3932168 | tf_op jit(solution)/shard_map/ppermute | solution.py:488
  12.6 55.4 %collective-permute-start.6 = (bf16[2560,256]{1,0:T(8,128)(2,1)}, bf16[2560,256]{1,0:T(8,128)(2,1)S(1)}, u32[]{:S(2)}, u32[]{:S(2)}) collective-permute-start(bf16[2560,256]{1,0:T(8,128)(2,1)} %message.2.refs_3_), channel_id=1, source_target_pairs={{2,0},{4,2},{6,4},{8,6},{10,8},{12,10},{14,12},{3,1},{5,3},{7,5},{... | collective-permute-start | bytes 3932168 | tf_op jit(solution)/shard_map/ppermute | solution.py:488
  16.6 41.6 %collective-permute-start.3 = (bf16[2,1024,256]{2,1,0:T(8,128)(2,1)}, bf16[2,1024,256]{2,1,0:T(8,128)(2,1)}, u32[]{:S(2)}, u32[]{:S(2)}) collective-permute-start(bf16[2,1024,256]{2,1,0:T(8,128)(2,1)} %refs_5_), channel_id=1, source_target_pairs={{0,1},{1,0},{2,3},{3,2},{4,5},{5,4},{6,7},{7,6},{8,9},{9,8},{10,11... | collective-permute-start | bytes 3145736 | tf_op jit(solution)/shard_map/ppermute | solution.py:440
  18.2 30.0 %collective-permute-start.1 = (bf16[80,512]{1,0:T(8,128)(2,1)S(1)}, bf16[80,512]{1,0:T(8,128)(2,1)S(1)}, u32[]{:S(2)}, u32[]{:S(2)}) collective-permute-start(bf16[80,512]{1,0:T(8,128)(2,1)S(1)} %pad_maximum_fusion.1), channel_id=1, source_target_pairs={{0,8},{2,10},{4,12},{6,14},{8,0},{10,2},{12,4},{14,6},{1,9},{3,11}... | collective-permute-start | bytes 245768 | tf_op jit(solution)/shard_map/ppermute | solution.py:445
  20.5 35.8 %collective-permute-start.4 = (bf16[2,256,512]{2,1,0:T(8,128)(2,1)S(1)}, bf16[2,256,512]{2,1,0:T(8,128)(2,1)}, u32[]{:S(2)}, u32[]{:S(2)}) collective-permute-start(bf16[2,256,512]{2,1,0:T(8,128)(2,1)S(1)} %copy-done), channel_id=1, source_target_pairs={{0,1},{1,0},{2,3},{3,2},{4,5},{5,4},{6,7},{7,6},{8,9},{9,8},{10,11... | collective-permute-start | bytes 1572872 | tf_op jit(solution)/shard_map/ppermute | solution.py:440
  48.2 10.0 %collective-permute-start.5 = (bf16[2,512,256]{2,1,0:T(8,128)(2,1)}, bf16[2,512,256]{2,1,0:T(8,128)(2,1)}, u32[]{:S(2)}, u32[]{:S(2)}) collective-permute-start(bf16[2,512,256]{2,1,0:T(8,128)(2,1)} %refs_7_), channel_id=1, source_target_pairs={{0,1},{1,0},{2,3},{3,2},{4,5},{5,4},{6,7},{7,6},{8,9},{9,8},{10,11... | collective-permute-start | bytes 1572872 | tf_op jit(solution)/shard_map/ppermute | solution.py:440
  56.3 5.9 %collective-permute-start.2 = (bf16[160,512]{1,0:T(8,128)(2,1)S(1)}, bf16[160,512]{1,0:T(8,128)(2,1)S(1)}, u32[]{:S(2)}, u32[]{:S(2)}) collective-permute-start(bf16[160,512]{1,0:T(8,128)(2,1)S(1)} %pad_maximum_fusion), channel_id=1, source_target_pairs={{0,12},{2,14},{4,0},{6,2},{8,4},{10,6},{12,8},{14,10},{1,13},{3,15... | collective-permute-start | bytes 491528 | tf_op jit(solution)/shard_map/ppermute | solution.py:445
  70.0 3.9 %collective-permute-start.8 = (bf16[1280,256]{1,0:T(8,128)(2,1)S(1)}, bf16[1280,256]{1,0:T(8,128)(2,1)S(1)}, u32[]{:S(2)}, u32[]{:S(2)}) collective-permute-start(bf16[1280,256]{1,0:T(8,128)(2,1)S(1)} %get-tuple-element.89), channel_id=1, source_target_pairs={{0,1},{1,0},{2,3},{3,2},{4,5},{5,4},{6,7},{7,6},{8,9},{9,8},{10,11... | collective-permute-start | bytes 1966088 | tf_op jit(solution)/shard_map/ppermute | solution.py:440
  70.6 3.4 %collective-permute-start.9 = (bf16[40,256]{1,0:T(8,128)(2,1)S(1)}, bf16[40,256]{1,0:T(8,128)(2,1)S(1)}, u32[]{:S(2)}, u32[]{:S(2)}) collective-permute-start(bf16[40,256]{1,0:T(8,128)(2,1)S(1)} %get-tuple-element.93), channel_id=1, source_target_pairs={{0,14},{2,0},{4,2},{6,4},{8,6},{10,8},{12,10},{14,12},{1,15},{3,1}... | collective-permute-start | bytes 61448 | tf_op jit(solution)/shard_map/ppermute | solution.py:445
  74.0 6.0 %collective-permute-start.10 = (bf16[80,256]{1,0:T(8,128)(2,1)S(1)}, bf16[80,256]{1,0:T(8,128)(2,1)S(1)}, u32[]{:S(2)}, u32[]{:S(2)}) collective-permute-start(bf16[80,256]{1,0:T(8,128)(2,1)S(1)} %pad_maximum_fusion.3), channel_id=1, source_target_pairs={{0,8},{2,10},{4,12},{6,14},{8,0},{10,2},{12,4},{14,6},{1,9},{3,11}... | collective-permute-start | bytes 122888 | tf_op jit(solution)/shard_map/ppermute | solution.py:445
  80.0 8.0 %collective-permute-start.11 = (bf16[1280,256]{1,0:T(8,128)(2,1)S(1)}, bf16[1280,256]{1,0:T(8,128)(2,1)S(1)}, u32[]{:S(2)}, u32[]{:S(2)}) collective-permute-start(bf16[1280,256]{1,0:T(8,128)(2,1)S(1)} %get-tuple-element.104), channel_id=1, source_target_pairs={{0,1},{1,0},{2,3},{3,2},{4,5},{5,4},{6,7},{7,6},{8,9},{9,8},{10,11... | collective-permute-start | bytes 1966088 | tf_op jit(solution)/shard_map/ppermute | solution.py:440
  81.8 6.3 %collective-permute-start.12 = (bf16[1280,256]{1,0:T(8,128)(2,1)S(1)}, bf16[1280,256]{1,0:T(8,128)(2,1)S(1)}, u32[]{:S(2)}, u32[]{:S(2)}) collective-permute-start(bf16[1280,256]{1,0:T(8,128)(2,1)S(1)} %get-tuple-element.108), channel_id=1, source_target_pairs={{0,1},{1,0},{2,3},{3,2},{4,5},{5,4},{6,7},{7,6},{8,9},{9,8},{10,11... | collective-permute-start | bytes 1966088 | tf_op jit(solution)/shard_map/ppermute | solution.py:440
  81.8 46.9 %collective-permute-start.15 = (bf16[1280,256]{1,0:T(8,128)(2,1)S(1)}, bf16[1280,256]{1,0:T(8,128)(2,1)S(1)}, u32[]{:S(2)}, u32[]{:S(2)}) collective-permute-start(bf16[1280,256]{1,0:T(8,128)(2,1)S(1)} %get-tuple-element.104), channel_id=1, source_target_pairs={{2,1},{4,3},{6,5},{8,7},{10,9},{12,11},{14,13},{1,2},{3,4},{5,6},{... | collective-permute-start | bytes 1966088 | tf_op jit(solution)/shard_map/ppermute | solution.py:546
  86.1 42.6 %collective-permute-start.14 = (bf16[1280,256]{1,0:T(8,128)(2,1)S(1)}, bf16[1280,256]{1,0:T(8,128)(2,1)S(1)}, u32[]{:S(2)}, u32[]{:S(2)}) collective-permute-start(bf16[1280,256]{1,0:T(8,128)(2,1)S(1)} %get-tuple-element.111.refs_0_), channel_id=1, source_target_pairs={{2,0},{4,2},{6,4},{8,6},{10,8},{12,10},{14,12},{1,3},{3,5},{5,7},{... | collective-permute-start | bytes 1966088 | tf_op jit(solution)/shard_map/ppermute | solution.py:546
  92.5 36.3 %collective-permute-start.13 = (bf16[1280,256]{1,0:T(8,128)(2,1)S(1)}, bf16[1280,256]{1,0:T(8,128)(2,1)S(1)}, u32[]{:S(2)}, u32[]{:S(2)}) collective-permute-start(bf16[1280,256]{1,0:T(8,128)(2,1)S(1)} %get-tuple-element.114), channel_id=1, source_target_pairs={{0,1},{1,0},{2,3},{3,2},{4,5},{5,4},{6,7},{7,6},{8,9},{9,8},{10,11... | collective-permute-start | bytes 1966088 | tf_op jit(solution)/shard_map/ppermute | solution.py:440
  92.6 46.2 %collective-permute-start.18 = (bf16[1280,256]{1,0:T(8,128)(2,1)S(1)}, bf16[1280,256]{1,0:T(8,128)(2,1)S(1)}, u32[]{:S(2)}, u32[]{:S(2)}) collective-permute-start(bf16[1280,256]{1,0:T(8,128)(2,1)S(1)} %get-tuple-element.113.refs_2_), channel_id=1, source_target_pairs={{2,0},{4,2},{6,4},{8,6},{10,8},{12,10},{14,12},{1,3},{3,5},{5,7},{... | collective-permute-start | bytes 1966088 | tf_op jit(solution)/shard_map/ppermute | solution.py:546
  95.2 48.3 %collective-permute-start.19 = (bf16[1280,256]{1,0:T(8,128)(2,1)S(1)}, bf16[1280,256]{1,0:T(8,128)(2,1)S(1)}, u32[]{:S(2)}, u32[]{:S(2)}) collective-permute-start(bf16[1280,256]{1,0:T(8,128)(2,1)S(1)} %get-tuple-element.114), channel_id=1, source_target_pairs={{2,1},{4,3},{6,5},{8,7},{10,9},{12,11},{14,13},{1,2},{3,4},{5,6},{... | collective-permute-start | bytes 1966088 | tf_op jit(solution)/shard_map/ppermute | solution.py:546
  130.1 3.9 %collective-permute-start.16 = (bf16[160,256]{1,0:T(8,128)(2,1)S(1)}, bf16[160,256]{1,0:T(8,128)(2,1)S(1)}, u32[]{:S(2)}, u32[]{:S(2)}) collective-permute-start(bf16[160,256]{1,0:T(8,128)(2,1)S(1)} %pad_maximum_fusion.2), channel_id=1, source_target_pairs={{0,12},{2,14},{4,0},{6,2},{8,4},{10,6},{12,8},{14,10},{1,13},{3,15... | collective-permute-start | bytes 245768 | tf_op jit(solution)/shard_map/ppermute | solution.py:445
  133.9 3.3 %collective-permute-start.17 = (bf16[320,256]{1,0:T(8,128)(2,1)S(1)}, bf16[320,256]{1,0:T(8,128)(2,1)S(1)}, u32[]{:S(2)}, u32[]{:S(2)}) collective-permute-start(bf16[320,256]{1,0:T(8,128)(2,1)S(1)} %constant_dynamic-update-slice_fusion.3.refs_1_), channel_id=1, source_target_pairs={{0,1},{1,0},{2,3},{3,2},{4,5},{5,4},{6,7},{7,6},{8,9},{9,8},{10,11... | collective-permute-start | bytes 491528 | tf_op jit(solution)/shard_map/ppermute | solution.py:440
  146.4 2.2 %collective-permute-start.20 = (bf16[1280,256]{1,0:T(8,128)(2,1)S(1)}, bf16[1280,256]{1,0:T(8,128)(2,1)S(1)}, u32[]{:S(2)}, u32[]{:S(2)}) collective-permute-start(bf16[1280,256]{1,0:T(8,128)(2,1)S(1)} %get-tuple-element.119), channel_id=1, source_target_pairs={{0,1},{1,0},{2,3},{3,2},{4,5},{5,4},{6,7},{7,6},{8,9},{9,8},{10,11... | collective-permute-start | bytes 1966088 | tf_op jit(solution)/shard_map/ppermute | solution.py:440
  148.5 4.8 %collective-permute-start.21 = (bf16[1280,256]{1,0:T(8,128)(2,1)S(1)}, bf16[1280,256]{1,0:T(8,128)(2,1)S(1)}, u32[]{:S(2)}, u32[]{:S(2)}) collective-permute-start(bf16[1280,256]{1,0:T(8,128)(2,1)S(1)} %get-tuple-element.122), channel_id=1, source_target_pairs={{0,1},{1,0},{2,3},{3,2},{4,5},{5,4},{6,7},{7,6},{8,9},{9,8},{10,11... | collective-permute-start | bytes 1966088 | tf_op jit(solution)/shard_map/ppermute | solution.py:440
  153.1 3.3 %collective-permute-start.23 = (bf16[1280,512]{1,0:T(8,128)(2,1)S(1)}, bf16[1280,512]{1,0:T(8,128)(2,1)S(1)}, u32[]{:S(2)}, u32[]{:S(2)}) collective-permute-start(bf16[1280,512]{1,0:T(8,128)(2,1)S(1)} %get-tuple-element.127), channel_id=1, source_target_pairs={{0,1},{1,0},{2,3},{3,2},{4,5},{5,4},{6,7},{7,6},{8,9},{9,8},{10,11... | collective-permute-start | bytes 3932168 | tf_op jit(solution)/shard_map/ppermute | solution.py:440
  156.0 3.3 %collective-permute-start.22 = (bf16[640,512]{1,0:T(8,128)(2,1)S(1)}, bf16[640,512]{1,0:T(8,128)(2,1)S(1)}, u32[]{:S(2)}, u32[]{:S(2)}) collective-permute-start(bf16[640,512]{1,0:T(8,128)(2,1)S(1)} %get-tuple-element.126), channel_id=1, source_target_pairs={{0,1},{1,0},{2,3},{3,2},{4,5},{5,4},{6,7},{7,6},{8,9},{9,8},{10,11... | collective-permute-start | bytes 1966088 | tf_op jit(solution)/shard_map/ppermute | solution.py:440
  159.0 2.2 %collective-permute-start.24 = (bf16[640,512]{1,0:T(8,128)(2,1)S(1)}, bf16[640,512]{1,0:T(8,128)(2,1)S(1)}, u32[]{:S(2)}, u32[]{:S(2)}) collective-permute-start(bf16[640,512]{1,0:T(8,128)(2,1)S(1)} %get-tuple-element.129), channel_id=1, source_target_pairs={{0,1},{1,0},{2,3},{3,2},{4,5},{5,4},{6,7},{7,6},{8,9},{9,8},{10,11... | collective-permute-start | bytes 1966088 | tf_op jit(solution)/shard_map/ppermute | solution.py:440

commit v7 on v6

--- a/solution.py
+++ b/solution.py
@@ -525,9 +525,7 @@
     recv = swap_feat(send)
     got = fetch(first_rows, 1)
     send_1, keep_1 = aggregate_call(feat, links, staged, coarse, degree, table, last_span)
-    recv, keep, send_1, got = barrier((recv, keep, send_1, got))
-    held = jnp.concatenate([first_rows, got], axis=0)
-    got = fetch(held, strides[0])
+    recv, keep, send_1 = barrier((recv, keep, send_1))
     inputs = [(keep, recv), (keep_1, swap_feat(send_1))]
     local = []
     local_places = []
@@ -539,7 +537,6 @@
         state, own, other = node_call("mid", 0, feat, state, at, 0, rows, *inputs[chunk], weights)
         if chunk == 0:
             own, other, got = barrier((own, other, got))
-            held = jnp.concatenate([held, got], axis=0)
         sibling = swap_feat(other)
         if chunk == 0:
             sibling, state = barrier((sibling, state))
@@ -557,9 +554,9 @@
 
     early = len(halo) - 2
     table = local_call(feat, local_places + halo_places[:early], local + halo[:early], table)
+    held = jnp.concatenate([first_rows, got], axis=0)
     held, table = barrier((held, table))
-    for stride in strides[1:]:
-        held = jnp.concatenate([held, fetch(held, stride)], axis=0)
+    held = jnp.concatenate([held] + [fetch(held, offset) for offset in evens[1:]], axis=0)
     (coarse,) = node_call(
         "coarse", 0, feat, coarse_state, 0, 0, held.shape[0], held, swap_feat(held), weights
     )

time: 163 us -> 161 us (0.988)
  waiting for transfers between devices: 76.8 us -> 69.5 us
  starting transfers between devices: 37.6 us -> 42 us
    ppermute x13, starting transfers between devices: 10.5 us -> 16.1 us  [swap_feat(): return lax.ppermute(array, 'feat', [(0, 1), (1, 0)])]
    ppermute x2, waiting for transfers between devices: 4.68 us -> 0.01 us  [shards(): lax.ppermute(other, ('patch', 'feat'), other_patch)]
    ppermute x2, starting transfers between devices: 7.63 us -> 4.28 us  [shards(): lax.ppermute(other, ('patch', 'feat'), other_patch)]
    ppermute x2, waiting for transfers between devices: 30.2 us -> 28.5 us  [shards(): lax.ppermute(own, ('patch', 'feat'), own_patch)]
    ppermute x6 -> x7, starting transfers between devices: 8.74 us -> 9.41 us  [fetch(): lax.ppermute(held, 'patch', [(pos, (pos - stride) % count) for pos in ran...]
    ppermute x6 -> x7, waiting for transfers between devices: 33.3 us -> 32.7 us  [fetch(): lax.ppermute(held, 'patch', [(pos, (pos - stride) % count) for pos in ran...]
  transfers between devices with their start and end apart: 25 -> 26, of which waited for: 10 -> 11; matrix products, arithmetic and copies ran while one was open for 0% -> 0% of each run, Pallas kernels for 25% -> 25%
where the time goes in v7:
time: 161 us; the launch traced here: 159 us
  waiting for transfers between devices  69.5 us (43%)
  Pallas kernels  46 us (29%)
  starting transfers between devices  42 us (26%)
    ppermute x7, waiting for transfers between devices, fetch(): lax.ppermute(held, 'patch', [(pos, (pos - stride) % count) for pos in ran...  32.7 us
    ppermute x2, waiting for transfers between devices, shards(): lax.ppermute(own, ('patch', 'feat'), own_patch)  28.5 us
    pallas_call x6, Pallas kernels, node_call(): pl.pallas_call(functools.partial(node_kernel, mode, layer, start, offset,...  19.9 us
    ppermute x13, starting transfers between devices, swap_feat(): return lax.ppermute(array, 'feat', [(0, 1), (1, 0)])  16.1 us
    ppermute x7, starting transfers between devices, fetch(): lax.ppermute(held, 'patch', [(pos, (pos - stride) % count) for pos in ran...  9.41 us
    pallas_call x4, Pallas kernels, aggregate_call(): pl.pallas_call(functools.partial(aggregate_kernel, places, start), grid_s...  8.54 us
    pallas_call x2, Pallas kernels, message_call(): pl.pallas_call(functools.partial(message_kernel, start, tile), in_specs=[...  8.26 us
    ppermute x2, starting transfers between devices, shards(): lax.ppermute(message, 'patch', backward if first < half else forward)  6.31 us
  transfers between devices with their start and end apart: 26, of which 11 were waited for; matrix products, arithmetic and copies ran while one was open for 0% of the time, Pallas kernels for 25%

profile of v7, /device:TPU:9, one launch (start us, length us, event | category | flops | bytes accessed | tf_op | source)
XLA Modules:
  0.0 159.4 jit_solution(17895000826100449993)
XLA Ops:
  0.0 0.8 slice.3
  0.8 1.1 collective-permute-start
  1.9 4.1 %message.3.refs_4_ = bf16[2560,256]{1,0:T(8,128)(2,1)} custom-call(bf16[5120,512]{1,0:T(8,128)(2,1)} %refs_2_.1, bf16[2,512,256]{2,1,0:T(8,128)(2,1)} %refs_7_), custom_call_target="tpu_custom_call" | custom-call | flops 1048576 | bytes 1024 | tf_op jit(solution)/shard_map/message/pallas_call | solution.py:95
  6.0 0.0 copy-start
  6.0 0.0 copy-start.2
  6.1 0.0 copy-start.3
  6.1 0.0 copy-start.1
  6.1 2.4 %collective-permute-start.7 = (bf16[2560,256]{1,0:T(8,128)(2,1)}, bf16[2560,256]{1,0:T(8,128)(2,1)S(1)}, u32[]{:S(2)}, u32[]{:S(2)}) collective-permute-start(bf16[2560,256]{1,0:T(8,128)(2,1)} %message.3.refs_4_), channel_id=1, source_target_pairs={{0,2},{2,4},{4,6},{6,8},{8,10},{10,12},{12,14},{1,3},{3,5},{5,7},{... | collective-permute-start | bytes 3932168 | tf_op jit(solution)/shard_map/ppermute | solution.py:488
  8.5 4.1 %message.2.refs_3_ = bf16[2560,256]{1,0:T(8,128)(2,1)} custom-call(bf16[5120,512]{1,0:T(8,128)(2,1)} %refs_2_.1, bf16[2,512,256]{2,1,0:T(8,128)(2,1)} %refs_7_), custom_call_target="tpu_custom_call" | custom-call | flops 1048576 | bytes 1024 | tf_op jit(solution)/shard_map/message/pallas_call | solution.py:95
  12.6 3.9 %collective-permute-start.6 = (bf16[2560,256]{1,0:T(8,128)(2,1)}, bf16[2560,256]{1,0:T(8,128)(2,1)S(1)}, u32[]{:S(2)}, u32[]{:S(2)}) collective-permute-start(bf16[2560,256]{1,0:T(8,128)(2,1)} %message.2.refs_3_), channel_id=1, source_target_pairs={{2,0},{4,2},{6,4},{8,6},{10,8},{12,10},{14,12},{3,1},{5,3},{7,5},{... | collective-permute-start | bytes 3932168 | tf_op jit(solution)/shard_map/ppermute | solution.py:488
  16.6 1.6 collective-permute-start.3
  18.2 2.3 %collective-permute-start.1 = (bf16[80,512]{1,0:T(8,128)(2,1)S(1)}, bf16[80,512]{1,0:T(8,128)(2,1)S(1)}, u32[]{:S(2)}, u32[]{:S(2)}) collective-permute-start(bf16[80,512]{1,0:T(8,128)(2,1)S(1)} %pad_maximum_fusion.1), channel_id=1, source_target_pairs={{0,8},{2,10},{4,12},{6,14},{8,0},{10,2},{12,4},{14,6},{1,9},{3,11}... | collective-permute-start | bytes 245768 | tf_op jit(solution)/shard_map/ppermute | solution.py:445
  20.5 0.3 collective-permute-start.4
  20.8 27.4 %collective-permute-done.1 = bf16[80,512]{1,0:T(8,128)(2,1)S(1)} collective-permute-done((bf16[80,512]{1,0:T(8,128)(2,1)S(1)}, bf16[80,512]{1,0:T(8,128)(2,1)S(1)}, u32[]{:S(2)}, u32[]{:S(2)}) %collective-permute-start.1) | collective-permute-done | bytes 81952 | tf_op jit(solution)/shard_map/ppermute | solution.py:445
  48.2 2.5 %collective-permute-start.5 = (bf16[2,512,256]{2,1,0:T(8,128)(2,1)}, bf16[2,512,256]{2,1,0:T(8,128)(2,1)}, u32[]{:S(2)}, u32[]{:S(2)}) collective-permute-start(bf16[2,512,256]{2,1,0:T(8,128)(2,1)} %refs_7_), channel_id=1, source_target_pairs={{0,1},{1,0},{2,3},{3,2},{4,5},{5,4},{6,7},{7,6},{8,9},{9,8},{10,11... | collective-permute-start | bytes 1572872 | tf_op jit(solution)/shard_map/ppermute | solution.py:440
  50.7 0.1 copy.18
  50.8 0.1 mul.15
  50.9 0.1 copy.19
  51.0 0.1 reshape.52
  51.1 0.1 pad_add_fusion.links
  51.2 5.0 %stage.1 = (bf16[40,128,512]{2,1,0:T(8,128)(2,1)S(1)}, bf16[40,128,160]{2,1,0:T(8,128)(2,1)S(1)}, bf16[2560,512]{1,0:T(8,128)(2,1)S(1)}, bf16[10240,256]{1,0:T(8...) custom-call(s32[1]{0:T(128)} %bitcast.feat_ref, ...), custom_call_target="tpu_custom_call" | custom-call | flops 1048576 | bytes 1024 | tf_op jit(solution)/shard_map/stage/pallas_call | solution.py:166
  56.2 1.9 %collective-permute-start.2 = (bf16[160,512]{1,0:T(8,128)(2,1)S(1)}, bf16[160,512]{1,0:T(8,128)(2,1)S(1)}, u32[]{:S(2)}, u32[]{:S(2)}) collective-permute-start(bf16[160,512]{1,0:T(8,128)(2,1)S(1)} %pad_maximum_fusion), channel_id=1, source_target_pairs={{0,12},{2,14},{4,0},{6,2},{8,4},{10,6},{12,8},{14,10},{1,13},{3,15... | collective-permute-start | bytes 491528 | tf_op jit(solution)/shard_map/ppermute | solution.py:445
  58.2 1.5 weights.1
  59.7 2.4 %collective-permute-done.2 = bf16[160,512]{1,0:T(8,128)(2,1)S(1)} collective-permute-done((bf16[160,512]{1,0:T(8,128)(2,1)S(1)}, bf16[160,512]{1,0:T(8,128)(2,1)S(1)}, u32[]{:S(2)}, u32[]{:S(2)}) %collective-permute-start.2) | collective-permute-done | bytes 163872 | tf_op jit(solution)/shard_map/ppermute | solution.py:445
  62.1 0.5 coarse_message.1.refs_2_
  62.6 1.4 collective-permute-done.7.refs_5_
  64.0 4.0 %collective-permute-done.6.refs_4_ = bf16[2560,256]{1,0:T(8,128)(2,1)S(1)} collective-permute-done((bf16[2560,256]{1,0:T(8,128)(2,1)}, bf16[2560,256]{1,0:T(8,128)(2,1)S(1)}, u32[]{:S(2)}, u32[]{:S(2)}) %collective-permute-start.6) | collective-permute-done | bytes 1310752 | tf_op jit(solution)/shard_map/ppermute | solution.py:488
  68.0 2.0 %aggregate.4 = (bf16[1280,256]{1,0:T(8,128)(2,1)S(1)}, bf16[1280,256]{1,0:T(8,128)(2,1)S(1)}, bf16[40,256]{1,0:T(8,128)(2,1)S(1)}, bf16[10240,256]{1,0:T(8,128)(2,1)S(1)}) custom-call(s32[1]{0:T(128)} %bitcast.feat_ref, s32[320]{0:T(512)S(1)} %pad_add_fusion.links, ...), custom_call_target="tpu_custom_call", output_to_operand_aliasing={{3}: (8, {})} | custom-call | flops 1048576 | bytes 1024 | tf_op jit(solution)/shard_map/aggregate/pallas_call | solution.py:287
  70.0 0.6 collective-permute-start.8
  70.6 1.5 collective-permute-start.9
  72.1 1.8 %aggregate.5 = (bf16[1280,256]{1,0:T(8,128)(2,1)S(1)}, bf16[1280,256]{1,0:T(8,128)(2,1)S(1)}) custom-call(s32[1]{0:T(128)} %bitcast.feat_ref, s32[320]{0:T(512)S(1)} %pad_add_fusion.links, bf16[40,128,512]{2,1,0:T(8,128)(2,1)S(1)} %get-tuple-element.78.refs_0_, bf16[40,128,160]{2,1,0:T(8,128)(2,1)S(1)} %get-tuple-element.79.refs_1_, ...), custom_call_target="tpu_custom_call" | custom-call | flops 1048576 | bytes 1024 | tf_op jit(solution)/shard_map/aggregate/pallas_call | solution.py:287
  74.0 4.4 %node_mid.2 = (bf16[2560,512]{1,0:T(8,128)(2,1)S(1)}, bf16[1280,256]{1,0:T(8,128)(2,1)S(1)}, bf16[1280,256]{1,0:T(8,128)(2,1)S(1)}) custom-call(s32[1]{0:T(128)} %bitcast.feat_ref, bf16[2560,512]{1,0:T(8,128)(2,1)S(1)} %get-tuple-element.71.refs_0_, bf16[1280,256]{1,0:T(8,128)(2,1)S(1)} %get-tuple-element.92.refs_1_, ...), custom_call_target="tpu_custom_call", output_to_operand_aliasing={{0}: (1, {})} | custom-call | flops 1048576 | bytes 1024 | tf_op jit(solution)/shard_map/node_mid/pallas_call | solution.py:398
  78.4 0.6 collective-permute-start.10
  79.0 0.1 collective-permute-start.11
  79.1 2.1 %collective-permute-start.14 = (bf16[1280,256]{1,0:T(8,128)(2,1)S(1)}, bf16[1280,256]{1,0:T(8,128)(2,1)S(1)}, u32[]{:S(2)}, u32[]{:S(2)}) collective-permute-start(bf16[1280,256]{1,0:T(8,128)(2,1)S(1)} %get-tuple-element.102), channel_id=1, source_target_pairs={{2,1},{4,3},{6,5},{8,7},{10,9},{12,11},{14,13},{1,2},{3,4},{5,6},{... | collective-permute-start | bytes 1966088 | tf_op jit(solution)/shard_map/ppermute | solution.py:543
  81.2 2.7 %collective-permute-start.13 = (bf16[1280,256]{1,0:T(8,128)(2,1)S(1)}, bf16[1280,256]{1,0:T(8,128)(2,1)S(1)}, u32[]{:S(2)}, u32[]{:S(2)}) collective-permute-start(bf16[1280,256]{1,0:T(8,128)(2,1)S(1)} %get-tuple-element.109.refs_0_), channel_id=1, source_target_pairs={{2,0},{4,2},{6,4},{8,6},{10,8},{12,10},{14,12},{1,3},{3,5},{5,7},{... | collective-permute-start | bytes 1966088 | tf_op jit(solution)/shard_map/ppermute | solution.py:543
  83.9 4.4 %node_mid.3 = (bf16[2560,512]{1,0:T(8,128)(2,1)S(1)}, bf16[1280,256]{1,0:T(8,128)(2,1)S(1)}, bf16[1280,256]{1,0:T(8,128)(2,1)S(1)}) custom-call(s32[1]{0:T(128)} %bitcast.feat_ref, bf16[2560,512]{1,0:T(8,128)(2,1)S(1)} %get-tuple-element.104.refs_0_, bf16[1280,256]{1,0:T(8,128)(2,1)S(1)} %get-tuple-element.105.refs_1_, ...), custom_call_target="tpu_custom_call", output_to_operand_aliasing={{0}: (1, {})} | custom-call | flops 1048576 | bytes 1024 | tf_op jit(solution)/shard_map/node_mid/pallas_call | solution.py:398
  88.4 2.0 %collective-permute-start.12 = (bf16[1280,256]{1,0:T(8,128)(2,1)S(1)}, bf16[1280,256]{1,0:T(8,128)(2,1)S(1)}, u32[]{:S(2)}, u32[]{:S(2)}) collective-permute-start(bf16[1280,256]{1,0:T(8,128)(2,1)S(1)} %get-tuple-element.112), channel_id=1, source_target_pairs={{0,1},{1,0},{2,3},{3,2},{4,5},{5,4},{6,7},{7,6},{8,9},{9,8},{10,11... | collective-permute-start | bytes 1966088 | tf_op jit(solution)/shard_map/ppermute | solution.py:440
  90.3 2.1 %collective-permute-start.20 = (bf16[1280,256]{1,0:T(8,128)(2,1)S(1)}, bf16[1280,256]{1,0:T(8,128)(2,1)S(1)}, u32[]{:S(2)}, u32[]{:S(2)}) collective-permute-start(bf16[1280,256]{1,0:T(8,128)(2,1)S(1)} %get-tuple-element.112), channel_id=1, source_target_pairs={{2,1},{4,3},{6,5},{8,7},{10,9},{12,11},{14,13},{1,2},{3,4},{5,6},{... | collective-permute-start | bytes 1966088 | tf_op jit(solution)/shard_map/ppermute | solution.py:543
  92.4 3.2 %collective-permute-start.19 = (bf16[1280,256]{1,0:T(8,128)(2,1)S(1)}, bf16[1280,256]{1,0:T(8,128)(2,1)S(1)}, u32[]{:S(2)}, u32[]{:S(2)}) collective-permute-start(bf16[1280,256]{1,0:T(8,128)(2,1)S(1)} %get-tuple-element.111.refs_2_), channel_id=1, source_target_pairs={{2,0},{4,2},{6,4},{8,6},{10,8},{12,10},{14,12},{1,3},{3,5},{5,7},{... | collective-permute-start | bytes 1966088 | tf_op jit(solution)/shard_map/ppermute | solution.py:543
  95.7 28.2 %collective-permute-done.13.refs_4_ = bf16[1280,256]{1,0:T(8,128)(2,1)S(1)} collective-permute-done((bf16[1280,256]{1,0:T(8,128)(2,1)S(1)}, bf16[1280,256]{1,0:T(8,128)(2,1)S(1)}, u32[]{:S(2)}, u32[]{:S(2)}) %collective-permute-start.13) | collective-permute-done | bytes 655392 | tf_op jit(solution)/shard_map/ppermute | solution.py:543
  123.9 1.3 local_messages.1.refs_6_
  125.2 0.1 collective-permute-start.15
  125.3 2.5 %collective-permute-start.16 = (bf16[80,256]{1,0:T(8,128)(2,1)S(1)}, bf16[80,256]{1,0:T(8,128)(2,1)S(1)}, u32[]{:S(2)}, u32[]{:S(2)}) collective-permute-start(bf16[80,256]{1,0:T(8,128)(2,1)S(1)} %pad_maximum_fusion.2), channel_id=1, source_target_pairs={{0,12},{2,14},{4,0},{6,2},{8,4},{10,6},{12,8},{14,10},{1,13},{3,15... | collective-permute-start | bytes 122888 | tf_op jit(solution)/shard_map/ppermute | solution.py:445
  127.7 0.0 collective-permute-start.17
  127.7 1.4 collective-permute-done.15
  129.1 0.8 collective-permute-done.16
  129.8 0.8 collective-permute-done.17
  130.7 4.3 %collective-permute-start.18 = (bf16[320,256]{1,0:T(8,128)(2,1)S(1)}, bf16[320,256]{1,0:T(8,128)(2,1)S(1)}, u32[]{:S(2)}, u32[]{:S(2)}) collective-permute-start(bf16[320,256]{1,0:T(8,128)(2,1)S(1)} %constant_dynamic-update-slice_fusion.3.refs_1_), channel_id=1, source_target_pairs={{0,1},{1,0},{2,3},{3,2},{4,5},{5,4},{6,7},{7,6},{8,9},{9,8},{10,11... | collective-permute-start | bytes 491528 | tf_op jit(solution)/shard_map/ppermute | solution.py:440
  135.0 1.0 collective-permute-done.18.refs_2_
  136.0 1.6 %node_coarse.1.refs_2_ = f32[320,256]{1,0:T(8,128)S(1)} custom-call(s32[1]{0:T(128)} %bitcast.feat_ref, bf16[320,512]{1,0:T(8,128)(2,1)S(1)} %constant_dynamic-update-slice_fusion.state_ref.refs_0_, bf16[320,256]{1,0:T(8,128)(2,1)S(1)} %constant_dynamic-update-slice_fusion.3.refs_1_, bf16[320,256]{1,0:T(8,128)(2,1)S(1)} %collective-permute-done.18.refs_2_, ...), custom_call_target="tpu_custom_call" | custom-call | flops 1048576 | bytes 1024 | tf_op jit(solution)/shard_map/node_coarse/pallas_call | solution.py:398
  137.6 0.3 collective-permute-done.19.refs_4_
  137.9 2.9 %aggregate.6 = (bf16[1280,256]{1,0:T(8,128)(2,1)S(1)}, bf16[1280,256]{1,0:T(8,128)(2,1)S(1)}, bf16[40,256]{1,0:T(8,128)(2,1)}, bf16[10240,256]{1,0:T(8,128)(2,1)S(1)}) custom-call(s32[1]{0:T(128)} %bitcast.feat_ref, s32[320]{0:T(512)S(1)} %pad_add_fusion.links, bf16[40,128,512]{2,1,0:T(8,128)(2,1)S(1)} %get-tuple-element.78.refs_0_, ...), custom_call_target="tpu_custom_call", output_to_operand_aliasing={{3}: (8, {})} | custom-call | flops 1048576 | bytes 1024 | tf_op jit(solution)/shard_map/aggregate/pallas_call | solution.py:287
  140.8 3.0 %collective-permute-start.21 = (bf16[1280,256]{1,0:T(8,128)(2,1)S(1)}, bf16[1280,256]{1,0:T(8,128)(2,1)S(1)}, u32[]{:S(2)}, u32[]{:S(2)}) collective-permute-start(bf16[1280,256]{1,0:T(8,128)(2,1)S(1)} %get-tuple-element.117), channel_id=1, source_target_pairs={{0,1},{1,0},{2,3},{3,2},{4,5},{5,4},{6,7},{7,6},{8,9},{9,8},{10,11... | collective-permute-start | bytes 1966088 | tf_op jit(solution)/shard_map/ppermute | solution.py:440
  143.8 1.8 %aggregate.7 = (bf16[1280,256]{1,0:T(8,128)(2,1)S(1)}, bf16[1280,256]{1,0:T(8,128)(2,1)S(1)}) custom-call(s32[1]{0:T(128)} %bitcast.feat_ref, s32[320]{0:T(512)S(1)} %pad_add_fusion.links, bf16[40,128,512]{2,1,0:T(8,128)(2,1)S(1)} %get-tuple-element.78.refs_0_, bf16[40,128,160]{2,1,0:T(8,128)(2,1)S(1)} %get-tuple-element.79.refs_1_, ...), custom_call_target="tpu_custom_call" | custom-call | flops 1048576 | bytes 1024 | tf_op jit(solution)/shard_map/aggregate/pallas_call | solution.py:287
  145.6 0.2 collective-permute-start.22
  145.8 4.2 %node_last.3 = (bf16[1280,512]{1,0:T(8,128)(2,1)S(1)}, bf16[5120,512]{1,0:T(8,128)(2,1)}) custom-call(s32[1]{0:T(128)} %bitcast.feat_ref, bf16[2560,512]{1,0:T(8,128)(2,1)S(1)} %get-tuple-element.107.refs_0_, bf16[1280,256]{1,0:T(8,128)(2,1)S(1)} %get-tuple-element.121.refs_1_, bf16[1280,256]{1,0:T(8,128)(2,1)S(1)} %collective-permute-done.21.refs_2_, ...), custom_call_target="tpu_custom_call" | custom-call | flops 8589934592 | bytes 1024 | tf_op jit(solution)/shard_map/node_last/pallas_call | solution.py:398
  150.1 0.4 collective-permute-start.24
  150.5 2.6 %node_last.4 = (bf16[640,512]{1,0:T(8,128)(2,1)S(1)}, bf16[5120,512]{1,0:T(8,128)(2,1)}) custom-call(s32[1]{0:T(128)} %bitcast.feat_ref, bf16[2560,512]{1,0:T(8,128)(2,1)S(1)} %get-tuple-element.107.refs_0_, bf16[1280,256]{1,0:T(8,128)(2,1)S(1)} %get-tuple-element.116.refs_1_, ...), custom_call_target="tpu_custom_call", output_to_operand_aliasing={{1}: (8, {})} | custom-call | flops 8589934592 | bytes 1024 | tf_op jit(solution)/shard_map/node_last/pallas_call | solution.py:398
  153.1 0.3 collective-permute-start.23
  153.3 2.6 %node_last.5 = (bf16[640,512]{1,0:T(8,128)(2,1)S(1)}, bf16[5120,512]{1,0:T(8,128)(2,1)}) custom-call(s32[1]{0:T(128)} %bitcast.feat_ref, bf16[2560,512]{1,0:T(8,128)(2,1)S(1)} %get-tuple-element.107.refs_0_, bf16[1280,256]{1,0:T(8,128)(2,1)S(1)} %get-tuple-element.116.refs_1_, ...), custom_call_target="tpu_custom_call", output_to_operand_aliasing={{1}: (9, {})} | custom-call | flops 8589934592 | bytes 1024 | tf_op jit(solution)/shard_map/node_last/pallas_call | solution.py:398
  156.0 0.4 collective-permute-start.25
  156.3 1.8 %collective-permute-done.25.refs_1_ = bf16[640,512]{1,0:T(8,128)(2,1)S(1)} collective-permute-done((bf16[640,512]{1,0:T(8,128)(2,1)S(1)}, bf16[640,512]{1,0:T(8,128)(2,1)S(1)}, u32[]{:S(2)}, u32[]{:S(2)}) %collective-permute-start.25) | collective-permute-done | bytes 655392 | tf_op jit(solution)/shard_map/ppermute | solution.py:440
  158.1 1.1 assemble.1
  (31 shorter events, 0.1 us)
Async XLA Ops:
  0.8 11.8 %collective-permute-start = (bf16[40,512]{1,0:T(8,128)(2,1)S(1)}, bf16[40,512]{1,0:T(8,128)(2,1)S(1)}, u32[]{:S(2)}, u32[]{:S(2)}) collective-permute-start(bf16[40,512]{1,0:T(8,128)(2,1)S(1)} %slice.3), channel_id=1, source_target_pairs={{0,14},{2,0},{4,2},{6,4},{8,6},{10,8},{12,10},{14,12},{1,15},{3,1}... | collective-permute-start | bytes 122888 | tf_op jit(solution)/shard_map/ppermute | solution.py:445
  6.0 14.5 %copy-start = (bf16[2,256,512]{2,1,0:T(8,128)(2,1)S(1)}, bf16[2,256,512]{2,1,0:T(8,128)(2,1)}, u32[]{:S(2)}) copy-start(bf16[2,256,512]{2,1,0:T(8,128)(2,1)} %refs_6_) | copy-start | bytes 1572868
  6.0 44.7 %copy-start.2 = (s32[40,4]{0,1:T(4,128)S(1)}, s32[40,4]{0,1:T(4,128)}, u32[]{:S(2)}) copy-start(s32[40,4]{0,1:T(4,128)} %param.13) | copy-start | bytes 1924
  6.1 44.7 %copy-start.3 = (s32[40,4]{0,1:T(4,128)S(1)}, s32[40,4]{0,1:T(4,128)}, u32[]{:S(2)}) copy-start(s32[40,4]{0,1:T(4,128)} %param.12) | copy-start | bytes 1924
  6.1 45.1 %copy-start.1 = (s32[5120]{0:T(1024)S(1)}, s32[5120]{0:T(1024)}, u32[]{:S(2)}) copy-start(s32[5120]{0:T(1024)} %param.14) | copy-start | bytes 61444
  6.1 57.9 %collective-permute-start.7 = (bf16[2560,256]{1,0:T(8,128)(2,1)}, bf16[2560,256]{1,0:T(8,128)(2,1)S(1)}, u32[]{:S(2)}, u32[]{:S(2)}) collective-permute-start(bf16[2560,256]{1,0:T(8,128)(2,1)} %message.3.refs_4_), channel_id=1, source_target_pairs={{0,2},{2,4},{4,6},{6,8},{8,10},{10,12},{12,14},{1,3},{3,5},{5,7},{... | collective-permute-start | bytes 3932168 | tf_op jit(solution)/shard_map/ppermute | solution.py:488
  12.6 55.4 %collective-permute-start.6 = (bf16[2560,256]{1,0:T(8,128)(2,1)}, bf16[2560,256]{1,0:T(8,128)(2,1)S(1)}, u32[]{:S(2)}, u32[]{:S(2)}) collective-permute-start(bf16[2560,256]{1,0:T(8,128)(2,1)} %message.2.refs_3_), channel_id=1, source_target_pairs={{2,0},{4,2},{6,4},{8,6},{10,8},{12,10},{14,12},{3,1},{5,3},{7,5},{... | collective-permute-start | bytes 3932168 | tf_op jit(solution)/shard_map/ppermute | solution.py:488
  16.6 41.6 %collective-permute-start.3 = (bf16[2,1024,256]{2,1,0:T(8,128)(2,1)}, bf16[2,1024,256]{2,1,0:T(8,128)(2,1)}, u32[]{:S(2)}, u32[]{:S(2)}) collective-permute-start(bf16[2,1024,256]{2,1,0:T(8,128)(2,1)} %refs_5_), channel_id=1, source_target_pairs={{0,1},{1,0},{2,3},{3,2},{4,5},{5,4},{6,7},{7,6},{8,9},{9,8},{10,11... | collective-permute-start | bytes 3145736 | tf_op jit(solution)/shard_map/ppermute | solution.py:440
  18.2 30.0 %collective-permute-start.1 = (bf16[80,512]{1,0:T(8,128)(2,1)S(1)}, bf16[80,512]{1,0:T(8,128)(2,1)S(1)}, u32[]{:S(2)}, u32[]{:S(2)}) collective-permute-start(bf16[80,512]{1,0:T(8,128)(2,1)S(1)} %pad_maximum_fusion.1), channel_id=1, source_target_pairs={{0,8},{2,10},{4,12},{6,14},{8,0},{10,2},{12,4},{14,6},{1,9},{3,11}... | collective-permute-start | bytes 245768 | tf_op jit(solution)/shard_map/ppermute | solution.py:445
  20.5 35.7 %collective-permute-start.4 = (bf16[2,256,512]{2,1,0:T(8,128)(2,1)S(1)}, bf16[2,256,512]{2,1,0:T(8,128)(2,1)}, u32[]{:S(2)}, u32[]{:S(2)}) collective-permute-start(bf16[2,256,512]{2,1,0:T(8,128)(2,1)S(1)} %copy-done), channel_id=1, source_target_pairs={{0,1},{1,0},{2,3},{3,2},{4,5},{5,4},{6,7},{7,6},{8,9},{9,8},{10,11... | collective-permute-start | bytes 1572872 | tf_op jit(solution)/shard_map/ppermute | solution.py:440
  48.2 9.9 %collective-permute-start.5 = (bf16[2,512,256]{2,1,0:T(8,128)(2,1)}, bf16[2,512,256]{2,1,0:T(8,128)(2,1)}, u32[]{:S(2)}, u32[]{:S(2)}) collective-permute-start(bf16[2,512,256]{2,1,0:T(8,128)(2,1)} %refs_7_), channel_id=1, source_target_pairs={{0,1},{1,0},{2,3},{3,2},{4,5},{5,4},{6,7},{7,6},{8,9},{9,8},{10,11... | collective-permute-start | bytes 1572872 | tf_op jit(solution)/shard_map/ppermute | solution.py:440
  56.2 5.9 %collective-permute-start.2 = (bf16[160,512]{1,0:T(8,128)(2,1)S(1)}, bf16[160,512]{1,0:T(8,128)(2,1)S(1)}, u32[]{:S(2)}, u32[]{:S(2)}) collective-permute-start(bf16[160,512]{1,0:T(8,128)(2,1)S(1)} %pad_maximum_fusion), channel_id=1, source_target_pairs={{0,12},{2,14},{4,0},{6,2},{8,4},{10,6},{12,8},{14,10},{1,13},{3,15... | collective-permute-start | bytes 491528 | tf_op jit(solution)/shard_map/ppermute | solution.py:445
  70.0 3.9 %collective-permute-start.8 = (bf16[1280,256]{1,0:T(8,128)(2,1)S(1)}, bf16[1280,256]{1,0:T(8,128)(2,1)S(1)}, u32[]{:S(2)}, u32[]{:S(2)}) collective-permute-start(bf16[1280,256]{1,0:T(8,128)(2,1)S(1)} %get-tuple-element.88), channel_id=1, source_target_pairs={{0,1},{1,0},{2,3},{3,2},{4,5},{5,4},{6,7},{7,6},{8,9},{9,8},{10,11... | collective-permute-start | bytes 1966088 | tf_op jit(solution)/shard_map/ppermute | solution.py:440
  70.6 7.8 %collective-permute-start.9 = (bf16[40,256]{1,0:T(8,128)(2,1)S(1)}, bf16[40,256]{1,0:T(8,128)(2,1)S(1)}, u32[]{:S(2)}, u32[]{:S(2)}) collective-permute-start(bf16[40,256]{1,0:T(8,128)(2,1)S(1)} %get-tuple-element.101), channel_id=1, source_target_pairs={{0,14},{2,0},{4,2},{6,4},{8,6},{10,8},{12,10},{14,12},{1,15},{3,1}... | collective-permute-start | bytes 61448 | tf_op jit(solution)/shard_map/ppermute | solution.py:445
  78.4 5.5 %collective-permute-start.10 = (bf16[1280,256]{1,0:T(8,128)(2,1)S(1)}, bf16[1280,256]{1,0:T(8,128)(2,1)S(1)}, u32[]{:S(2)}, u32[]{:S(2)}) collective-permute-start(bf16[1280,256]{1,0:T(8,128)(2,1)S(1)} %get-tuple-element.102), channel_id=1, source_target_pairs={{0,1},{1,0},{2,3},{3,2},{4,5},{5,4},{6,7},{7,6},{8,9},{9,8},{10,11... | collective-permute-start | bytes 1966088 | tf_op jit(solution)/shard_map/ppermute | solution.py:440
  79.0 4.9 %collective-permute-start.11 = (bf16[1280,256]{1,0:T(8,128)(2,1)S(1)}, bf16[1280,256]{1,0:T(8,128)(2,1)S(1)}, u32[]{:S(2)}, u32[]{:S(2)}) collective-permute-start(bf16[1280,256]{1,0:T(8,128)(2,1)S(1)} %get-tuple-element.106), channel_id=1, source_target_pairs={{0,1},{1,0},{2,3},{3,2},{4,5},{5,4},{6,7},{7,6},{8,9},{9,8},{10,11... | collective-permute-start | bytes 1966088 | tf_op jit(solution)/shard_map/ppermute | solution.py:440
  79.1 44.8 %collective-permute-start.14 = (bf16[1280,256]{1,0:T(8,128)(2,1)S(1)}, bf16[1280,256]{1,0:T(8,128)(2,1)S(1)}, u32[]{:S(2)}, u32[]{:S(2)}) collective-permute-start(bf16[1280,256]{1,0:T(8,128)(2,1)S(1)} %get-tuple-element.102), channel_id=1, source_target_pairs={{2,1},{4,3},{6,5},{8,7},{10,9},{12,11},{14,13},{1,2},{3,4},{5,6},{... | collective-permute-start | bytes 1966088 | tf_op jit(solution)/shard_map/ppermute | solution.py:543
  81.2 42.6 %collective-permute-start.13 = (bf16[1280,256]{1,0:T(8,128)(2,1)S(1)}, bf16[1280,256]{1,0:T(8,128)(2,1)S(1)}, u32[]{:S(2)}, u32[]{:S(2)}) collective-permute-start(bf16[1280,256]{1,0:T(8,128)(2,1)S(1)} %get-tuple-element.109.refs_0_), channel_id=1, source_target_pairs={{2,0},{4,2},{6,4},{8,6},{10,8},{12,10},{14,12},{1,3},{3,5},{5,7},{... | collective-permute-start | bytes 1966088 | tf_op jit(solution)/shard_map/ppermute | solution.py:543
  88.4 35.5 %collective-permute-start.12 = (bf16[1280,256]{1,0:T(8,128)(2,1)S(1)}, bf16[1280,256]{1,0:T(8,128)(2,1)S(1)}, u32[]{:S(2)}, u32[]{:S(2)}) collective-permute-start(bf16[1280,256]{1,0:T(8,128)(2,1)S(1)} %get-tuple-element.112), channel_id=1, source_target_pairs={{0,1},{1,0},{2,3},{3,2},{4,5},{5,4},{6,7},{7,6},{8,9},{9,8},{10,11... | collective-permute-start | bytes 1966088 | tf_op jit(solution)/shard_map/ppermute | solution.py:440
  90.3 47.6 %collective-permute-start.20 = (bf16[1280,256]{1,0:T(8,128)(2,1)S(1)}, bf16[1280,256]{1,0:T(8,128)(2,1)S(1)}, u32[]{:S(2)}, u32[]{:S(2)}) collective-permute-start(bf16[1280,256]{1,0:T(8,128)(2,1)S(1)} %get-tuple-element.112), channel_id=1, source_target_pairs={{2,1},{4,3},{6,5},{8,7},{10,9},{12,11},{14,13},{1,2},{3,4},{5,6},{... | collective-permute-start | bytes 1966088 | tf_op jit(solution)/shard_map/ppermute | solution.py:543
  92.4 45.5 %collective-permute-start.19 = (bf16[1280,256]{1,0:T(8,128)(2,1)S(1)}, bf16[1280,256]{1,0:T(8,128)(2,1)S(1)}, u32[]{:S(2)}, u32[]{:S(2)}) collective-permute-start(bf16[1280,256]{1,0:T(8,128)(2,1)S(1)} %get-tuple-element.111.refs_2_), channel_id=1, source_target_pairs={{2,0},{4,2},{6,4},{8,6},{10,8},{12,10},{14,12},{1,3},{3,5},{5,7},{... | collective-permute-start | bytes 1966088 | tf_op jit(solution)/shard_map/ppermute | solution.py:543
  125.2 3.9 %collective-permute-start.15 = (bf16[80,256]{1,0:T(8,128)(2,1)S(1)}, bf16[80,256]{1,0:T(8,128)(2,1)S(1)}, u32[]{:S(2)}, u32[]{:S(2)}) collective-permute-start(bf16[80,256]{1,0:T(8,128)(2,1)S(1)} %pad_maximum_fusion.2), channel_id=1, source_target_pairs={{0,8},{2,10},{4,12},{6,14},{8,0},{10,2},{12,4},{14,6},{1,9},{3,11}... | collective-permute-start | bytes 122888 | tf_op jit(solution)/shard_map/ppermute | solution.py:445
  125.3 4.6 %collective-permute-start.16 = (bf16[80,256]{1,0:T(8,128)(2,1)S(1)}, bf16[80,256]{1,0:T(8,128)(2,1)S(1)}, u32[]{:S(2)}, u32[]{:S(2)}) collective-permute-start(bf16[80,256]{1,0:T(8,128)(2,1)S(1)} %pad_maximum_fusion.2), channel_id=1, source_target_pairs={{0,12},{2,14},{4,0},{6,2},{8,4},{10,6},{12,8},{14,10},{1,13},{3,15... | collective-permute-start | bytes 122888 | tf_op jit(solution)/shard_map/ppermute | solution.py:445
  127.7 3.0 %collective-permute-start.17 = (bf16[80,256]{1,0:T(8,128)(2,1)S(1)}, bf16[80,256]{1,0:T(8,128)(2,1)S(1)}, u32[]{:S(2)}, u32[]{:S(2)}) collective-permute-start(bf16[80,256]{1,0:T(8,128)(2,1)S(1)} %pad_maximum_fusion.2), channel_id=1, source_target_pairs={{0,4},{2,6},{4,8},{6,10},{8,12},{10,14},{12,0},{14,2},{1,5},{3,7},... | collective-permute-start | bytes 122888 | tf_op jit(solution)/shard_map/ppermute | solution.py:445
  130.7 5.3 %collective-permute-start.18 = (bf16[320,256]{1,0:T(8,128)(2,1)S(1)}, bf16[320,256]{1,0:T(8,128)(2,1)S(1)}, u32[]{:S(2)}, u32[]{:S(2)}) collective-permute-start(bf16[320,256]{1,0:T(8,128)(2,1)S(1)} %constant_dynamic-update-slice_fusion.3.refs_1_), channel_id=1, source_target_pairs={{0,1},{1,0},{2,3},{3,2},{4,5},{5,4},{6,7},{7,6},{8,9},{9,8},{10,11... | collective-permute-start | bytes 491528 | tf_op jit(solution)/shard_map/ppermute | solution.py:440
  140.8 4.8 %collective-permute-start.21 = (bf16[1280,256]{1,0:T(8,128)(2,1)S(1)}, bf16[1280,256]{1,0:T(8,128)(2,1)S(1)}, u32[]{:S(2)}, u32[]{:S(2)}) collective-permute-start(bf16[1280,256]{1,0:T(8,128)(2,1)S(1)} %get-tuple-element.117), channel_id=1, source_target_pairs={{0,1},{1,0},{2,3},{3,2},{4,5},{5,4},{6,7},{7,6},{8,9},{9,8},{10,11... | collective-permute-start | bytes 1966088 | tf_op jit(solution)/shard_map/ppermute | solution.py:440
  145.6 4.9 %collective-permute-start.22 = (bf16[1280,256]{1,0:T(8,128)(2,1)S(1)}, bf16[1280,256]{1,0:T(8,128)(2,1)S(1)}, u32[]{:S(2)}, u32[]{:S(2)}) collective-permute-start(bf16[1280,256]{1,0:T(8,128)(2,1)S(1)} %get-tuple-element.120), channel_id=1, source_target_pairs={{0,1},{1,0},{2,3},{3,2},{4,5},{5,4},{6,7},{7,6},{8,9},{9,8},{10,11... | collective-permute-start | bytes 1966088 | tf_op jit(solution)/shard_map/ppermute | solution.py:440
  150.1 3.3 %collective-permute-start.24 = (bf16[1280,512]{1,0:T(8,128)(2,1)S(1)}, bf16[1280,512]{1,0:T(8,128)(2,1)S(1)}, u32[]{:S(2)}, u32[]{:S(2)}) collective-permute-start(bf16[1280,512]{1,0:T(8,128)(2,1)S(1)} %get-tuple-element.125), channel_id=1, source_target_pairs={{0,1},{1,0},{2,3},{3,2},{4,5},{5,4},{6,7},{7,6},{8,9},{9,8},{10,11... | collective-permute-start | bytes 3932168 | tf_op jit(solution)/shard_map/ppermute | solution.py:440
  153.1 3.3 %collective-permute-start.23 = (bf16[640,512]{1,0:T(8,128)(2,1)S(1)}, bf16[640,512]{1,0:T(8,128)(2,1)S(1)}, u32[]{:S(2)}, u32[]{:S(2)}) collective-permute-start(bf16[640,512]{1,0:T(8,128)(2,1)S(1)} %get-tuple-element.124), channel_id=1, source_target_pairs={{0,1},{1,0},{2,3},{3,2},{4,5},{5,4},{6,7},{7,6},{8,9},{9,8},{10,11... | collective-permute-start | bytes 1966088 | tf_op jit(solution)/shard_map/ppermute | solution.py:440
  156.0 2.2 %collective-permute-start.25 = (bf16[640,512]{1,0:T(8,128)(2,1)S(1)}, bf16[640,512]{1,0:T(8,128)(2,1)S(1)}, u32[]{:S(2)}, u32[]{:S(2)}) collective-permute-start(bf16[640,512]{1,0:T(8,128)(2,1)S(1)} %get-tuple-element.127), channel_id=1, source_target_pairs={{0,1},{1,0},{2,3},{3,2},{4,5},{5,4},{6,7},{7,6},{8,9},{9,8},{10,11... | collective-permute-start | bytes 1966088 | tf_op jit(solution)/shard_map/ppermute | solution.py:440

commit v8 on v7

--- a/solution.py
+++ b/solution.py
@@ -304,8 +304,9 @@
     state_ref, keep, recv, in_own, in_other, out_own, out_other = refs[:7]
     refs = refs[7:]
     feat = feat_ref[0]
-    columns = keep.shape[1]
+    columns = in_own.shape[2]
     width = state_ref.shape[1]
+    sides = ((keep, 0), (recv, columns if mode == "coarse" else 0))
     if mode == "last":
         state_out, out, sems = refs[-3:]
         half_rows = out.shape[0] // 2
@@ -323,7 +324,7 @@
     def join(at):
         joined[at] = normalize(
             [state_ref[start + at : start + at + size, :].astype(F32)]
-            + [ref[offset + at : offset + at + size, :].astype(F32) for ref in (keep, recv)]
+            + [ref[offset + at : offset + at + size, col : col + columns].astype(F32) for ref, col in sides]
         )
 
     def hide(at):
@@ -369,7 +370,7 @@
 
 
 def node_call(mode, layer, feat, state, start, offset, rows, keep, recv, weights, out=None, total=0, placed=(), pieces=()):
-    columns = keep.shape[1]
+    columns = weights[0].shape[2]
     width = state.shape[1]
     operands = [state, keep, recv, *weights[:4]]
     aliases = {}
@@ -553,12 +554,13 @@
         at += rows
 
     early = len(halo) - 2
+    held = jnp.concatenate([first_rows, got], axis=0)
+    held = jnp.concatenate([held, swap_feat(held)], axis=1)
+    held, local[-1], *halo[:early] = barrier((held, local[-1], *halo[:early]))
     table = local_call(feat, local_places + halo_places[:early], local + halo[:early], table)
-    held = jnp.concatenate([first_rows, got], axis=0)
-    held, table = barrier((held, table))
     held = jnp.concatenate([held] + [fetch(held, offset) for offset in evens[1:]], axis=0)
     (coarse,) = node_call(
-        "coarse", 0, feat, coarse_state, 0, 0, held.shape[0], held, swap_feat(held), weights
+        "coarse", 0, feat, coarse_state, 0, 0, held.shape[0], held, held, weights
     )
     send, keep, _, table = aggregate_call(
         feat, links, staged, coarse, degree, table, (0, LAST_BLOCKS[0]), halo_places[early:], halo[early:]

time: 161 us -> 160 us (level)
  waiting for transfers between devices: 69.5 us -> 72.9 us
  starting transfers between devices: 42 us -> 38.6 us
    ppermute x2, waiting for transfers between devices: 0.01 us -> 23.1 us  [shards(): lax.ppermute(other, ('patch', 'feat'), other_patch)]
    ppermute x2, waiting for transfers between devices: 28.5 us -> 9.29 us  [shards(): lax.ppermute(own, ('patch', 'feat'), own_patch)]
    ppermute x13, starting transfers between devices: 16.1 us -> 12 us  [swap_feat(): return lax.ppermute(array, 'feat', [(0, 1), (1, 0)])]
where the time goes in v8:
time: 160 us; the launch traced here: 159 us
  waiting for transfers between devices  72.9 us (46%)
  Pallas kernels  46 us (29%)
  starting transfers between devices  38.6 us (24%)
    ppermute x7, waiting for transfers between devices, fetch(): lax.ppermute(held, 'patch', [(pos, (pos - stride) % count) for pos in ran...  33.3 us
    ppermute x2, waiting for transfers between devices, shards(): lax.ppermute(other, ('patch', 'feat'), other_patch)  23.1 us
    pallas_call x6, Pallas kernels, node_call(): pl.pallas_call(functools.partial(node_kernel, mode, layer, start, offset,...  19.9 us
    ppermute x13, starting transfers between devices, swap_feat(): return lax.ppermute(array, 'feat', [(0, 1), (1, 0)])  12 us
    ppermute x7, starting transfers between devices, fetch(): lax.ppermute(held, 'patch', [(pos, (pos - stride) % count) for pos in ran...  9.74 us
    ppermute x2, waiting for transfers between devices, shards(): lax.ppermute(own, ('patch', 'feat'), own_patch)  9.29 us
    pallas_call x4, Pallas kernels, aggregate_call(): pl.pallas_call(functools.partial(aggregate_kernel, places, start), grid_s...  8.54 us
    pallas_call x2, Pallas kernels, message_call(): pl.pallas_call(functools.partial(message_kernel, start, tile), in_specs=[...  8.26 us
  transfers between devices with their start and end apart: 26, of which 11 were waited for; matrix products, arithmetic and copies ran while one was open for 0% of the time, Pallas kernels for 25%

profile of v8, /device:TPU:9, one launch (start us, length us, event | category | flops | bytes accessed | tf_op | source)
XLA Modules:
  0.0 159.4 jit_solution(7369014531387413570)
XLA Ops:
  0.0 0.8 slice.3
  0.8 1.1 collective-permute-start
  1.9 4.1 %message.3.refs_4_ = bf16[2560,256]{1,0:T(8,128)(2,1)} custom-call(bf16[5120,512]{1,0:T(8,128)(2,1)} %refs_2_.1, bf16[2,512,256]{2,1,0:T(8,128)(2,1)} %refs_7_), custom_call_target="tpu_custom_call" | custom-call | flops 1048576 | bytes 1024 | tf_op jit(solution)/shard_map/message/pallas_call | solution.py:95
  6.0 0.0 copy-start
  6.0 0.0 copy-start.2
  6.1 0.0 copy-start.3
  6.1 0.0 copy-start.1
  6.1 2.4 %collective-permute-start.7 = (bf16[2560,256]{1,0:T(8,128)(2,1)}, bf16[2560,256]{1,0:T(8,128)(2,1)S(1)}, u32[]{:S(2)}, u32[]{:S(2)}) collective-permute-start(bf16[2560,256]{1,0:T(8,128)(2,1)} %message.3.refs_4_), channel_id=1, source_target_pairs={{0,2},{2,4},{4,6},{6,8},{8,10},{10,12},{12,14},{1,3},{3,5},{5,7},{... | collective-permute-start | bytes 3932168 | tf_op jit(solution)/shard_map/ppermute | solution.py:489
  8.5 4.1 %message.2.refs_3_ = bf16[2560,256]{1,0:T(8,128)(2,1)} custom-call(bf16[5120,512]{1,0:T(8,128)(2,1)} %refs_2_.1, bf16[2,512,256]{2,1,0:T(8,128)(2,1)} %refs_7_), custom_call_target="tpu_custom_call" | custom-call | flops 1048576 | bytes 1024 | tf_op jit(solution)/shard_map/message/pallas_call | solution.py:95
  12.6 3.9 %collective-permute-start.6 = (bf16[2560,256]{1,0:T(8,128)(2,1)}, bf16[2560,256]{1,0:T(8,128)(2,1)S(1)}, u32[]{:S(2)}, u32[]{:S(2)}) collective-permute-start(bf16[2560,256]{1,0:T(8,128)(2,1)} %message.2.refs_3_), channel_id=1, source_target_pairs={{2,0},{4,2},{6,4},{8,6},{10,8},{12,10},{14,12},{3,1},{5,3},{7,5},{... | collective-permute-start | bytes 3932168 | tf_op jit(solution)/shard_map/ppermute | solution.py:489
  16.6 1.6 collective-permute-start.3
  18.2 2.3 %collective-permute-start.1 = (bf16[80,512]{1,0:T(8,128)(2,1)S(1)}, bf16[80,512]{1,0:T(8,128)(2,1)S(1)}, u32[]{:S(2)}, u32[]{:S(2)}) collective-permute-start(bf16[80,512]{1,0:T(8,128)(2,1)S(1)} %pad_maximum_fusion.2), channel_id=1, source_target_pairs={{0,8},{2,10},{4,12},{6,14},{8,0},{10,2},{12,4},{14,6},{1,9},{3,11}... | collective-permute-start | bytes 245768 | tf_op jit(solution)/shard_map/ppermute | solution.py:446
  20.5 0.3 collective-permute-start.4
  20.8 27.4 %collective-permute-done.1 = bf16[80,512]{1,0:T(8,128)(2,1)S(1)} collective-permute-done((bf16[80,512]{1,0:T(8,128)(2,1)S(1)}, bf16[80,512]{1,0:T(8,128)(2,1)S(1)}, u32[]{:S(2)}, u32[]{:S(2)}) %collective-permute-start.1) | collective-permute-done | bytes 81952 | tf_op jit(solution)/shard_map/ppermute | solution.py:446
  48.2 2.5 %collective-permute-start.5 = (bf16[2,512,256]{2,1,0:T(8,128)(2,1)}, bf16[2,512,256]{2,1,0:T(8,128)(2,1)}, u32[]{:S(2)}, u32[]{:S(2)}) collective-permute-start(bf16[2,512,256]{2,1,0:T(8,128)(2,1)} %refs_7_), channel_id=1, source_target_pairs={{0,1},{1,0},{2,3},{3,2},{4,5},{5,4},{6,7},{7,6},{8,9},{9,8},{10,11... | collective-permute-start | bytes 1572872 | tf_op jit(solution)/shard_map/ppermute | solution.py:441
  50.7 0.1 copy.19
  50.8 0.1 reshape.52
  50.9 0.1 copy.18
  51.0 0.1 mul.15
  51.1 0.1 pad_add_fusion.links
  51.2 5.0 %stage.1 = (bf16[40,128,512]{2,1,0:T(8,128)(2,1)S(1)}, bf16[40,128,160]{2,1,0:T(8,128)(2,1)S(1)}, bf16[2560,512]{1,0:T(8,128)(2,1)S(1)}, bf16[10240,256]{1,0:T(8...) custom-call(s32[1]{0:T(128)} %bitcast.feat_ref, ...), custom_call_target="tpu_custom_call" | custom-call | flops 1048576 | bytes 1024 | tf_op jit(solution)/shard_map/stage/pallas_call | solution.py:166
  56.2 1.9 %collective-permute-start.2 = (bf16[160,512]{1,0:T(8,128)(2,1)S(1)}, bf16[160,512]{1,0:T(8,128)(2,1)S(1)}, u32[]{:S(2)}, u32[]{:S(2)}) collective-permute-start(bf16[160,512]{1,0:T(8,128)(2,1)S(1)} %pad_maximum_fusion.1), channel_id=1, source_target_pairs={{0,12},{2,14},{4,0},{6,2},{8,4},{10,6},{12,8},{14,10},{1,13},{3,15... | collective-permute-start | bytes 491528 | tf_op jit(solution)/shard_map/ppermute | solution.py:446
  58.2 1.5 weights.1
  59.7 2.4 %collective-permute-done.2 = bf16[160,512]{1,0:T(8,128)(2,1)S(1)} collective-permute-done((bf16[160,512]{1,0:T(8,128)(2,1)S(1)}, bf16[160,512]{1,0:T(8,128)(2,1)S(1)}, u32[]{:S(2)}, u32[]{:S(2)}) %collective-permute-start.2) | collective-permute-done | bytes 163872 | tf_op jit(solution)/shard_map/ppermute | solution.py:446
  62.1 0.5 coarse_message.1.refs_2_
  62.6 1.4 collective-permute-done.7.refs_5_
  64.0 4.0 %collective-permute-done.6.refs_4_ = bf16[2560,256]{1,0:T(8,128)(2,1)S(1)} collective-permute-done((bf16[2560,256]{1,0:T(8,128)(2,1)}, bf16[2560,256]{1,0:T(8,128)(2,1)S(1)}, u32[]{:S(2)}, u32[]{:S(2)}) %collective-permute-start.6) | collective-permute-done | bytes 1310752 | tf_op jit(solution)/shard_map/ppermute | solution.py:489
  68.0 2.0 %aggregate.4 = (bf16[1280,256]{1,0:T(8,128)(2,1)S(1)}, bf16[1280,256]{1,0:T(8,128)(2,1)S(1)}, bf16[40,256]{1,0:T(8,128)(2,1)S(1)}, bf16[10240,256]{1,0:T(8,128)(2,1)S(1)}) custom-call(s32[1]{0:T(128)} %bitcast.feat_ref, s32[320]{0:T(512)S(1)} %pad_add_fusion.links, ...), custom_call_target="tpu_custom_call", output_to_operand_aliasing={{3}: (8, {})} | custom-call | flops 1048576 | bytes 1024 | tf_op jit(solution)/shard_map/aggregate/pallas_call | solution.py:287
  70.0 0.6 collective-permute-start.8
  70.6 1.5 collective-permute-start.9
  72.1 1.8 %aggregate.5 = (bf16[1280,256]{1,0:T(8,128)(2,1)S(1)}, bf16[1280,256]{1,0:T(8,128)(2,1)S(1)}) custom-call(s32[1]{0:T(128)} %bitcast.feat_ref, s32[320]{0:T(512)S(1)} %pad_add_fusion.links, bf16[40,128,512]{2,1,0:T(8,128)(2,1)S(1)} %get-tuple-element.80.refs_0_, bf16[40,128,160]{2,1,0:T(8,128)(2,1)S(1)} %get-tuple-element.81.refs_1_, ...), custom_call_target="tpu_custom_call" | custom-call | flops 1048576 | bytes 1024 | tf_op jit(solution)/shard_map/aggregate/pallas_call | solution.py:287
  74.0 4.4 %node_mid.2 = (bf16[2560,512]{1,0:T(8,128)(2,1)S(1)}, bf16[1280,256]{1,0:T(8,128)(2,1)S(1)}, bf16[1280,256]{1,0:T(8,128)(2,1)S(1)}) custom-call(s32[1]{0:T(128)} %bitcast.feat_ref, bf16[2560,512]{1,0:T(8,128)(2,1)S(1)} %get-tuple-element.73.refs_0_, bf16[1280,256]{1,0:T(8,128)(2,1)S(1)} %get-tuple-element.94.refs_1_, ...), custom_call_target="tpu_custom_call", output_to_operand_aliasing={{0}: (1, {})} | custom-call | flops 1048576 | bytes 1024 | tf_op jit(solution)/shard_map/node_mid/pallas_call | solution.py:399
  78.4 0.6 collective-permute-start.10
  79.0 0.1 collective-permute-start.11
  79.1 2.1 %collective-permute-start.15 = (bf16[1280,256]{1,0:T(8,128)(2,1)S(1)}, bf16[1280,256]{1,0:T(8,128)(2,1)S(1)}, u32[]{:S(2)}, u32[]{:S(2)}) collective-permute-start(bf16[1280,256]{1,0:T(8,128)(2,1)S(1)} %get-tuple-element.104), channel_id=1, source_target_pairs={{2,1},{4,3},{6,5},{8,7},{10,9},{12,11},{14,13},{1,2},{3,4},{5,6},{... | collective-permute-start | bytes 1966088 | tf_op jit(solution)/shard_map/ppermute | solution.py:544
  81.2 2.7 %collective-permute-start.14 = (bf16[1280,256]{1,0:T(8,128)(2,1)S(1)}, bf16[1280,256]{1,0:T(8,128)(2,1)S(1)}, u32[]{:S(2)}, u32[]{:S(2)}) collective-permute-start(bf16[1280,256]{1,0:T(8,128)(2,1)S(1)} %get-tuple-element.112.refs_0_), channel_id=1, source_target_pairs={{2,0},{4,2},{6,4},{8,6},{10,8},{12,10},{14,12},{1,3},{3,5},{5,7},{... | collective-permute-start | bytes 1966088 | tf_op jit(solution)/shard_map/ppermute | solution.py:544
  83.9 4.4 %node_mid.3 = (bf16[2560,512]{1,0:T(8,128)(2,1)S(1)}, bf16[1280,256]{1,0:T(8,128)(2,1)S(1)}, bf16[1280,256]{1,0:T(8,128)(2,1)S(1)}) custom-call(s32[1]{0:T(128)} %bitcast.feat_ref, bf16[2560,512]{1,0:T(8,128)(2,1)S(1)} %get-tuple-element.106.refs_0_, bf16[1280,256]{1,0:T(8,128)(2,1)S(1)} %get-tuple-element.107.refs_1_, ...), custom_call_target="tpu_custom_call", output_to_operand_aliasing={{0}: (1, {})} | custom-call | flops 1048576 | bytes 1024 | tf_op jit(solution)/shard_map/node_mid/pallas_call | solution.py:399
  88.3 2.0 %collective-permute-start.13 = (bf16[1280,256]{1,0:T(8,128)(2,1)S(1)}, bf16[1280,256]{1,0:T(8,128)(2,1)S(1)}, u32[]{:S(2)}, u32[]{:S(2)}) collective-permute-start(bf16[1280,256]{1,0:T(8,128)(2,1)S(1)} %get-tuple-element.111), channel_id=1, source_target_pairs={{0,1},{1,0},{2,3},{3,2},{4,5},{5,4},{6,7},{7,6},{8,9},{9,8},{10,11... | collective-permute-start | bytes 1966088 | tf_op jit(solution)/shard_map/ppermute | solution.py:441
  90.3 0.1 collective-permute-start.12
  90.4 2.1 %collective-permute-start.20 = (bf16[1280,256]{1,0:T(8,128)(2,1)S(1)}, bf16[1280,256]{1,0:T(8,128)(2,1)S(1)}, u32[]{:S(2)}, u32[]{:S(2)}) collective-permute-start(bf16[1280,256]{1,0:T(8,128)(2,1)S(1)} %get-tuple-element.111), channel_id=1, source_target_pairs={{2,1},{4,3},{6,5},{8,7},{10,9},{12,11},{14,13},{1,2},{3,4},{5,6},{... | collective-permute-start | bytes 1966088 | tf_op jit(solution)/shard_map/ppermute | solution.py:544
  92.5 3.6 %collective-permute-start.19 = (bf16[1280,256]{1,0:T(8,128)(2,1)S(1)}, bf16[1280,256]{1,0:T(8,128)(2,1)S(1)}, u32[]{:S(2)}, u32[]{:S(2)}) collective-permute-start(bf16[1280,256]{1,0:T(8,128)(2,1)S(1)} %get-tuple-element.114.refs_2_), channel_id=1, source_target_pairs={{2,0},{4,2},{6,4},{8,6},{10,8},{12,10},{14,12},{1,3},{3,5},{5,7},{... | collective-permute-start | bytes 1966088 | tf_op jit(solution)/shard_map/ppermute | solution.py:544
  96.2 22.9 %collective-permute-done.15.refs_5_ = bf16[1280,256]{1,0:T(8,128)(2,1)S(1)} collective-permute-done((bf16[1280,256]{1,0:T(8,128)(2,1)S(1)}, bf16[1280,256]{1,0:T(8,128)(2,1)S(1)}, u32[]{:S(2)}, u32[]{:S(2)}) %collective-permute-start.15) | collective-permute-done | bytes 655392 | tf_op jit(solution)/shard_map/ppermute | solution.py:544
  119.1 4.8 %collective-permute-done.14.refs_4_ = bf16[1280,256]{1,0:T(8,128)(2,1)S(1)} collective-permute-done((bf16[1280,256]{1,0:T(8,128)(2,1)S(1)}, bf16[1280,256]{1,0:T(8,128)(2,1)S(1)}, u32[]{:S(2)}, u32[]{:S(2)}) %collective-permute-start.14) | collective-permute-done | bytes 655392 | tf_op jit(solution)/shard_map/ppermute | solution.py:544
  123.9 1.3 collective-permute-start.18
  125.1 0.2 collective-permute-start.17
  125.3 1.4 collective-permute-start.16
  126.7 1.3 local_messages.1.refs_6_
  128.0 2.2 %collective-permute-done.17 = bf16[80,512]{1,0:T(8,128)(2,1)S(1)} collective-permute-done((bf16[80,512]{1,0:T(8,128)(2,1)S(1)}, bf16[80,512]{1,0:T(8,128)(2,1)S(1)}, u32[]{:S(2)}, u32[]{:S(2)}) %collective-permute-start.17) | collective-permute-done | bytes 81952 | tf_op jit(solution)/shard_map/ppermute | solution.py:446
  130.2 1.4 collective-permute-done.16
  131.6 1.6 %node_coarse.1.refs_2_ = f32[320,256]{1,0:T(8,128)S(1)} custom-call(s32[1]{0:T(128)} %bitcast.feat_ref, bf16[320,512]{1,0:T(8,128)(2,1)S(1)} %constant_dynamic-update-slice_fusion.state_ref.refs_0_, bf16[320,512]{1,0:T(8,128)(2,1)S(1)} %pad_maximum_fusion.refs_1_.refs_2_, bf16[320,512]{1,0:T(8,128)(2,1)S(1)} %pad_maximum_fusion.refs_1_.refs_2_, ...), custom_call_target="tpu_custom_call" | custom-call | flops 1048576 | bytes 1024 | tf_op jit(solution)/shard_map/node_coarse/pallas_call | solution.py:399
  133.2 0.2 collective-permute-done.20.refs_5_
  133.4 4.5 %collective-permute-done.19.refs_4_ = bf16[1280,256]{1,0:T(8,128)(2,1)S(1)} collective-permute-done((bf16[1280,256]{1,0:T(8,128)(2,1)S(1)}, bf16[1280,256]{1,0:T(8,128)(2,1)S(1)}, u32[]{:S(2)}, u32[]{:S(2)}) %collective-permute-start.19) | collective-permute-done | bytes 655392 | tf_op jit(solution)/shard_map/ppermute | solution.py:544
  137.9 2.9 %aggregate.6 = (bf16[1280,256]{1,0:T(8,128)(2,1)S(1)}, bf16[1280,256]{1,0:T(8,128)(2,1)S(1)}, bf16[40,256]{1,0:T(8,128)(2,1)}, bf16[10240,256]{1,0:T(8,128)(2,1)S(1)}) custom-call(s32[1]{0:T(128)} %bitcast.feat_ref, s32[320]{0:T(512)S(1)} %pad_add_fusion.links, bf16[40,128,512]{2,1,0:T(8,128)(2,1)S(1)} %get-tuple-element.80.refs_0_, ...), custom_call_target="tpu_custom_call", output_to_operand_aliasing={{3}: (8, {})} | custom-call | flops 1048576 | bytes 1024 | tf_op jit(solution)/shard_map/aggregate/pallas_call | solution.py:287
  140.8 3.0 %collective-permute-start.21 = (bf16[1280,256]{1,0:T(8,128)(2,1)S(1)}, bf16[1280,256]{1,0:T(8,128)(2,1)S(1)}, u32[]{:S(2)}, u32[]{:S(2)}) collective-permute-start(bf16[1280,256]{1,0:T(8,128)(2,1)S(1)} %get-tuple-element.121), channel_id=1, source_target_pairs={{0,1},{1,0},{2,3},{3,2},{4,5},{5,4},{6,7},{7,6},{8,9},{9,8},{10,11... | collective-permute-start | bytes 1966088 | tf_op jit(solution)/shard_map/ppermute | solution.py:441
  143.7 1.8 %aggregate.7 = (bf16[1280,256]{1,0:T(8,128)(2,1)S(1)}, bf16[1280,256]{1,0:T(8,128)(2,1)S(1)}) custom-call(s32[1]{0:T(128)} %bitcast.feat_ref, s32[320]{0:T(512)S(1)} %pad_add_fusion.links, bf16[40,128,512]{2,1,0:T(8,128)(2,1)S(1)} %get-tuple-element.80.refs_0_, bf16[40,128,160]{2,1,0:T(8,128)(2,1)S(1)} %get-tuple-element.81.refs_1_, ...), custom_call_target="tpu_custom_call" | custom-call | flops 1048576 | bytes 1024 | tf_op jit(solution)/shard_map/aggregate/pallas_call | solution.py:287
  145.6 0.2 collective-permute-start.22
  145.8 4.2 %node_last.3 = (bf16[1280,512]{1,0:T(8,128)(2,1)S(1)}, bf16[5120,512]{1,0:T(8,128)(2,1)}) custom-call(s32[1]{0:T(128)} %bitcast.feat_ref, bf16[2560,512]{1,0:T(8,128)(2,1)S(1)} %get-tuple-element.109.refs_0_, bf16[1280,256]{1,0:T(8,128)(2,1)S(1)} %get-tuple-element.125.refs_1_, bf16[1280,256]{1,0:T(8,128)(2,1)S(1)} %collective-permute-done.21.refs_2_, ...), custom_call_target="tpu_custom_call" | custom-call | flops 8589934592 | bytes 1024 | tf_op jit(solution)/shard_map/node_last/pallas_call | solution.py:399
  150.1 0.4 collective-permute-start.24
  150.5 2.6 %node_last.4 = (bf16[640,512]{1,0:T(8,128)(2,1)S(1)}, bf16[5120,512]{1,0:T(8,128)(2,1)}) custom-call(s32[1]{0:T(128)} %bitcast.feat_ref, bf16[2560,512]{1,0:T(8,128)(2,1)S(1)} %get-tuple-element.109.refs_0_, bf16[1280,256]{1,0:T(8,128)(2,1)S(1)} %get-tuple-element.120.refs_1_, ...), custom_call_target="tpu_custom_call", output_to_operand_aliasing={{1}: (8, {})} | custom-call | flops 8589934592 | bytes 1024 | tf_op jit(solution)/shard_map/node_last/pallas_call | solution.py:399
  153.1 0.2 collective-permute-start.23
  153.3 2.6 %node_last.5 = (bf16[640,512]{1,0:T(8,128)(2,1)S(1)}, bf16[5120,512]{1,0:T(8,128)(2,1)}) custom-call(s32[1]{0:T(128)} %bitcast.feat_ref, bf16[2560,512]{1,0:T(8,128)(2,1)S(1)} %get-tuple-element.109.refs_0_, bf16[1280,256]{1,0:T(8,128)(2,1)S(1)} %get-tuple-element.120.refs_1_, ...), custom_call_target="tpu_custom_call", output_to_operand_aliasing={{1}: (9, {})} | custom-call | flops 8589934592 | bytes 1024 | tf_op jit(solution)/shard_map/node_last/pallas_call | solution.py:399
  155.9 0.4 collective-permute-start.25
  156.3 1.8 %collective-permute-done.25.refs_1_ = bf16[640,512]{1,0:T(8,128)(2,1)S(1)} collective-permute-done((bf16[640,512]{1,0:T(8,128)(2,1)S(1)}, bf16[640,512]{1,0:T(8,128)(2,1)S(1)}, u32[]{:S(2)}, u32[]{:S(2)}) %collective-permute-start.25) | collective-permute-done | bytes 655392 | tf_op jit(solution)/shard_map/ppermute | solution.py:441
  158.1 1.1 assemble.1
  (30 shorter events, 0.1 us)
Async XLA Ops:
  0.8 11.8 %collective-permute-start = (bf16[40,512]{1,0:T(8,128)(2,1)S(1)}, bf16[40,512]{1,0:T(8,128)(2,1)S(1)}, u32[]{:S(2)}, u32[]{:S(2)}) collective-permute-start(bf16[40,512]{1,0:T(8,128)(2,1)S(1)} %slice.3), channel_id=1, source_target_pairs={{0,14},{2,0},{4,2},{6,4},{8,6},{10,8},{12,10},{14,12},{1,15},{3,1}... | collective-permute-start | bytes 122888 | tf_op jit(solution)/shard_map/ppermute | solution.py:446
  6.0 14.5 %copy-start = (bf16[2,256,512]{2,1,0:T(8,128)(2,1)S(1)}, bf16[2,256,512]{2,1,0:T(8,128)(2,1)}, u32[]{:S(2)}) copy-start(bf16[2,256,512]{2,1,0:T(8,128)(2,1)} %refs_6_) | copy-start | bytes 1572868
  6.0 44.7 %copy-start.2 = (s32[40,4]{0,1:T(4,128)S(1)}, s32[40,4]{0,1:T(4,128)}, u32[]{:S(2)}) copy-start(s32[40,4]{0,1:T(4,128)} %param.13) | copy-start | bytes 1924
  6.1 44.7 %copy-start.3 = (s32[40,4]{0,1:T(4,128)S(1)}, s32[40,4]{0,1:T(4,128)}, u32[]{:S(2)}) copy-start(s32[40,4]{0,1:T(4,128)} %param.12) | copy-start | bytes 1924
  6.1 45.1 %copy-start.1 = (s32[5120]{0:T(1024)S(1)}, s32[5120]{0:T(1024)}, u32[]{:S(2)}) copy-start(s32[5120]{0:T(1024)} %param.14) | copy-start | bytes 61444
  6.1 57.9 %collective-permute-start.7 = (bf16[2560,256]{1,0:T(8,128)(2,1)}, bf16[2560,256]{1,0:T(8,128)(2,1)S(1)}, u32[]{:S(2)}, u32[]{:S(2)}) collective-permute-start(bf16[2560,256]{1,0:T(8,128)(2,1)} %message.3.refs_4_), channel_id=1, source_target_pairs={{0,2},{2,4},{4,6},{6,8},{8,10},{10,12},{12,14},{1,3},{3,5},{5,7},{... | collective-permute-start | bytes 3932168 | tf_op jit(solution)/shard_map/ppermute | solution.py:489
  12.6 55.4 %collective-permute-start.6 = (bf16[2560,256]{1,0:T(8,128)(2,1)}, bf16[2560,256]{1,0:T(8,128)(2,1)S(1)}, u32[]{:S(2)}, u32[]{:S(2)}) collective-permute-start(bf16[2560,256]{1,0:T(8,128)(2,1)} %message.2.refs_3_), channel_id=1, source_target_pairs={{2,0},{4,2},{6,4},{8,6},{10,8},{12,10},{14,12},{3,1},{5,3},{7,5},{... | collective-permute-start | bytes 3932168 | tf_op jit(solution)/shard_map/ppermute | solution.py:489
  16.6 41.6 %collective-permute-start.3 = (bf16[2,1024,256]{2,1,0:T(8,128)(2,1)}, bf16[2,1024,256]{2,1,0:T(8,128)(2,1)}, u32[]{:S(2)}, u32[]{:S(2)}) collective-permute-start(bf16[2,1024,256]{2,1,0:T(8,128)(2,1)} %refs_5_), channel_id=1, source_target_pairs={{0,1},{1,0},{2,3},{3,2},{4,5},{5,4},{6,7},{7,6},{8,9},{9,8},{10,11... | collective-permute-start | bytes 3145736 | tf_op jit(solution)/shard_map/ppermute | solution.py:441
  18.2 30.0 %collective-permute-start.1 = (bf16[80,512]{1,0:T(8,128)(2,1)S(1)}, bf16[80,512]{1,0:T(8,128)(2,1)S(1)}, u32[]{:S(2)}, u32[]{:S(2)}) collective-permute-start(bf16[80,512]{1,0:T(8,128)(2,1)S(1)} %pad_maximum_fusion.2), channel_id=1, source_target_pairs={{0,8},{2,10},{4,12},{6,14},{8,0},{10,2},{12,4},{14,6},{1,9},{3,11}... | collective-permute-start | bytes 245768 | tf_op jit(solution)/shard_map/ppermute | solution.py:446
  20.5 35.7 %collective-permute-start.4 = (bf16[2,256,512]{2,1,0:T(8,128)(2,1)S(1)}, bf16[2,256,512]{2,1,0:T(8,128)(2,1)}, u32[]{:S(2)}, u32[]{:S(2)}) collective-permute-start(bf16[2,256,512]{2,1,0:T(8,128)(2,1)S(1)} %copy-done), channel_id=1, source_target_pairs={{0,1},{1,0},{2,3},{3,2},{4,5},{5,4},{6,7},{7,6},{8,9},{9,8},{10,11... | collective-permute-start | bytes 1572872 | tf_op jit(solution)/shard_map/ppermute | solution.py:441
  48.2 9.9 %collective-permute-start.5 = (bf16[2,512,256]{2,1,0:T(8,128)(2,1)}, bf16[2,512,256]{2,1,0:T(8,128)(2,1)}, u32[]{:S(2)}, u32[]{:S(2)}) collective-permute-start(bf16[2,512,256]{2,1,0:T(8,128)(2,1)} %refs_7_), channel_id=1, source_target_pairs={{0,1},{1,0},{2,3},{3,2},{4,5},{5,4},{6,7},{7,6},{8,9},{9,8},{10,11... | collective-permute-start | bytes 1572872 | tf_op jit(solution)/shard_map/ppermute | solution.py:441
  56.2 5.9 %collective-permute-start.2 = (bf16[160,512]{1,0:T(8,128)(2,1)S(1)}, bf16[160,512]{1,0:T(8,128)(2,1)S(1)}, u32[]{:S(2)}, u32[]{:S(2)}) collective-permute-start(bf16[160,512]{1,0:T(8,128)(2,1)S(1)} %pad_maximum_fusion.1), channel_id=1, source_target_pairs={{0,12},{2,14},{4,0},{6,2},{8,4},{10,6},{12,8},{14,10},{1,13},{3,15... | collective-permute-start | bytes 491528 | tf_op jit(solution)/shard_map/ppermute | solution.py:446
  70.0 3.9 %collective-permute-start.8 = (bf16[1280,256]{1,0:T(8,128)(2,1)S(1)}, bf16[1280,256]{1,0:T(8,128)(2,1)S(1)}, u32[]{:S(2)}, u32[]{:S(2)}) collective-permute-start(bf16[1280,256]{1,0:T(8,128)(2,1)S(1)} %get-tuple-element.90), channel_id=1, source_target_pairs={{0,1},{1,0},{2,3},{3,2},{4,5},{5,4},{6,7},{7,6},{8,9},{9,8},{10,11... | collective-permute-start | bytes 1966088 | tf_op jit(solution)/shard_map/ppermute | solution.py:441
  70.6 7.8 %collective-permute-start.9 = (bf16[40,256]{1,0:T(8,128)(2,1)S(1)}, bf16[40,256]{1,0:T(8,128)(2,1)S(1)}, u32[]{:S(2)}, u32[]{:S(2)}) collective-permute-start(bf16[40,256]{1,0:T(8,128)(2,1)S(1)} %get-tuple-element.103), channel_id=1, source_target_pairs={{0,14},{2,0},{4,2},{6,4},{8,6},{10,8},{12,10},{14,12},{1,15},{3,1}... | collective-permute-start | bytes 61448 | tf_op jit(solution)/shard_map/ppermute | solution.py:446
  78.4 5.5 %collective-permute-start.10 = (bf16[1280,256]{1,0:T(8,128)(2,1)S(1)}, bf16[1280,256]{1,0:T(8,128)(2,1)S(1)}, u32[]{:S(2)}, u32[]{:S(2)}) collective-permute-start(bf16[1280,256]{1,0:T(8,128)(2,1)S(1)} %get-tuple-element.104), channel_id=1, source_target_pairs={{0,1},{1,0},{2,3},{3,2},{4,5},{5,4},{6,7},{7,6},{8,9},{9,8},{10,11... | collective-permute-start | bytes 1966088 | tf_op jit(solution)/shard_map/ppermute | solution.py:441
  79.0 4.9 %collective-permute-start.11 = (bf16[1280,256]{1,0:T(8,128)(2,1)S(1)}, bf16[1280,256]{1,0:T(8,128)(2,1)S(1)}, u32[]{:S(2)}, u32[]{:S(2)}) collective-permute-start(bf16[1280,256]{1,0:T(8,128)(2,1)S(1)} %get-tuple-element.108), channel_id=1, source_target_pairs={{0,1},{1,0},{2,3},{3,2},{4,5},{5,4},{6,7},{7,6},{8,9},{9,8},{10,11... | collective-permute-start | bytes 1966088 | tf_op jit(solution)/shard_map/ppermute | solution.py:441
  79.1 40.0 %collective-permute-start.15 = (bf16[1280,256]{1,0:T(8,128)(2,1)S(1)}, bf16[1280,256]{1,0:T(8,128)(2,1)S(1)}, u32[]{:S(2)}, u32[]{:S(2)}) collective-permute-start(bf16[1280,256]{1,0:T(8,128)(2,1)S(1)} %get-tuple-element.104), channel_id=1, source_target_pairs={{2,1},{4,3},{6,5},{8,7},{10,9},{12,11},{14,13},{1,2},{3,4},{5,6},{... | collective-permute-start | bytes 1966088 | tf_op jit(solution)/shard_map/ppermute | solution.py:544
  81.2 42.6 %collective-permute-start.14 = (bf16[1280,256]{1,0:T(8,128)(2,1)S(1)}, bf16[1280,256]{1,0:T(8,128)(2,1)S(1)}, u32[]{:S(2)}, u32[]{:S(2)}) collective-permute-start(bf16[1280,256]{1,0:T(8,128)(2,1)S(1)} %get-tuple-element.112.refs_0_), channel_id=1, source_target_pairs={{2,0},{4,2},{6,4},{8,6},{10,8},{12,10},{14,12},{1,3},{3,5},{5,7},{... | collective-permute-start | bytes 1966088 | tf_op jit(solution)/shard_map/ppermute | solution.py:544
  88.3 35.5 %collective-permute-start.13 = (bf16[1280,256]{1,0:T(8,128)(2,1)S(1)}, bf16[1280,256]{1,0:T(8,128)(2,1)S(1)}, u32[]{:S(2)}, u32[]{:S(2)}) collective-permute-start(bf16[1280,256]{1,0:T(8,128)(2,1)S(1)} %get-tuple-element.111), channel_id=1, source_target_pairs={{0,1},{1,0},{2,3},{3,2},{4,5},{5,4},{6,7},{7,6},{8,9},{9,8},{10,11... | collective-permute-start | bytes 1966088 | tf_op jit(solution)/shard_map/ppermute | solution.py:441
  90.3 2.2 %collective-permute-start.12 = (bf16[80,256]{1,0:T(8,128)(2,1)S(1)}, bf16[80,256]{1,0:T(8,128)(2,1)S(1)}, u32[]{:S(2)}, u32[]{:S(2)}) collective-permute-start(bf16[80,256]{1,0:T(8,128)(2,1)S(1)} %constant_dynamic-update-slice_fusion.3), channel_id=1, source_target_pairs={{0,1},{1,0},{2,3},{3,2},{4,5},{5,4},{6,7},{7,6},{8,9},{9,8},{10,11... | collective-permute-start | bytes 122888 | tf_op jit(solution)/shard_map/ppermute | solution.py:441
  90.4 43.0 %collective-permute-start.20 = (bf16[1280,256]{1,0:T(8,128)(2,1)S(1)}, bf16[1280,256]{1,0:T(8,128)(2,1)S(1)}, u32[]{:S(2)}, u32[]{:S(2)}) collective-permute-start(bf16[1280,256]{1,0:T(8,128)(2,1)S(1)} %get-tuple-element.111), channel_id=1, source_target_pairs={{2,1},{4,3},{6,5},{8,7},{10,9},{12,11},{14,13},{1,2},{3,4},{5,6},{... | collective-permute-start | bytes 1966088 | tf_op jit(solution)/shard_map/ppermute | solution.py:544
  92.5 45.3 %collective-permute-start.19 = (bf16[1280,256]{1,0:T(8,128)(2,1)S(1)}, bf16[1280,256]{1,0:T(8,128)(2,1)S(1)}, u32[]{:S(2)}, u32[]{:S(2)}) collective-permute-start(bf16[1280,256]{1,0:T(8,128)(2,1)S(1)} %get-tuple-element.114.refs_2_), channel_id=1, source_target_pairs={{2,0},{4,2},{6,4},{8,6},{10,8},{12,10},{14,12},{1,3},{3,5},{5,7},{... | collective-permute-start | bytes 1966088 | tf_op jit(solution)/shard_map/ppermute | solution.py:544
  123.9 4.2 %collective-permute-start.18 = (bf16[80,512]{1,0:T(8,128)(2,1)S(1)}, bf16[80,512]{1,0:T(8,128)(2,1)S(1)}, u32[]{:S(2)}, u32[]{:S(2)}) collective-permute-start(bf16[80,512]{1,0:T(8,128)(2,1)S(1)} %pad_maximum_fusion.3), channel_id=1, source_target_pairs={{0,4},{2,6},{4,8},{6,10},{8,12},{10,14},{12,0},{14,2},{1,5},{3,7},... | collective-permute-start | bytes 245768 | tf_op jit(solution)/shard_map/ppermute | solution.py:446
  125.1 5.1 %collective-permute-start.17 = (bf16[80,512]{1,0:T(8,128)(2,1)S(1)}, bf16[80,512]{1,0:T(8,128)(2,1)S(1)}, u32[]{:S(2)}, u32[]{:S(2)}) collective-permute-start(bf16[80,512]{1,0:T(8,128)(2,1)S(1)} %pad_maximum_fusion.3), channel_id=1, source_target_pairs={{0,12},{2,14},{4,0},{6,2},{8,4},{10,6},{12,8},{14,10},{1,13},{3,15... | collective-permute-start | bytes 245768 | tf_op jit(solution)/shard_map/ppermute | solution.py:446
  125.3 6.2 %collective-permute-start.16 = (bf16[80,512]{1,0:T(8,128)(2,1)S(1)}, bf16[80,512]{1,0:T(8,128)(2,1)S(1)}, u32[]{:S(2)}, u32[]{:S(2)}) collective-permute-start(bf16[80,512]{1,0:T(8,128)(2,1)S(1)} %pad_maximum_fusion.3), channel_id=1, source_target_pairs={{0,8},{2,10},{4,12},{6,14},{8,0},{10,2},{12,4},{14,6},{1,9},{3,11}... | collective-permute-start | bytes 245768 | tf_op jit(solution)/shard_map/ppermute | solution.py:446
  140.8 4.8 %collective-permute-start.21 = (bf16[1280,256]{1,0:T(8,128)(2,1)S(1)}, bf16[1280,256]{1,0:T(8,128)(2,1)S(1)}, u32[]{:S(2)}, u32[]{:S(2)}) collective-permute-start(bf16[1280,256]{1,0:T(8,128)(2,1)S(1)} %get-tuple-element.121), channel_id=1, source_target_pairs={{0,1},{1,0},{2,3},{3,2},{4,5},{5,4},{6,7},{7,6},{8,9},{9,8},{10,11... | collective-permute-start | bytes 1966088 | tf_op jit(solution)/shard_map/ppermute | solution.py:441
  145.6 4.9 %collective-permute-start.22 = (bf16[1280,256]{1,0:T(8,128)(2,1)S(1)}, bf16[1280,256]{1,0:T(8,128)(2,1)S(1)}, u32[]{:S(2)}, u32[]{:S(2)}) collective-permute-start(bf16[1280,256]{1,0:T(8,128)(2,1)S(1)} %get-tuple-element.124), channel_id=1, source_target_pairs={{0,1},{1,0},{2,3},{3,2},{4,5},{5,4},{6,7},{7,6},{8,9},{9,8},{10,11... | collective-permute-start | bytes 1966088 | tf_op jit(solution)/shard_map/ppermute | solution.py:441
  150.1 3.3 %collective-permute-start.24 = (bf16[1280,512]{1,0:T(8,128)(2,1)S(1)}, bf16[1280,512]{1,0:T(8,128)(2,1)S(1)}, u32[]{:S(2)}, u32[]{:S(2)}) collective-permute-start(bf16[1280,512]{1,0:T(8,128)(2,1)S(1)} %get-tuple-element.129), channel_id=1, source_target_pairs={{0,1},{1,0},{2,3},{3,2},{4,5},{5,4},{6,7},{7,6},{8,9},{9,8},{10,11... | collective-permute-start | bytes 3932168 | tf_op jit(solution)/shard_map/ppermute | solution.py:441
  153.1 3.3 %collective-permute-start.23 = (bf16[640,512]{1,0:T(8,128)(2,1)S(1)}, bf16[640,512]{1,0:T(8,128)(2,1)S(1)}, u32[]{:S(2)}, u32[]{:S(2)}) collective-permute-start(bf16[640,512]{1,0:T(8,128)(2,1)S(1)} %get-tuple-element.128), channel_id=1, source_target_pairs={{0,1},{1,0},{2,3},{3,2},{4,5},{5,4},{6,7},{7,6},{8,9},{9,8},{10,11... | collective-permute-start | bytes 1966088 | tf_op jit(solution)/shard_map/ppermute | solution.py:441
  155.9 2.2 %collective-permute-start.25 = (bf16[640,512]{1,0:T(8,128)(2,1)S(1)}, bf16[640,512]{1,0:T(8,128)(2,1)S(1)}, u32[]{:S(2)}, u32[]{:S(2)}) collective-permute-start(bf16[640,512]{1,0:T(8,128)(2,1)S(1)} %get-tuple-element.131), channel_id=1, source_target_pairs={{0,1},{1,0},{2,3},{3,2},{4,5},{5,4},{6,7},{7,6},{8,9},{9,8},{10,11... | collective-permute-start | bytes 1966088 | tf_op jit(solution)/shard_map/ppermute | solution.py:441

commit v9 on v8

--- a/solution.py
+++ b/solution.py
@@ -228,7 +228,7 @@
     fine, coarse_tile, coarse, degree = refs[:4]
     pieces = refs[4 : 4 + len(places)]
     if places:
-        send, keep, first_rows, table, sems = refs[5 + len(places) :]
+        send, keep, *first_rows, table, sems = refs[5 + len(places) :]
         pairs = []
         for place, piece in zip(places, pieces):
             at = pl.multiple_of(place(feat_ref[0]), 16)
@@ -261,18 +261,18 @@
             summed = dot(fine[first + pos], chosen) + dot(coarse_tile[first + pos], stacked)
             result = (summed * scale[:, start + pos : start + pos + 1]).astype(BF16)
             out_ref[pos * block : (pos + 1) * block, :] = result
-    if places:
+    if places and first_rows:
 
         @pl.when(feat == 0)
         def _():
-            first_rows[...] = keep[:CN_DEV, :]
+            first_rows[0][...] = keep[:CN_DEV, :]
 
         @pl.when(feat != 0)
         def _():
-            first_rows[...] = send[:CN_DEV, :]
-
-
-def aggregate_call(feat, links, staged, coarse, degree, table, span, places=(), pieces=()):
+            first_rows[0][...] = send[:CN_DEV, :]
+
+
+def aggregate_call(feat, links, staged, coarse, degree, table, span, places=(), pieces=(), wants_first=False):
     fine, coarse_tile = staged
     blocks, block, _ = fine.shape
     columns = table.shape[1]
@@ -281,8 +281,8 @@
     aliases = {}
     scratch = []
     if pieces:
-        out_shape += [pltpu.VMEM((CN_DEV, columns), BF16), pltpu.VMEM(table.shape, BF16)]
-        aliases = {6 + len(pieces): 3}
+        out_shape += [pltpu.VMEM((CN_DEV, columns), BF16)] * wants_first + [pltpu.VMEM(table.shape, BF16)]
+        aliases = {6 + len(pieces): len(out_shape) - 1}
         scratch = [pltpu.SemaphoreType.DMA((len(pieces),))]
     return pl.pallas_call(
         functools.partial(aggregate_kernel, places, start),
@@ -443,7 +443,7 @@
 
 def fetch(held, stride):
     count = lax.axis_size("patch")
-    return lax.ppermute(held, "patch", [(pos, (pos - stride) % count) for pos in range(count)])
+    return lax.ppermute(held, "patch", [(pos, pos ^ stride) for pos in range(count)])
 
 
 def even_offsets(count):
@@ -494,7 +494,7 @@
         (fine_index, coarse_index, node_degree, w_in, w_out, w_msg, high)
     )
     links = (fine_index - (patch_pos * blocks - HALO_BLK)).reshape(-1) * block
-    away = ((coarse_index - patch_pos) % patches).reshape(-1)
+    away = (coarse_index ^ patch_pos).reshape(-1)
     coarse_links = sum(jnp.where(away == offset, pos * CN_DEV, 0) for pos, offset in enumerate(offsets))
     links = jnp.concatenate([links, coarse_links])
     degree = node_degree.reshape(2, half, block)
@@ -521,7 +521,7 @@
     ]
     first_span, last_span = (0, MID_BLOCKS[0]), MID_BLOCKS
     send, keep, first_rows, table = aggregate_call(
-        feat, links, staged, coarse, degree, table, first_span, halo_places, halo
+        feat, links, staged, coarse, degree, table, first_span, halo_places, halo, True
     )
     recv = swap_feat(send)
     got = fetch(first_rows, 1)
@@ -562,7 +562,7 @@
     (coarse,) = node_call(
         "coarse", 0, feat, coarse_state, 0, 0, held.shape[0], held, held, weights
     )
-    send, keep, _, table = aggregate_call(
+    send, keep, table = aggregate_call(
         feat, links, staged, coarse, degree, table, (0, LAST_BLOCKS[0]), halo_places[early:], halo[early:]
     )
     recv = swap_feat(send)

time: 160 us -> 158 us (0.988)
  starting transfers between devices: 38.6 us -> 36.2 us
    ppermute x13, starting transfers between devices: 12 us -> 8.92 us  [swap_feat(): return lax.ppermute(array, 'feat', [(0, 1), (1, 0)])]
    ppermute x2, waiting for transfers between devices: 9.29 us -> 12.2 us  [shards(): lax.ppermute(own, ('patch', 'feat'), own_patch)]
    ppermute x2, starting transfers between devices: 4.28 us -> 7.06 us  [shards(): lax.ppermute(other, ('patch', 'feat'), other_patch)]
    ppermute x7, starting transfers between devices: 9.74 us -> 8.1 us  [fetch(): lax.ppermute(held, 'patch', [(pos, pos ^ stride) for pos in range(count)])]
where the time goes in v9:
time: 158 us; the launch traced here: 157 us
  waiting for transfers between devices  73.7 us (47%)
  Pallas kernels  45.6 us (29%)
  starting transfers between devices  36.2 us (23%)
    ppermute x7, waiting for transfers between devices, fetch(): lax.ppermute(held, 'patch', [(pos, pos ^ stride) for pos in range(count)])  32.6 us
    ppermute x2, waiting for transfers between devices, shards(): lax.ppermute(other, ('patch', 'feat'), other_patch)  22.3 us
    pallas_call x6, Pallas kernels, node_call(): pl.pallas_call(functools.partial(node_kernel, mode, layer, start, offset,...  19.9 us
    ppermute x2, waiting for transfers between devices, shards(): lax.ppermute(own, ('patch', 'feat'), own_patch)  12.2 us
    ppermute x13, starting transfers between devices, swap_feat(): return lax.ppermute(array, 'feat', [(0, 1), (1, 0)])  8.92 us
    pallas_call x2, Pallas kernels, message_call(): pl.pallas_call(functools.partial(message_kernel, start, tile), in_specs=[...  8.26 us
    pallas_call x4, Pallas kernels, aggregate_call(): pl.pallas_call(functools.partial(aggregate_kernel, places, start), grid_s...  8.12 us
    ppermute x7, starting transfers between devices, fetch(): lax.ppermute(held, 'patch', [(pos, pos ^ stride) for pos in range(count)])  8.1 us
  transfers between devices with their start and end apart: 26, of which 11 were waited for; matrix products, arithmetic and copies ran while one was open for 0% of the time, Pallas kernels for 25%

profile of v9, /device:TPU:9, one launch (start us, length us, event | category | flops | bytes accessed | tf_op | source)
XLA Modules:
  0.0 157.4 jit_solution(12584473161004516466)
XLA Ops:
  0.0 0.8 slice.3
  0.8 1.2 collective-permute-start
  2.0 4.1 %message.3.refs_4_ = bf16[2560,256]{1,0:T(8,128)(2,1)} custom-call(bf16[5120,512]{1,0:T(8,128)(2,1)} %refs_2_.1, bf16[2,512,256]{2,1,0:T(8,128)(2,1)} %refs_7_), custom_call_target="tpu_custom_call" | custom-call | flops 1048576 | bytes 1024 | tf_op jit(solution)/shard_map/message/pallas_call | solution.py:95
  6.2 0.0 copy-start
  6.2 0.0 copy-start.2
  6.2 0.0 copy-start.3
  6.2 0.0 copy-start.1
  6.2 2.3 %collective-permute-start.7 = (bf16[2560,256]{1,0:T(8,128)(2,1)}, bf16[2560,256]{1,0:T(8,128)(2,1)S(1)}, u32[]{:S(2)}, u32[]{:S(2)}) collective-permute-start(bf16[2560,256]{1,0:T(8,128)(2,1)} %message.3.refs_4_), channel_id=1, source_target_pairs={{0,2},{2,4},{4,6},{6,8},{8,10},{10,12},{12,14},{1,3},{3,5},{5,7},{... | collective-permute-start | bytes 3932168 | tf_op jit(solution)/shard_map/ppermute | solution.py:489
  8.5 4.1 %message.2.refs_3_ = bf16[2560,256]{1,0:T(8,128)(2,1)} custom-call(bf16[5120,512]{1,0:T(8,128)(2,1)} %refs_2_.1, bf16[2,512,256]{2,1,0:T(8,128)(2,1)} %refs_7_), custom_call_target="tpu_custom_call" | custom-call | flops 1048576 | bytes 1024 | tf_op jit(solution)/shard_map/message/pallas_call | solution.py:95
  12.6 0.0 collective-permute-done
  12.6 4.0 %collective-permute-start.6 = (bf16[2560,256]{1,0:T(8,128)(2,1)}, bf16[2560,256]{1,0:T(8,128)(2,1)S(1)}, u32[]{:S(2)}, u32[]{:S(2)}) collective-permute-start(bf16[2560,256]{1,0:T(8,128)(2,1)} %message.2.refs_3_), channel_id=1, source_target_pairs={{2,0},{4,2},{6,4},{8,6},{10,8},{12,10},{14,12},{3,1},{5,3},{7,5},{... | collective-permute-start | bytes 3932168 | tf_op jit(solution)/shard_map/ppermute | solution.py:489
  16.7 1.6 %collective-permute-start.3 = (bf16[2,1024,256]{2,1,0:T(8,128)(2,1)}, bf16[2,1024,256]{2,1,0:T(8,128)(2,1)}, u32[]{:S(2)}, u32[]{:S(2)}) collective-permute-start(bf16[2,1024,256]{2,1,0:T(8,128)(2,1)} %refs_5_), channel_id=1, source_target_pairs={{0,1},{1,0},{2,3},{3,2},{4,5},{5,4},{6,7},{7,6},{8,9},{9,8},{10,11... | collective-permute-start | bytes 3145736 | tf_op jit(solution)/shard_map/ppermute | solution.py:441
  18.3 2.3 %collective-permute-start.1 = (bf16[80,512]{1,0:T(8,128)(2,1)S(1)}, bf16[80,512]{1,0:T(8,128)(2,1)S(1)}, u32[]{:S(2)}, u32[]{:S(2)}) collective-permute-start(bf16[80,512]{1,0:T(8,128)(2,1)S(1)} %pad_maximum_fusion.2), channel_id=1, source_target_pairs={{0,8},{2,10},{4,12},{6,14},{8,0},{10,2},{12,4},{14,6},{1,9},{3,11}... | collective-permute-start | bytes 245768 | tf_op jit(solution)/shard_map/ppermute | solution.py:446
  20.6 0.3 collective-permute-start.4
  21.0 27.4 %collective-permute-done.1 = bf16[80,512]{1,0:T(8,128)(2,1)S(1)} collective-permute-done((bf16[80,512]{1,0:T(8,128)(2,1)S(1)}, bf16[80,512]{1,0:T(8,128)(2,1)S(1)}, u32[]{:S(2)}, u32[]{:S(2)}) %collective-permute-start.1) | collective-permute-done | bytes 81952 | tf_op jit(solution)/shard_map/ppermute | solution.py:446
  48.3 2.5 %collective-permute-start.5 = (bf16[2,512,256]{2,1,0:T(8,128)(2,1)}, bf16[2,512,256]{2,1,0:T(8,128)(2,1)}, u32[]{:S(2)}, u32[]{:S(2)}) collective-permute-start(bf16[2,512,256]{2,1,0:T(8,128)(2,1)} %refs_7_), channel_id=1, source_target_pairs={{0,1},{1,0},{2,3},{3,2},{4,5},{5,4},{6,7},{7,6},{8,9},{9,8},{10,11... | collective-permute-start | bytes 1572872 | tf_op jit(solution)/shard_map/ppermute | solution.py:441
  50.8 0.1 copy.19
  50.9 0.1 reshape.52
  51.0 0.1 copy.18
  51.1 0.1 mul.15
  51.3 0.1 pad_add_fusion.links
  51.3 5.0 %stage.1 = (bf16[40,128,512]{2,1,0:T(8,128)(2,1)S(1)}, bf16[40,128,160]{2,1,0:T(8,128)(2,1)S(1)}, bf16[2560,512]{1,0:T(8,128)(2,1)S(1)}, bf16[10240,256]{1,0:T(8...) custom-call(s32[1]{0:T(128)} %bitcast.feat_ref, ...), custom_call_target="tpu_custom_call" | custom-call | flops 1048576 | bytes 1024 | tf_op jit(solution)/shard_map/stage/pallas_call | solution.py:166
  56.4 1.9 %collective-permute-start.2 = (bf16[160,512]{1,0:T(8,128)(2,1)S(1)}, bf16[160,512]{1,0:T(8,128)(2,1)S(1)}, u32[]{:S(2)}, u32[]{:S(2)}) collective-permute-start(bf16[160,512]{1,0:T(8,128)(2,1)S(1)} %pad_maximum_fusion.1), channel_id=1, source_target_pairs={{0,4},{2,6},{4,0},{6,2},{8,12},{10,14},{12,8},{14,10},{1,5},{3,7},... | collective-permute-start | bytes 491528 | tf_op jit(solution)/shard_map/ppermute | solution.py:446
  58.3 0.0 collective-permute-done.3.refs_0_
  58.3 1.5 weights.1
  59.8 3.0 %collective-permute-done.2 = bf16[160,512]{1,0:T(8,128)(2,1)S(1)} collective-permute-done((bf16[160,512]{1,0:T(8,128)(2,1)S(1)}, bf16[160,512]{1,0:T(8,128)(2,1)S(1)}, u32[]{:S(2)}, u32[]{:S(2)}) %collective-permute-start.2) | collective-permute-done | bytes 163872 | tf_op jit(solution)/shard_map/ppermute | solution.py:446
  62.8 0.5 coarse_message.1.refs_2_
  63.3 0.7 collective-permute-done.7.refs_5_
  64.0 4.1 %collective-permute-done.6.refs_4_ = bf16[2560,256]{1,0:T(8,128)(2,1)S(1)} collective-permute-done((bf16[2560,256]{1,0:T(8,128)(2,1)}, bf16[2560,256]{1,0:T(8,128)(2,1)S(1)}, u32[]{:S(2)}, u32[]{:S(2)}) %collective-permute-start.6) | collective-permute-done | bytes 1310752 | tf_op jit(solution)/shard_map/ppermute | solution.py:489
  68.1 2.2 %aggregate.4 = (bf16[1280,256]{1,0:T(8,128)(2,1)S(1)}, bf16[1280,256]{1,0:T(8,128)(2,1)S(1)}, bf16[40,256]{1,0:T(8,128)(2,1)S(1)}, bf16[10240,256]{1,0:T(8,128)(2,1)S(1)}) custom-call(s32[1]{0:T(128)} %bitcast.feat_ref, s32[320]{0:T(512)S(1)} %pad_add_fusion.links, ...), custom_call_target="tpu_custom_call", output_to_operand_aliasing={{3}: (8, {})} | custom-call | flops 1048576 | bytes 1024 | tf_op jit(solution)/shard_map/aggregate/pallas_call | solution.py:287
  70.3 0.6 collective-permute-start.8
  70.9 1.8 %aggregate.5 = (bf16[1280,256]{1,0:T(8,128)(2,1)S(1)}, bf16[1280,256]{1,0:T(8,128)(2,1)S(1)}) custom-call(s32[1]{0:T(128)} %bitcast.feat_ref, s32[320]{0:T(512)S(1)} %pad_add_fusion.links, bf16[40,128,512]{2,1,0:T(8,128)(2,1)S(1)} %get-tuple-element.80.refs_0_, bf16[40,128,160]{2,1,0:T(8,128)(2,1)S(1)} %get-tuple-element.81.refs_1_, ...), custom_call_target="tpu_custom_call" | custom-call | flops 1048576 | bytes 1024 | tf_op jit(solution)/shard_map/aggregate/pallas_call | solution.py:287
  72.7 4.4 %node_mid.2 = (bf16[2560,512]{1,0:T(8,128)(2,1)S(1)}, bf16[1280,256]{1,0:T(8,128)(2,1)S(1)}, bf16[1280,256]{1,0:T(8,128)(2,1)S(1)}) custom-call(s32[1]{0:T(128)} %bitcast.feat_ref, bf16[2560,512]{1,0:T(8,128)(2,1)S(1)} %get-tuple-element.73.refs_0_, bf16[1280,256]{1,0:T(8,128)(2,1)S(1)} %get-tuple-element.94.refs_1_, ...), custom_call_target="tpu_custom_call", output_to_operand_aliasing={{0}: (1, {})} | custom-call | flops 1048576 | bytes 1024 | tf_op jit(solution)/shard_map/node_mid/pallas_call | solution.py:399
  77.2 0.3 collective-permute-start.10
  77.5 0.3 collective-permute-start.11
  77.7 3.6 %collective-permute-start.15 = (bf16[1280,256]{1,0:T(8,128)(2,1)S(1)}, bf16[1280,256]{1,0:T(8,128)(2,1)S(1)}, u32[]{:S(2)}, u32[]{:S(2)}) collective-permute-start(bf16[1280,256]{1,0:T(8,128)(2,1)S(1)} %get-tuple-element.104), channel_id=1, source_target_pairs={{2,1},{4,3},{6,5},{8,7},{10,9},{12,11},{14,13},{1,2},{3,4},{5,6},{... | collective-permute-start | bytes 1966088 | tf_op jit(solution)/shard_map/ppermute | solution.py:544
  81.4 2.8 %collective-permute-start.14 = (bf16[1280,256]{1,0:T(8,128)(2,1)S(1)}, bf16[1280,256]{1,0:T(8,128)(2,1)S(1)}, u32[]{:S(2)}, u32[]{:S(2)}) collective-permute-start(bf16[1280,256]{1,0:T(8,128)(2,1)S(1)} %get-tuple-element.112.refs_0_), channel_id=1, source_target_pairs={{2,0},{4,2},{6,4},{8,6},{10,8},{12,10},{14,12},{1,3},{3,5},{5,7},{... | collective-permute-start | bytes 1966088 | tf_op jit(solution)/shard_map/ppermute | solution.py:544
  84.2 4.4 %node_mid.3 = (bf16[2560,512]{1,0:T(8,128)(2,1)S(1)}, bf16[1280,256]{1,0:T(8,128)(2,1)S(1)}, bf16[1280,256]{1,0:T(8,128)(2,1)S(1)}) custom-call(s32[1]{0:T(128)} %bitcast.feat_ref, bf16[2560,512]{1,0:T(8,128)(2,1)S(1)} %get-tuple-element.106.refs_0_, bf16[1280,256]{1,0:T(8,128)(2,1)S(1)} %get-tuple-element.107.refs_1_, ...), custom_call_target="tpu_custom_call", output_to_operand_aliasing={{0}: (1, {})} | custom-call | flops 1048576 | bytes 1024 | tf_op jit(solution)/shard_map/node_mid/pallas_call | solution.py:399
  88.6 0.1 collective-permute-start.13
  88.7 0.5 collective-permute-start.12
  89.2 3.5 %collective-permute-start.20 = (bf16[1280,256]{1,0:T(8,128)(2,1)S(1)}, bf16[1280,256]{1,0:T(8,128)(2,1)S(1)}, u32[]{:S(2)}, u32[]{:S(2)}) collective-permute-start(bf16[1280,256]{1,0:T(8,128)(2,1)S(1)} %get-tuple-element.111), channel_id=1, source_target_pairs={{2,1},{4,3},{6,5},{8,7},{10,9},{12,11},{14,13},{1,2},{3,4},{5,6},{... | collective-permute-start | bytes 1966088 | tf_op jit(solution)/shard_map/ppermute | solution.py:544
  92.7 3.0 %collective-permute-start.19 = (bf16[1280,256]{1,0:T(8,128)(2,1)S(1)}, bf16[1280,256]{1,0:T(8,128)(2,1)S(1)}, u32[]{:S(2)}, u32[]{:S(2)}) collective-permute-start(bf16[1280,256]{1,0:T(8,128)(2,1)S(1)} %get-tuple-element.114.refs_2_), channel_id=1, source_target_pairs={{2,0},{4,2},{6,4},{8,6},{10,8},{12,10},{14,12},{1,3},{3,5},{5,7},{... | collective-permute-start | bytes 1966088 | tf_op jit(solution)/shard_map/ppermute | solution.py:544
  95.7 22.0 %collective-permute-done.15.refs_5_ = bf16[1280,256]{1,0:T(8,128)(2,1)S(1)} collective-permute-done((bf16[1280,256]{1,0:T(8,128)(2,1)S(1)}, bf16[1280,256]{1,0:T(8,128)(2,1)S(1)}, u32[]{:S(2)}, u32[]{:S(2)}) %collective-permute-start.15) | collective-permute-done | bytes 655392 | tf_op jit(solution)/shard_map/ppermute | solution.py:544
  117.7 6.2 %collective-permute-done.14.refs_4_ = bf16[1280,256]{1,0:T(8,128)(2,1)S(1)} collective-permute-done((bf16[1280,256]{1,0:T(8,128)(2,1)S(1)}, bf16[1280,256]{1,0:T(8,128)(2,1)S(1)}, u32[]{:S(2)}, u32[]{:S(2)}) %collective-permute-start.14) | collective-permute-done | bytes 655392 | tf_op jit(solution)/shard_map/ppermute | solution.py:544
  124.0 1.3 collective-permute-start.18
  125.3 1.4 collective-permute-start.16
  126.6 1.3 local_messages.1.refs_6_
  127.9 0.9 collective-permute-done.17
  128.9 1.3 collective-permute-done.16
  130.2 1.6 %node_coarse.1.refs_2_ = f32[320,256]{1,0:T(8,128)S(1)} custom-call(s32[1]{0:T(128)} %bitcast.feat_ref, bf16[320,512]{1,0:T(8,128)(2,1)S(1)} %constant_dynamic-update-slice_fusion.state_ref.refs_0_, bf16[320,512]{1,0:T(8,128)(2,1)S(1)} %pad_maximum_fusion.refs_1_.refs_2_, bf16[320,512]{1,0:T(8,128)(2,1)S(1)} %pad_maximum_fusion.refs_1_.refs_2_, ...), custom_call_target="tpu_custom_call" | custom-call | flops 1048576 | bytes 1024 | tf_op jit(solution)/shard_map/node_coarse/pallas_call | solution.py:399
  131.8 0.3 collective-permute-done.20.refs_5_
  132.1 6.0 %collective-permute-done.19.refs_4_ = bf16[1280,256]{1,0:T(8,128)(2,1)S(1)} collective-permute-done((bf16[1280,256]{1,0:T(8,128)(2,1)S(1)}, bf16[1280,256]{1,0:T(8,128)(2,1)S(1)}, u32[]{:S(2)}, u32[]{:S(2)}) %collective-permute-start.19) | collective-permute-done | bytes 655392 | tf_op jit(solution)/shard_map/ppermute | solution.py:544
  138.0 2.3 %aggregate.6 = (bf16[1280,256]{1,0:T(8,128)(2,1)S(1)}, bf16[1280,256]{1,0:T(8,128)(2,1)S(1)}, bf16[10240,256]{1,0:T(8,128)(2,1)S(1)}) custom-call(s32[1]{0:T(128)} %bitcast.feat_ref, s32[320]{0:T(512)S(1)} %pad_add_fusion.links, bf16[40,128,512]{2,1,0:T(8,128)(2,1)S(1)} %get-tuple-element.80.refs_0_, ...), custom_call_target="tpu_custom_call", output_to_operand_aliasing={{2}: (8, {})} | custom-call | flops 1048576 | bytes 1024 | tf_op jit(solution)/shard_map/aggregate/pallas_call | solution.py:287
  140.3 1.5 collective-permute-start.21
  141.8 1.8 %aggregate.7 = (bf16[1280,256]{1,0:T(8,128)(2,1)S(1)}, bf16[1280,256]{1,0:T(8,128)(2,1)S(1)}) custom-call(s32[1]{0:T(128)} %bitcast.feat_ref, s32[320]{0:T(512)S(1)} %pad_add_fusion.links, bf16[40,128,512]{2,1,0:T(8,128)(2,1)S(1)} %get-tuple-element.80.refs_0_, bf16[40,128,160]{2,1,0:T(8,128)(2,1)S(1)} %get-tuple-element.81.refs_1_, ...), custom_call_target="tpu_custom_call" | custom-call | flops 1048576 | bytes 1024 | tf_op jit(solution)/shard_map/aggregate/pallas_call | solution.py:287
  143.7 0.2 collective-permute-start.22
  143.9 4.2 %node_last.3 = (bf16[1280,512]{1,0:T(8,128)(2,1)S(1)}, bf16[5120,512]{1,0:T(8,128)(2,1)}) custom-call(s32[1]{0:T(128)} %bitcast.feat_ref, bf16[2560,512]{1,0:T(8,128)(2,1)S(1)} %get-tuple-element.109.refs_0_, bf16[1280,256]{1,0:T(8,128)(2,1)S(1)} %get-tuple-element.125.refs_1_, bf16[1280,256]{1,0:T(8,128)(2,1)S(1)} %collective-permute-done.21.refs_2_, ...), custom_call_target="tpu_custom_call" | custom-call | flops 8589934592 | bytes 1024 | tf_op jit(solution)/shard_map/node_last/pallas_call | solution.py:399
  148.1 0.4 collective-permute-start.24
  148.5 2.6 %node_last.4 = (bf16[640,512]{1,0:T(8,128)(2,1)S(1)}, bf16[5120,512]{1,0:T(8,128)(2,1)}) custom-call(s32[1]{0:T(128)} %bitcast.feat_ref, bf16[2560,512]{1,0:T(8,128)(2,1)S(1)} %get-tuple-element.109.refs_0_, bf16[1280,256]{1,0:T(8,128)(2,1)S(1)} %get-tuple-element.120.refs_1_, ...), custom_call_target="tpu_custom_call", output_to_operand_aliasing={{1}: (8, {})} | custom-call | flops 8589934592 | bytes 1024 | tf_op jit(solution)/shard_map/node_last/pallas_call | solution.py:399
  151.1 0.3 collective-permute-start.23
  151.4 2.6 %node_last.5 = (bf16[640,512]{1,0:T(8,128)(2,1)S(1)}, bf16[5120,512]{1,0:T(8,128)(2,1)}) custom-call(s32[1]{0:T(128)} %bitcast.feat_ref, bf16[2560,512]{1,0:T(8,128)(2,1)S(1)} %get-tuple-element.109.refs_0_, bf16[1280,256]{1,0:T(8,128)(2,1)S(1)} %get-tuple-element.120.refs_1_, ...), custom_call_target="tpu_custom_call", output_to_operand_aliasing={{1}: (9, {})} | custom-call | flops 8589934592 | bytes 1024 | tf_op jit(solution)/shard_map/node_last/pallas_call | solution.py:399
  154.0 0.4 collective-permute-start.25
  154.4 1.8 %collective-permute-done.25.refs_1_ = bf16[640,512]{1,0:T(8,128)(2,1)S(1)} collective-permute-done((bf16[640,512]{1,0:T(8,128)(2,1)S(1)}, bf16[640,512]{1,0:T(8,128)(2,1)S(1)}, u32[]{:S(2)}, u32[]{:S(2)}) %collective-permute-start.25) | collective-permute-done | bytes 655392 | tf_op jit(solution)/shard_map/ppermute | solution.py:441
  156.2 1.1 assemble.1
  (30 shorter events, 0.1 us)
Async XLA Ops:
  0.8 11.8 %collective-permute-start = (bf16[40,512]{1,0:T(8,128)(2,1)S(1)}, bf16[40,512]{1,0:T(8,128)(2,1)S(1)}, u32[]{:S(2)}, u32[]{:S(2)}) collective-permute-start(bf16[40,512]{1,0:T(8,128)(2,1)S(1)} %slice.3), channel_id=1, source_target_pairs={{0,2},{2,0},{4,6},{6,4},{8,10},{10,8},{12,14},{14,12},{1,3},{3,1},... | collective-permute-start | bytes 122888 | tf_op jit(solution)/shard_map/ppermute | solution.py:446
  6.2 14.5 %copy-start = (bf16[2,256,512]{2,1,0:T(8,128)(2,1)S(1)}, bf16[2,256,512]{2,1,0:T(8,128)(2,1)}, u32[]{:S(2)}) copy-start(bf16[2,256,512]{2,1,0:T(8,128)(2,1)} %refs_6_) | copy-start | bytes 1572868
  6.2 44.7 %copy-start.2 = (s32[40,4]{0,1:T(4,128)S(1)}, s32[40,4]{0,1:T(4,128)}, u32[]{:S(2)}) copy-start(s32[40,4]{0,1:T(4,128)} %param.13) | copy-start | bytes 1924
  6.2 44.7 %copy-start.3 = (s32[40,4]{0,1:T(4,128)S(1)}, s32[40,4]{0,1:T(4,128)}, u32[]{:S(2)}) copy-start(s32[40,4]{0,1:T(4,128)} %param.12) | copy-start | bytes 1924
  6.2 45.1 %copy-start.1 = (s32[5120]{0:T(1024)S(1)}, s32[5120]{0:T(1024)}, u32[]{:S(2)}) copy-start(s32[5120]{0:T(1024)} %param.14) | copy-start | bytes 61444
  6.2 57.8 %collective-permute-start.7 = (bf16[2560,256]{1,0:T(8,128)(2,1)}, bf16[2560,256]{1,0:T(8,128)(2,1)S(1)}, u32[]{:S(2)}, u32[]{:S(2)}) collective-permute-start(bf16[2560,256]{1,0:T(8,128)(2,1)} %message.3.refs_4_), channel_id=1, source_target_pairs={{0,2},{2,4},{4,6},{6,8},{8,10},{10,12},{12,14},{1,3},{3,5},{5,7},{... | collective-permute-start | bytes 3932168 | tf_op jit(solution)/shard_map/ppermute | solution.py:489
  12.6 55.5 %collective-permute-start.6 = (bf16[2560,256]{1,0:T(8,128)(2,1)}, bf16[2560,256]{1,0:T(8,128)(2,1)S(1)}, u32[]{:S(2)}, u32[]{:S(2)}) collective-permute-start(bf16[2560,256]{1,0:T(8,128)(2,1)} %message.2.refs_3_), channel_id=1, source_target_pairs={{2,0},{4,2},{6,4},{8,6},{10,8},{12,10},{14,12},{3,1},{5,3},{7,5},{... | collective-permute-start | bytes 3932168 | tf_op jit(solution)/shard_map/ppermute | solution.py:489
  16.7 41.6 %collective-permute-start.3 = (bf16[2,1024,256]{2,1,0:T(8,128)(2,1)}, bf16[2,1024,256]{2,1,0:T(8,128)(2,1)}, u32[]{:S(2)}, u32[]{:S(2)}) collective-permute-start(bf16[2,1024,256]{2,1,0:T(8,128)(2,1)} %refs_5_), channel_id=1, source_target_pairs={{0,1},{1,0},{2,3},{3,2},{4,5},{5,4},{6,7},{7,6},{8,9},{9,8},{10,11... | collective-permute-start | bytes 3145736 | tf_op jit(solution)/shard_map/ppermute | solution.py:441
  18.3 30.0 %collective-permute-start.1 = (bf16[80,512]{1,0:T(8,128)(2,1)S(1)}, bf16[80,512]{1,0:T(8,128)(2,1)S(1)}, u32[]{:S(2)}, u32[]{:S(2)}) collective-permute-start(bf16[80,512]{1,0:T(8,128)(2,1)S(1)} %pad_maximum_fusion.2), channel_id=1, source_target_pairs={{0,8},{2,10},{4,12},{6,14},{8,0},{10,2},{12,4},{14,6},{1,9},{3,11}... | collective-permute-start | bytes 245768 | tf_op jit(solution)/shard_map/ppermute | solution.py:446
  20.6 35.7 %collective-permute-start.4 = (bf16[2,256,512]{2,1,0:T(8,128)(2,1)S(1)}, bf16[2,256,512]{2,1,0:T(8,128)(2,1)}, u32[]{:S(2)}, u32[]{:S(2)}) collective-permute-start(bf16[2,256,512]{2,1,0:T(8,128)(2,1)S(1)} %copy-done), channel_id=1, source_target_pairs={{0,1},{1,0},{2,3},{3,2},{4,5},{5,4},{6,7},{7,6},{8,9},{9,8},{10,11... | collective-permute-start | bytes 1572872 | tf_op jit(solution)/shard_map/ppermute | solution.py:441
  48.3 9.9 %collective-permute-start.5 = (bf16[2,512,256]{2,1,0:T(8,128)(2,1)}, bf16[2,512,256]{2,1,0:T(8,128)(2,1)}, u32[]{:S(2)}, u32[]{:S(2)}) collective-permute-start(bf16[2,512,256]{2,1,0:T(8,128)(2,1)} %refs_7_), channel_id=1, source_target_pairs={{0,1},{1,0},{2,3},{3,2},{4,5},{5,4},{6,7},{7,6},{8,9},{9,8},{10,11... | collective-permute-start | bytes 1572872 | tf_op jit(solution)/shard_map/ppermute | solution.py:441
  56.4 6.5 %collective-permute-start.2 = (bf16[160,512]{1,0:T(8,128)(2,1)S(1)}, bf16[160,512]{1,0:T(8,128)(2,1)S(1)}, u32[]{:S(2)}, u32[]{:S(2)}) collective-permute-start(bf16[160,512]{1,0:T(8,128)(2,1)S(1)} %pad_maximum_fusion.1), channel_id=1, source_target_pairs={{0,4},{2,6},{4,0},{6,2},{8,12},{10,14},{12,8},{14,10},{1,5},{3,7},... | collective-permute-start | bytes 491528 | tf_op jit(solution)/shard_map/ppermute | solution.py:446
  70.3 2.4 %collective-permute-start.8 = (bf16[1280,256]{1,0:T(8,128)(2,1)S(1)}, bf16[1280,256]{1,0:T(8,128)(2,1)S(1)}, u32[]{:S(2)}, u32[]{:S(2)}) collective-permute-start(bf16[1280,256]{1,0:T(8,128)(2,1)S(1)} %get-tuple-element.90), channel_id=1, source_target_pairs={{0,1},{1,0},{2,3},{3,2},{4,5},{5,4},{6,7},{7,6},{8,9},{9,8},{10,11... | collective-permute-start | bytes 1966088 | tf_op jit(solution)/shard_map/ppermute | solution.py:441
  70.9 6.3 %collective-permute-start.9 = (bf16[40,256]{1,0:T(8,128)(2,1)S(1)}, bf16[40,256]{1,0:T(8,128)(2,1)S(1)}, u32[]{:S(2)}, u32[]{:S(2)}) collective-permute-start(bf16[40,256]{1,0:T(8,128)(2,1)S(1)} %get-tuple-element.103), channel_id=1, source_target_pairs={{0,2},{2,0},{4,6},{6,4},{8,10},{10,8},{12,14},{14,12},{1,3},{3,1},... | collective-permute-start | bytes 61448 | tf_op jit(solution)/shard_map/ppermute | solution.py:446
  77.2 7.0 %collective-permute-start.10 = (bf16[1280,256]{1,0:T(8,128)(2,1)S(1)}, bf16[1280,256]{1,0:T(8,128)(2,1)S(1)}, u32[]{:S(2)}, u32[]{:S(2)}) collective-permute-start(bf16[1280,256]{1,0:T(8,128)(2,1)S(1)} %get-tuple-element.104), channel_id=1, source_target_pairs={{0,1},{1,0},{2,3},{3,2},{4,5},{5,4},{6,7},{7,6},{8,9},{9,8},{10,11... | collective-permute-start | bytes 1966088 | tf_op jit(solution)/shard_map/ppermute | solution.py:441
  77.5 6.7 %collective-permute-start.11 = (bf16[1280,256]{1,0:T(8,128)(2,1)S(1)}, bf16[1280,256]{1,0:T(8,128)(2,1)S(1)}, u32[]{:S(2)}, u32[]{:S(2)}) collective-permute-start(bf16[1280,256]{1,0:T(8,128)(2,1)S(1)} %get-tuple-element.108), channel_id=1, source_target_pairs={{0,1},{1,0},{2,3},{3,2},{4,5},{5,4},{6,7},{7,6},{8,9},{9,8},{10,11... | collective-permute-start | bytes 1966088 | tf_op jit(solution)/shard_map/ppermute | solution.py:441
  77.7 40.0 %collective-permute-start.15 = (bf16[1280,256]{1,0:T(8,128)(2,1)S(1)}, bf16[1280,256]{1,0:T(8,128)(2,1)S(1)}, u32[]{:S(2)}, u32[]{:S(2)}) collective-permute-start(bf16[1280,256]{1,0:T(8,128)(2,1)S(1)} %get-tuple-element.104), channel_id=1, source_target_pairs={{2,1},{4,3},{6,5},{8,7},{10,9},{12,11},{14,13},{1,2},{3,4},{5,6},{... | collective-permute-start | bytes 1966088 | tf_op jit(solution)/shard_map/ppermute | solution.py:544
  81.4 42.6 %collective-permute-start.14 = (bf16[1280,256]{1,0:T(8,128)(2,1)S(1)}, bf16[1280,256]{1,0:T(8,128)(2,1)S(1)}, u32[]{:S(2)}, u32[]{:S(2)}) collective-permute-start(bf16[1280,256]{1,0:T(8,128)(2,1)S(1)} %get-tuple-element.112.refs_0_), channel_id=1, source_target_pairs={{2,0},{4,2},{6,4},{8,6},{10,8},{12,10},{14,12},{1,3},{3,5},{5,7},{... | collective-permute-start | bytes 1966088 | tf_op jit(solution)/shard_map/ppermute | solution.py:544
  88.6 35.4 %collective-permute-start.13 = (bf16[1280,256]{1,0:T(8,128)(2,1)S(1)}, bf16[1280,256]{1,0:T(8,128)(2,1)S(1)}, u32[]{:S(2)}, u32[]{:S(2)}) collective-permute-start(bf16[1280,256]{1,0:T(8,128)(2,1)S(1)} %get-tuple-element.111), channel_id=1, source_target_pairs={{0,1},{1,0},{2,3},{3,2},{4,5},{5,4},{6,7},{7,6},{8,9},{9,8},{10,11... | collective-permute-start | bytes 1966088 | tf_op jit(solution)/shard_map/ppermute | solution.py:441
  88.7 4.0 %collective-permute-start.12 = (bf16[80,256]{1,0:T(8,128)(2,1)S(1)}, bf16[80,256]{1,0:T(8,128)(2,1)S(1)}, u32[]{:S(2)}, u32[]{:S(2)}) collective-permute-start(bf16[80,256]{1,0:T(8,128)(2,1)S(1)} %constant_dynamic-update-slice_fusion.3), channel_id=1, source_target_pairs={{0,1},{1,0},{2,3},{3,2},{4,5},{5,4},{6,7},{7,6},{8,9},{9,8},{10,11... | collective-permute-start | bytes 122888 | tf_op jit(solution)/shard_map/ppermute | solution.py:441
  89.2 42.9 %collective-permute-start.20 = (bf16[1280,256]{1,0:T(8,128)(2,1)S(1)}, bf16[1280,256]{1,0:T(8,128)(2,1)S(1)}, u32[]{:S(2)}, u32[]{:S(2)}) collective-permute-start(bf16[1280,256]{1,0:T(8,128)(2,1)S(1)} %get-tuple-element.111), channel_id=1, source_target_pairs={{2,1},{4,3},{6,5},{8,7},{10,9},{12,11},{14,13},{1,2},{3,4},{5,6},{... | collective-permute-start | bytes 1966088 | tf_op jit(solution)/shard_map/ppermute | solution.py:544
  92.7 45.4 %collective-permute-start.19 = (bf16[1280,256]{1,0:T(8,128)(2,1)S(1)}, bf16[1280,256]{1,0:T(8,128)(2,1)S(1)}, u32[]{:S(2)}, u32[]{:S(2)}) collective-permute-start(bf16[1280,256]{1,0:T(8,128)(2,1)S(1)} %get-tuple-element.114.refs_2_), channel_id=1, source_target_pairs={{2,0},{4,2},{6,4},{8,6},{10,8},{12,10},{14,12},{1,3},{3,5},{5,7},{... | collective-permute-start | bytes 1966088 | tf_op jit(solution)/shard_map/ppermute | solution.py:544
  124.0 3.9 %collective-permute-start.18 = (bf16[80,512]{1,0:T(8,128)(2,1)S(1)}, bf16[80,512]{1,0:T(8,128)(2,1)S(1)}, u32[]{:S(2)}, u32[]{:S(2)}) collective-permute-start(bf16[80,512]{1,0:T(8,128)(2,1)S(1)} %pad_maximum_fusion.3), channel_id=1, source_target_pairs={{0,12},{2,14},{4,8},{6,10},{8,4},{10,6},{12,0},{14,2},{1,13},{3,15... | collective-permute-start | bytes 245768 | tf_op jit(solution)/shard_map/ppermute | solution.py:446
  125.3 3.6 %collective-permute-start.17 = (bf16[80,512]{1,0:T(8,128)(2,1)S(1)}, bf16[80,512]{1,0:T(8,128)(2,1)S(1)}, u32[]{:S(2)}, u32[]{:S(2)}) collective-permute-start(bf16[80,512]{1,0:T(8,128)(2,1)S(1)} %pad_maximum_fusion.3), channel_id=1, source_target_pairs={{0,4},{2,6},{4,0},{6,2},{8,12},{10,14},{12,8},{14,10},{1,5},{3,7},... | collective-permute-start | bytes 245768 | tf_op jit(solution)/shard_map/ppermute | solution.py:446
  125.3 4.9 %collective-permute-start.16 = (bf16[80,512]{1,0:T(8,128)(2,1)S(1)}, bf16[80,512]{1,0:T(8,128)(2,1)S(1)}, u32[]{:S(2)}, u32[]{:S(2)}) collective-permute-start(bf16[80,512]{1,0:T(8,128)(2,1)S(1)} %pad_maximum_fusion.3), channel_id=1, source_target_pairs={{0,8},{2,10},{4,12},{6,14},{8,0},{10,2},{12,4},{14,6},{1,9},{3,11}... | collective-permute-start | bytes 245768 | tf_op jit(solution)/shard_map/ppermute | solution.py:446
  140.3 3.4 %collective-permute-start.21 = (bf16[1280,256]{1,0:T(8,128)(2,1)S(1)}, bf16[1280,256]{1,0:T(8,128)(2,1)S(1)}, u32[]{:S(2)}, u32[]{:S(2)}) collective-permute-start(bf16[1280,256]{1,0:T(8,128)(2,1)S(1)} %get-tuple-element.121), channel_id=1, source_target_pairs={{0,1},{1,0},{2,3},{3,2},{4,5},{5,4},{6,7},{7,6},{8,9},{9,8},{10,11... | collective-permute-start | bytes 1966088 | tf_op jit(solution)/shard_map/ppermute | solution.py:441
  143.7 4.9 %collective-permute-start.22 = (bf16[1280,256]{1,0:T(8,128)(2,1)S(1)}, bf16[1280,256]{1,0:T(8,128)(2,1)S(1)}, u32[]{:S(2)}, u32[]{:S(2)}) collective-permute-start(bf16[1280,256]{1,0:T(8,128)(2,1)S(1)} %get-tuple-element.124), channel_id=1, source_target_pairs={{0,1},{1,0},{2,3},{3,2},{4,5},{5,4},{6,7},{7,6},{8,9},{9,8},{10,11... | collective-permute-start | bytes 1966088 | tf_op jit(solution)/shard_map/ppermute | solution.py:441
  148.1 3.3 %collective-permute-start.24 = (bf16[1280,512]{1,0:T(8,128)(2,1)S(1)}, bf16[1280,512]{1,0:T(8,128)(2,1)S(1)}, u32[]{:S(2)}, u32[]{:S(2)}) collective-permute-start(bf16[1280,512]{1,0:T(8,128)(2,1)S(1)} %get-tuple-element.129), channel_id=1, source_target_pairs={{0,1},{1,0},{2,3},{3,2},{4,5},{5,4},{6,7},{7,6},{8,9},{9,8},{10,11... | collective-permute-start | bytes 3932168 | tf_op jit(solution)/shard_map/ppermute | solution.py:441
  151.1 3.3 %collective-permute-start.23 = (bf16[640,512]{1,0:T(8,128)(2,1)S(1)}, bf16[640,512]{1,0:T(8,128)(2,1)S(1)}, u32[]{:S(2)}, u32[]{:S(2)}) collective-permute-start(bf16[640,512]{1,0:T(8,128)(2,1)S(1)} %get-tuple-element.128), channel_id=1, source_target_pairs={{0,1},{1,0},{2,3},{3,2},{4,5},{5,4},{6,7},{7,6},{8,9},{9,8},{10,11... | collective-permute-start | bytes 1966088 | tf_op jit(solution)/shard_map/ppermute | solution.py:441
  154.0 2.2 %collective-permute-start.25 = (bf16[640,512]{1,0:T(8,128)(2,1)S(1)}, bf16[640,512]{1,0:T(8,128)(2,1)S(1)}, u32[]{:S(2)}, u32[]{:S(2)}) collective-permute-start(bf16[640,512]{1,0:T(8,128)(2,1)S(1)} %get-tuple-element.131), channel_id=1, source_target_pairs={{0,1},{1,0},{2,3},{3,2},{4,5},{5,4},{6,7},{7,6},{8,9},{9,8},{10,11... | collective-permute-start | bytes 1966088 | tf_op jit(solution)/shard_map/ppermute | solution.py:441

commit v10 on v9

--- a/solution.py
+++ b/solution.py
@@ -12,9 +12,9 @@
 HALO_BLK = 20
 MID_BLOCKS = (10, 10)
 LAST_BLOCKS = (10, 10)
-LAST_ROWS = ((0, 0, 10), (1, 0, 5), (1, 5, 5))
+LAST_ROWS = ((0, 0, 10), (1, 0, 7), (1, 7, 3))
 MESSAGE_ROWS = ((0, 20), (20, 20))
-MESSAGE_TILE = 640
+MESSAGE_TILES = (512, 640, 640, 512, 256)
 NODE_SPLIT = 2
 F32 = jnp.float32
 BF16 = jnp.bfloat16
@@ -66,9 +66,8 @@
     out_ref[...] = silu(dot(normed, weight_ref[0])).astype(BF16).astype(F32)
 
 
-def message_kernel(start, tile, state, weight, out, state_buf, weight_buf, out_ref, sems):
-    rows = out_ref.shape[0]
-    tiles = [(at, tile) for at in range(0, rows, tile)]
+def message_kernel(start, sizes, state, weight, out, state_buf, weight_buf, out_ref, sems):
+    tiles = [(sum(sizes[:pos]), size) for pos, size in enumerate(sizes)]
     pairs = [(state.at[pl.ds(start + at, size)], state_buf.at[pl.ds(at, size)]) for at, size in tiles]
     copies = run_copies(pairs[:1] + [(weight.at[0], weight_buf)] + pairs[1:], sems)
     weight_copy = copies.pop(1)
@@ -90,10 +89,11 @@
     wait_all(copies[len(tiles) :])
 
 
-def message_call(state, weight, start, rows, tile):
+def message_call(state, weight, start, rows, sizes):
+    assert sum(sizes) == rows
     width, columns = weight.shape[1:]
     return pl.pallas_call(
-        functools.partial(message_kernel, start, tile),
+        functools.partial(message_kernel, start, sizes),
         in_specs=[IN_HBM, IN_HBM],
         out_specs=IN_HBM,
         out_shape=jax.ShapeDtypeStruct((rows, columns), BF16),
@@ -101,7 +101,7 @@
             pltpu.VMEM((rows, width), BF16),
             pltpu.VMEM((width, columns), BF16),
             pltpu.VMEM((rows, columns), BF16),
-            pltpu.SemaphoreType.DMA((1 + 2 * (rows // tile),)),
+            pltpu.SemaphoreType.DMA((1 + 2 * len(sizes),)),
         ],
         compiler_params=params(56),
         cost_estimate=SMALL,
@@ -482,7 +482,7 @@
     sends = []
     halo = []
     for first, count in MESSAGE_ROWS:
-        message = message_call(node_state, w_msg, first * block, count * block, MESSAGE_TILE)
+        message = message_call(node_state, w_msg, first * block, count * block, MESSAGE_TILES)
         if not sends:
             message, held = barrier((message, held))
         sends.append(message)

time: 158 us -> 158 us (level)
  transfers between devices with their start and end apart: 26 -> 26, of which waited for: 11 -> 11; matrix products, arithmetic and copies ran while one was open for 0% -> 0% of each run, Pallas kernels for 25% -> 26%
where the time goes in v10:
time: 158 us; the launch traced here: 157 us
  waiting for transfers between devices  73.2 us (46%)
  Pallas kernels  45.8 us (29%)
  starting transfers between devices  36.2 us (23%)
    ppermute x7, waiting for transfers between devices, fetch(): lax.ppermute(held, 'patch', [(pos, pos ^ stride) for pos in range(count)])  32.6 us
    ppermute x2, waiting for transfers between devices, shards(): lax.ppermute(other, ('patch', 'feat'), other_patch)  22.3 us
    pallas_call x6, Pallas kernels, node_call(): pl.pallas_call(functools.partial(node_kernel, mode, layer, start, offset,...  19.9 us
    ppermute x2, waiting for transfers between devices, shards(): lax.ppermute(own, ('patch', 'feat'), own_patch)  12.2 us
    ppermute x13, starting transfers between devices, swap_feat(): return lax.ppermute(array, 'feat', [(0, 1), (1, 0)])  8.93 us
    pallas_call x2, Pallas kernels, message_call(): pl.pallas_call(functools.partial(message_kernel, start, sizes), in_specs=...  8.44 us
    pallas_call x4, Pallas kernels, aggregate_call(): pl.pallas_call(functools.partial(aggregate_kernel, places, start), grid_s...  8.12 us
    ppermute x7, starting transfers between devices, fetch(): lax.ppermute(held, 'patch', [(pos, pos ^ stride) for pos in range(count)])  8.1 us
  transfers between devices with their start and end apart: 26, of which 11 were waited for; matrix products, arithmetic and copies ran while one was open for 0% of the time, Pallas kernels for 26%

profile of v10, /device:TPU:9, one launch (start us, length us, event | category | flops | bytes accessed | tf_op | source)
XLA Modules:
  0.0 157.2 jit_solution(9079634211467012047)
XLA Ops:
  0.0 0.8 slice.3
  0.8 1.2 collective-permute-start
  2.0 4.2 %message.3.refs_4_ = bf16[2560,256]{1,0:T(8,128)(2,1)} custom-call(bf16[5120,512]{1,0:T(8,128)(2,1)} %refs_2_.1, bf16[2,512,256]{2,1,0:T(8,128)(2,1)} %refs_7_), custom_call_target="tpu_custom_call" | custom-call | flops 1048576 | bytes 1024 | tf_op jit(solution)/shard_map/message/pallas_call | solution.py:95
  6.2 0.0 copy-start
  6.3 0.0 copy-start.2
  6.3 0.0 copy-start.3
  6.3 0.0 copy-start.1
  6.3 2.3 %collective-permute-start.7 = (bf16[2560,256]{1,0:T(8,128)(2,1)}, bf16[2560,256]{1,0:T(8,128)(2,1)S(1)}, u32[]{:S(2)}, u32[]{:S(2)}) collective-permute-start(bf16[2560,256]{1,0:T(8,128)(2,1)} %message.3.refs_4_), channel_id=1, source_target_pairs={{0,2},{2,4},{4,6},{6,8},{8,10},{10,12},{12,14},{1,3},{3,5},{5,7},{... | collective-permute-start | bytes 3932168 | tf_op jit(solution)/shard_map/ppermute | solution.py:489
  8.6 4.2 %message.2.refs_3_ = bf16[2560,256]{1,0:T(8,128)(2,1)} custom-call(bf16[5120,512]{1,0:T(8,128)(2,1)} %refs_2_.1, bf16[2,512,256]{2,1,0:T(8,128)(2,1)} %refs_7_), custom_call_target="tpu_custom_call" | custom-call | flops 1048576 | bytes 1024 | tf_op jit(solution)/shard_map/message/pallas_call | solution.py:95
  12.8 0.0 collective-permute-done
  12.8 4.0 %collective-permute-start.6 = (bf16[2560,256]{1,0:T(8,128)(2,1)}, bf16[2560,256]{1,0:T(8,128)(2,1)S(1)}, u32[]{:S(2)}, u32[]{:S(2)}) collective-permute-start(bf16[2560,256]{1,0:T(8,128)(2,1)} %message.2.refs_3_), channel_id=1, source_target_pairs={{2,0},{4,2},{6,4},{8,6},{10,8},{12,10},{14,12},{3,1},{5,3},{7,5},{... | collective-permute-start | bytes 3932168 | tf_op jit(solution)/shard_map/ppermute | solution.py:489
  16.9 1.6 %collective-permute-start.3 = (bf16[2,1024,256]{2,1,0:T(8,128)(2,1)}, bf16[2,1024,256]{2,1,0:T(8,128)(2,1)}, u32[]{:S(2)}, u32[]{:S(2)}) collective-permute-start(bf16[2,1024,256]{2,1,0:T(8,128)(2,1)} %refs_5_), channel_id=1, source_target_pairs={{0,1},{1,0},{2,3},{3,2},{4,5},{5,4},{6,7},{7,6},{8,9},{9,8},{10,11... | collective-permute-start | bytes 3145736 | tf_op jit(solution)/shard_map/ppermute | solution.py:441
  18.5 2.3 %collective-permute-start.1 = (bf16[80,512]{1,0:T(8,128)(2,1)S(1)}, bf16[80,512]{1,0:T(8,128)(2,1)S(1)}, u32[]{:S(2)}, u32[]{:S(2)}) collective-permute-start(bf16[80,512]{1,0:T(8,128)(2,1)S(1)} %pad_maximum_fusion.2), channel_id=1, source_target_pairs={{0,8},{2,10},{4,12},{6,14},{8,0},{10,2},{12,4},{14,6},{1,9},{3,11}... | collective-permute-start | bytes 245768 | tf_op jit(solution)/shard_map/ppermute | solution.py:446
  20.8 0.3 collective-permute-start.4
  21.1 27.4 %collective-permute-done.1 = bf16[80,512]{1,0:T(8,128)(2,1)S(1)} collective-permute-done((bf16[80,512]{1,0:T(8,128)(2,1)S(1)}, bf16[80,512]{1,0:T(8,128)(2,1)S(1)}, u32[]{:S(2)}, u32[]{:S(2)}) %collective-permute-start.1) | collective-permute-done | bytes 81952 | tf_op jit(solution)/shard_map/ppermute | solution.py:446
  48.5 2.5 %collective-permute-start.5 = (bf16[2,512,256]{2,1,0:T(8,128)(2,1)}, bf16[2,512,256]{2,1,0:T(8,128)(2,1)}, u32[]{:S(2)}, u32[]{:S(2)}) collective-permute-start(bf16[2,512,256]{2,1,0:T(8,128)(2,1)} %refs_7_), channel_id=1, source_target_pairs={{0,1},{1,0},{2,3},{3,2},{4,5},{5,4},{6,7},{7,6},{8,9},{9,8},{10,11... | collective-permute-start | bytes 1572872 | tf_op jit(solution)/shard_map/ppermute | solution.py:441
  51.0 0.1 copy.19
  51.1 0.1 reshape.52
  51.2 0.1 copy.18
  51.3 0.1 mul.15
  51.4 0.1 pad_add_fusion.links
  51.5 5.0 %stage.1 = (bf16[40,128,512]{2,1,0:T(8,128)(2,1)S(1)}, bf16[40,128,160]{2,1,0:T(8,128)(2,1)S(1)}, bf16[2560,512]{1,0:T(8,128)(2,1)S(1)}, bf16[10240,256]{1,0:T(8...) custom-call(s32[1]{0:T(128)} %bitcast.feat_ref, ...), custom_call_target="tpu_custom_call" | custom-call | flops 1048576 | bytes 1024 | tf_op jit(solution)/shard_map/stage/pallas_call | solution.py:166
  56.5 0.0 collective-permute-done.4.refs_1_
  56.5 1.9 %collective-permute-start.2 = (bf16[160,512]{1,0:T(8,128)(2,1)S(1)}, bf16[160,512]{1,0:T(8,128)(2,1)S(1)}, u32[]{:S(2)}, u32[]{:S(2)}) collective-permute-start(bf16[160,512]{1,0:T(8,128)(2,1)S(1)} %pad_maximum_fusion.1), channel_id=1, source_target_pairs={{0,4},{2,6},{4,0},{6,2},{8,12},{10,14},{12,8},{14,10},{1,5},{3,7},... | collective-permute-start | bytes 491528 | tf_op jit(solution)/shard_map/ppermute | solution.py:446
  58.5 1.5 weights.1
  60.0 3.0 %collective-permute-done.2 = bf16[160,512]{1,0:T(8,128)(2,1)S(1)} collective-permute-done((bf16[160,512]{1,0:T(8,128)(2,1)S(1)}, bf16[160,512]{1,0:T(8,128)(2,1)S(1)}, u32[]{:S(2)}, u32[]{:S(2)}) %collective-permute-start.2) | collective-permute-done | bytes 163872 | tf_op jit(solution)/shard_map/ppermute | solution.py:446
  63.0 0.5 coarse_message.1.refs_2_
  63.5 0.6 collective-permute-done.7.refs_5_
  64.1 4.1 %collective-permute-done.6.refs_4_ = bf16[2560,256]{1,0:T(8,128)(2,1)S(1)} collective-permute-done((bf16[2560,256]{1,0:T(8,128)(2,1)}, bf16[2560,256]{1,0:T(8,128)(2,1)S(1)}, u32[]{:S(2)}, u32[]{:S(2)}) %collective-permute-start.6) | collective-permute-done | bytes 1310752 | tf_op jit(solution)/shard_map/ppermute | solution.py:489
  68.2 2.2 %aggregate.4 = (bf16[1280,256]{1,0:T(8,128)(2,1)S(1)}, bf16[1280,256]{1,0:T(8,128)(2,1)S(1)}, bf16[40,256]{1,0:T(8,128)(2,1)S(1)}, bf16[10240,256]{1,0:T(8,128)(2,1)S(1)}) custom-call(s32[1]{0:T(128)} %bitcast.feat_ref, s32[320]{0:T(512)S(1)} %pad_add_fusion.links, ...), custom_call_target="tpu_custom_call", output_to_operand_aliasing={{3}: (8, {})} | custom-call | flops 1048576 | bytes 1024 | tf_op jit(solution)/shard_map/aggregate/pallas_call | solution.py:287
  70.4 0.6 collective-permute-start.8
  71.0 1.8 %aggregate.5 = (bf16[1280,256]{1,0:T(8,128)(2,1)S(1)}, bf16[1280,256]{1,0:T(8,128)(2,1)S(1)}) custom-call(s32[1]{0:T(128)} %bitcast.feat_ref, s32[320]{0:T(512)S(1)} %pad_add_fusion.links, bf16[40,128,512]{2,1,0:T(8,128)(2,1)S(1)} %get-tuple-element.80.refs_0_, bf16[40,128,160]{2,1,0:T(8,128)(2,1)S(1)} %get-tuple-element.81.refs_1_, ...), custom_call_target="tpu_custom_call" | custom-call | flops 1048576 | bytes 1024 | tf_op jit(solution)/shard_map/aggregate/pallas_call | solution.py:287
  72.8 4.4 %node_mid.2 = (bf16[2560,512]{1,0:T(8,128)(2,1)S(1)}, bf16[1280,256]{1,0:T(8,128)(2,1)S(1)}, bf16[1280,256]{1,0:T(8,128)(2,1)S(1)}) custom-call(s32[1]{0:T(128)} %bitcast.feat_ref, bf16[2560,512]{1,0:T(8,128)(2,1)S(1)} %get-tuple-element.73.refs_0_, bf16[1280,256]{1,0:T(8,128)(2,1)S(1)} %get-tuple-element.94.refs_1_, ...), custom_call_target="tpu_custom_call", output_to_operand_aliasing={{0}: (1, {})} | custom-call | flops 1048576 | bytes 1024 | tf_op jit(solution)/shard_map/node_mid/pallas_call | solution.py:399
  77.3 0.3 collective-permute-start.10
  77.6 0.3 collective-permute-start.11
  77.8 3.6 %collective-permute-start.15 = (bf16[1280,256]{1,0:T(8,128)(2,1)S(1)}, bf16[1280,256]{1,0:T(8,128)(2,1)S(1)}, u32[]{:S(2)}, u32[]{:S(2)}) collective-permute-start(bf16[1280,256]{1,0:T(8,128)(2,1)S(1)} %get-tuple-element.104), channel_id=1, source_target_pairs={{2,1},{4,3},{6,5},{8,7},{10,9},{12,11},{14,13},{1,2},{3,4},{5,6},{... | collective-permute-start | bytes 1966088 | tf_op jit(solution)/shard_map/ppermute | solution.py:544
  81.5 2.8 %collective-permute-start.14 = (bf16[1280,256]{1,0:T(8,128)(2,1)S(1)}, bf16[1280,256]{1,0:T(8,128)(2,1)S(1)}, u32[]{:S(2)}, u32[]{:S(2)}) collective-permute-start(bf16[1280,256]{1,0:T(8,128)(2,1)S(1)} %get-tuple-element.112.refs_0_), channel_id=1, source_target_pairs={{2,0},{4,2},{6,4},{8,6},{10,8},{12,10},{14,12},{1,3},{3,5},{5,7},{... | collective-permute-start | bytes 1966088 | tf_op jit(solution)/shard_map/ppermute | solution.py:544
  84.3 4.4 %node_mid.3 = (bf16[2560,512]{1,0:T(8,128)(2,1)S(1)}, bf16[1280,256]{1,0:T(8,128)(2,1)S(1)}, bf16[1280,256]{1,0:T(8,128)(2,1)S(1)}) custom-call(s32[1]{0:T(128)} %bitcast.feat_ref, bf16[2560,512]{1,0:T(8,128)(2,1)S(1)} %get-tuple-element.106.refs_0_, bf16[1280,256]{1,0:T(8,128)(2,1)S(1)} %get-tuple-element.107.refs_1_, ...), custom_call_target="tpu_custom_call", output_to_operand_aliasing={{0}: (1, {})} | custom-call | flops 1048576 | bytes 1024 | tf_op jit(solution)/shard_map/node_mid/pallas_call | solution.py:399
  88.7 0.1 collective-permute-start.13
  88.8 0.5 collective-permute-start.12
  89.3 3.5 %collective-permute-start.20 = (bf16[1280,256]{1,0:T(8,128)(2,1)S(1)}, bf16[1280,256]{1,0:T(8,128)(2,1)S(1)}, u32[]{:S(2)}, u32[]{:S(2)}) collective-permute-start(bf16[1280,256]{1,0:T(8,128)(2,1)S(1)} %get-tuple-element.111), channel_id=1, source_target_pairs={{2,1},{4,3},{6,5},{8,7},{10,9},{12,11},{14,13},{1,2},{3,4},{5,6},{... | collective-permute-start | bytes 1966088 | tf_op jit(solution)/shard_map/ppermute | solution.py:544
  92.8 3.0 %collective-permute-start.19 = (bf16[1280,256]{1,0:T(8,128)(2,1)S(1)}, bf16[1280,256]{1,0:T(8,128)(2,1)S(1)}, u32[]{:S(2)}, u32[]{:S(2)}) collective-permute-start(bf16[1280,256]{1,0:T(8,128)(2,1)S(1)} %get-tuple-element.114.refs_2_), channel_id=1, source_target_pairs={{2,0},{4,2},{6,4},{8,6},{10,8},{12,10},{14,12},{1,3},{3,5},{5,7},{... | collective-permute-start | bytes 1966088 | tf_op jit(solution)/shard_map/ppermute | solution.py:544
  95.8 22.0 %collective-permute-done.15.refs_5_ = bf16[1280,256]{1,0:T(8,128)(2,1)S(1)} collective-permute-done((bf16[1280,256]{1,0:T(8,128)(2,1)S(1)}, bf16[1280,256]{1,0:T(8,128)(2,1)S(1)}, u32[]{:S(2)}, u32[]{:S(2)}) %collective-permute-start.15) | collective-permute-done | bytes 655392 | tf_op jit(solution)/shard_map/ppermute | solution.py:544
  117.8 6.2 %collective-permute-done.14.refs_4_ = bf16[1280,256]{1,0:T(8,128)(2,1)S(1)} collective-permute-done((bf16[1280,256]{1,0:T(8,128)(2,1)S(1)}, bf16[1280,256]{1,0:T(8,128)(2,1)S(1)}, u32[]{:S(2)}, u32[]{:S(2)}) %collective-permute-start.14) | collective-permute-done | bytes 655392 | tf_op jit(solution)/shard_map/ppermute | solution.py:544
  124.1 1.3 collective-permute-start.18
  125.4 1.4 collective-permute-start.16
  126.7 1.3 local_messages.1.refs_6_
  128.0 0.9 collective-permute-done.17
  129.0 1.3 collective-permute-done.16
  130.3 1.6 %node_coarse.1.refs_2_ = f32[320,256]{1,0:T(8,128)S(1)} custom-call(s32[1]{0:T(128)} %bitcast.feat_ref, bf16[320,512]{1,0:T(8,128)(2,1)S(1)} %constant_dynamic-update-slice_fusion.state_ref.refs_0_, bf16[320,512]{1,0:T(8,128)(2,1)S(1)} %pad_maximum_fusion.refs_1_.refs_2_, bf16[320,512]{1,0:T(8,128)(2,1)S(1)} %pad_maximum_fusion.refs_1_.refs_2_, ...), custom_call_target="tpu_custom_call" | custom-call | flops 1048576 | bytes 1024 | tf_op jit(solution)/shard_map/node_coarse/pallas_call | solution.py:399
  131.9 0.3 collective-permute-done.20.refs_5_
  132.2 6.0 %collective-permute-done.19.refs_4_ = bf16[1280,256]{1,0:T(8,128)(2,1)S(1)} collective-permute-done((bf16[1280,256]{1,0:T(8,128)(2,1)S(1)}, bf16[1280,256]{1,0:T(8,128)(2,1)S(1)}, u32[]{:S(2)}, u32[]{:S(2)}) %collective-permute-start.19) | collective-permute-done | bytes 655392 | tf_op jit(solution)/shard_map/ppermute | solution.py:544
  138.1 2.3 %aggregate.6 = (bf16[1280,256]{1,0:T(8,128)(2,1)S(1)}, bf16[1280,256]{1,0:T(8,128)(2,1)S(1)}, bf16[10240,256]{1,0:T(8,128)(2,1)S(1)}) custom-call(s32[1]{0:T(128)} %bitcast.feat_ref, s32[320]{0:T(512)S(1)} %pad_add_fusion.links, bf16[40,128,512]{2,1,0:T(8,128)(2,1)S(1)} %get-tuple-element.80.refs_0_, ...), custom_call_target="tpu_custom_call", output_to_operand_aliasing={{2}: (8, {})} | custom-call | flops 1048576 | bytes 1024 | tf_op jit(solution)/shard_map/aggregate/pallas_call | solution.py:287
  140.4 1.5 collective-permute-start.21
  141.9 1.8 %aggregate.7 = (bf16[1280,256]{1,0:T(8,128)(2,1)S(1)}, bf16[1280,256]{1,0:T(8,128)(2,1)S(1)}) custom-call(s32[1]{0:T(128)} %bitcast.feat_ref, s32[320]{0:T(512)S(1)} %pad_add_fusion.links, bf16[40,128,512]{2,1,0:T(8,128)(2,1)S(1)} %get-tuple-element.80.refs_0_, bf16[40,128,160]{2,1,0:T(8,128)(2,1)S(1)} %get-tuple-element.81.refs_1_, ...), custom_call_target="tpu_custom_call" | custom-call | flops 1048576 | bytes 1024 | tf_op jit(solution)/shard_map/aggregate/pallas_call | solution.py:287
  143.8 0.3 collective-permute-start.22
  144.0 4.2 %node_last.3 = (bf16[1280,512]{1,0:T(8,128)(2,1)S(1)}, bf16[5120,512]{1,0:T(8,128)(2,1)}) custom-call(s32[1]{0:T(128)} %bitcast.feat_ref, bf16[2560,512]{1,0:T(8,128)(2,1)S(1)} %get-tuple-element.109.refs_0_, bf16[1280,256]{1,0:T(8,128)(2,1)S(1)} %get-tuple-element.125.refs_1_, bf16[1280,256]{1,0:T(8,128)(2,1)S(1)} %collective-permute-done.21.refs_2_, ...), custom_call_target="tpu_custom_call" | custom-call | flops 8589934592 | bytes 1024 | tf_op jit(solution)/shard_map/node_last/pallas_call | solution.py:399
  148.2 0.4 collective-permute-start.24
  148.6 3.3 %node_last.4 = (bf16[896,512]{1,0:T(8,128)(2,1)S(1)}, bf16[5120,512]{1,0:T(8,128)(2,1)}) custom-call(s32[1]{0:T(128)} %bitcast.feat_ref, bf16[2560,512]{1,0:T(8,128)(2,1)S(1)} %get-tuple-element.109.refs_0_, bf16[1280,256]{1,0:T(8,128)(2,1)S(1)} %get-tuple-element.120.refs_1_, ...), custom_call_target="tpu_custom_call", output_to_operand_aliasing={{1}: (8, {})} | custom-call | flops 8589934592 | bytes 1024 | tf_op jit(solution)/shard_map/node_last/pallas_call | solution.py:399
  151.9 0.2 collective-permute-start.23
  152.2 2.0 %node_last.5 = (bf16[384,512]{1,0:T(8,128)(2,1)S(1)}, bf16[5120,512]{1,0:T(8,128)(2,1)}) custom-call(s32[1]{0:T(128)} %bitcast.feat_ref, bf16[2560,512]{1,0:T(8,128)(2,1)S(1)} %get-tuple-element.109.refs_0_, bf16[1280,256]{1,0:T(8,128)(2,1)S(1)} %get-tuple-element.120.refs_1_, ...), custom_call_target="tpu_custom_call", output_to_operand_aliasing={{1}: (9, {})} | custom-call | flops 8589934592 | bytes 1024 | tf_op jit(solution)/shard_map/node_last/pallas_call | solution.py:399
  154.2 0.4 collective-permute-start.25
  154.6 1.4 collective-permute-done.25.refs_1_
  156.0 1.1 assemble.1
  (30 shorter events, 0.1 us)
Async XLA Ops:
  0.8 12.0 %collective-permute-start = (bf16[40,512]{1,0:T(8,128)(2,1)S(1)}, bf16[40,512]{1,0:T(8,128)(2,1)S(1)}, u32[]{:S(2)}, u32[]{:S(2)}) collective-permute-start(bf16[40,512]{1,0:T(8,128)(2,1)S(1)} %slice.3), channel_id=1, source_target_pairs={{0,2},{2,0},{4,6},{6,4},{8,10},{10,8},{12,14},{14,12},{1,3},{3,1},... | collective-permute-start | bytes 122888 | tf_op jit(solution)/shard_map/ppermute | solution.py:446
  6.2 14.5 %copy-start = (bf16[2,256,512]{2,1,0:T(8,128)(2,1)S(1)}, bf16[2,256,512]{2,1,0:T(8,128)(2,1)}, u32[]{:S(2)}) copy-start(bf16[2,256,512]{2,1,0:T(8,128)(2,1)} %refs_6_) | copy-start | bytes 1572868
  6.3 44.7 %copy-start.2 = (s32[40,4]{0,1:T(4,128)S(1)}, s32[40,4]{0,1:T(4,128)}, u32[]{:S(2)}) copy-start(s32[40,4]{0,1:T(4,128)} %param.13) | copy-start | bytes 1924
  6.3 44.7 %copy-start.3 = (s32[40,4]{0,1:T(4,128)S(1)}, s32[40,4]{0,1:T(4,128)}, u32[]{:S(2)}) copy-start(s32[40,4]{0,1:T(4,128)} %param.12) | copy-start | bytes 1924
  6.3 45.1 %copy-start.1 = (s32[5120]{0:T(1024)S(1)}, s32[5120]{0:T(1024)}, u32[]{:S(2)}) copy-start(s32[5120]{0:T(1024)} %param.14) | copy-start | bytes 61444
  6.3 57.8 %collective-permute-start.7 = (bf16[2560,256]{1,0:T(8,128)(2,1)}, bf16[2560,256]{1,0:T(8,128)(2,1)S(1)}, u32[]{:S(2)}, u32[]{:S(2)}) collective-permute-start(bf16[2560,256]{1,0:T(8,128)(2,1)} %message.3.refs_4_), channel_id=1, source_target_pairs={{0,2},{2,4},{4,6},{6,8},{8,10},{10,12},{12,14},{1,3},{3,5},{5,7},{... | collective-permute-start | bytes 3932168 | tf_op jit(solution)/shard_map/ppermute | solution.py:489
  12.8 55.4 %collective-permute-start.6 = (bf16[2560,256]{1,0:T(8,128)(2,1)}, bf16[2560,256]{1,0:T(8,128)(2,1)S(1)}, u32[]{:S(2)}, u32[]{:S(2)}) collective-permute-start(bf16[2560,256]{1,0:T(8,128)(2,1)} %message.2.refs_3_), channel_id=1, source_target_pairs={{2,0},{4,2},{6,4},{8,6},{10,8},{12,10},{14,12},{3,1},{5,3},{7,5},{... | collective-permute-start | bytes 3932168 | tf_op jit(solution)/shard_map/ppermute | solution.py:489
  16.9 41.6 %collective-permute-start.3 = (bf16[2,1024,256]{2,1,0:T(8,128)(2,1)}, bf16[2,1024,256]{2,1,0:T(8,128)(2,1)}, u32[]{:S(2)}, u32[]{:S(2)}) collective-permute-start(bf16[2,1024,256]{2,1,0:T(8,128)(2,1)} %refs_5_), channel_id=1, source_target_pairs={{0,1},{1,0},{2,3},{3,2},{4,5},{5,4},{6,7},{7,6},{8,9},{9,8},{10,11... | collective-permute-start | bytes 3145736 | tf_op jit(solution)/shard_map/ppermute | solution.py:441
  18.5 30.0 %collective-permute-start.1 = (bf16[80,512]{1,0:T(8,128)(2,1)S(1)}, bf16[80,512]{1,0:T(8,128)(2,1)S(1)}, u32[]{:S(2)}, u32[]{:S(2)}) collective-permute-start(bf16[80,512]{1,0:T(8,128)(2,1)S(1)} %pad_maximum_fusion.2), channel_id=1, source_target_pairs={{0,8},{2,10},{4,12},{6,14},{8,0},{10,2},{12,4},{14,6},{1,9},{3,11}... | collective-permute-start | bytes 245768 | tf_op jit(solution)/shard_map/ppermute | solution.py:446
  20.8 35.7 %collective-permute-start.4 = (bf16[2,256,512]{2,1,0:T(8,128)(2,1)S(1)}, bf16[2,256,512]{2,1,0:T(8,128)(2,1)}, u32[]{:S(2)}, u32[]{:S(2)}) collective-permute-start(bf16[2,256,512]{2,1,0:T(8,128)(2,1)S(1)} %copy-done), channel_id=1, source_target_pairs={{0,1},{1,0},{2,3},{3,2},{4,5},{5,4},{6,7},{7,6},{8,9},{9,8},{10,11... | collective-permute-start | bytes 1572872 | tf_op jit(solution)/shard_map/ppermute | solution.py:441
  48.5 9.9 %collective-permute-start.5 = (bf16[2,512,256]{2,1,0:T(8,128)(2,1)}, bf16[2,512,256]{2,1,0:T(8,128)(2,1)}, u32[]{:S(2)}, u32[]{:S(2)}) collective-permute-start(bf16[2,512,256]{2,1,0:T(8,128)(2,1)} %refs_7_), channel_id=1, source_target_pairs={{0,1},{1,0},{2,3},{3,2},{4,5},{5,4},{6,7},{7,6},{8,9},{9,8},{10,11... | collective-permute-start | bytes 1572872 | tf_op jit(solution)/shard_map/ppermute | solution.py:441
  56.5 6.5 %collective-permute-start.2 = (bf16[160,512]{1,0:T(8,128)(2,1)S(1)}, bf16[160,512]{1,0:T(8,128)(2,1)S(1)}, u32[]{:S(2)}, u32[]{:S(2)}) collective-permute-start(bf16[160,512]{1,0:T(8,128)(2,1)S(1)} %pad_maximum_fusion.1), channel_id=1, source_target_pairs={{0,4},{2,6},{4,0},{6,2},{8,12},{10,14},{12,8},{14,10},{1,5},{3,7},... | collective-permute-start | bytes 491528 | tf_op jit(solution)/shard_map/ppermute | solution.py:446
  70.4 2.4 %collective-permute-start.8 = (bf16[1280,256]{1,0:T(8,128)(2,1)S(1)}, bf16[1280,256]{1,0:T(8,128)(2,1)S(1)}, u32[]{:S(2)}, u32[]{:S(2)}) collective-permute-start(bf16[1280,256]{1,0:T(8,128)(2,1)S(1)} %get-tuple-element.90), channel_id=1, source_target_pairs={{0,1},{1,0},{2,3},{3,2},{4,5},{5,4},{6,7},{7,6},{8,9},{9,8},{10,11... | collective-permute-start | bytes 1966088 | tf_op jit(solution)/shard_map/ppermute | solution.py:441
  71.0 6.3 %collective-permute-start.9 = (bf16[40,256]{1,0:T(8,128)(2,1)S(1)}, bf16[40,256]{1,0:T(8,128)(2,1)S(1)}, u32[]{:S(2)}, u32[]{:S(2)}) collective-permute-start(bf16[40,256]{1,0:T(8,128)(2,1)S(1)} %get-tuple-element.103), channel_id=1, source_target_pairs={{0,2},{2,0},{4,6},{6,4},{8,10},{10,8},{12,14},{14,12},{1,3},{3,1},... | collective-permute-start | bytes 61448 | tf_op jit(solution)/shard_map/ppermute | solution.py:446
  77.3 7.0 %collective-permute-start.10 = (bf16[1280,256]{1,0:T(8,128)(2,1)S(1)}, bf16[1280,256]{1,0:T(8,128)(2,1)S(1)}, u32[]{:S(2)}, u32[]{:S(2)}) collective-permute-start(bf16[1280,256]{1,0:T(8,128)(2,1)S(1)} %get-tuple-element.104), channel_id=1, source_target_pairs={{0,1},{1,0},{2,3},{3,2},{4,5},{5,4},{6,7},{7,6},{8,9},{9,8},{10,11... | collective-permute-start | bytes 1966088 | tf_op jit(solution)/shard_map/ppermute | solution.py:441
  77.6 6.7 %collective-permute-start.11 = (bf16[1280,256]{1,0:T(8,128)(2,1)S(1)}, bf16[1280,256]{1,0:T(8,128)(2,1)S(1)}, u32[]{:S(2)}, u32[]{:S(2)}) collective-permute-start(bf16[1280,256]{1,0:T(8,128)(2,1)S(1)} %get-tuple-element.108), channel_id=1, source_target_pairs={{0,1},{1,0},{2,3},{3,2},{4,5},{5,4},{6,7},{7,6},{8,9},{9,8},{10,11... | collective-permute-start | bytes 1966088 | tf_op jit(solution)/shard_map/ppermute | solution.py:441
  77.8 40.0 %collective-permute-start.15 = (bf16[1280,256]{1,0:T(8,128)(2,1)S(1)}, bf16[1280,256]{1,0:T(8,128)(2,1)S(1)}, u32[]{:S(2)}, u32[]{:S(2)}) collective-permute-start(bf16[1280,256]{1,0:T(8,128)(2,1)S(1)} %get-tuple-element.104), channel_id=1, source_target_pairs={{2,1},{4,3},{6,5},{8,7},{10,9},{12,11},{14,13},{1,2},{3,4},{5,6},{... | collective-permute-start | bytes 1966088 | tf_op jit(solution)/shard_map/ppermute | solution.py:544
  81.5 42.6 %collective-permute-start.14 = (bf16[1280,256]{1,0:T(8,128)(2,1)S(1)}, bf16[1280,256]{1,0:T(8,128)(2,1)S(1)}, u32[]{:S(2)}, u32[]{:S(2)}) collective-permute-start(bf16[1280,256]{1,0:T(8,128)(2,1)S(1)} %get-tuple-element.112.refs_0_), channel_id=1, source_target_pairs={{2,0},{4,2},{6,4},{8,6},{10,8},{12,10},{14,12},{1,3},{3,5},{5,7},{... | collective-permute-start | bytes 1966088 | tf_op jit(solution)/shard_map/ppermute | solution.py:544
  88.7 35.4 %collective-permute-start.13 = (bf16[1280,256]{1,0:T(8,128)(2,1)S(1)}, bf16[1280,256]{1,0:T(8,128)(2,1)S(1)}, u32[]{:S(2)}, u32[]{:S(2)}) collective-permute-start(bf16[1280,256]{1,0:T(8,128)(2,1)S(1)} %get-tuple-element.111), channel_id=1, source_target_pairs={{0,1},{1,0},{2,3},{3,2},{4,5},{5,4},{6,7},{7,6},{8,9},{9,8},{10,11... | collective-permute-start | bytes 1966088 | tf_op jit(solution)/shard_map/ppermute | solution.py:441
  88.8 4.0 %collective-permute-start.12 = (bf16[80,256]{1,0:T(8,128)(2,1)S(1)}, bf16[80,256]{1,0:T(8,128)(2,1)S(1)}, u32[]{:S(2)}, u32[]{:S(2)}) collective-permute-start(bf16[80,256]{1,0:T(8,128)(2,1)S(1)} %constant_dynamic-update-slice_fusion.3), channel_id=1, source_target_pairs={{0,1},{1,0},{2,3},{3,2},{4,5},{5,4},{6,7},{7,6},{8,9},{9,8},{10,11... | collective-permute-start | bytes 122888 | tf_op jit(solution)/shard_map/ppermute | solution.py:441
  89.3 42.9 %collective-permute-start.20 = (bf16[1280,256]{1,0:T(8,128)(2,1)S(1)}, bf16[1280,256]{1,0:T(8,128)(2,1)S(1)}, u32[]{:S(2)}, u32[]{:S(2)}) collective-permute-start(bf16[1280,256]{1,0:T(8,128)(2,1)S(1)} %get-tuple-element.111), channel_id=1, source_target_pairs={{2,1},{4,3},{6,5},{8,7},{10,9},{12,11},{14,13},{1,2},{3,4},{5,6},{... | collective-permute-start | bytes 1966088 | tf_op jit(solution)/shard_map/ppermute | solution.py:544
  92.8 45.4 %collective-permute-start.19 = (bf16[1280,256]{1,0:T(8,128)(2,1)S(1)}, bf16[1280,256]{1,0:T(8,128)(2,1)S(1)}, u32[]{:S(2)}, u32[]{:S(2)}) collective-permute-start(bf16[1280,256]{1,0:T(8,128)(2,1)S(1)} %get-tuple-element.114.refs_2_), channel_id=1, source_target_pairs={{2,0},{4,2},{6,4},{8,6},{10,8},{12,10},{14,12},{1,3},{3,5},{5,7},{... | collective-permute-start | bytes 1966088 | tf_op jit(solution)/shard_map/ppermute | solution.py:544
  124.1 3.9 %collective-permute-start.18 = (bf16[80,512]{1,0:T(8,128)(2,1)S(1)}, bf16[80,512]{1,0:T(8,128)(2,1)S(1)}, u32[]{:S(2)}, u32[]{:S(2)}) collective-permute-start(bf16[80,512]{1,0:T(8,128)(2,1)S(1)} %pad_maximum_fusion.3), channel_id=1, source_target_pairs={{0,12},{2,14},{4,8},{6,10},{8,4},{10,6},{12,0},{14,2},{1,13},{3,15... | collective-permute-start | bytes 245768 | tf_op jit(solution)/shard_map/ppermute | solution.py:446
  125.4 3.6 %collective-permute-start.17 = (bf16[80,512]{1,0:T(8,128)(2,1)S(1)}, bf16[80,512]{1,0:T(8,128)(2,1)S(1)}, u32[]{:S(2)}, u32[]{:S(2)}) collective-permute-start(bf16[80,512]{1,0:T(8,128)(2,1)S(1)} %pad_maximum_fusion.3), channel_id=1, source_target_pairs={{0,4},{2,6},{4,0},{6,2},{8,12},{10,14},{12,8},{14,10},{1,5},{3,7},... | collective-permute-start | bytes 245768 | tf_op jit(solution)/shard_map/ppermute | solution.py:446
  125.4 4.9 %collective-permute-start.16 = (bf16[80,512]{1,0:T(8,128)(2,1)S(1)}, bf16[80,512]{1,0:T(8,128)(2,1)S(1)}, u32[]{:S(2)}, u32[]{:S(2)}) collective-permute-start(bf16[80,512]{1,0:T(8,128)(2,1)S(1)} %pad_maximum_fusion.3), channel_id=1, source_target_pairs={{0,8},{2,10},{4,12},{6,14},{8,0},{10,2},{12,4},{14,6},{1,9},{3,11}... | collective-permute-start | bytes 245768 | tf_op jit(solution)/shard_map/ppermute | solution.py:446
  140.4 3.4 %collective-permute-start.21 = (bf16[1280,256]{1,0:T(8,128)(2,1)S(1)}, bf16[1280,256]{1,0:T(8,128)(2,1)S(1)}, u32[]{:S(2)}, u32[]{:S(2)}) collective-permute-start(bf16[1280,256]{1,0:T(8,128)(2,1)S(1)} %get-tuple-element.121), channel_id=1, source_target_pairs={{0,1},{1,0},{2,3},{3,2},{4,5},{5,4},{6,7},{7,6},{8,9},{9,8},{10,11... | collective-permute-start | bytes 1966088 | tf_op jit(solution)/shard_map/ppermute | solution.py:441
  143.8 4.9 %collective-permute-start.22 = (bf16[1280,256]{1,0:T(8,128)(2,1)S(1)}, bf16[1280,256]{1,0:T(8,128)(2,1)S(1)}, u32[]{:S(2)}, u32[]{:S(2)}) collective-permute-start(bf16[1280,256]{1,0:T(8,128)(2,1)S(1)} %get-tuple-element.124), channel_id=1, source_target_pairs={{0,1},{1,0},{2,3},{3,2},{4,5},{5,4},{6,7},{7,6},{8,9},{9,8},{10,11... | collective-permute-start | bytes 1966088 | tf_op jit(solution)/shard_map/ppermute | solution.py:441
  148.2 3.9 %collective-permute-start.24 = (bf16[1280,512]{1,0:T(8,128)(2,1)S(1)}, bf16[1280,512]{1,0:T(8,128)(2,1)S(1)}, u32[]{:S(2)}, u32[]{:S(2)}) collective-permute-start(bf16[1280,512]{1,0:T(8,128)(2,1)S(1)} %get-tuple-element.129), channel_id=1, source_target_pairs={{0,1},{1,0},{2,3},{3,2},{4,5},{5,4},{6,7},{7,6},{8,9},{9,8},{10,11... | collective-permute-start | bytes 3932168 | tf_op jit(solution)/shard_map/ppermute | solution.py:441
  151.9 2.7 %collective-permute-start.23 = (bf16[896,512]{1,0:T(8,128)(2,1)S(1)}, bf16[896,512]{1,0:T(8,128)(2,1)S(1)}, u32[]{:S(2)}, u32[]{:S(2)}) collective-permute-start(bf16[896,512]{1,0:T(8,128)(2,1)S(1)} %get-tuple-element.128), channel_id=1, source_target_pairs={{0,1},{1,0},{2,3},{3,2},{4,5},{5,4},{6,7},{7,6},{8,9},{9,8},{10,11... | collective-permute-start | bytes 2752520 | tf_op jit(solution)/shard_map/ppermute | solution.py:441
  154.2 1.8 %collective-permute-start.25 = (bf16[384,512]{1,0:T(8,128)(2,1)S(1)}, bf16[384,512]{1,0:T(8,128)(2,1)S(1)}, u32[]{:S(2)}, u32[]{:S(2)}) collective-permute-start(bf16[384,512]{1,0:T(8,128)(2,1)S(1)} %get-tuple-element.131), channel_id=1, source_target_pairs={{0,1},{1,0},{2,3},{3,2},{4,5},{5,4},{6,7},{7,6},{8,9},{9,8},{10,11... | collective-permute-start | bytes 1179656 | tf_op jit(solution)/shard_map/ppermute | solution.py:441

commit v11 on v10

--- a/solution.py
+++ b/solution.py
@@ -446,16 +446,6 @@
     return lax.ppermute(held, "patch", [(pos, pos ^ stride) for pos in range(count)])
 
 
-def even_offsets(count):
-    assert count & (count - 1) == 0
-    offsets = [0]
-    stride = count // 2
-    while stride > 1:
-        offsets += [offset + stride for offset in offsets]
-        stride //= 2
-    return offsets
-
-
 def shards(
     node_state, fine_tile, coarse_tile, fine_index, coarse_index, node_degree, w_msg, w_in, w_out
 ):
@@ -475,27 +465,22 @@
     sides = ((0, backward), (1, forward))
     own_patch = [(2 * src + side, 2 * dst + side) for side, pairs in sides for src, dst in pairs]
     other_patch = [(2 * src + side, 2 * dst + 1 - side) for side, pairs in sides for src, dst in pairs]
-    evens = even_offsets(patches)
-
-    held = node_state[:CN_DEV]
-    held = jnp.concatenate([held, fetch(held, 1)], axis=0)
+    assert patches & (patches - 1) == 0
+
     sends = []
     halo = []
     for first, count in MESSAGE_ROWS:
         message = message_call(node_state, w_msg, first * block, count * block, MESSAGE_TILES)
-        if not sends:
-            message, held = barrier((message, held))
         sends.append(message)
         halo.append(lax.ppermute(message, "patch", backward if first < half else forward))
     high = sends[-1]
 
-    offsets = [even + odd for even in evens for odd in (0, 1)]
     fine_index, coarse_index, node_degree, w_in, w_out, w_late, _ = barrier(
         (fine_index, coarse_index, node_degree, w_in, w_out, w_msg, high)
     )
     links = (fine_index - (patch_pos * blocks - HALO_BLK)).reshape(-1) * block
     away = (coarse_index ^ patch_pos).reshape(-1)
-    coarse_links = sum(jnp.where(away == offset, pos * CN_DEV, 0) for pos, offset in enumerate(offsets))
+    coarse_links = away * CN_DEV
     links = jnp.concatenate([links, coarse_links])
     degree = node_degree.reshape(2, half, block)
     fine, ctile, state, table, in_own, out_own, msg_own = stage_call(
@@ -503,14 +488,13 @@
     )
     staged = (fine, ctile)
     others = weights_call([swap_feat(w_in), swap_feat(w_out), swap_feat(w_late)])
-    strides = [patches >> step for step in range(1, patches.bit_length() - 1)]
-    for step, stride in enumerate(strides):
-        got = fetch(held, stride)
-        if step == 0:
-            got, links, degree, table = barrier((got, links, degree, table))
-        if step == len(strides) - 1:
-            got, others = barrier((got, others))
-        held = jnp.concatenate([held, got], axis=0)
+    first_rows, _ = barrier((node_state[:CN_DEV], high))
+    near_half = [fetch(first_rows, offset) for offset in range(1, patches // 2)]
+    *near_half, links, degree, table = barrier((*near_half, links, degree, table))
+    held = jnp.concatenate([first_rows, *near_half], axis=0)
+    got = fetch(held, patches // 2)
+    got, others = barrier((got, others))
+    held = jnp.concatenate([held, got], axis=0)
     coarse_state = held
     weights = [in_own, others[0], out_own, others[1], msg_own, others[2]]
     coarse = coarse_message_call(coarse_state, msg_own)
@@ -558,7 +542,7 @@
     held = jnp.concatenate([held, swap_feat(held)], axis=1)
     held, local[-1], *halo[:early] = barrier((held, local[-1], *halo[:early]))
     table = local_call(feat, local_places + halo_places[:early], local + halo[:early], table)
-    held = jnp.concatenate([held] + [fetch(held, offset) for offset in evens[1:]], axis=0)
+    held = jnp.concatenate([held] + [fetch(held, offset) for offset in range(2, patches, 2)], axis=0)
     (coarse,) = node_call(
         "coarse", 0, feat, coarse_state, 0, 0, held.shape[0], held, held, weights
     )

time: 158 us -> 170 us (1.076)
  waiting for transfers between devices: 73.2 us -> 80.7 us
  local copies, waits for them, and re-layouts: 1.23 us -> 3.34 us
    ppermute x7 -> x8, waiting for transfers between devices: 32.6 us -> 46.7 us  [fetch(): lax.ppermute(held, 'patch', [(pos, pos ^ stride) for pos in range(count)])]
    ppermute x2, waiting for transfers between devices: 4.76 us -> 0.01 us  [shards(): lax.ppermute(message, 'patch', backward if first < half else forward)]
    ppermute x13, starting transfers between devices: 8.93 us -> 10.7 us  [swap_feat(): return lax.ppermute(array, 'feat', [(0, 1), (1, 0)])]
    ppermute x7 -> x8, starting transfers between devices: 8.1 us -> 9.41 us  [fetch(): lax.ppermute(held, 'patch', [(pos, pos ^ stride) for pos in range(count)])]
  transfers between devices with their start and end apart: 26 -> 27, of which waited for: 11 -> 8; matrix products, arithmetic and copies ran while one was open for 0% -> 2% of each run, Pallas kernels for 26% -> 21%
where the time goes in v11:
time: 170 us; the launch traced here: 169 us
  waiting for transfers between devices  80.7 us (47%)
  Pallas kernels  45.8 us (27%)
  starting transfers between devices  37.3 us (22%)
  local copies, waits for them, and re-layouts  3.34 us (2%)
    ppermute x8, waiting for transfers between devices, fetch(): lax.ppermute(held, 'patch', [(pos, pos ^ stride) for pos in range(count)])  46.7 us
    ppermute x2, waiting for transfers between devices, shards(): lax.ppermute(other, ('patch', 'feat'), other_patch)  21.2 us
    pallas_call x6, Pallas kernels, node_call(): pl.pallas_call(functools.partial(node_kernel, mode, layer, start, offset,...  20 us
    ppermute x2, waiting for transfers between devices, shards(): lax.ppermute(own, ('patch', 'feat'), own_patch)  11.3 us
    ppermute x13, starting transfers between devices, swap_feat(): return lax.ppermute(array, 'feat', [(0, 1), (1, 0)])  10.7 us
    ppermute x8, starting transfers between devices, fetch(): lax.ppermute(held, 'patch', [(pos, pos ^ stride) for pos in range(count)])  9.41 us
    pallas_call x2, Pallas kernels, message_call(): pl.pallas_call(functools.partial(message_kernel, start, sizes), in_specs=...  8.45 us
    pallas_call x4, Pallas kernels, aggregate_call(): pl.pallas_call(functools.partial(aggregate_kernel, places, start), grid_s...  8.11 us
  transfers between devices with their start and end apart: 27, of which 8 were waited for; matrix products, arithmetic and copies ran while one was open for 2% of the time, Pallas kernels for 21%

profile of v11, /device:TPU:9, one launch (start us, length us, event | category | flops | bytes accessed | tf_op | source)
XLA Modules:
  0.0 168.5 jit_solution(10421547724040830073)
XLA Ops:
  0.0 4.2 %message.2.refs_3_ = bf16[2560,256]{1,0:T(8,128)(2,1)} custom-call(bf16[5120,512]{1,0:T(8,128)(2,1)} %refs_2_.1, bf16[2,512,256]{2,1,0:T(8,128)(2,1)} %refs_7_), custom_call_target="tpu_custom_call" | custom-call | flops 1048576 | bytes 1024 | tf_op jit(solution)/shard_map/message/pallas_call | solution.py:95
  4.2 0.0 copy-start
  4.2 0.0 copy-start.6
  4.2 0.0 copy-start.7
  4.3 3.2 %collective-permute-start.7 = (bf16[2560,256]{1,0:T(8,128)(2,1)}, bf16[2560,256]{1,0:T(8,128)(2,1)S(1)}, u32[]{:S(2)}, u32[]{:S(2)}) collective-permute-start(bf16[2560,256]{1,0:T(8,128)(2,1)} %message.2.refs_3_), channel_id=1, source_target_pairs={{2,0},{4,2},{6,4},{8,6},{10,8},{12,10},{14,12},{3,1},{5,3},{7,5},{... | collective-permute-start | bytes 3932168 | tf_op jit(solution)/shard_map/ppermute | solution.py:475
  7.4 4.2 %message.3.refs_4_ = bf16[2560,256]{1,0:T(8,128)(2,1)} custom-call(bf16[5120,512]{1,0:T(8,128)(2,1)} %refs_2_.1, bf16[2,512,256]{2,1,0:T(8,128)(2,1)} %refs_7_), custom_call_target="tpu_custom_call" | custom-call | flops 1048576 | bytes 1024 | tf_op jit(solution)/shard_map/message/pallas_call | solution.py:95
  11.7 2.3 %collective-permute-start.8 = (bf16[2560,256]{1,0:T(8,128)(2,1)}, bf16[2560,256]{1,0:T(8,128)(2,1)S(1)}, u32[]{:S(2)}, u32[]{:S(2)}) collective-permute-start(bf16[2560,256]{1,0:T(8,128)(2,1)} %message.3.refs_4_), channel_id=1, source_target_pairs={{0,2},{2,4},{4,6},{6,8},{8,10},{10,12},{12,14},{1,3},{3,5},{5,7},{... | collective-permute-start | bytes 3932168 | tf_op jit(solution)/shard_map/ppermute | solution.py:475
  13.9 1.3 collective-permute-start.4
  15.2 0.8 slice.3
  16.0 2.0 %collective-permute-start.2 = (bf16[40,512]{1,0:T(8,128)(2,1)S(1)}, bf16[40,512]{1,0:T(8,128)(2,1)S(1)}, u32[]{:S(2)}, u32[]{:S(2)}) collective-permute-start(bf16[40,512]{1,0:T(8,128)(2,1)S(1)} %slice.3), channel_id=1, source_target_pairs={{0,6},{2,4},{4,2},{6,0},{8,14},{10,12},{12,10},{14,8},{1,7},{3,5},... | collective-permute-start | bytes 122888 | tf_op jit(solution)/shard_map/ppermute | solution.py:446
  18.0 1.3 collective-permute-start.1
  19.3 25.6 %collective-permute-done.2 = bf16[40,512]{1,0:T(8,128)(2,1)S(1)} collective-permute-done((bf16[40,512]{1,0:T(8,128)(2,1)S(1)}, bf16[40,512]{1,0:T(8,128)(2,1)S(1)}, u32[]{:S(2)}, u32[]{:S(2)}) %collective-permute-start.2) | collective-permute-done | bytes 40992 | tf_op jit(solution)/shard_map/ppermute | solution.py:446
  45.0 2.3 %collective-permute-start.5 = (bf16[2,256,512]{2,1,0:T(8,128)(2,1)S(1)}, bf16[2,256,512]{2,1,0:T(8,128)(2,1)}, u32[]{:S(2)}, u32[]{:S(2)}) collective-permute-start(bf16[2,256,512]{2,1,0:T(8,128)(2,1)S(1)} %copy-done), channel_id=1, source_target_pairs={{0,1},{1,0},{2,3},{3,2},{4,5},{5,4},{6,7},{7,6},{8,9},{9,8},{10,11... | collective-permute-start | bytes 1572872 | tf_op jit(solution)/shard_map/ppermute | solution.py:441
  47.3 0.6 copy-done.4
  47.9 0.0 collective-permute-start
  47.9 0.1 copy.19
  48.0 0.1 mul.27
  48.1 0.1 copy.18
  48.2 0.1 mul.24
  48.3 0.7 reshape.13.refs_3_
  49.1 5.0 %stage.1 = (bf16[40,128,512]{2,1,0:T(8,128)(2,1)S(1)}, bf16[40,128,160]{2,1,0:T(8,128)(2,1)S(1)}, bf16[2560,512]{1,0:T(8,128)(2,1)S(1)}, bf16[10240,256]{1,0:T(8...) custom-call(s32[1]{0:T(128)} %bitcast.feat_ref, ...), custom_call_target="tpu_custom_call" | custom-call | flops 1048576 | bytes 1024 | tf_op jit(solution)/shard_map/stage/pallas_call | solution.py:166
  54.1 12.9 %collective-permute-done = bf16[40,512]{1,0:T(8,128)(2,1)} collective-permute-done((bf16[40,512]{1,0:T(8,128)(2,1)S(1)}, bf16[40,512]{1,0:T(8,128)(2,1)}, u32[]{:S(2)}, u32[]{:S(2)}) %collective-permute-start) | collective-permute-done | bytes 40992 | tf_op jit(solution)/shard_map/ppermute | solution.py:446
  67.0 0.7 collective-permute-start.6
  67.6 0.1 pad_add_fusion.links
  67.7 0.8 constant_dynamic-update-slice_fusion.3
  68.5 0.8 pad_maximum_fusion.1
  69.3 0.0 collective-permute-done.5.refs_1_
  69.3 2.4 %collective-permute-start.3 = (bf16[160,512]{1,0:T(8,128)(2,1)S(1)}, bf16[160,512]{1,0:T(8,128)(2,1)S(1)}, u32[]{:S(2)}, u32[]{:S(2)}) collective-permute-start(bf16[160,512]{1,0:T(8,128)(2,1)S(1)} %pad_maximum_fusion.1), channel_id=1, source_target_pairs={{0,8},{2,10},{4,12},{6,14},{8,0},{10,2},{12,4},{14,6},{1,9},{3,11}... | collective-permute-start | bytes 491528 | tf_op jit(solution)/shard_map/ppermute | solution.py:446
  71.7 0.0 collective-permute-done.4.refs_0_
  71.7 1.4 weights.1
  73.1 5.9 %collective-permute-done.3 = bf16[160,512]{1,0:T(8,128)(2,1)S(1)} collective-permute-done((bf16[160,512]{1,0:T(8,128)(2,1)S(1)}, bf16[160,512]{1,0:T(8,128)(2,1)S(1)}, u32[]{:S(2)}, u32[]{:S(2)}) %collective-permute-start.3) | collective-permute-done | bytes 163872 | tf_op jit(solution)/shard_map/ppermute | solution.py:446
  79.1 0.5 coarse_message.1.refs_2_
  79.5 2.2 %aggregate.4 = (bf16[1280,256]{1,0:T(8,128)(2,1)S(1)}, bf16[1280,256]{1,0:T(8,128)(2,1)S(1)}, bf16[40,256]{1,0:T(8,128)(2,1)S(1)}, bf16[10240,256]{1,0:T(8,128)(2,1)S(1)}) custom-call(s32[1]{0:T(128)} %bitcast.feat_ref, s32[320]{0:T(512)S(1)} %pad_add_fusion.links, ...), custom_call_target="tpu_custom_call", output_to_operand_aliasing={{3}: (8, {})} | custom-call | flops 1048576 | bytes 1024 | tf_op jit(solution)/shard_map/aggregate/pallas_call | solution.py:287
  81.8 0.5 collective-permute-start.9
  82.3 1.8 %aggregate.5 = (bf16[1280,256]{1,0:T(8,128)(2,1)S(1)}, bf16[1280,256]{1,0:T(8,128)(2,1)S(1)}) custom-call(s32[1]{0:T(128)} %bitcast.feat_ref, s32[320]{0:T(512)S(1)} %pad_add_fusion.links, bf16[40,128,512]{2,1,0:T(8,128)(2,1)S(1)} %get-tuple-element.80.refs_0_, bf16[40,128,160]{2,1,0:T(8,128)(2,1)S(1)} %get-tuple-element.81.refs_1_, ...), custom_call_target="tpu_custom_call" | custom-call | flops 1048576 | bytes 1024 | tf_op jit(solution)/shard_map/aggregate/pallas_call | solution.py:287
  84.1 4.4 %node_mid.2 = (bf16[2560,512]{1,0:T(8,128)(2,1)S(1)}, bf16[1280,256]{1,0:T(8,128)(2,1)S(1)}, bf16[1280,256]{1,0:T(8,128)(2,1)S(1)}) custom-call(s32[1]{0:T(128)} %bitcast.feat_ref, bf16[2560,512]{1,0:T(8,128)(2,1)S(1)} %get-tuple-element.73.refs_0_, bf16[1280,256]{1,0:T(8,128)(2,1)S(1)} %get-tuple-element.96.refs_1_, ...), custom_call_target="tpu_custom_call", output_to_operand_aliasing={{0}: (1, {})} | custom-call | flops 1048576 | bytes 1024 | tf_op jit(solution)/shard_map/node_mid/pallas_call | solution.py:399
  88.6 0.4 collective-permute-start.11
  88.9 0.2 collective-permute-start.12
  89.1 3.6 %collective-permute-start.16 = (bf16[1280,256]{1,0:T(8,128)(2,1)S(1)}, bf16[1280,256]{1,0:T(8,128)(2,1)S(1)}, u32[]{:S(2)}, u32[]{:S(2)}) collective-permute-start(bf16[1280,256]{1,0:T(8,128)(2,1)S(1)} %get-tuple-element.106), channel_id=1, source_target_pairs={{2,1},{4,3},{6,5},{8,7},{10,9},{12,11},{14,13},{1,2},{3,4},{5,6},{... | collective-permute-start | bytes 1966088 | tf_op jit(solution)/shard_map/ppermute | solution.py:528
  92.8 2.9 %collective-permute-start.15 = (bf16[1280,256]{1,0:T(8,128)(2,1)S(1)}, bf16[1280,256]{1,0:T(8,128)(2,1)S(1)}, u32[]{:S(2)}, u32[]{:S(2)}) collective-permute-start(bf16[1280,256]{1,0:T(8,128)(2,1)S(1)} %get-tuple-element.114.refs_0_), channel_id=1, source_target_pairs={{2,0},{4,2},{6,4},{8,6},{10,8},{12,10},{14,12},{1,3},{3,5},{5,7},{... | collective-permute-start | bytes 1966088 | tf_op jit(solution)/shard_map/ppermute | solution.py:528
  95.7 4.4 %node_mid.3 = (bf16[2560,512]{1,0:T(8,128)(2,1)S(1)}, bf16[1280,256]{1,0:T(8,128)(2,1)S(1)}, bf16[1280,256]{1,0:T(8,128)(2,1)S(1)}) custom-call(s32[1]{0:T(128)} %bitcast.feat_ref, bf16[2560,512]{1,0:T(8,128)(2,1)S(1)} %get-tuple-element.108.refs_0_, bf16[1280,256]{1,0:T(8,128)(2,1)S(1)} %get-tuple-element.109.refs_1_, ...), custom_call_target="tpu_custom_call", output_to_operand_aliasing={{0}: (1, {})} | custom-call | flops 1048576 | bytes 1024 | tf_op jit(solution)/shard_map/node_mid/pallas_call | solution.py:399
  100.1 2.4 %collective-permute-start.14 = (bf16[1280,256]{1,0:T(8,128)(2,1)S(1)}, bf16[1280,256]{1,0:T(8,128)(2,1)S(1)}, u32[]{:S(2)}, u32[]{:S(2)}) collective-permute-start(bf16[1280,256]{1,0:T(8,128)(2,1)S(1)} %get-tuple-element.113), channel_id=1, source_target_pairs={{0,1},{1,0},{2,3},{3,2},{4,5},{5,4},{6,7},{7,6},{8,9},{9,8},{10,11... | collective-permute-start | bytes 1966088 | tf_op jit(solution)/shard_map/ppermute | solution.py:441
  102.6 0.1 collective-permute-start.13
  102.6 2.2 %collective-permute-start.21 = (bf16[1280,256]{1,0:T(8,128)(2,1)S(1)}, bf16[1280,256]{1,0:T(8,128)(2,1)S(1)}, u32[]{:S(2)}, u32[]{:S(2)}) collective-permute-start(bf16[1280,256]{1,0:T(8,128)(2,1)S(1)} %get-tuple-element.113), channel_id=1, source_target_pairs={{2,1},{4,3},{6,5},{8,7},{10,9},{12,11},{14,13},{1,2},{3,4},{5,6},{... | collective-permute-start | bytes 1966088 | tf_op jit(solution)/shard_map/ppermute | solution.py:528
  104.8 3.1 %collective-permute-start.20 = (bf16[1280,256]{1,0:T(8,128)(2,1)S(1)}, bf16[1280,256]{1,0:T(8,128)(2,1)S(1)}, u32[]{:S(2)}, u32[]{:S(2)}) collective-permute-start(bf16[1280,256]{1,0:T(8,128)(2,1)S(1)} %get-tuple-element.116.refs_2_), channel_id=1, source_target_pairs={{2,0},{4,2},{6,4},{8,6},{10,8},{12,10},{14,12},{1,3},{3,5},{5,7},{... | collective-permute-start | bytes 1966088 | tf_op jit(solution)/shard_map/ppermute | solution.py:528
  108.0 21.2 %collective-permute-done.16.refs_5_ = bf16[1280,256]{1,0:T(8,128)(2,1)S(1)} collective-permute-done((bf16[1280,256]{1,0:T(8,128)(2,1)S(1)}, bf16[1280,256]{1,0:T(8,128)(2,1)S(1)}, u32[]{:S(2)}, u32[]{:S(2)}) %collective-permute-start.16) | collective-permute-done | bytes 655392 | tf_op jit(solution)/shard_map/ppermute | solution.py:528
  129.1 6.3 %collective-permute-done.15.refs_4_ = bf16[1280,256]{1,0:T(8,128)(2,1)S(1)} collective-permute-done((bf16[1280,256]{1,0:T(8,128)(2,1)S(1)}, bf16[1280,256]{1,0:T(8,128)(2,1)S(1)}, u32[]{:S(2)}, u32[]{:S(2)}) %collective-permute-start.15) | collective-permute-done | bytes 655392 | tf_op jit(solution)/shard_map/ppermute | solution.py:528
  135.4 3.7 %collective-permute-start.18 = (bf16[80,512]{1,0:T(8,128)(2,1)S(1)}, bf16[80,512]{1,0:T(8,128)(2,1)S(1)}, u32[]{:S(2)}, u32[]{:S(2)}) collective-permute-start(bf16[80,512]{1,0:T(8,128)(2,1)S(1)} %pad_maximum_fusion.2), channel_id=1, source_target_pairs={{0,8},{2,10},{4,12},{6,14},{8,0},{10,2},{12,4},{14,6},{1,9},{3,11}... | collective-permute-start | bytes 245768 | tf_op jit(solution)/shard_map/ppermute | solution.py:446
  139.1 1.3 local_messages.1.refs_6_
  140.4 2.3 %collective-permute-done.18 = bf16[80,512]{1,0:T(8,128)(2,1)S(1)} collective-permute-done((bf16[80,512]{1,0:T(8,128)(2,1)S(1)}, bf16[80,512]{1,0:T(8,128)(2,1)S(1)}, u32[]{:S(2)}, u32[]{:S(2)}) %collective-permute-start.18) | collective-permute-done | bytes 81952 | tf_op jit(solution)/shard_map/ppermute | solution.py:446
  142.7 1.6 node_coarse.1.refs_2_
  144.3 5.1 %collective-permute-done.20.refs_4_ = bf16[1280,256]{1,0:T(8,128)(2,1)S(1)} collective-permute-done((bf16[1280,256]{1,0:T(8,128)(2,1)S(1)}, bf16[1280,256]{1,0:T(8,128)(2,1)S(1)}, u32[]{:S(2)}, u32[]{:S(2)}) %collective-permute-start.20) | collective-permute-done | bytes 655392 | tf_op jit(solution)/shard_map/ppermute | solution.py:528
  149.4 2.2 %aggregate.6 = (bf16[1280,256]{1,0:T(8,128)(2,1)S(1)}, bf16[1280,256]{1,0:T(8,128)(2,1)S(1)}, bf16[10240,256]{1,0:T(8,128)(2,1)S(1)}) custom-call(s32[1]{0:T(128)} %bitcast.feat_ref, s32[320]{0:T(512)S(1)} %pad_add_fusion.links, bf16[40,128,512]{2,1,0:T(8,128)(2,1)S(1)} %get-tuple-element.80.refs_0_, ...), custom_call_target="tpu_custom_call", output_to_operand_aliasing={{2}: (8, {})} | custom-call | flops 1048576 | bytes 1024 | tf_op jit(solution)/shard_map/aggregate/pallas_call | solution.py:287
  151.7 1.5 collective-permute-start.22
  153.2 1.8 %aggregate.7 = (bf16[1280,256]{1,0:T(8,128)(2,1)S(1)}, bf16[1280,256]{1,0:T(8,128)(2,1)S(1)}) custom-call(s32[1]{0:T(128)} %bitcast.feat_ref, s32[320]{0:T(512)S(1)} %pad_add_fusion.links, bf16[40,128,512]{2,1,0:T(8,128)(2,1)S(1)} %get-tuple-element.80.refs_0_, bf16[40,128,160]{2,1,0:T(8,128)(2,1)S(1)} %get-tuple-element.81.refs_1_, ...), custom_call_target="tpu_custom_call" | custom-call | flops 1048576 | bytes 1024 | tf_op jit(solution)/shard_map/aggregate/pallas_call | solution.py:287
  155.1 0.2 collective-permute-start.23
  155.3 4.2 %node_last.3 = (bf16[1280,512]{1,0:T(8,128)(2,1)S(1)}, bf16[5120,512]{1,0:T(8,128)(2,1)}) custom-call(s32[1]{0:T(128)} %bitcast.feat_ref, bf16[2560,512]{1,0:T(8,128)(2,1)S(1)} %get-tuple-element.111.refs_0_, bf16[1280,256]{1,0:T(8,128)(2,1)S(1)} %get-tuple-element.127.refs_1_, bf16[1280,256]{1,0:T(8,128)(2,1)S(1)} %collective-permute-done.22.refs_2_, ...), custom_call_target="tpu_custom_call" | custom-call | flops 8589934592 | bytes 1024 | tf_op jit(solution)/shard_map/node_last/pallas_call | solution.py:399
  159.5 0.4 collective-permute-start.25
  159.9 3.3 %node_last.4 = (bf16[896,512]{1,0:T(8,128)(2,1)S(1)}, bf16[5120,512]{1,0:T(8,128)(2,1)}) custom-call(s32[1]{0:T(128)} %bitcast.feat_ref, bf16[2560,512]{1,0:T(8,128)(2,1)S(1)} %get-tuple-element.111.refs_0_, bf16[1280,256]{1,0:T(8,128)(2,1)S(1)} %get-tuple-element.122.refs_1_, ...), custom_call_target="tpu_custom_call", output_to_operand_aliasing={{1}: (8, {})} | custom-call | flops 8589934592 | bytes 1024 | tf_op jit(solution)/shard_map/node_last/pallas_call | solution.py:399
  163.2 0.3 collective-permute-start.24
  163.5 2.0 %node_last.5 = (bf16[384,512]{1,0:T(8,128)(2,1)S(1)}, bf16[5120,512]{1,0:T(8,128)(2,1)}) custom-call(s32[1]{0:T(128)} %bitcast.feat_ref, bf16[2560,512]{1,0:T(8,128)(2,1)S(1)} %get-tuple-element.111.refs_0_, bf16[1280,256]{1,0:T(8,128)(2,1)S(1)} %get-tuple-element.122.refs_1_, ...), custom_call_target="tpu_custom_call", output_to_operand_aliasing={{1}: (9, {})} | custom-call | flops 8589934592 | bytes 1024 | tf_op jit(solution)/shard_map/node_last/pallas_call | solution.py:399
  165.5 0.4 collective-permute-start.26
  165.9 1.4 collective-permute-done.26.refs_1_
  167.3 1.1 assemble.1
  (41 shorter events, 0.1 us)
Async XLA Ops:
  4.2 40.8 %copy-start = (bf16[2,256,512]{2,1,0:T(8,128)(2,1)S(1)}, bf16[2,256,512]{2,1,0:T(8,128)(2,1)}, u32[]{:S(2)}) copy-start(bf16[2,256,512]{2,1,0:T(8,128)(2,1)} %refs_6_) | copy-start | bytes 1572868
  4.2 43.1 %copy-start.6 = (s32[40,4]{0,1:T(4,128)S(1)}, s32[40,4]{0,1:T(4,128)}, u32[]{:S(2)}) copy-start(s32[40,4]{0,1:T(4,128)} %param.13) | copy-start | bytes 1924
  4.2 43.1 %copy-start.7 = (s32[40,4]{0,1:T(4,128)S(1)}, s32[40,4]{0,1:T(4,128)}, u32[]{:S(2)}) copy-start(s32[40,4]{0,1:T(4,128)} %param.12) | copy-start | bytes 1924
  4.3 75.3 %collective-permute-start.7 = (bf16[2560,256]{1,0:T(8,128)(2,1)}, bf16[2560,256]{1,0:T(8,128)(2,1)S(1)}, u32[]{:S(2)}, u32[]{:S(2)}) collective-permute-start(bf16[2560,256]{1,0:T(8,128)(2,1)} %message.2.refs_3_), channel_id=1, source_target_pairs={{2,0},{4,2},{6,4},{8,6},{10,8},{12,10},{14,12},{3,1},{5,3},{7,5},{... | collective-permute-start | bytes 3932168 | tf_op jit(solution)/shard_map/ppermute | solution.py:475
  11.7 67.9 %collective-permute-start.8 = (bf16[2560,256]{1,0:T(8,128)(2,1)}, bf16[2560,256]{1,0:T(8,128)(2,1)S(1)}, u32[]{:S(2)}, u32[]{:S(2)}) collective-permute-start(bf16[2560,256]{1,0:T(8,128)(2,1)} %message.3.refs_4_), channel_id=1, source_target_pairs={{0,2},{2,4},{4,6},{6,8},{8,10},{10,12},{12,14},{1,3},{3,5},{5,7},{... | collective-permute-start | bytes 3932168 | tf_op jit(solution)/shard_map/ppermute | solution.py:475
  13.9 57.8 %collective-permute-start.4 = (bf16[2,1024,256]{2,1,0:T(8,128)(2,1)}, bf16[2,1024,256]{2,1,0:T(8,128)(2,1)}, u32[]{:S(2)}, u32[]{:S(2)}) collective-permute-start(bf16[2,1024,256]{2,1,0:T(8,128)(2,1)} %refs_5_), channel_id=1, source_target_pairs={{0,1},{1,0},{2,3},{3,2},{4,5},{5,4},{6,7},{7,6},{8,9},{9,8},{10,11... | collective-permute-start | bytes 3145736 | tf_op jit(solution)/shard_map/ppermute | solution.py:441
  16.0 29.0 %collective-permute-start.2 = (bf16[40,512]{1,0:T(8,128)(2,1)S(1)}, bf16[40,512]{1,0:T(8,128)(2,1)S(1)}, u32[]{:S(2)}, u32[]{:S(2)}) collective-permute-start(bf16[40,512]{1,0:T(8,128)(2,1)S(1)} %slice.3), channel_id=1, source_target_pairs={{0,6},{2,4},{4,2},{6,0},{8,14},{10,12},{12,10},{14,8},{1,7},{3,5},... | collective-permute-start | bytes 122888 | tf_op jit(solution)/shard_map/ppermute | solution.py:446
  18.0 29.3 %collective-permute-start.1 = (bf16[40,512]{1,0:T(8,128)(2,1)S(1)}, bf16[40,512]{1,0:T(8,128)(2,1)S(1)}, u32[]{:S(2)}, u32[]{:S(2)}) collective-permute-start(bf16[40,512]{1,0:T(8,128)(2,1)S(1)} %slice.3), channel_id=1, source_target_pairs={{0,4},{2,6},{4,0},{6,2},{8,12},{10,14},{12,8},{14,10},{1,5},{3,7},... | collective-permute-start | bytes 122888 | tf_op jit(solution)/shard_map/ppermute | solution.py:446
  45.0 2.3 %copy-start.2 = (bf16[40,512]{1,0:T(8,128)(2,1)}, bf16[40,512]{1,0:T(8,128)(2,1)S(1)}, u32[]{:S(2)}) copy-start(bf16[40,512]{1,0:T(8,128)(2,1)S(1)} %collective-permute-done.2) | copy-start | bytes 122884
  45.0 24.3 %collective-permute-start.5 = (bf16[2,256,512]{2,1,0:T(8,128)(2,1)S(1)}, bf16[2,256,512]{2,1,0:T(8,128)(2,1)}, u32[]{:S(2)}, u32[]{:S(2)}) collective-permute-start(bf16[2,256,512]{2,1,0:T(8,128)(2,1)S(1)} %copy-done), channel_id=1, source_target_pairs={{0,1},{1,0},{2,3},{3,2},{4,5},{5,4},{6,7},{7,6},{8,9},{9,8},{10,11... | collective-permute-start | bytes 1572872 | tf_op jit(solution)/shard_map/ppermute | solution.py:441
  47.3 0.6 copy-start.4
  47.9 19.0 %collective-permute-start = (bf16[40,512]{1,0:T(8,128)(2,1)S(1)}, bf16[40,512]{1,0:T(8,128)(2,1)}, u32[]{:S(2)}, u32[]{:S(2)}) collective-permute-start(bf16[40,512]{1,0:T(8,128)(2,1)S(1)} %slice.3), channel_id=1, source_target_pairs={{0,2},{2,0},{4,6},{6,4},{8,10},{10,8},{12,14},{14,12},{1,3},{3,1},... | collective-permute-start | bytes 122888 | tf_op jit(solution)/shard_map/ppermute | solution.py:446
  49.1 17.9 %copy-start.1 = (bf16[2,512,256]{2,1,0:T(8,128)(2,1)S(1)}, bf16[2,512,256]{2,1,0:T(8,128)(2,1)}, u32[]{:S(2)}) copy-start(bf16[2,512,256]{2,1,0:T(8,128)(2,1)} %refs_7_) | copy-start | bytes 1572868
  49.1 19.4 %copy-start.3 = (bf16[40,512]{1,0:T(8,128)(2,1)S(1)}, bf16[40,512]{1,0:T(8,128)(2,1)}, u32[]{:S(2)}) copy-start(bf16[40,512]{1,0:T(8,128)(2,1)} %copy-done.2) | copy-start | bytes 122884
  49.1 19.4 %copy-start.5 = (bf16[40,512]{1,0:T(8,128)(2,1)S(1)}, bf16[40,512]{1,0:T(8,128)(2,1)}, u32[]{:S(2)}) copy-start(bf16[40,512]{1,0:T(8,128)(2,1)} %copy-done.4) | copy-start | bytes 122884
  67.0 4.7 %collective-permute-start.6 = (bf16[2,512,256]{2,1,0:T(8,128)(2,1)S(1)}, bf16[2,512,256]{2,1,0:T(8,128)(2,1)S(1)}, u32[]{:S(2)}, u32[]{:S(2)}) collective-permute-start(bf16[2,512,256]{2,1,0:T(8,128)(2,1)S(1)} %copy-done.1), channel_id=1, source_target_pairs={{0,1},{1,0},{2,3},{3,2},{4,5},{5,4},{6,7},{7,6},{8,9},{9,8},{10,11... | collective-permute-start | bytes 1572872 | tf_op jit(solution)/shard_map/ppermute | solution.py:441
  69.3 9.7 %collective-permute-start.3 = (bf16[160,512]{1,0:T(8,128)(2,1)S(1)}, bf16[160,512]{1,0:T(8,128)(2,1)S(1)}, u32[]{:S(2)}, u32[]{:S(2)}) collective-permute-start(bf16[160,512]{1,0:T(8,128)(2,1)S(1)} %pad_maximum_fusion.1), channel_id=1, source_target_pairs={{0,8},{2,10},{4,12},{6,14},{8,0},{10,2},{12,4},{14,6},{1,9},{3,11}... | collective-permute-start | bytes 491528 | tf_op jit(solution)/shard_map/ppermute | solution.py:446
  81.8 2.4 %collective-permute-start.9 = (bf16[1280,256]{1,0:T(8,128)(2,1)S(1)}, bf16[1280,256]{1,0:T(8,128)(2,1)S(1)}, u32[]{:S(2)}, u32[]{:S(2)}) collective-permute-start(bf16[1280,256]{1,0:T(8,128)(2,1)S(1)} %get-tuple-element.92), channel_id=1, source_target_pairs={{0,1},{1,0},{2,3},{3,2},{4,5},{5,4},{6,7},{7,6},{8,9},{9,8},{10,11... | collective-permute-start | bytes 1966088 | tf_op jit(solution)/shard_map/ppermute | solution.py:441
  82.3 6.3 %collective-permute-start.10 = (bf16[40,256]{1,0:T(8,128)(2,1)S(1)}, bf16[40,256]{1,0:T(8,128)(2,1)S(1)}, u32[]{:S(2)}, u32[]{:S(2)}) collective-permute-start(bf16[40,256]{1,0:T(8,128)(2,1)S(1)} %get-tuple-element.105), channel_id=1, source_target_pairs={{0,2},{2,0},{4,6},{6,4},{8,10},{10,8},{12,14},{14,12},{1,3},{3,1},... | collective-permute-start | bytes 61448 | tf_op jit(solution)/shard_map/ppermute | solution.py:446
  88.6 7.1 %collective-permute-start.11 = (bf16[1280,256]{1,0:T(8,128)(2,1)S(1)}, bf16[1280,256]{1,0:T(8,128)(2,1)S(1)}, u32[]{:S(2)}, u32[]{:S(2)}) collective-permute-start(bf16[1280,256]{1,0:T(8,128)(2,1)S(1)} %get-tuple-element.106), channel_id=1, source_target_pairs={{0,1},{1,0},{2,3},{3,2},{4,5},{5,4},{6,7},{7,6},{8,9},{9,8},{10,11... | collective-permute-start | bytes 1966088 | tf_op jit(solution)/shard_map/ppermute | solution.py:441
  88.9 6.8 %collective-permute-start.12 = (bf16[1280,256]{1,0:T(8,128)(2,1)S(1)}, bf16[1280,256]{1,0:T(8,128)(2,1)S(1)}, u32[]{:S(2)}, u32[]{:S(2)}) collective-permute-start(bf16[1280,256]{1,0:T(8,128)(2,1)S(1)} %get-tuple-element.110), channel_id=1, source_target_pairs={{0,1},{1,0},{2,3},{3,2},{4,5},{5,4},{6,7},{7,6},{8,9},{9,8},{10,11... | collective-permute-start | bytes 1966088 | tf_op jit(solution)/shard_map/ppermute | solution.py:441
  89.1 40.0 %collective-permute-start.16 = (bf16[1280,256]{1,0:T(8,128)(2,1)S(1)}, bf16[1280,256]{1,0:T(8,128)(2,1)S(1)}, u32[]{:S(2)}, u32[]{:S(2)}) collective-permute-start(bf16[1280,256]{1,0:T(8,128)(2,1)S(1)} %get-tuple-element.106), channel_id=1, source_target_pairs={{2,1},{4,3},{6,5},{8,7},{10,9},{12,11},{14,13},{1,2},{3,4},{5,6},{... | collective-permute-start | bytes 1966088 | tf_op jit(solution)/shard_map/ppermute | solution.py:528
  92.8 42.6 %collective-permute-start.15 = (bf16[1280,256]{1,0:T(8,128)(2,1)S(1)}, bf16[1280,256]{1,0:T(8,128)(2,1)S(1)}, u32[]{:S(2)}, u32[]{:S(2)}) collective-permute-start(bf16[1280,256]{1,0:T(8,128)(2,1)S(1)} %get-tuple-element.114.refs_0_), channel_id=1, source_target_pairs={{2,0},{4,2},{6,4},{8,6},{10,8},{12,10},{14,12},{1,3},{3,5},{5,7},{... | collective-permute-start | bytes 1966088 | tf_op jit(solution)/shard_map/ppermute | solution.py:528
  100.1 35.3 %collective-permute-start.14 = (bf16[1280,256]{1,0:T(8,128)(2,1)S(1)}, bf16[1280,256]{1,0:T(8,128)(2,1)S(1)}, u32[]{:S(2)}, u32[]{:S(2)}) collective-permute-start(bf16[1280,256]{1,0:T(8,128)(2,1)S(1)} %get-tuple-element.113), channel_id=1, source_target_pairs={{0,1},{1,0},{2,3},{3,2},{4,5},{5,4},{6,7},{7,6},{8,9},{9,8},{10,11... | collective-permute-start | bytes 1966088 | tf_op jit(solution)/shard_map/ppermute | solution.py:441
  102.6 2.3 %collective-permute-start.13 = (bf16[80,256]{1,0:T(8,128)(2,1)S(1)}, bf16[80,256]{1,0:T(8,128)(2,1)S(1)}, u32[]{:S(2)}, u32[]{:S(2)}) collective-permute-start(bf16[80,256]{1,0:T(8,128)(2,1)S(1)} %constant_dynamic-update-slice_fusion.5), channel_id=1, source_target_pairs={{0,1},{1,0},{2,3},{3,2},{4,5},{5,4},{6,7},{7,6},{8,9},{9,8},{10,11... | collective-permute-start | bytes 122888 | tf_op jit(solution)/shard_map/ppermute | solution.py:441
  102.6 41.7 %collective-permute-start.21 = (bf16[1280,256]{1,0:T(8,128)(2,1)S(1)}, bf16[1280,256]{1,0:T(8,128)(2,1)S(1)}, u32[]{:S(2)}, u32[]{:S(2)}) collective-permute-start(bf16[1280,256]{1,0:T(8,128)(2,1)S(1)} %get-tuple-element.113), channel_id=1, source_target_pairs={{2,1},{4,3},{6,5},{8,7},{10,9},{12,11},{14,13},{1,2},{3,4},{5,6},{... | collective-permute-start | bytes 1966088 | tf_op jit(solution)/shard_map/ppermute | solution.py:528
  104.8 44.6 %collective-permute-start.20 = (bf16[1280,256]{1,0:T(8,128)(2,1)S(1)}, bf16[1280,256]{1,0:T(8,128)(2,1)S(1)}, u32[]{:S(2)}, u32[]{:S(2)}) collective-permute-start(bf16[1280,256]{1,0:T(8,128)(2,1)S(1)} %get-tuple-element.116.refs_2_), channel_id=1, source_target_pairs={{2,0},{4,2},{6,4},{8,6},{10,8},{12,10},{14,12},{1,3},{3,5},{5,7},{... | collective-permute-start | bytes 1966088 | tf_op jit(solution)/shard_map/ppermute | solution.py:528
  135.4 5.0 %collective-permute-start.19 = (bf16[80,512]{1,0:T(8,128)(2,1)S(1)}, bf16[80,512]{1,0:T(8,128)(2,1)S(1)}, u32[]{:S(2)}, u32[]{:S(2)}) collective-permute-start(bf16[80,512]{1,0:T(8,128)(2,1)S(1)} %pad_maximum_fusion.2), channel_id=1, source_target_pairs={{0,12},{2,14},{4,8},{6,10},{8,4},{10,6},{12,0},{14,2},{1,13},{3,15... | collective-permute-start | bytes 245768 | tf_op jit(solution)/shard_map/ppermute | solution.py:446
  135.4 7.3 %collective-permute-start.18 = (bf16[80,512]{1,0:T(8,128)(2,1)S(1)}, bf16[80,512]{1,0:T(8,128)(2,1)S(1)}, u32[]{:S(2)}, u32[]{:S(2)}) collective-permute-start(bf16[80,512]{1,0:T(8,128)(2,1)S(1)} %pad_maximum_fusion.2), channel_id=1, source_target_pairs={{0,8},{2,10},{4,12},{6,14},{8,0},{10,2},{12,4},{14,6},{1,9},{3,11}... | collective-permute-start | bytes 245768 | tf_op jit(solution)/shard_map/ppermute | solution.py:446
  139.1 3.6 %collective-permute-start.17 = (bf16[80,512]{1,0:T(8,128)(2,1)S(1)}, bf16[80,512]{1,0:T(8,128)(2,1)S(1)}, u32[]{:S(2)}, u32[]{:S(2)}) collective-permute-start(bf16[80,512]{1,0:T(8,128)(2,1)S(1)} %pad_maximum_fusion.2), channel_id=1, source_target_pairs={{0,4},{2,6},{4,0},{6,2},{8,12},{10,14},{12,8},{14,10},{1,5},{3,7},... | collective-permute-start | bytes 245768 | tf_op jit(solution)/shard_map/ppermute | solution.py:446
  151.7 3.4 %collective-permute-start.22 = (bf16[1280,256]{1,0:T(8,128)(2,1)S(1)}, bf16[1280,256]{1,0:T(8,128)(2,1)S(1)}, u32[]{:S(2)}, u32[]{:S(2)}) collective-permute-start(bf16[1280,256]{1,0:T(8,128)(2,1)S(1)} %get-tuple-element.123), channel_id=1, source_target_pairs={{0,1},{1,0},{2,3},{3,2},{4,5},{5,4},{6,7},{7,6},{8,9},{9,8},{10,11... | collective-permute-start | bytes 1966088 | tf_op jit(solution)/shard_map/ppermute | solution.py:441
  155.1 4.9 %collective-permute-start.23 = (bf16[1280,256]{1,0:T(8,128)(2,1)S(1)}, bf16[1280,256]{1,0:T(8,128)(2,1)S(1)}, u32[]{:S(2)}, u32[]{:S(2)}) collective-permute-start(bf16[1280,256]{1,0:T(8,128)(2,1)S(1)} %get-tuple-element.126), channel_id=1, source_target_pairs={{0,1},{1,0},{2,3},{3,2},{4,5},{5,4},{6,7},{7,6},{8,9},{9,8},{10,11... | collective-permute-start | bytes 1966088 | tf_op jit(solution)/shard_map/ppermute | solution.py:441
  159.5 3.9 %collective-permute-start.25 = (bf16[1280,512]{1,0:T(8,128)(2,1)S(1)}, bf16[1280,512]{1,0:T(8,128)(2,1)S(1)}, u32[]{:S(2)}, u32[]{:S(2)}) collective-permute-start(bf16[1280,512]{1,0:T(8,128)(2,1)S(1)} %get-tuple-element.131), channel_id=1, source_target_pairs={{0,1},{1,0},{2,3},{3,2},{4,5},{5,4},{6,7},{7,6},{8,9},{9,8},{10,11... | collective-permute-start | bytes 3932168 | tf_op jit(solution)/shard_map/ppermute | solution.py:441
  163.2 2.7 %collective-permute-start.24 = (bf16[896,512]{1,0:T(8,128)(2,1)S(1)}, bf16[896,512]{1,0:T(8,128)(2,1)S(1)}, u32[]{:S(2)}, u32[]{:S(2)}) collective-permute-start(bf16[896,512]{1,0:T(8,128)(2,1)S(1)} %get-tuple-element.130), channel_id=1, source_target_pairs={{0,1},{1,0},{2,3},{3,2},{4,5},{5,4},{6,7},{7,6},{8,9},{9,8},{10,11... | collective-permute-start | bytes 2752520 | tf_op jit(solution)/shard_map/ppermute | solution.py:441
  165.5 1.8 %collective-permute-start.26 = (bf16[384,512]{1,0:T(8,128)(2,1)S(1)}, bf16[384,512]{1,0:T(8,128)(2,1)S(1)}, u32[]{:S(2)}, u32[]{:S(2)}) collective-permute-start(bf16[384,512]{1,0:T(8,128)(2,1)S(1)} %get-tuple-element.133), channel_id=1, source_target_pairs={{0,1},{1,0},{2,3},{3,2},{4,5},{5,4},{6,7},{7,6},{8,9},{9,8},{10,11... | collective-permute-start | bytes 1179656 | tf_op jit(solution)/shard_map/ppermute | solution.py:441

commit v12 on v10

--- a/solution.py
+++ b/solution.py
@@ -12,7 +12,7 @@
 HALO_BLK = 20
 MID_BLOCKS = (10, 10)
 LAST_BLOCKS = (10, 10)
-LAST_ROWS = ((0, 0, 10), (1, 0, 7), (1, 7, 3))
+LAST_ROWS = ((0, 0, 10), (1, 0, 8), (1, 8, 2))
 MESSAGE_ROWS = ((0, 20), (20, 20))
 MESSAGE_TILES = (512, 640, 640, 512, 256)
 NODE_SPLIT = 2
@@ -317,7 +317,7 @@
         copies = run_copies(pairs, sems)
     keep_at = pl.multiple_of(width + feat * columns, columns)
     recv_at = pl.multiple_of(width + (1 - feat) * columns, columns)
-    split = NODE_SPLIT if rows % (NODE_SPLIT * 640) == 0 else 1
+    split = NODE_SPLIT if rows >= 1024 else 1
     size = rows // split
     joined, hidden, state = {}, {}, {}
 

time: 158 us -> 157 us (level)
  no operation moved by 1% of the time
where the time goes in v12:
time: 157 us
  waiting for transfers between devices  73.1 us (47%)
  Pallas kernels  45.7 us (29%)
  starting transfers between devices  36.2 us (23%)
    ppermute x7, waiting for transfers between devices, fetch(): lax.ppermute(held, 'patch', [(pos, pos ^ stride) for pos in range(count)])  32.6 us
    ppermute x2, waiting for transfers between devices, shards(): lax.ppermute(other, ('patch', 'feat'), other_patch)  22.2 us
    pallas_call x6, Pallas kernels, node_call(): pl.pallas_call(functools.partial(node_kernel, mode, layer, start, offset,...  19.9 us
    ppermute x2, waiting for transfers between devices, shards(): lax.ppermute(own, ('patch', 'feat'), own_patch)  12.2 us
    ppermute x13, starting transfers between devices, swap_feat(): return lax.ppermute(array, 'feat', [(0, 1), (1, 0)])  8.94 us
    pallas_call x2, Pallas kernels, message_call(): pl.pallas_call(functools.partial(message_kernel, start, sizes), in_specs=...  8.44 us
    ppermute x7, starting transfers between devices, fetch(): lax.ppermute(held, 'patch', [(pos, pos ^ stride) for pos in range(count)])  8.1 us
    pallas_call x4, Pallas kernels, aggregate_call(): pl.pallas_call(functools.partial(aggregate_kernel, places, start), grid_s...  8.1 us
  transfers between devices with their start and end apart: 26, of which 11 were waited for; matrix products, arithmetic and copies ran while one was open for 0% of the time, Pallas kernels for 26%

profile of v12, /device:TPU:9, one launch (start us, length us, event | category | flops | bytes accessed | tf_op | source)
XLA Modules:
  0.0 157.0 jit_solution(9524553458490235614)
XLA Ops:
  0.0 0.8 slice.3
  0.8 1.2 collective-permute-start
  2.0 4.2 %message.3.refs_4_ = bf16[2560,256]{1,0:T(8,128)(2,1)} custom-call(bf16[5120,512]{1,0:T(8,128)(2,1)} %refs_2_.1, bf16[2,512,256]{2,1,0:T(8,128)(2,1)} %refs_7_), custom_call_target="tpu_custom_call" | custom-call | flops 1048576 | bytes 1024 | tf_op jit(solution)/shard_map/message/pallas_call | solution.py:95
  6.2 0.0 copy-start
  6.3 0.0 copy-start.2
  6.3 0.0 copy-start.3
  6.3 0.0 copy-start.1
  6.3 2.3 %collective-permute-start.7 = (bf16[2560,256]{1,0:T(8,128)(2,1)}, bf16[2560,256]{1,0:T(8,128)(2,1)S(1)}, u32[]{:S(2)}, u32[]{:S(2)}) collective-permute-start(bf16[2560,256]{1,0:T(8,128)(2,1)} %message.3.refs_4_), channel_id=1, source_target_pairs={{0,2},{2,4},{4,6},{6,8},{8,10},{10,12},{12,14},{1,3},{3,5},{5,7},{... | collective-permute-start | bytes 3932168 | tf_op jit(solution)/shard_map/ppermute | solution.py:489
  8.6 4.2 %message.2.refs_3_ = bf16[2560,256]{1,0:T(8,128)(2,1)} custom-call(bf16[5120,512]{1,0:T(8,128)(2,1)} %refs_2_.1, bf16[2,512,256]{2,1,0:T(8,128)(2,1)} %refs_7_), custom_call_target="tpu_custom_call" | custom-call | flops 1048576 | bytes 1024 | tf_op jit(solution)/shard_map/message/pallas_call | solution.py:95
  12.8 0.0 collective-permute-done
  12.8 4.0 %collective-permute-start.6 = (bf16[2560,256]{1,0:T(8,128)(2,1)}, bf16[2560,256]{1,0:T(8,128)(2,1)S(1)}, u32[]{:S(2)}, u32[]{:S(2)}) collective-permute-start(bf16[2560,256]{1,0:T(8,128)(2,1)} %message.2.refs_3_), channel_id=1, source_target_pairs={{2,0},{4,2},{6,4},{8,6},{10,8},{12,10},{14,12},{3,1},{5,3},{7,5},{... | collective-permute-start | bytes 3932168 | tf_op jit(solution)/shard_map/ppermute | solution.py:489
  16.9 1.6 %collective-permute-start.3 = (bf16[2,1024,256]{2,1,0:T(8,128)(2,1)}, bf16[2,1024,256]{2,1,0:T(8,128)(2,1)}, u32[]{:S(2)}, u32[]{:S(2)}) collective-permute-start(bf16[2,1024,256]{2,1,0:T(8,128)(2,1)} %refs_5_), channel_id=1, source_target_pairs={{0,1},{1,0},{2,3},{3,2},{4,5},{5,4},{6,7},{7,6},{8,9},{9,8},{10,11... | collective-permute-start | bytes 3145736 | tf_op jit(solution)/shard_map/ppermute | solution.py:441
  18.5 2.3 %collective-permute-start.1 = (bf16[80,512]{1,0:T(8,128)(2,1)S(1)}, bf16[80,512]{1,0:T(8,128)(2,1)S(1)}, u32[]{:S(2)}, u32[]{:S(2)}) collective-permute-start(bf16[80,512]{1,0:T(8,128)(2,1)S(1)} %pad_maximum_fusion.2), channel_id=1, source_target_pairs={{0,8},{2,10},{4,12},{6,14},{8,0},{10,2},{12,4},{14,6},{1,9},{3,11}... | collective-permute-start | bytes 245768 | tf_op jit(solution)/shard_map/ppermute | solution.py:446
  20.8 0.3 collective-permute-start.4
  21.1 27.4 %collective-permute-done.1 = bf16[80,512]{1,0:T(8,128)(2,1)S(1)} collective-permute-done((bf16[80,512]{1,0:T(8,128)(2,1)S(1)}, bf16[80,512]{1,0:T(8,128)(2,1)S(1)}, u32[]{:S(2)}, u32[]{:S(2)}) %collective-permute-start.1) | collective-permute-done | bytes 81952 | tf_op jit(solution)/shard_map/ppermute | solution.py:446
  48.5 2.5 %collective-permute-start.5 = (bf16[2,512,256]{2,1,0:T(8,128)(2,1)}, bf16[2,512,256]{2,1,0:T(8,128)(2,1)}, u32[]{:S(2)}, u32[]{:S(2)}) collective-permute-start(bf16[2,512,256]{2,1,0:T(8,128)(2,1)} %refs_7_), channel_id=1, source_target_pairs={{0,1},{1,0},{2,3},{3,2},{4,5},{5,4},{6,7},{7,6},{8,9},{9,8},{10,11... | collective-permute-start | bytes 1572872 | tf_op jit(solution)/shard_map/ppermute | solution.py:441
  51.0 0.1 copy.19
  51.1 0.1 reshape.52
  51.2 0.1 copy.18
  51.3 0.1 mul.15
  51.4 0.1 pad_add_fusion.links
  51.5 5.0 %stage.1 = (bf16[40,128,512]{2,1,0:T(8,128)(2,1)S(1)}, bf16[40,128,160]{2,1,0:T(8,128)(2,1)S(1)}, bf16[2560,512]{1,0:T(8,128)(2,1)S(1)}, bf16[10240,256]{1,0:T(8...) custom-call(s32[1]{0:T(128)} %bitcast.feat_ref, ...), custom_call_target="tpu_custom_call" | custom-call | flops 1048576 | bytes 1024 | tf_op jit(solution)/shard_map/stage/pallas_call | solution.py:166
  56.5 1.9 %collective-permute-start.2 = (bf16[160,512]{1,0:T(8,128)(2,1)S(1)}, bf16[160,512]{1,0:T(8,128)(2,1)S(1)}, u32[]{:S(2)}, u32[]{:S(2)}) collective-permute-start(bf16[160,512]{1,0:T(8,128)(2,1)S(1)} %pad_maximum_fusion.1), channel_id=1, source_target_pairs={{0,4},{2,6},{4,0},{6,2},{8,12},{10,14},{12,8},{14,10},{1,5},{3,7},... | collective-permute-start | bytes 491528 | tf_op jit(solution)/shard_map/ppermute | solution.py:446
  58.4 0.0 collective-permute-done.3.refs_0_
  58.5 1.5 weights.1
  60.0 3.0 %collective-permute-done.2 = bf16[160,512]{1,0:T(8,128)(2,1)S(1)} collective-permute-done((bf16[160,512]{1,0:T(8,128)(2,1)S(1)}, bf16[160,512]{1,0:T(8,128)(2,1)S(1)}, u32[]{:S(2)}, u32[]{:S(2)}) %collective-permute-start.2) | collective-permute-done | bytes 163872 | tf_op jit(solution)/shard_map/ppermute | solution.py:446
  63.0 0.5 coarse_message.1.refs_2_
  63.5 0.6 collective-permute-done.7.refs_5_
  64.1 4.1 %collective-permute-done.6.refs_4_ = bf16[2560,256]{1,0:T(8,128)(2,1)S(1)} collective-permute-done((bf16[2560,256]{1,0:T(8,128)(2,1)}, bf16[2560,256]{1,0:T(8,128)(2,1)S(1)}, u32[]{:S(2)}, u32[]{:S(2)}) %collective-permute-start.6) | collective-permute-done | bytes 1310752 | tf_op jit(solution)/shard_map/ppermute | solution.py:489
  68.2 2.2 %aggregate.4 = (bf16[1280,256]{1,0:T(8,128)(2,1)S(1)}, bf16[1280,256]{1,0:T(8,128)(2,1)S(1)}, bf16[40,256]{1,0:T(8,128)(2,1)S(1)}, bf16[10240,256]{1,0:T(8,128)(2,1)S(1)}) custom-call(s32[1]{0:T(128)} %bitcast.feat_ref, s32[320]{0:T(512)S(1)} %pad_add_fusion.links, ...), custom_call_target="tpu_custom_call", output_to_operand_aliasing={{3}: (8, {})} | custom-call | flops 1048576 | bytes 1024 | tf_op jit(solution)/shard_map/aggregate/pallas_call | solution.py:287
  70.4 0.6 collective-permute-start.8
  71.0 1.8 %aggregate.5 = (bf16[1280,256]{1,0:T(8,128)(2,1)S(1)}, bf16[1280,256]{1,0:T(8,128)(2,1)S(1)}) custom-call(s32[1]{0:T(128)} %bitcast.feat_ref, s32[320]{0:T(512)S(1)} %pad_add_fusion.links, bf16[40,128,512]{2,1,0:T(8,128)(2,1)S(1)} %get-tuple-element.80.refs_0_, bf16[40,128,160]{2,1,0:T(8,128)(2,1)S(1)} %get-tuple-element.81.refs_1_, ...), custom_call_target="tpu_custom_call" | custom-call | flops 1048576 | bytes 1024 | tf_op jit(solution)/shard_map/aggregate/pallas_call | solution.py:287
  72.8 4.4 %node_mid.2 = (bf16[2560,512]{1,0:T(8,128)(2,1)S(1)}, bf16[1280,256]{1,0:T(8,128)(2,1)S(1)}, bf16[1280,256]{1,0:T(8,128)(2,1)S(1)}) custom-call(s32[1]{0:T(128)} %bitcast.feat_ref, bf16[2560,512]{1,0:T(8,128)(2,1)S(1)} %get-tuple-element.73.refs_0_, bf16[1280,256]{1,0:T(8,128)(2,1)S(1)} %get-tuple-element.94.refs_1_, ...), custom_call_target="tpu_custom_call", output_to_operand_aliasing={{0}: (1, {})} | custom-call | flops 1048576 | bytes 1024 | tf_op jit(solution)/shard_map/node_mid/pallas_call | solution.py:399
  77.3 0.3 collective-permute-start.10
  77.6 0.2 collective-permute-start.11
  77.8 3.6 %collective-permute-start.15 = (bf16[1280,256]{1,0:T(8,128)(2,1)S(1)}, bf16[1280,256]{1,0:T(8,128)(2,1)S(1)}, u32[]{:S(2)}, u32[]{:S(2)}) collective-permute-start(bf16[1280,256]{1,0:T(8,128)(2,1)S(1)} %get-tuple-element.104), channel_id=1, source_target_pairs={{2,1},{4,3},{6,5},{8,7},{10,9},{12,11},{14,13},{1,2},{3,4},{5,6},{... | collective-permute-start | bytes 1966088 | tf_op jit(solution)/shard_map/ppermute | solution.py:544
  81.5 2.8 %collective-permute-start.14 = (bf16[1280,256]{1,0:T(8,128)(2,1)S(1)}, bf16[1280,256]{1,0:T(8,128)(2,1)S(1)}, u32[]{:S(2)}, u32[]{:S(2)}) collective-permute-start(bf16[1280,256]{1,0:T(8,128)(2,1)S(1)} %get-tuple-element.112.refs_0_), channel_id=1, source_target_pairs={{2,0},{4,2},{6,4},{8,6},{10,8},{12,10},{14,12},{1,3},{3,5},{5,7},{... | collective-permute-start | bytes 1966088 | tf_op jit(solution)/shard_map/ppermute | solution.py:544
  84.3 4.4 %node_mid.3 = (bf16[2560,512]{1,0:T(8,128)(2,1)S(1)}, bf16[1280,256]{1,0:T(8,128)(2,1)S(1)}, bf16[1280,256]{1,0:T(8,128)(2,1)S(1)}) custom-call(s32[1]{0:T(128)} %bitcast.feat_ref, bf16[2560,512]{1,0:T(8,128)(2,1)S(1)} %get-tuple-element.106.refs_0_, bf16[1280,256]{1,0:T(8,128)(2,1)S(1)} %get-tuple-element.107.refs_1_, ...), custom_call_target="tpu_custom_call", output_to_operand_aliasing={{0}: (1, {})} | custom-call | flops 1048576 | bytes 1024 | tf_op jit(solution)/shard_map/node_mid/pallas_call | solution.py:399
  88.7 0.1 collective-permute-start.13
  88.8 0.5 collective-permute-start.12
  89.3 3.5 %collective-permute-start.20 = (bf16[1280,256]{1,0:T(8,128)(2,1)S(1)}, bf16[1280,256]{1,0:T(8,128)(2,1)S(1)}, u32[]{:S(2)}, u32[]{:S(2)}) collective-permute-start(bf16[1280,256]{1,0:T(8,128)(2,1)S(1)} %get-tuple-element.111), channel_id=1, source_target_pairs={{2,1},{4,3},{6,5},{8,7},{10,9},{12,11},{14,13},{1,2},{3,4},{5,6},{... | collective-permute-start | bytes 1966088 | tf_op jit(solution)/shard_map/ppermute | solution.py:544
  92.8 3.0 %collective-permute-start.19 = (bf16[1280,256]{1,0:T(8,128)(2,1)S(1)}, bf16[1280,256]{1,0:T(8,128)(2,1)S(1)}, u32[]{:S(2)}, u32[]{:S(2)}) collective-permute-start(bf16[1280,256]{1,0:T(8,128)(2,1)S(1)} %get-tuple-element.114.refs_2_), channel_id=1, source_target_pairs={{2,0},{4,2},{6,4},{8,6},{10,8},{12,10},{14,12},{1,3},{3,5},{5,7},{... | collective-permute-start | bytes 1966088 | tf_op jit(solution)/shard_map/ppermute | solution.py:544
  95.8 22.0 %collective-permute-done.15.refs_5_ = bf16[1280,256]{1,0:T(8,128)(2,1)S(1)} collective-permute-done((bf16[1280,256]{1,0:T(8,128)(2,1)S(1)}, bf16[1280,256]{1,0:T(8,128)(2,1)S(1)}, u32[]{:S(2)}, u32[]{:S(2)}) %collective-permute-start.15) | collective-permute-done | bytes 655392 | tf_op jit(solution)/shard_map/ppermute | solution.py:544
  117.8 6.3 %collective-permute-done.14.refs_4_ = bf16[1280,256]{1,0:T(8,128)(2,1)S(1)} collective-permute-done((bf16[1280,256]{1,0:T(8,128)(2,1)S(1)}, bf16[1280,256]{1,0:T(8,128)(2,1)S(1)}, u32[]{:S(2)}, u32[]{:S(2)}) %collective-permute-start.14) | collective-permute-done | bytes 655392 | tf_op jit(solution)/shard_map/ppermute | solution.py:544
  124.1 1.3 collective-permute-start.18
  125.4 1.3 collective-permute-start.16
  126.7 1.3 local_messages.1.refs_6_
  128.0 0.9 collective-permute-done.17
  129.0 1.3 collective-permute-done.16
  130.3 1.6 %node_coarse.1.refs_2_ = f32[320,256]{1,0:T(8,128)S(1)} custom-call(s32[1]{0:T(128)} %bitcast.feat_ref, bf16[320,512]{1,0:T(8,128)(2,1)S(1)} %constant_dynamic-update-slice_fusion.state_ref.refs_0_, bf16[320,512]{1,0:T(8,128)(2,1)S(1)} %pad_maximum_fusion.refs_1_.refs_2_, bf16[320,512]{1,0:T(8,128)(2,1)S(1)} %pad_maximum_fusion.refs_1_.refs_2_, ...), custom_call_target="tpu_custom_call" | custom-call | flops 1048576 | bytes 1024 | tf_op jit(solution)/shard_map/node_coarse/pallas_call | solution.py:399
  131.9 0.2 collective-permute-done.20.refs_5_
  132.2 6.0 %collective-permute-done.19.refs_4_ = bf16[1280,256]{1,0:T(8,128)(2,1)S(1)} collective-permute-done((bf16[1280,256]{1,0:T(8,128)(2,1)S(1)}, bf16[1280,256]{1,0:T(8,128)(2,1)S(1)}, u32[]{:S(2)}, u32[]{:S(2)}) %collective-permute-start.19) | collective-permute-done | bytes 655392 | tf_op jit(solution)/shard_map/ppermute | solution.py:544
  138.1 2.3 %aggregate.6 = (bf16[1280,256]{1,0:T(8,128)(2,1)S(1)}, bf16[1280,256]{1,0:T(8,128)(2,1)S(1)}, bf16[10240,256]{1,0:T(8,128)(2,1)S(1)}) custom-call(s32[1]{0:T(128)} %bitcast.feat_ref, s32[320]{0:T(512)S(1)} %pad_add_fusion.links, bf16[40,128,512]{2,1,0:T(8,128)(2,1)S(1)} %get-tuple-element.80.refs_0_, ...), custom_call_target="tpu_custom_call", output_to_operand_aliasing={{2}: (8, {})} | custom-call | flops 1048576 | bytes 1024 | tf_op jit(solution)/shard_map/aggregate/pallas_call | solution.py:287
  140.4 1.5 collective-permute-start.21
  141.9 1.8 %aggregate.7 = (bf16[1280,256]{1,0:T(8,128)(2,1)S(1)}, bf16[1280,256]{1,0:T(8,128)(2,1)S(1)}) custom-call(s32[1]{0:T(128)} %bitcast.feat_ref, s32[320]{0:T(512)S(1)} %pad_add_fusion.links, bf16[40,128,512]{2,1,0:T(8,128)(2,1)S(1)} %get-tuple-element.80.refs_0_, bf16[40,128,160]{2,1,0:T(8,128)(2,1)S(1)} %get-tuple-element.81.refs_1_, ...), custom_call_target="tpu_custom_call" | custom-call | flops 1048576 | bytes 1024 | tf_op jit(solution)/shard_map/aggregate/pallas_call | solution.py:287
  143.7 0.3 collective-permute-start.22
  144.0 4.2 %node_last.3 = (bf16[1280,512]{1,0:T(8,128)(2,1)S(1)}, bf16[5120,512]{1,0:T(8,128)(2,1)}) custom-call(s32[1]{0:T(128)} %bitcast.feat_ref, bf16[2560,512]{1,0:T(8,128)(2,1)S(1)} %get-tuple-element.109.refs_0_, bf16[1280,256]{1,0:T(8,128)(2,1)S(1)} %get-tuple-element.125.refs_1_, bf16[1280,256]{1,0:T(8,128)(2,1)S(1)} %collective-permute-done.21.refs_2_, ...), custom_call_target="tpu_custom_call" | custom-call | flops 8589934592 | bytes 1024 | tf_op jit(solution)/shard_map/node_last/pallas_call | solution.py:399
  148.2 0.4 collective-permute-start.24
  148.6 3.5 %node_last.4 = (bf16[1024,512]{1,0:T(8,128)(2,1)S(1)}, bf16[5120,512]{1,0:T(8,128)(2,1)}) custom-call(s32[1]{0:T(128)} %bitcast.feat_ref, bf16[2560,512]{1,0:T(8,128)(2,1)S(1)} %get-tuple-element.109.refs_0_, bf16[1280,256]{1,0:T(8,128)(2,1)S(1)} %get-tuple-element.120.refs_1_, ...), custom_call_target="tpu_custom_call", output_to_operand_aliasing={{1}: (8, {})} | custom-call | flops 8589934592 | bytes 1024 | tf_op jit(solution)/shard_map/node_last/pallas_call | solution.py:399
  152.1 0.3 collective-permute-start.23
  152.4 1.7 %node_last.5 = (bf16[256,512]{1,0:T(8,128)(2,1)S(1)}, bf16[5120,512]{1,0:T(8,128)(2,1)}) custom-call(s32[1]{0:T(128)} %bitcast.feat_ref, bf16[2560,512]{1,0:T(8,128)(2,1)S(1)} %get-tuple-element.109.refs_0_, bf16[1280,256]{1,0:T(8,128)(2,1)S(1)} %get-tuple-element.120.refs_1_, ...), custom_call_target="tpu_custom_call", output_to_operand_aliasing={{1}: (9, {})} | custom-call | flops 8589934592 | bytes 1024 | tf_op jit(solution)/shard_map/node_last/pallas_call | solution.py:399
  154.1 0.4 collective-permute-start.25
  154.5 1.2 collective-permute-done.25.refs_1_
  155.7 1.1 assemble.1
  (30 shorter events, 0.1 us)
Async XLA Ops:
  0.8 12.0 %collective-permute-start = (bf16[40,512]{1,0:T(8,128)(2,1)S(1)}, bf16[40,512]{1,0:T(8,128)(2,1)S(1)}, u32[]{:S(2)}, u32[]{:S(2)}) collective-permute-start(bf16[40,512]{1,0:T(8,128)(2,1)S(1)} %slice.3), channel_id=1, source_target_pairs={{0,2},{2,0},{4,6},{6,4},{8,10},{10,8},{12,14},{14,12},{1,3},{3,1},... | collective-permute-start | bytes 122888 | tf_op jit(solution)/shard_map/ppermute | solution.py:446
  6.2 14.5 %copy-start = (bf16[2,256,512]{2,1,0:T(8,128)(2,1)S(1)}, bf16[2,256,512]{2,1,0:T(8,128)(2,1)}, u32[]{:S(2)}) copy-start(bf16[2,256,512]{2,1,0:T(8,128)(2,1)} %refs_6_) | copy-start | bytes 1572868
  6.3 44.7 %copy-start.2 = (s32[40,4]{0,1:T(4,128)S(1)}, s32[40,4]{0,1:T(4,128)}, u32[]{:S(2)}) copy-start(s32[40,4]{0,1:T(4,128)} %param.13) | copy-start | bytes 1924
  6.3 44.7 %copy-start.3 = (s32[40,4]{0,1:T(4,128)S(1)}, s32[40,4]{0,1:T(4,128)}, u32[]{:S(2)}) copy-start(s32[40,4]{0,1:T(4,128)} %param.12) | copy-start | bytes 1924
  6.3 45.1 %copy-start.1 = (s32[5120]{0:T(1024)S(1)}, s32[5120]{0:T(1024)}, u32[]{:S(2)}) copy-start(s32[5120]{0:T(1024)} %param.14) | copy-start | bytes 61444
  6.3 57.8 %collective-permute-start.7 = (bf16[2560,256]{1,0:T(8,128)(2,1)}, bf16[2560,256]{1,0:T(8,128)(2,1)S(1)}, u32[]{:S(2)}, u32[]{:S(2)}) collective-permute-start(bf16[2560,256]{1,0:T(8,128)(2,1)} %message.3.refs_4_), channel_id=1, source_target_pairs={{0,2},{2,4},{4,6},{6,8},{8,10},{10,12},{12,14},{1,3},{3,5},{5,7},{... | collective-permute-start | bytes 3932168 | tf_op jit(solution)/shard_map/ppermute | solution.py:489
  12.8 55.4 %collective-permute-start.6 = (bf16[2560,256]{1,0:T(8,128)(2,1)}, bf16[2560,256]{1,0:T(8,128)(2,1)S(1)}, u32[]{:S(2)}, u32[]{:S(2)}) collective-permute-start(bf16[2560,256]{1,0:T(8,128)(2,1)} %message.2.refs_3_), channel_id=1, source_target_pairs={{2,0},{4,2},{6,4},{8,6},{10,8},{12,10},{14,12},{3,1},{5,3},{7,5},{... | collective-permute-start | bytes 3932168 | tf_op jit(solution)/shard_map/ppermute | solution.py:489
  16.9 41.6 %collective-permute-start.3 = (bf16[2,1024,256]{2,1,0:T(8,128)(2,1)}, bf16[2,1024,256]{2,1,0:T(8,128)(2,1)}, u32[]{:S(2)}, u32[]{:S(2)}) collective-permute-start(bf16[2,1024,256]{2,1,0:T(8,128)(2,1)} %refs_5_), channel_id=1, source_target_pairs={{0,1},{1,0},{2,3},{3,2},{4,5},{5,4},{6,7},{7,6},{8,9},{9,8},{10,11... | collective-permute-start | bytes 3145736 | tf_op jit(solution)/shard_map/ppermute | solution.py:441
  18.5 30.0 %collective-permute-start.1 = (bf16[80,512]{1,0:T(8,128)(2,1)S(1)}, bf16[80,512]{1,0:T(8,128)(2,1)S(1)}, u32[]{:S(2)}, u32[]{:S(2)}) collective-permute-start(bf16[80,512]{1,0:T(8,128)(2,1)S(1)} %pad_maximum_fusion.2), channel_id=1, source_target_pairs={{0,8},{2,10},{4,12},{6,14},{8,0},{10,2},{12,4},{14,6},{1,9},{3,11}... | collective-permute-start | bytes 245768 | tf_op jit(solution)/shard_map/ppermute | solution.py:446
  20.8 35.7 %collective-permute-start.4 = (bf16[2,256,512]{2,1,0:T(8,128)(2,1)S(1)}, bf16[2,256,512]{2,1,0:T(8,128)(2,1)}, u32[]{:S(2)}, u32[]{:S(2)}) collective-permute-start(bf16[2,256,512]{2,1,0:T(8,128)(2,1)S(1)} %copy-done), channel_id=1, source_target_pairs={{0,1},{1,0},{2,3},{3,2},{4,5},{5,4},{6,7},{7,6},{8,9},{9,8},{10,11... | collective-permute-start | bytes 1572872 | tf_op jit(solution)/shard_map/ppermute | solution.py:441
  48.5 9.9 %collective-permute-start.5 = (bf16[2,512,256]{2,1,0:T(8,128)(2,1)}, bf16[2,512,256]{2,1,0:T(8,128)(2,1)}, u32[]{:S(2)}, u32[]{:S(2)}) collective-permute-start(bf16[2,512,256]{2,1,0:T(8,128)(2,1)} %refs_7_), channel_id=1, source_target_pairs={{0,1},{1,0},{2,3},{3,2},{4,5},{5,4},{6,7},{7,6},{8,9},{9,8},{10,11... | collective-permute-start | bytes 1572872 | tf_op jit(solution)/shard_map/ppermute | solution.py:441
  56.5 6.5 %collective-permute-start.2 = (bf16[160,512]{1,0:T(8,128)(2,1)S(1)}, bf16[160,512]{1,0:T(8,128)(2,1)S(1)}, u32[]{:S(2)}, u32[]{:S(2)}) collective-permute-start(bf16[160,512]{1,0:T(8,128)(2,1)S(1)} %pad_maximum_fusion.1), channel_id=1, source_target_pairs={{0,4},{2,6},{4,0},{6,2},{8,12},{10,14},{12,8},{14,10},{1,5},{3,7},... | collective-permute-start | bytes 491528 | tf_op jit(solution)/shard_map/ppermute | solution.py:446
  70.4 2.4 %collective-permute-start.8 = (bf16[1280,256]{1,0:T(8,128)(2,1)S(1)}, bf16[1280,256]{1,0:T(8,128)(2,1)S(1)}, u32[]{:S(2)}, u32[]{:S(2)}) collective-permute-start(bf16[1280,256]{1,0:T(8,128)(2,1)S(1)} %get-tuple-element.90), channel_id=1, source_target_pairs={{0,1},{1,0},{2,3},{3,2},{4,5},{5,4},{6,7},{7,6},{8,9},{9,8},{10,11... | collective-permute-start | bytes 1966088 | tf_op jit(solution)/shard_map/ppermute | solution.py:441
  71.0 6.3 %collective-permute-start.9 = (bf16[40,256]{1,0:T(8,128)(2,1)S(1)}, bf16[40,256]{1,0:T(8,128)(2,1)S(1)}, u32[]{:S(2)}, u32[]{:S(2)}) collective-permute-start(bf16[40,256]{1,0:T(8,128)(2,1)S(1)} %get-tuple-element.103), channel_id=1, source_target_pairs={{0,2},{2,0},{4,6},{6,4},{8,10},{10,8},{12,14},{14,12},{1,3},{3,1},... | collective-permute-start | bytes 61448 | tf_op jit(solution)/shard_map/ppermute | solution.py:446
  77.3 7.0 %collective-permute-start.10 = (bf16[1280,256]{1,0:T(8,128)(2,1)S(1)}, bf16[1280,256]{1,0:T(8,128)(2,1)S(1)}, u32[]{:S(2)}, u32[]{:S(2)}) collective-permute-start(bf16[1280,256]{1,0:T(8,128)(2,1)S(1)} %get-tuple-element.104), channel_id=1, source_target_pairs={{0,1},{1,0},{2,3},{3,2},{4,5},{5,4},{6,7},{7,6},{8,9},{9,8},{10,11... | collective-permute-start | bytes 1966088 | tf_op jit(solution)/shard_map/ppermute | solution.py:441
  77.6 6.7 %collective-permute-start.11 = (bf16[1280,256]{1,0:T(8,128)(2,1)S(1)}, bf16[1280,256]{1,0:T(8,128)(2,1)S(1)}, u32[]{:S(2)}, u32[]{:S(2)}) collective-permute-start(bf16[1280,256]{1,0:T(8,128)(2,1)S(1)} %get-tuple-element.108), channel_id=1, source_target_pairs={{0,1},{1,0},{2,3},{3,2},{4,5},{5,4},{6,7},{7,6},{8,9},{9,8},{10,11... | collective-permute-start | bytes 1966088 | tf_op jit(solution)/shard_map/ppermute | solution.py:441
  77.8 40.0 %collective-permute-start.15 = (bf16[1280,256]{1,0:T(8,128)(2,1)S(1)}, bf16[1280,256]{1,0:T(8,128)(2,1)S(1)}, u32[]{:S(2)}, u32[]{:S(2)}) collective-permute-start(bf16[1280,256]{1,0:T(8,128)(2,1)S(1)} %get-tuple-element.104), channel_id=1, source_target_pairs={{2,1},{4,3},{6,5},{8,7},{10,9},{12,11},{14,13},{1,2},{3,4},{5,6},{... | collective-permute-start | bytes 1966088 | tf_op jit(solution)/shard_map/ppermute | solution.py:544
  81.5 42.6 %collective-permute-start.14 = (bf16[1280,256]{1,0:T(8,128)(2,1)S(1)}, bf16[1280,256]{1,0:T(8,128)(2,1)S(1)}, u32[]{:S(2)}, u32[]{:S(2)}) collective-permute-start(bf16[1280,256]{1,0:T(8,128)(2,1)S(1)} %get-tuple-element.112.refs_0_), channel_id=1, source_target_pairs={{2,0},{4,2},{6,4},{8,6},{10,8},{12,10},{14,12},{1,3},{3,5},{5,7},{... | collective-permute-start | bytes 1966088 | tf_op jit(solution)/shard_map/ppermute | solution.py:544
  88.7 35.3 %collective-permute-start.13 = (bf16[1280,256]{1,0:T(8,128)(2,1)S(1)}, bf16[1280,256]{1,0:T(8,128)(2,1)S(1)}, u32[]{:S(2)}, u32[]{:S(2)}) collective-permute-start(bf16[1280,256]{1,0:T(8,128)(2,1)S(1)} %get-tuple-element.111), channel_id=1, source_target_pairs={{0,1},{1,0},{2,3},{3,2},{4,5},{5,4},{6,7},{7,6},{8,9},{9,8},{10,11... | collective-permute-start | bytes 1966088 | tf_op jit(solution)/shard_map/ppermute | solution.py:441
  88.8 3.9 %collective-permute-start.12 = (bf16[80,256]{1,0:T(8,128)(2,1)S(1)}, bf16[80,256]{1,0:T(8,128)(2,1)S(1)}, u32[]{:S(2)}, u32[]{:S(2)}) collective-permute-start(bf16[80,256]{1,0:T(8,128)(2,1)S(1)} %constant_dynamic-update-slice_fusion.3), channel_id=1, source_target_pairs={{0,1},{1,0},{2,3},{3,2},{4,5},{5,4},{6,7},{7,6},{8,9},{9,8},{10,11... | collective-permute-start | bytes 122888 | tf_op jit(solution)/shard_map/ppermute | solution.py:441
  89.3 42.8 %collective-permute-start.20 = (bf16[1280,256]{1,0:T(8,128)(2,1)S(1)}, bf16[1280,256]{1,0:T(8,128)(2,1)S(1)}, u32[]{:S(2)}, u32[]{:S(2)}) collective-permute-start(bf16[1280,256]{1,0:T(8,128)(2,1)S(1)} %get-tuple-element.111), channel_id=1, source_target_pairs={{2,1},{4,3},{6,5},{8,7},{10,9},{12,11},{14,13},{1,2},{3,4},{5,6},{... | collective-permute-start | bytes 1966088 | tf_op jit(solution)/shard_map/ppermute | solution.py:544
  92.8 45.3 %collective-permute-start.19 = (bf16[1280,256]{1,0:T(8,128)(2,1)S(1)}, bf16[1280,256]{1,0:T(8,128)(2,1)S(1)}, u32[]{:S(2)}, u32[]{:S(2)}) collective-permute-start(bf16[1280,256]{1,0:T(8,128)(2,1)S(1)} %get-tuple-element.114.refs_2_), channel_id=1, source_target_pairs={{2,0},{4,2},{6,4},{8,6},{10,8},{12,10},{14,12},{1,3},{3,5},{5,7},{... | collective-permute-start | bytes 1966088 | tf_op jit(solution)/shard_map/ppermute | solution.py:544
  124.1 3.9 %collective-permute-start.18 = (bf16[80,512]{1,0:T(8,128)(2,1)S(1)}, bf16[80,512]{1,0:T(8,128)(2,1)S(1)}, u32[]{:S(2)}, u32[]{:S(2)}) collective-permute-start(bf16[80,512]{1,0:T(8,128)(2,1)S(1)} %pad_maximum_fusion.3), channel_id=1, source_target_pairs={{0,12},{2,14},{4,8},{6,10},{8,4},{10,6},{12,0},{14,2},{1,13},{3,15... | collective-permute-start | bytes 245768 | tf_op jit(solution)/shard_map/ppermute | solution.py:446
  125.4 3.6 %collective-permute-start.17 = (bf16[80,512]{1,0:T(8,128)(2,1)S(1)}, bf16[80,512]{1,0:T(8,128)(2,1)S(1)}, u32[]{:S(2)}, u32[]{:S(2)}) collective-permute-start(bf16[80,512]{1,0:T(8,128)(2,1)S(1)} %pad_maximum_fusion.3), channel_id=1, source_target_pairs={{0,4},{2,6},{4,0},{6,2},{8,12},{10,14},{12,8},{14,10},{1,5},{3,7},... | collective-permute-start | bytes 245768 | tf_op jit(solution)/shard_map/ppermute | solution.py:446
  125.4 4.9 %collective-permute-start.16 = (bf16[80,512]{1,0:T(8,128)(2,1)S(1)}, bf16[80,512]{1,0:T(8,128)(2,1)S(1)}, u32[]{:S(2)}, u32[]{:S(2)}) collective-permute-start(bf16[80,512]{1,0:T(8,128)(2,1)S(1)} %pad_maximum_fusion.3), channel_id=1, source_target_pairs={{0,8},{2,10},{4,12},{6,14},{8,0},{10,2},{12,4},{14,6},{1,9},{3,11}... | collective-permute-start | bytes 245768 | tf_op jit(solution)/shard_map/ppermute | solution.py:446
  140.4 3.4 %collective-permute-start.21 = (bf16[1280,256]{1,0:T(8,128)(2,1)S(1)}, bf16[1280,256]{1,0:T(8,128)(2,1)S(1)}, u32[]{:S(2)}, u32[]{:S(2)}) collective-permute-start(bf16[1280,256]{1,0:T(8,128)(2,1)S(1)} %get-tuple-element.121), channel_id=1, source_target_pairs={{0,1},{1,0},{2,3},{3,2},{4,5},{5,4},{6,7},{7,6},{8,9},{9,8},{10,11... | collective-permute-start | bytes 1966088 | tf_op jit(solution)/shard_map/ppermute | solution.py:441
  143.7 4.9 %collective-permute-start.22 = (bf16[1280,256]{1,0:T(8,128)(2,1)S(1)}, bf16[1280,256]{1,0:T(8,128)(2,1)S(1)}, u32[]{:S(2)}, u32[]{:S(2)}) collective-permute-start(bf16[1280,256]{1,0:T(8,128)(2,1)S(1)} %get-tuple-element.124), channel_id=1, source_target_pairs={{0,1},{1,0},{2,3},{3,2},{4,5},{5,4},{6,7},{7,6},{8,9},{9,8},{10,11... | collective-permute-start | bytes 1966088 | tf_op jit(solution)/shard_map/ppermute | solution.py:441
  148.2 4.1 %collective-permute-start.24 = (bf16[1280,512]{1,0:T(8,128)(2,1)S(1)}, bf16[1280,512]{1,0:T(8,128)(2,1)S(1)}, u32[]{:S(2)}, u32[]{:S(2)}) collective-permute-start(bf16[1280,512]{1,0:T(8,128)(2,1)S(1)} %get-tuple-element.129), channel_id=1, source_target_pairs={{0,1},{1,0},{2,3},{3,2},{4,5},{5,4},{6,7},{7,6},{8,9},{9,8},{10,11... | collective-permute-start | bytes 3932168 | tf_op jit(solution)/shard_map/ppermute | solution.py:441
  152.1 3.6 %collective-permute-start.23 = (bf16[1024,512]{1,0:T(8,128)(2,1)S(1)}, bf16[1024,512]{1,0:T(8,128)(2,1)S(1)}, u32[]{:S(2)}, u32[]{:S(2)}) collective-permute-start(bf16[1024,512]{1,0:T(8,128)(2,1)S(1)} %get-tuple-element.128), channel_id=1, source_target_pairs={{0,1},{1,0},{2,3},{3,2},{4,5},{5,4},{6,7},{7,6},{8,9},{9,8},{10,11... | collective-permute-start | bytes 3145736 | tf_op jit(solution)/shard_map/ppermute | solution.py:441
  154.1 1.6 %collective-permute-start.25 = (bf16[256,512]{1,0:T(8,128)(2,1)S(1)}, bf16[256,512]{1,0:T(8,128)(2,1)S(1)}, u32[]{:S(2)}, u32[]{:S(2)}) collective-permute-start(bf16[256,512]{1,0:T(8,128)(2,1)S(1)} %get-tuple-element.131), channel_id=1, source_target_pairs={{0,1},{1,0},{2,3},{3,2},{4,5},{5,4},{6,7},{7,6},{8,9},{9,8},{10,11... | collective-permute-start | bytes 786440 | tf_op jit(solution)/shard_map/ppermute | solution.py:441

commit v13 on v12

--- a/solution.py
+++ b/solution.py
@@ -25,7 +25,8 @@
 
 
 def silu(v):
-    return 0.5 * v * (1.0 + jnp.tanh(0.5 * v))
+    half = 0.5 * v
+    return half + half * jnp.tanh(half)
 
 
 def dot(a, b):

time: 157 us -> 158 us (level)
  no operation moved by 1% of the time
where the time goes in v13:
time: 158 us; the launch traced here: 157 us
  waiting for transfers between devices  72.8 us (46%)
  Pallas kernels  46.2 us (29%)
  starting transfers between devices  36.3 us (23%)
    ppermute x7, waiting for transfers between devices, fetch(): lax.ppermute(held, 'patch', [(pos, pos ^ stride) for pos in range(count)])  32.5 us
    ppermute x2, waiting for transfers between devices, shards(): lax.ppermute(other, ('patch', 'feat'), other_patch)  22.2 us
    pallas_call x6, Pallas kernels, node_call(): pl.pallas_call(functools.partial(node_kernel, mode, layer, start, offset,...  20.3 us
    ppermute x2, waiting for transfers between devices, shards(): lax.ppermute(own, ('patch', 'feat'), own_patch)  12.2 us
    ppermute x13, starting transfers between devices, swap_feat(): return lax.ppermute(array, 'feat', [(0, 1), (1, 0)])  8.93 us
    pallas_call x2, Pallas kernels, message_call(): pl.pallas_call(functools.partial(message_kernel, start, sizes), in_specs=...  8.48 us
    ppermute x7, starting transfers between devices, fetch(): lax.ppermute(held, 'patch', [(pos, pos ^ stride) for pos in range(count)])  8.1 us
    pallas_call x4, Pallas kernels, aggregate_call(): pl.pallas_call(functools.partial(aggregate_kernel, places, start), grid_s...  8.1 us
  transfers between devices with their start and end apart: 26, of which 11 were waited for; matrix products, arithmetic and copies ran while one was open for 0% of the time, Pallas kernels for 26%

profile of v13, /device:TPU:9, one launch (start us, length us, event | category | flops | bytes accessed | tf_op | source)
XLA Modules:
  0.0 157.2 jit_solution(5572270657663267851)
XLA Ops:
  0.0 0.8 slice.3
  0.8 1.2 collective-permute-start
  2.0 4.2 %message.3.refs_4_ = bf16[2560,256]{1,0:T(8,128)(2,1)} custom-call(bf16[5120,512]{1,0:T(8,128)(2,1)} %refs_2_.1, bf16[2,512,256]{2,1,0:T(8,128)(2,1)} %refs_7_), custom_call_target="tpu_custom_call" | custom-call | flops 1048576 | bytes 1024 | tf_op jit(solution)/shard_map/message/pallas_call | solution.py:96
  6.3 0.0 copy-start
  6.3 0.0 copy-start.2
  6.3 0.0 copy-start.3
  6.3 0.0 copy-start.1
  6.3 2.3 %collective-permute-start.7 = (bf16[2560,256]{1,0:T(8,128)(2,1)}, bf16[2560,256]{1,0:T(8,128)(2,1)S(1)}, u32[]{:S(2)}, u32[]{:S(2)}) collective-permute-start(bf16[2560,256]{1,0:T(8,128)(2,1)} %message.3.refs_4_), channel_id=1, source_target_pairs={{0,2},{2,4},{4,6},{6,8},{8,10},{10,12},{12,14},{1,3},{3,5},{5,7},{... | collective-permute-start | bytes 3932168 | tf_op jit(solution)/shard_map/ppermute | solution.py:490
  8.6 4.2 %message.2.refs_3_ = bf16[2560,256]{1,0:T(8,128)(2,1)} custom-call(bf16[5120,512]{1,0:T(8,128)(2,1)} %refs_2_.1, bf16[2,512,256]{2,1,0:T(8,128)(2,1)} %refs_7_), custom_call_target="tpu_custom_call" | custom-call | flops 1048576 | bytes 1024 | tf_op jit(solution)/shard_map/message/pallas_call | solution.py:96
  12.8 0.0 collective-permute-done
  12.9 4.0 %collective-permute-start.6 = (bf16[2560,256]{1,0:T(8,128)(2,1)}, bf16[2560,256]{1,0:T(8,128)(2,1)S(1)}, u32[]{:S(2)}, u32[]{:S(2)}) collective-permute-start(bf16[2560,256]{1,0:T(8,128)(2,1)} %message.2.refs_3_), channel_id=1, source_target_pairs={{2,0},{4,2},{6,4},{8,6},{10,8},{12,10},{14,12},{3,1},{5,3},{7,5},{... | collective-permute-start | bytes 3932168 | tf_op jit(solution)/shard_map/ppermute | solution.py:490
  16.9 1.6 %collective-permute-start.3 = (bf16[2,1024,256]{2,1,0:T(8,128)(2,1)}, bf16[2,1024,256]{2,1,0:T(8,128)(2,1)}, u32[]{:S(2)}, u32[]{:S(2)}) collective-permute-start(bf16[2,1024,256]{2,1,0:T(8,128)(2,1)} %refs_5_), channel_id=1, source_target_pairs={{0,1},{1,0},{2,3},{3,2},{4,5},{5,4},{6,7},{7,6},{8,9},{9,8},{10,11... | collective-permute-start | bytes 3145736 | tf_op jit(solution)/shard_map/ppermute | solution.py:442
  18.5 2.3 %collective-permute-start.1 = (bf16[80,512]{1,0:T(8,128)(2,1)S(1)}, bf16[80,512]{1,0:T(8,128)(2,1)S(1)}, u32[]{:S(2)}, u32[]{:S(2)}) collective-permute-start(bf16[80,512]{1,0:T(8,128)(2,1)S(1)} %pad_maximum_fusion.2), channel_id=1, source_target_pairs={{0,8},{2,10},{4,12},{6,14},{8,0},{10,2},{12,4},{14,6},{1,9},{3,11}... | collective-permute-start | bytes 245768 | tf_op jit(solution)/shard_map/ppermute | solution.py:447
  20.8 0.3 collective-permute-start.4
  21.2 27.4 %collective-permute-done.1 = bf16[80,512]{1,0:T(8,128)(2,1)S(1)} collective-permute-done((bf16[80,512]{1,0:T(8,128)(2,1)S(1)}, bf16[80,512]{1,0:T(8,128)(2,1)S(1)}, u32[]{:S(2)}, u32[]{:S(2)}) %collective-permute-start.1) | collective-permute-done | bytes 81952 | tf_op jit(solution)/shard_map/ppermute | solution.py:447
  48.5 2.5 %collective-permute-start.5 = (bf16[2,512,256]{2,1,0:T(8,128)(2,1)}, bf16[2,512,256]{2,1,0:T(8,128)(2,1)}, u32[]{:S(2)}, u32[]{:S(2)}) collective-permute-start(bf16[2,512,256]{2,1,0:T(8,128)(2,1)} %refs_7_), channel_id=1, source_target_pairs={{0,1},{1,0},{2,3},{3,2},{4,5},{5,4},{6,7},{7,6},{8,9},{9,8},{10,11... | collective-permute-start | bytes 1572872 | tf_op jit(solution)/shard_map/ppermute | solution.py:442
  51.1 0.1 copy.19
  51.2 0.1 reshape.52
  51.3 0.1 copy.18
  51.4 0.1 mul.15
  51.5 0.1 pad_add_fusion.links
  51.6 5.0 %stage.1 = (bf16[40,128,512]{2,1,0:T(8,128)(2,1)S(1)}, bf16[40,128,160]{2,1,0:T(8,128)(2,1)S(1)}, bf16[2560,512]{1,0:T(8,128)(2,1)S(1)}, bf16[10240,256]{1,0:T(8...) custom-call(s32[1]{0:T(128)} %bitcast.feat_ref, ...), custom_call_target="tpu_custom_call" | custom-call | flops 1048576 | bytes 1024 | tf_op jit(solution)/shard_map/stage/pallas_call | solution.py:167
  56.6 0.0 collective-permute-done.4.refs_1_
  56.6 1.9 %collective-permute-start.2 = (bf16[160,512]{1,0:T(8,128)(2,1)S(1)}, bf16[160,512]{1,0:T(8,128)(2,1)S(1)}, u32[]{:S(2)}, u32[]{:S(2)}) collective-permute-start(bf16[160,512]{1,0:T(8,128)(2,1)S(1)} %pad_maximum_fusion.1), channel_id=1, source_target_pairs={{0,4},{2,6},{4,0},{6,2},{8,12},{10,14},{12,8},{14,10},{1,5},{3,7},... | collective-permute-start | bytes 491528 | tf_op jit(solution)/shard_map/ppermute | solution.py:447
  58.5 1.5 weights.1
  60.1 3.0 %collective-permute-done.2 = bf16[160,512]{1,0:T(8,128)(2,1)S(1)} collective-permute-done((bf16[160,512]{1,0:T(8,128)(2,1)S(1)}, bf16[160,512]{1,0:T(8,128)(2,1)S(1)}, u32[]{:S(2)}, u32[]{:S(2)}) %collective-permute-start.2) | collective-permute-done | bytes 163872 | tf_op jit(solution)/shard_map/ppermute | solution.py:447
  63.0 0.5 coarse_message.1.refs_2_
  63.5 0.6 collective-permute-done.7.refs_5_
  64.1 4.1 %collective-permute-done.6.refs_4_ = bf16[2560,256]{1,0:T(8,128)(2,1)S(1)} collective-permute-done((bf16[2560,256]{1,0:T(8,128)(2,1)}, bf16[2560,256]{1,0:T(8,128)(2,1)S(1)}, u32[]{:S(2)}, u32[]{:S(2)}) %collective-permute-start.6) | collective-permute-done | bytes 1310752 | tf_op jit(solution)/shard_map/ppermute | solution.py:490
  68.2 2.2 %aggregate.4 = (bf16[1280,256]{1,0:T(8,128)(2,1)S(1)}, bf16[1280,256]{1,0:T(8,128)(2,1)S(1)}, bf16[40,256]{1,0:T(8,128)(2,1)S(1)}, bf16[10240,256]{1,0:T(8,128)(2,1)S(1)}) custom-call(s32[1]{0:T(128)} %bitcast.feat_ref, s32[320]{0:T(512)S(1)} %pad_add_fusion.links, ...), custom_call_target="tpu_custom_call", output_to_operand_aliasing={{3}: (8, {})} | custom-call | flops 1048576 | bytes 1024 | tf_op jit(solution)/shard_map/aggregate/pallas_call | solution.py:288
  70.4 0.6 collective-permute-start.8
  71.0 1.8 %aggregate.5 = (bf16[1280,256]{1,0:T(8,128)(2,1)S(1)}, bf16[1280,256]{1,0:T(8,128)(2,1)S(1)}) custom-call(s32[1]{0:T(128)} %bitcast.feat_ref, s32[320]{0:T(512)S(1)} %pad_add_fusion.links, bf16[40,128,512]{2,1,0:T(8,128)(2,1)S(1)} %get-tuple-element.80.refs_0_, bf16[40,128,160]{2,1,0:T(8,128)(2,1)S(1)} %get-tuple-element.81.refs_1_, ...), custom_call_target="tpu_custom_call" | custom-call | flops 1048576 | bytes 1024 | tf_op jit(solution)/shard_map/aggregate/pallas_call | solution.py:288
  72.8 4.6 %node_mid.2 = (bf16[2560,512]{1,0:T(8,128)(2,1)S(1)}, bf16[1280,256]{1,0:T(8,128)(2,1)S(1)}, bf16[1280,256]{1,0:T(8,128)(2,1)S(1)}) custom-call(s32[1]{0:T(128)} %bitcast.feat_ref, bf16[2560,512]{1,0:T(8,128)(2,1)S(1)} %get-tuple-element.73.refs_0_, bf16[1280,256]{1,0:T(8,128)(2,1)S(1)} %get-tuple-element.94.refs_1_, ...), custom_call_target="tpu_custom_call", output_to_operand_aliasing={{0}: (1, {})} | custom-call | flops 1048576 | bytes 1024 | tf_op jit(solution)/shard_map/node_mid/pallas_call | solution.py:400
  77.4 0.3 collective-permute-start.10
  77.7 0.3 collective-permute-start.11
  78.0 3.6 %collective-permute-start.15 = (bf16[1280,256]{1,0:T(8,128)(2,1)S(1)}, bf16[1280,256]{1,0:T(8,128)(2,1)S(1)}, u32[]{:S(2)}, u32[]{:S(2)}) collective-permute-start(bf16[1280,256]{1,0:T(8,128)(2,1)S(1)} %get-tuple-element.104), channel_id=1, source_target_pairs={{2,1},{4,3},{6,5},{8,7},{10,9},{12,11},{14,13},{1,2},{3,4},{5,6},{... | collective-permute-start | bytes 1966088 | tf_op jit(solution)/shard_map/ppermute | solution.py:545
  81.6 2.8 %collective-permute-start.14 = (bf16[1280,256]{1,0:T(8,128)(2,1)S(1)}, bf16[1280,256]{1,0:T(8,128)(2,1)S(1)}, u32[]{:S(2)}, u32[]{:S(2)}) collective-permute-start(bf16[1280,256]{1,0:T(8,128)(2,1)S(1)} %get-tuple-element.112.refs_0_), channel_id=1, source_target_pairs={{2,0},{4,2},{6,4},{8,6},{10,8},{12,10},{14,12},{1,3},{3,5},{5,7},{... | collective-permute-start | bytes 1966088 | tf_op jit(solution)/shard_map/ppermute | solution.py:545
  84.4 4.6 %node_mid.3 = (bf16[2560,512]{1,0:T(8,128)(2,1)S(1)}, bf16[1280,256]{1,0:T(8,128)(2,1)S(1)}, bf16[1280,256]{1,0:T(8,128)(2,1)S(1)}) custom-call(s32[1]{0:T(128)} %bitcast.feat_ref, bf16[2560,512]{1,0:T(8,128)(2,1)S(1)} %get-tuple-element.106.refs_0_, bf16[1280,256]{1,0:T(8,128)(2,1)S(1)} %get-tuple-element.107.refs_1_, ...), custom_call_target="tpu_custom_call", output_to_operand_aliasing={{0}: (1, {})} | custom-call | flops 1048576 | bytes 1024 | tf_op jit(solution)/shard_map/node_mid/pallas_call | solution.py:400
  89.0 0.1 collective-permute-start.13
  89.1 0.5 collective-permute-start.12
  89.6 3.5 %collective-permute-start.20 = (bf16[1280,256]{1,0:T(8,128)(2,1)S(1)}, bf16[1280,256]{1,0:T(8,128)(2,1)S(1)}, u32[]{:S(2)}, u32[]{:S(2)}) collective-permute-start(bf16[1280,256]{1,0:T(8,128)(2,1)S(1)} %get-tuple-element.111), channel_id=1, source_target_pairs={{2,1},{4,3},{6,5},{8,7},{10,9},{12,11},{14,13},{1,2},{3,4},{5,6},{... | collective-permute-start | bytes 1966088 | tf_op jit(solution)/shard_map/ppermute | solution.py:545
  93.1 3.1 %collective-permute-start.19 = (bf16[1280,256]{1,0:T(8,128)(2,1)S(1)}, bf16[1280,256]{1,0:T(8,128)(2,1)S(1)}, u32[]{:S(2)}, u32[]{:S(2)}) collective-permute-start(bf16[1280,256]{1,0:T(8,128)(2,1)S(1)} %get-tuple-element.114.refs_2_), channel_id=1, source_target_pairs={{2,0},{4,2},{6,4},{8,6},{10,8},{12,10},{14,12},{1,3},{3,5},{5,7},{... | collective-permute-start | bytes 1966088 | tf_op jit(solution)/shard_map/ppermute | solution.py:545
  96.1 21.8 %collective-permute-done.15.refs_5_ = bf16[1280,256]{1,0:T(8,128)(2,1)S(1)} collective-permute-done((bf16[1280,256]{1,0:T(8,128)(2,1)S(1)}, bf16[1280,256]{1,0:T(8,128)(2,1)S(1)}, u32[]{:S(2)}, u32[]{:S(2)}) %collective-permute-start.15) | collective-permute-done | bytes 655392 | tf_op jit(solution)/shard_map/ppermute | solution.py:545
  118.0 6.2 %collective-permute-done.14.refs_4_ = bf16[1280,256]{1,0:T(8,128)(2,1)S(1)} collective-permute-done((bf16[1280,256]{1,0:T(8,128)(2,1)S(1)}, bf16[1280,256]{1,0:T(8,128)(2,1)S(1)}, u32[]{:S(2)}, u32[]{:S(2)}) %collective-permute-start.14) | collective-permute-done | bytes 655392 | tf_op jit(solution)/shard_map/ppermute | solution.py:545
  124.2 1.3 collective-permute-start.18
  125.5 1.3 collective-permute-start.16
  126.9 1.3 local_messages.1.refs_6_
  128.2 0.9 collective-permute-done.17
  129.1 1.3 collective-permute-done.16
  130.4 1.6 %node_coarse.1.refs_2_ = f32[320,256]{1,0:T(8,128)S(1)} custom-call(s32[1]{0:T(128)} %bitcast.feat_ref, bf16[320,512]{1,0:T(8,128)(2,1)S(1)} %constant_dynamic-update-slice_fusion.state_ref.refs_0_, bf16[320,512]{1,0:T(8,128)(2,1)S(1)} %pad_maximum_fusion.refs_1_.refs_2_, bf16[320,512]{1,0:T(8,128)(2,1)S(1)} %pad_maximum_fusion.refs_1_.refs_2_, ...), custom_call_target="tpu_custom_call" | custom-call | flops 1048576 | bytes 1024 | tf_op jit(solution)/shard_map/node_coarse/pallas_call | solution.py:400
  132.0 0.3 collective-permute-done.20.refs_5_
  132.3 5.9 %collective-permute-done.19.refs_4_ = bf16[1280,256]{1,0:T(8,128)(2,1)S(1)} collective-permute-done((bf16[1280,256]{1,0:T(8,128)(2,1)S(1)}, bf16[1280,256]{1,0:T(8,128)(2,1)S(1)}, u32[]{:S(2)}, u32[]{:S(2)}) %collective-permute-start.19) | collective-permute-done | bytes 655392 | tf_op jit(solution)/shard_map/ppermute | solution.py:545
  138.3 2.3 %aggregate.6 = (bf16[1280,256]{1,0:T(8,128)(2,1)S(1)}, bf16[1280,256]{1,0:T(8,128)(2,1)S(1)}, bf16[10240,256]{1,0:T(8,128)(2,1)S(1)}) custom-call(s32[1]{0:T(128)} %bitcast.feat_ref, s32[320]{0:T(512)S(1)} %pad_add_fusion.links, bf16[40,128,512]{2,1,0:T(8,128)(2,1)S(1)} %get-tuple-element.80.refs_0_, ...), custom_call_target="tpu_custom_call", output_to_operand_aliasing={{2}: (8, {})} | custom-call | flops 1048576 | bytes 1024 | tf_op jit(solution)/shard_map/aggregate/pallas_call | solution.py:288
  140.5 1.5 collective-permute-start.21
  142.1 1.8 %aggregate.7 = (bf16[1280,256]{1,0:T(8,128)(2,1)S(1)}, bf16[1280,256]{1,0:T(8,128)(2,1)S(1)}) custom-call(s32[1]{0:T(128)} %bitcast.feat_ref, s32[320]{0:T(512)S(1)} %pad_add_fusion.links, bf16[40,128,512]{2,1,0:T(8,128)(2,1)S(1)} %get-tuple-element.80.refs_0_, bf16[40,128,160]{2,1,0:T(8,128)(2,1)S(1)} %get-tuple-element.81.refs_1_, ...), custom_call_target="tpu_custom_call" | custom-call | flops 1048576 | bytes 1024 | tf_op jit(solution)/shard_map/aggregate/pallas_call | solution.py:288
  143.9 0.3 collective-permute-start.22
  144.2 4.3 %node_last.3 = (bf16[1280,512]{1,0:T(8,128)(2,1)S(1)}, bf16[5120,512]{1,0:T(8,128)(2,1)}) custom-call(s32[1]{0:T(128)} %bitcast.feat_ref, bf16[2560,512]{1,0:T(8,128)(2,1)S(1)} %get-tuple-element.109.refs_0_, bf16[1280,256]{1,0:T(8,128)(2,1)S(1)} %get-tuple-element.125.refs_1_, bf16[1280,256]{1,0:T(8,128)(2,1)S(1)} %collective-permute-done.21.refs_2_, ...), custom_call_target="tpu_custom_call" | custom-call | flops 8589934592 | bytes 1024 | tf_op jit(solution)/shard_map/node_last/pallas_call | solution.py:400
  148.4 0.4 collective-permute-start.24
  148.8 3.6 %node_last.4 = (bf16[1024,512]{1,0:T(8,128)(2,1)S(1)}, bf16[5120,512]{1,0:T(8,128)(2,1)}) custom-call(s32[1]{0:T(128)} %bitcast.feat_ref, bf16[2560,512]{1,0:T(8,128)(2,1)S(1)} %get-tuple-element.109.refs_0_, bf16[1280,256]{1,0:T(8,128)(2,1)S(1)} %get-tuple-element.120.refs_1_, ...), custom_call_target="tpu_custom_call", output_to_operand_aliasing={{1}: (8, {})} | custom-call | flops 8589934592 | bytes 1024 | tf_op jit(solution)/shard_map/node_last/pallas_call | solution.py:400
  152.4 0.2 collective-permute-start.23
  152.6 1.7 %node_last.5 = (bf16[256,512]{1,0:T(8,128)(2,1)S(1)}, bf16[5120,512]{1,0:T(8,128)(2,1)}) custom-call(s32[1]{0:T(128)} %bitcast.feat_ref, bf16[2560,512]{1,0:T(8,128)(2,1)S(1)} %get-tuple-element.109.refs_0_, bf16[1280,256]{1,0:T(8,128)(2,1)S(1)} %get-tuple-element.120.refs_1_, ...), custom_call_target="tpu_custom_call", output_to_operand_aliasing={{1}: (9, {})} | custom-call | flops 8589934592 | bytes 1024 | tf_op jit(solution)/shard_map/node_last/pallas_call | solution.py:400
  154.4 0.4 collective-permute-start.25
  154.8 1.2 collective-permute-done.25.refs_1_
  156.0 1.1 assemble.1
  (30 shorter events, 0.1 us)
Async XLA Ops:
  0.8 12.1 %collective-permute-start = (bf16[40,512]{1,0:T(8,128)(2,1)S(1)}, bf16[40,512]{1,0:T(8,128)(2,1)S(1)}, u32[]{:S(2)}, u32[]{:S(2)}) collective-permute-start(bf16[40,512]{1,0:T(8,128)(2,1)S(1)} %slice.3), channel_id=1, source_target_pairs={{0,2},{2,0},{4,6},{6,4},{8,10},{10,8},{12,14},{14,12},{1,3},{3,1},... | collective-permute-start | bytes 122888 | tf_op jit(solution)/shard_map/ppermute | solution.py:447
  6.3 14.6 %copy-start = (bf16[2,256,512]{2,1,0:T(8,128)(2,1)S(1)}, bf16[2,256,512]{2,1,0:T(8,128)(2,1)}, u32[]{:S(2)}) copy-start(bf16[2,256,512]{2,1,0:T(8,128)(2,1)} %refs_6_) | copy-start | bytes 1572868
  6.3 44.8 %copy-start.2 = (s32[40,4]{0,1:T(4,128)S(1)}, s32[40,4]{0,1:T(4,128)}, u32[]{:S(2)}) copy-start(s32[40,4]{0,1:T(4,128)} %param.13) | copy-start | bytes 1924
  6.3 44.8 %copy-start.3 = (s32[40,4]{0,1:T(4,128)S(1)}, s32[40,4]{0,1:T(4,128)}, u32[]{:S(2)}) copy-start(s32[40,4]{0,1:T(4,128)} %param.12) | copy-start | bytes 1924
  6.3 45.2 %copy-start.1 = (s32[5120]{0:T(1024)S(1)}, s32[5120]{0:T(1024)}, u32[]{:S(2)}) copy-start(s32[5120]{0:T(1024)} %param.14) | copy-start | bytes 61444
  6.3 57.8 %collective-permute-start.7 = (bf16[2560,256]{1,0:T(8,128)(2,1)}, bf16[2560,256]{1,0:T(8,128)(2,1)S(1)}, u32[]{:S(2)}, u32[]{:S(2)}) collective-permute-start(bf16[2560,256]{1,0:T(8,128)(2,1)} %message.3.refs_4_), channel_id=1, source_target_pairs={{0,2},{2,4},{4,6},{6,8},{8,10},{10,12},{12,14},{1,3},{3,5},{5,7},{... | collective-permute-start | bytes 3932168 | tf_op jit(solution)/shard_map/ppermute | solution.py:490
  12.9 55.4 %collective-permute-start.6 = (bf16[2560,256]{1,0:T(8,128)(2,1)}, bf16[2560,256]{1,0:T(8,128)(2,1)S(1)}, u32[]{:S(2)}, u32[]{:S(2)}) collective-permute-start(bf16[2560,256]{1,0:T(8,128)(2,1)} %message.2.refs_3_), channel_id=1, source_target_pairs={{2,0},{4,2},{6,4},{8,6},{10,8},{12,10},{14,12},{3,1},{5,3},{7,5},{... | collective-permute-start | bytes 3932168 | tf_op jit(solution)/shard_map/ppermute | solution.py:490
  16.9 41.6 %collective-permute-start.3 = (bf16[2,1024,256]{2,1,0:T(8,128)(2,1)}, bf16[2,1024,256]{2,1,0:T(8,128)(2,1)}, u32[]{:S(2)}, u32[]{:S(2)}) collective-permute-start(bf16[2,1024,256]{2,1,0:T(8,128)(2,1)} %refs_5_), channel_id=1, source_target_pairs={{0,1},{1,0},{2,3},{3,2},{4,5},{5,4},{6,7},{7,6},{8,9},{9,8},{10,11... | collective-permute-start | bytes 3145736 | tf_op jit(solution)/shard_map/ppermute | solution.py:442
  18.5 30.0 %collective-permute-start.1 = (bf16[80,512]{1,0:T(8,128)(2,1)S(1)}, bf16[80,512]{1,0:T(8,128)(2,1)S(1)}, u32[]{:S(2)}, u32[]{:S(2)}) collective-permute-start(bf16[80,512]{1,0:T(8,128)(2,1)S(1)} %pad_maximum_fusion.2), channel_id=1, source_target_pairs={{0,8},{2,10},{4,12},{6,14},{8,0},{10,2},{12,4},{14,6},{1,9},{3,11}... | collective-permute-start | bytes 245768 | tf_op jit(solution)/shard_map/ppermute | solution.py:447
  20.8 35.7 %collective-permute-start.4 = (bf16[2,256,512]{2,1,0:T(8,128)(2,1)S(1)}, bf16[2,256,512]{2,1,0:T(8,128)(2,1)}, u32[]{:S(2)}, u32[]{:S(2)}) collective-permute-start(bf16[2,256,512]{2,1,0:T(8,128)(2,1)S(1)} %copy-done), channel_id=1, source_target_pairs={{0,1},{1,0},{2,3},{3,2},{4,5},{5,4},{6,7},{7,6},{8,9},{9,8},{10,11... | collective-permute-start | bytes 1572872 | tf_op jit(solution)/shard_map/ppermute | solution.py:442
  48.5 9.9 %collective-permute-start.5 = (bf16[2,512,256]{2,1,0:T(8,128)(2,1)}, bf16[2,512,256]{2,1,0:T(8,128)(2,1)}, u32[]{:S(2)}, u32[]{:S(2)}) collective-permute-start(bf16[2,512,256]{2,1,0:T(8,128)(2,1)} %refs_7_), channel_id=1, source_target_pairs={{0,1},{1,0},{2,3},{3,2},{4,5},{5,4},{6,7},{7,6},{8,9},{9,8},{10,11... | collective-permute-start | bytes 1572872 | tf_op jit(solution)/shard_map/ppermute | solution.py:442
  56.6 6.5 %collective-permute-start.2 = (bf16[160,512]{1,0:T(8,128)(2,1)S(1)}, bf16[160,512]{1,0:T(8,128)(2,1)S(1)}, u32[]{:S(2)}, u32[]{:S(2)}) collective-permute-start(bf16[160,512]{1,0:T(8,128)(2,1)S(1)} %pad_maximum_fusion.1), channel_id=1, source_target_pairs={{0,4},{2,6},{4,0},{6,2},{8,12},{10,14},{12,8},{14,10},{1,5},{3,7},... | collective-permute-start | bytes 491528 | tf_op jit(solution)/shard_map/ppermute | solution.py:447
  70.4 2.4 %collective-permute-start.8 = (bf16[1280,256]{1,0:T(8,128)(2,1)S(1)}, bf16[1280,256]{1,0:T(8,128)(2,1)S(1)}, u32[]{:S(2)}, u32[]{:S(2)}) collective-permute-start(bf16[1280,256]{1,0:T(8,128)(2,1)S(1)} %get-tuple-element.90), channel_id=1, source_target_pairs={{0,1},{1,0},{2,3},{3,2},{4,5},{5,4},{6,7},{7,6},{8,9},{9,8},{10,11... | collective-permute-start | bytes 1966088 | tf_op jit(solution)/shard_map/ppermute | solution.py:442
  71.0 6.4 %collective-permute-start.9 = (bf16[40,256]{1,0:T(8,128)(2,1)S(1)}, bf16[40,256]{1,0:T(8,128)(2,1)S(1)}, u32[]{:S(2)}, u32[]{:S(2)}) collective-permute-start(bf16[40,256]{1,0:T(8,128)(2,1)S(1)} %get-tuple-element.103), channel_id=1, source_target_pairs={{0,2},{2,0},{4,6},{6,4},{8,10},{10,8},{12,14},{14,12},{1,3},{3,1},... | collective-permute-start | bytes 61448 | tf_op jit(solution)/shard_map/ppermute | solution.py:447
  77.4 7.0 %collective-permute-start.10 = (bf16[1280,256]{1,0:T(8,128)(2,1)S(1)}, bf16[1280,256]{1,0:T(8,128)(2,1)S(1)}, u32[]{:S(2)}, u32[]{:S(2)}) collective-permute-start(bf16[1280,256]{1,0:T(8,128)(2,1)S(1)} %get-tuple-element.104), channel_id=1, source_target_pairs={{0,1},{1,0},{2,3},{3,2},{4,5},{5,4},{6,7},{7,6},{8,9},{9,8},{10,11... | collective-permute-start | bytes 1966088 | tf_op jit(solution)/shard_map/ppermute | solution.py:442
  77.7 6.7 %collective-permute-start.11 = (bf16[1280,256]{1,0:T(8,128)(2,1)S(1)}, bf16[1280,256]{1,0:T(8,128)(2,1)S(1)}, u32[]{:S(2)}, u32[]{:S(2)}) collective-permute-start(bf16[1280,256]{1,0:T(8,128)(2,1)S(1)} %get-tuple-element.108), channel_id=1, source_target_pairs={{0,1},{1,0},{2,3},{3,2},{4,5},{5,4},{6,7},{7,6},{8,9},{9,8},{10,11... | collective-permute-start | bytes 1966088 | tf_op jit(solution)/shard_map/ppermute | solution.py:442
  78.0 40.0 %collective-permute-start.15 = (bf16[1280,256]{1,0:T(8,128)(2,1)S(1)}, bf16[1280,256]{1,0:T(8,128)(2,1)S(1)}, u32[]{:S(2)}, u32[]{:S(2)}) collective-permute-start(bf16[1280,256]{1,0:T(8,128)(2,1)S(1)} %get-tuple-element.104), channel_id=1, source_target_pairs={{2,1},{4,3},{6,5},{8,7},{10,9},{12,11},{14,13},{1,2},{3,4},{5,6},{... | collective-permute-start | bytes 1966088 | tf_op jit(solution)/shard_map/ppermute | solution.py:545
  81.6 42.6 %collective-permute-start.14 = (bf16[1280,256]{1,0:T(8,128)(2,1)S(1)}, bf16[1280,256]{1,0:T(8,128)(2,1)S(1)}, u32[]{:S(2)}, u32[]{:S(2)}) collective-permute-start(bf16[1280,256]{1,0:T(8,128)(2,1)S(1)} %get-tuple-element.112.refs_0_), channel_id=1, source_target_pairs={{2,0},{4,2},{6,4},{8,6},{10,8},{12,10},{14,12},{1,3},{3,5},{5,7},{... | collective-permute-start | bytes 1966088 | tf_op jit(solution)/shard_map/ppermute | solution.py:545
  89.0 35.2 %collective-permute-start.13 = (bf16[1280,256]{1,0:T(8,128)(2,1)S(1)}, bf16[1280,256]{1,0:T(8,128)(2,1)S(1)}, u32[]{:S(2)}, u32[]{:S(2)}) collective-permute-start(bf16[1280,256]{1,0:T(8,128)(2,1)S(1)} %get-tuple-element.111), channel_id=1, source_target_pairs={{0,1},{1,0},{2,3},{3,2},{4,5},{5,4},{6,7},{7,6},{8,9},{9,8},{10,11... | collective-permute-start | bytes 1966088 | tf_op jit(solution)/shard_map/ppermute | solution.py:442
  89.1 3.9 %collective-permute-start.12 = (bf16[80,256]{1,0:T(8,128)(2,1)S(1)}, bf16[80,256]{1,0:T(8,128)(2,1)S(1)}, u32[]{:S(2)}, u32[]{:S(2)}) collective-permute-start(bf16[80,256]{1,0:T(8,128)(2,1)S(1)} %constant_dynamic-update-slice_fusion.3), channel_id=1, source_target_pairs={{0,1},{1,0},{2,3},{3,2},{4,5},{5,4},{6,7},{7,6},{8,9},{9,8},{10,11... | collective-permute-start | bytes 122888 | tf_op jit(solution)/shard_map/ppermute | solution.py:442
  89.6 42.7 %collective-permute-start.20 = (bf16[1280,256]{1,0:T(8,128)(2,1)S(1)}, bf16[1280,256]{1,0:T(8,128)(2,1)S(1)}, u32[]{:S(2)}, u32[]{:S(2)}) collective-permute-start(bf16[1280,256]{1,0:T(8,128)(2,1)S(1)} %get-tuple-element.111), channel_id=1, source_target_pairs={{2,1},{4,3},{6,5},{8,7},{10,9},{12,11},{14,13},{1,2},{3,4},{5,6},{... | collective-permute-start | bytes 1966088 | tf_op jit(solution)/shard_map/ppermute | solution.py:545
  93.1 45.2 %collective-permute-start.19 = (bf16[1280,256]{1,0:T(8,128)(2,1)S(1)}, bf16[1280,256]{1,0:T(8,128)(2,1)S(1)}, u32[]{:S(2)}, u32[]{:S(2)}) collective-permute-start(bf16[1280,256]{1,0:T(8,128)(2,1)S(1)} %get-tuple-element.114.refs_2_), channel_id=1, source_target_pairs={{2,0},{4,2},{6,4},{8,6},{10,8},{12,10},{14,12},{1,3},{3,5},{5,7},{... | collective-permute-start | bytes 1966088 | tf_op jit(solution)/shard_map/ppermute | solution.py:545
  124.2 3.9 %collective-permute-start.18 = (bf16[80,512]{1,0:T(8,128)(2,1)S(1)}, bf16[80,512]{1,0:T(8,128)(2,1)S(1)}, u32[]{:S(2)}, u32[]{:S(2)}) collective-permute-start(bf16[80,512]{1,0:T(8,128)(2,1)S(1)} %pad_maximum_fusion.3), channel_id=1, source_target_pairs={{0,12},{2,14},{4,8},{6,10},{8,4},{10,6},{12,0},{14,2},{1,13},{3,15... | collective-permute-start | bytes 245768 | tf_op jit(solution)/shard_map/ppermute | solution.py:447
  125.5 3.6 %collective-permute-start.17 = (bf16[80,512]{1,0:T(8,128)(2,1)S(1)}, bf16[80,512]{1,0:T(8,128)(2,1)S(1)}, u32[]{:S(2)}, u32[]{:S(2)}) collective-permute-start(bf16[80,512]{1,0:T(8,128)(2,1)S(1)} %pad_maximum_fusion.3), channel_id=1, source_target_pairs={{0,4},{2,6},{4,0},{6,2},{8,12},{10,14},{12,8},{14,10},{1,5},{3,7},... | collective-permute-start | bytes 245768 | tf_op jit(solution)/shard_map/ppermute | solution.py:447
  125.5 4.8 %collective-permute-start.16 = (bf16[80,512]{1,0:T(8,128)(2,1)S(1)}, bf16[80,512]{1,0:T(8,128)(2,1)S(1)}, u32[]{:S(2)}, u32[]{:S(2)}) collective-permute-start(bf16[80,512]{1,0:T(8,128)(2,1)S(1)} %pad_maximum_fusion.3), channel_id=1, source_target_pairs={{0,8},{2,10},{4,12},{6,14},{8,0},{10,2},{12,4},{14,6},{1,9},{3,11}... | collective-permute-start | bytes 245768 | tf_op jit(solution)/shard_map/ppermute | solution.py:447
  140.5 3.4 %collective-permute-start.21 = (bf16[1280,256]{1,0:T(8,128)(2,1)S(1)}, bf16[1280,256]{1,0:T(8,128)(2,1)S(1)}, u32[]{:S(2)}, u32[]{:S(2)}) collective-permute-start(bf16[1280,256]{1,0:T(8,128)(2,1)S(1)} %get-tuple-element.121), channel_id=1, source_target_pairs={{0,1},{1,0},{2,3},{3,2},{4,5},{5,4},{6,7},{7,6},{8,9},{9,8},{10,11... | collective-permute-start | bytes 1966088 | tf_op jit(solution)/shard_map/ppermute | solution.py:442
  143.9 4.9 %collective-permute-start.22 = (bf16[1280,256]{1,0:T(8,128)(2,1)S(1)}, bf16[1280,256]{1,0:T(8,128)(2,1)S(1)}, u32[]{:S(2)}, u32[]{:S(2)}) collective-permute-start(bf16[1280,256]{1,0:T(8,128)(2,1)S(1)} %get-tuple-element.124), channel_id=1, source_target_pairs={{0,1},{1,0},{2,3},{3,2},{4,5},{5,4},{6,7},{7,6},{8,9},{9,8},{10,11... | collective-permute-start | bytes 1966088 | tf_op jit(solution)/shard_map/ppermute | solution.py:442
  148.4 4.2 %collective-permute-start.24 = (bf16[1280,512]{1,0:T(8,128)(2,1)S(1)}, bf16[1280,512]{1,0:T(8,128)(2,1)S(1)}, u32[]{:S(2)}, u32[]{:S(2)}) collective-permute-start(bf16[1280,512]{1,0:T(8,128)(2,1)S(1)} %get-tuple-element.129), channel_id=1, source_target_pairs={{0,1},{1,0},{2,3},{3,2},{4,5},{5,4},{6,7},{7,6},{8,9},{9,8},{10,11... | collective-permute-start | bytes 3932168 | tf_op jit(solution)/shard_map/ppermute | solution.py:442
  152.4 3.6 %collective-permute-start.23 = (bf16[1024,512]{1,0:T(8,128)(2,1)S(1)}, bf16[1024,512]{1,0:T(8,128)(2,1)S(1)}, u32[]{:S(2)}, u32[]{:S(2)}) collective-permute-start(bf16[1024,512]{1,0:T(8,128)(2,1)S(1)} %get-tuple-element.128), channel_id=1, source_target_pairs={{0,1},{1,0},{2,3},{3,2},{4,5},{5,4},{6,7},{7,6},{8,9},{9,8},{10,11... | collective-permute-start | bytes 3145736 | tf_op jit(solution)/shard_map/ppermute | solution.py:442
  154.4 1.6 %collective-permute-start.25 = (bf16[256,512]{1,0:T(8,128)(2,1)S(1)}, bf16[256,512]{1,0:T(8,128)(2,1)S(1)}, u32[]{:S(2)}, u32[]{:S(2)}) collective-permute-start(bf16[256,512]{1,0:T(8,128)(2,1)S(1)} %get-tuple-element.131), channel_id=1, source_target_pairs={{0,1},{1,0},{2,3},{3,2},{4,5},{5,4},{6,7},{7,6},{8,9},{9,8},{10,11... | collective-permute-start | bytes 786440 | tf_op jit(solution)/shard_map/ppermute | solution.py:442
